TPU v7x, 32 devices: a whole 2x2x4 slice. The times are simulated.
32 devices in a mesh: groups: 2 (over y), dp: 16 (over z, x, core).
Axes of the slice: x: 2, y: 2, z: 4, core: 2. Of those that a mesh axis runs over, the one named last changes fastest.
Arguments:
- merger_input: bfloat16 [3072, 2304], P(('groups', 'dp')), parts along dimension 0, may hold values from -6 to 6
- merger_weight: bfloat16 [2304, 2048], P('dp'), may hold values from -0.125 to 0.125
- merger_bias: float32 [2048], replicated, may hold values from -3 to 3
- norm_gain: float32 [2048], replicated, may hold values from 0.5 to 1.5
- gate_weight: bfloat16 [16, 2048, 768], P('dp'), may hold values from -0.125 to 0.125
- up_weight: bfloat16 [16, 2048, 768], P('dp'), may hold values from -0.125 to 0.125
- down_weight: bfloat16 [16, 768, 2048], P('dp'), may hold values from -0.21875 to 0.21875
- expert_ids: int32 [3072, 8], P(('groups', 'dp')), parts along dimension 0, may hold values from 0 to 15, all different within a row; in each aligned block of 96 rows (0 to 95, 96 to 191, ...) at most 72 rows name the same one
- combine_ints: int32 [3072, 8], P(('groups', 'dp')), parts along dimension 0, may hold values from 1 to 16
Outputs:
- mixed: bfloat16 [3072, 2048], P(('groups', 'dp')), parts along dimension 0
There are 2 independent parts, one for each index of `groups`. A program takes and returns all parts, laid end to end along the dimension named above; an argument that names none is the same for every part. Nothing has to cross between parts.
Inputs may be any that keep to these rules, and one draw needn't show every extreme that they name: `expert_ids`: each row names 8 different experts; in the rows of one device no expert is named more than 72 times, and that many is reached.
All inputs are finite; a program needn't handle non-finite values.
Results may differ from a plain program's by a relative error of at most 0.0051.
Values may be sent and summed in bfloat16 or wider, within the bound.
No kernel may reach another device: no remote copies, remote signals or barrier semaphores. Data moves between devices by JAX's collectives and lax.ppermute only.
A program may use at most 128 MiB of HBM per device.

v0:
```python
import functools

import jax
import jax.numpy as jnp
from jax import lax
from jax.experimental import pallas as pl
from jax.experimental.pallas import tpu as pltpu
from jax.sharding import PartitionSpec as P


LANES = 128
MIB = 1024 * 1024
PARTS = 2
DP = "dp"
GROUPS = "groups"
VMEM = pl.BlockSpec(memory_space=pltpu.VMEM)


def run_experts(received, gate_weight, up_weight, down_weight, ndevices):
    local = gate_weight.shape[0]
    slots = received.shape[1]
    width = received.shape[2]
    inputs = received.reshape(ndevices, local, slots, width)
    gate = jnp.einsum("jlcd,ldh->jlch", inputs, gate_weight, preferred_element_type=jnp.float32)
    up = jnp.einsum("jlcd,ldh->jlch", inputs, up_weight, preferred_element_type=jnp.float32)
    hidden = (jax.nn.silu(gate) * up).astype(jnp.bfloat16)
    output = jnp.einsum("jlch,lhd->jlcd", hidden, down_weight, preferred_element_type=jnp.float32)
    return output.astype(jnp.bfloat16).reshape(ndevices * local, slots, width)


def routed(
    merger_input,
    merger_weight,
    merger_bias,
    norm_gain,
    gate_weight,
    up_weight,
    down_weight,
    expert_ids,
    combine_ints,
):
    ndevices = lax.axis_size("dp")
    rows = merger_input.shape[0]
    width = merger_weight.shape[1]
    choose = expert_ids.shape[1]
    experts_all = gate_weight.shape[0] * ndevices
    capacity = (3 * rows * choose + 2 * ndevices - 1) // (2 * ndevices)
    act = jax.nn.gelu(merger_input.astype(jnp.float32), approximate=False).astype(jnp.bfloat16)
    merged = jnp.dot(
        act,
        lax.all_gather(merger_weight, "dp", axis=0, tiled=True),
        preferred_element_type=jnp.float32,
    )
    merged = merged + merger_bias
    scale = lax.rsqrt(jnp.mean(merged * merged, axis=1, keepdims=True) + 1e-06)
    normed = (merged * scale * norm_gain).astype(jnp.bfloat16)
    onehot = (
        expert_ids[:, :, None] == jnp.arange(experts_all, dtype=jnp.int32)[None, None, :]
    ).astype(jnp.int32)
    flat_hot = onehot.reshape(rows * choose, experts_all)
    before = jnp.cumsum(flat_hot, axis=0) - flat_hot
    position = jnp.sum(before * flat_hot, axis=1)
    slot_flat = expert_ids.reshape(rows * choose) * capacity + position
    repeated = jnp.repeat(normed, choose, axis=0)
    outgoing = jnp.zeros((experts_all * capacity, width), jnp.bfloat16).at[slot_flat].set(repeated)
    outgoing = outgoing.reshape(experts_all, capacity, width)
    received = lax.all_to_all(outgoing, "dp", split_axis=0, concat_axis=0, tiled=True)
    served = run_experts(received, gate_weight, up_weight, down_weight, ndevices)
    returned = lax.all_to_all(served, "dp", split_axis=0, concat_axis=0, tiled=True)
    returned = returned.reshape(experts_all * capacity, width)
    picked = returned[slot_flat].reshape(rows, choose, width)
    counts = combine_ints.astype(jnp.float32)
    weights = counts / jnp.sum(counts, axis=1, keepdims=True)
    combined = jnp.sum(weights[:, :, None] * picked.astype(jnp.float32), axis=1)
    return (merged + combined).astype(jnp.bfloat16)


def swap_pairs(n):
    return [(i, i ^ 1) for i in range(n)]


def ring_order(chips):
    half = chips // 2
    return [2 * z for z in range(half)] + [2 * z + 1 for z in reversed(range(half))]


def ring_pairs(chips, by):
    order = ring_order(chips)
    pairs = []
    for spot, chip in enumerate(order):
        target = order[(spot + by) % chips]
        pairs += [(2 * chip, 2 * target), (2 * chip + 1, 2 * target + 1)]
    return pairs


def chip_at(chips, offset):
    chip = lax.axis_index(DP) // 2
    spot = jnp.where(chip % 2 == 0, chip // 2, chips - 1 - chip // 2)
    spot = lax.rem(spot + offset, chips)
    return jnp.where(spot < chips // 2, 2 * spot, 2 * (chips - 1 - spot) + 1)


def tile_of(extent, most):
    return max(t for t in range(LANES, most + 1, LANES) if extent % t == 0)


def kernel(body, outs, ins, scratch=(), limit=12 * MIB, flops=0, moved=0):
    return pl.pallas_call(
        body,
        out_shape=outs,
        in_specs=[VMEM] * len(ins),
        out_specs=jax.tree.map(lambda _: VMEM, outs),
        scratch_shapes=list(scratch),
        compiler_params=pltpu.CompilerParams(vmem_limit_bytes=limit),
        cost_estimate=pl.CostEstimate(flops=flops, bytes_accessed=moved, transcendentals=0),
    )(*ins)


def shaped(rows, width, dtype=jnp.bfloat16):
    return jax.ShapeDtypeStruct((rows, width), dtype)


def serve_body(blocks, *refs):
    ins = refs[:blocks]
    gate_ref, up_ref, down_ref, own_ref, other_ref, x_ref, h_ref = refs[blocks:]
    width, wide = gate_ref.shape
    expert = lax.axis_index(DP)
    start = 0
    share = []
    for ref in ins:
        size = ref.shape[0]
        x_ref[start : start + size, :] = ref[:, :width]
        tags = ref[:, width:].astype(jnp.float32)
        mine = lax.broadcasted_iota(jnp.int32, tags.shape, 1) == expert
        chosen = jnp.sum(jnp.where(mine, tags, 0.0), axis=1, keepdims=True)
        share.append(chosen / jnp.sum(tags, axis=1, keepdims=True))
        start += size
    share = jnp.concatenate(share, axis=0)
    tile = tile_of(wide, 256)
    for at in range(0, wide, tile):
        x = x_ref[...]
        gate = jnp.dot(x, gate_ref[:, at : at + tile], preferred_element_type=jnp.float32)
        up = jnp.dot(x, up_ref[:, at : at + tile], preferred_element_type=jnp.float32)
        h_ref[:, at : at + tile] = (gate * (1.0 / (1.0 + jnp.exp(-gate))) * up * share).astype(jnp.bfloat16)
    half = start // 2
    tile = tile_of(width, 512)
    for at in range(0, width, tile):
        out = jnp.dot(h_ref[...], down_ref[:, at : at + tile], preferred_element_type=jnp.float32)
        own_ref[:, at : at + tile] = out[:half].astype(jnp.bfloat16)
        other_ref[:, at : at + tile] = out[half:].astype(jnp.bfloat16)


def serve(ins, experts):
    rows = sum(x.shape[0] for x in ins)
    width, wide = experts[0].shape
    return kernel(
        functools.partial(serve_body, len(ins)),
        [shaped(rows // 2, width)] * 2,
        [*ins, *experts],
        [pltpu.VMEM((rows, width), jnp.bfloat16), pltpu.VMEM((rows, wide), jnp.bfloat16)],
        24 * MIB,
        6 * rows * width * wide,
        6 * width * wide,
    )


def tag_body(ids_ref, counts_ref, out_ref):
    rows, lanes = out_ref.shape
    expert = lax.broadcasted_iota(jnp.int32, (lanes, rows), 0)
    total = jnp.zeros((lanes, rows), jnp.float32)
    for k in range(ids_ref.shape[0]):
        total += jnp.where(expert == ids_ref[k : k + 1, :], counts_ref[k : k + 1, :].astype(jnp.float32), 0.0)
    out_ref[...] = total.T.astype(jnp.bfloat16)


def bulk_body(chips, offsets, act_ref, *refs):
    pieces, out_ref = refs[:-1], refs[-1]
    width = out_ref.shape[1]
    tile = tile_of(width, 512)
    for at in range(0, width, tile):
        total = None
        for offset, piece in zip(offsets, pieces):
            act = act_ref[chip_at(chips, offset)]
            part = jnp.dot(act, piece[:, at : at + tile], preferred_element_type=jnp.float32)
            total = part if total is None else total + part
        out_ref[:, at : at + tile] = total


def last_body(chips, act_ref, total_ref, top_ref, bottom_ref, *outs):
    width = total_ref.shape[1]
    mid = top_ref.shape[0]
    rows = outs[0].shape[0]
    tile = tile_of(width, 512)
    act = act_ref[chip_at(chips, chips // 2)]
    for at in range(0, width, tile):
        to = at + tile
        total = total_ref[:, at:to]
        total += jnp.dot(act[:, :mid], top_ref[:, at:to], preferred_element_type=jnp.float32)
        total += jnp.dot(act[:, mid:], bottom_ref[:, at:to], preferred_element_type=jnp.float32)
        for index, out in enumerate(outs):
            out[:, at:to] = total[index * rows : (index + 1) * rows]


def norm_body(parts, *refs):
    bias_ref, gain_ref, tags_ref, merged_ref, low_ref, high_ref = refs[3 * parts :]
    width = merged_ref.shape[1]
    cut = low_ref.shape[0]
    low_ref[:, width:] = tags_ref[:cut, :]
    high_ref[:, width:] = tags_ref[cut:, :]
    at = 0
    square = 0.0
    for index in range(parts):
        own_ref, other_ref, cross_ref = refs[3 * index : 3 * index + 3]
        to = at + own_ref.shape[1]
        merged = own_ref[...] + other_ref[...] + bias_ref[:, at:to] + cross_ref[...].astype(jnp.float32)
        merged_ref[:, at:to] = merged
        square += jnp.sum(merged * merged, axis=1, keepdims=True)
        at = to
    scale = lax.rsqrt(square / width + 1e-06)
    low_ref[:, :width] = (merged_ref[:cut, :] * scale[:cut] * gain_ref[...]).astype(jnp.bfloat16)
    high_ref[:, :width] = (merged_ref[cut:, :] * scale[cut:] * gain_ref[...]).astype(jnp.bfloat16)


def plus_body(*refs):
    refs[-1][...] = (refs[0][...] + refs[1][...]).astype(refs[-1].dtype)


def add_body(at, own_ref, other_ref, *refs):
    out_ref = refs[-1]
    size = out_ref.shape[0]
    total = own_ref[at : at + size, :].astype(jnp.float32) + other_ref[at : at + size, :].astype(jnp.float32)
    for ref in refs[:-1]:
        total += ref[...].astype(jnp.float32)
    out_ref[...] = total.astype(jnp.bfloat16)


def add(own, other, at, size, total=None):
    ins = [own, other] + ([] if total is None else [total])
    return kernel(functools.partial(add_body, at), shaped(size, own.shape[1]), ins)


def finish_body(merged_ref, *refs):
    out_ref = refs[-1]
    at = 0
    for index in range(0, len(refs) - 1, 4):
        ins = refs[index : index + 4]
        to = at + ins[0].shape[0]
        total = sum(ref[...].astype(jnp.float32) for ref in ins)
        out_ref[at:to, :] = (merged_ref[at:to, :] + total).astype(jnp.bfloat16)
        at = to


def dense(
    merger_input,
    merger_weight,
    merger_bias,
    norm_gain,
    gate_weight,
    up_weight,
    down_weight,
    expert_ids,
    combine_ints,
):
    n = lax.axis_size(DP)
    chips = n // 2
    far = chips // 2
    rows = merger_input.shape[0]
    depth, width = merger_weight.shape
    half = depth // 2
    cut = rows // 2
    first_core = lax.axis_index(DP) % 2 == 0
    first_group = lax.axis_index(GROUPS) == 0

    swap = functools.partial(lax.ppermute, axis_name=DP, perm=swap_pairs(n))
    cross = functools.partial(lax.ppermute, axis_name=GROUPS, perm=swap_pairs(2))
    rings = [functools.partial(lax.ppermute, axis_name=DP, perm=ring_pairs(chips, by)) for by in (1, -1)]

    def hop(way, array):
        return rings[way](array)

    zero = jnp.uint32(0)
    weight = lax.dynamic_slice(merger_weight, (lax.axis_index(GROUPS).astype(jnp.uint32) * half, zero), (half, width))
    act = jax.nn.gelu(merger_input.astype(jnp.float32), approximate=False).astype(jnp.bfloat16)
    act = act.reshape(rows, chips, 2, 2, half)
    kept = jnp.where(first_core, act[:, :, 0], act[:, :, 1])
    given = jnp.where(first_core, act[:, :, 1], act[:, :, 0])
    given = swap(given)
    act = jnp.concatenate([kept, given], axis=0)
    kept = jnp.where(first_group, act[:, :, 0], act[:, :, 1])
    given = jnp.where(first_group, act[:, :, 1], act[:, :, 0])
    given = cross(given)
    act = jnp.concatenate([kept, given], axis=0).transpose(1, 0, 2)

    lanes = -(-n // LANES) * LANES
    tags = kernel(tag_body, shaped(rows, lanes), [expert_ids.T, combine_ints.T])

    mid = (half + 15) // 16 * 8
    share = width // PARTS
    streams = []
    for part in range(PARTS):
        left = right = weight[:, part * share : (part + 1) * share]
        offsets, pieces = [0], [left]
        for step in range(1, far):
            left, right = hop(0, left), hop(1, right)
            offsets += [chips - step, step]
            pieces += [left, right]
        top, bottom = hop(0, left[:mid]), hop(1, right[mid:])
        size = 4 * rows * share
        total = kernel(
            functools.partial(bulk_body, chips, offsets),
            shaped(4 * rows, share, jnp.float32),
            [act, *pieces],
            flops=2 * size * half * chips,
            moved=4 * size,
        )
        own, own_other, theirs, theirs_other = kernel(
            functools.partial(last_body, chips),
            [shaped(rows, share, jnp.float32)] * 4,
            [act, total, top, bottom],
            flops=2 * size * half,
            moved=8 * size,
        )
        theirs = kernel(plus_body, shaped(rows, share), [theirs, swap(theirs_other)])
        theirs = cross(theirs)
        streams += [own, swap(own_other), theirs]
    merged, *block = kernel(
        functools.partial(norm_body, PARTS),
        [shaped(rows, width, jnp.float32)] + [shaped(cut, width + lanes)] * 2,
        [*streams, merger_bias[None], norm_gain[None], tags],
    )

    experts = [w[0] for w in (gate_weight, up_weight, down_weight)]
    arrived = [[(own,) for own in block]]
    sides = [(own, own) for own in block]
    for _ in range(1, far):
        sides = [tuple(hop(way, side[way]) for way in (0, 1)) for side in sides]
        arrived.append(sides)
    distant = hop(0, sides[0][0]), hop(1, sides[1][1])

    def served(ins):
        others = [swap(x) for x in ins]
        own, other = serve([*ins, *others], experts)
        return own, swap(other)

    outs = [[served(ins) for ins in pair] for pair in arrived]
    distant = served(distant)

    def home(way, which, at, total):
        for step in reversed(range(1, far)):
            total = add(*outs[step][which], at, cut, total)
            total = hop(way, total)
        return total

    near = home(0, 1, cut, None), home(1, 0, 0, None)
    top, bottom = (hop(way, add(*distant, way * cut, cut)) for way in (0, 1))
    top, bottom = home(0, 0, cut, top), home(1, 1, 0, bottom)
    ins = [merged, *outs[0][0], top, near[1], *outs[0][1], near[0], bottom]
    return kernel(finish_body, shaped(rows, width), ins)


def shards(*arrays):
    gate_weight, expert_ids = arrays[4], arrays[7]
    n = lax.axis_size(DP)
    rows, choose = expert_ids.shape
    capacity = (3 * rows * choose + 2 * n - 1) // (2 * n)
    if lax.axis_size(GROUPS) == 2 and gate_weight.shape[0] == 1 and n % 4 == 0 and n >= 16 and 2 * capacity >= rows:
        return dense(*arrays)
    return routed(*arrays)


def solution(mesh):
    placed = (
        P(("groups", "dp"), None),
        P("dp", None),
        P(),
        P(),
        P("dp", None, None),
        P("dp", None, None),
        P("dp", None, None),
        P(("groups", "dp"), None),
        P(("groups", "dp"), None),
    )
    return jax.shard_map(
        shards, mesh=mesh, in_specs=placed, out_specs=P(("groups", "dp"), None), check_vma=False
    )
```

profile of v0, /device:TPU:0, one launch (start us, length us, event | category | flops | bytes accessed | tf_op | source)
XLA Modules:
  0.0 139.6 jit_solution(4051119610148133314)
XLA Ops:
  0.0 1.3 copy.10
  1.3 2.6 %fusion.1 = bf16[96,2304]{0,1:T(8,128)(2,1)S(1)} fusion(bf16[96,2304]{0,1:T(8,128)(2,1)S(1)} %copy.10), kind=kLoop, calls=%fused_computation.4 | loop fusion | flops 14598144 | bytes 884736 | tf_op jit(solution)/shard_map/convert_element_type | solution.py:283
  5.4 3.1 %collective-permute-start.2 = (bf16[72,1024]{1,0:T(8,128)(2,1)S(1)}, bf16[72,1024]{1,0:T(8,128)(2,1)S(1)}, u32[]{:S(2)}, u32[]{:S(2)}) collective-permute-start(bf16[72,1024]{1,0:T(8,128)(2,1)S(1)} %get-tuple-element.68.refs_0_), channel_id=1, source_target_pairs={{0,4},{1,5},{4,8},{5,9},{8,12},{9,13},{12,14},{13,15},{14,10},{15,... | collective-permute-start | bytes 442376 | tf_op jit(solution)/shard_map/ppermute | solution.py:279
  8.5 2.0 %collective-permute-start.13 = (bf16[72,1024]{1,0:T(8,128)(2,1)S(1)}, bf16[72,1024]{1,0:T(8,128)(2,1)S(1)}, u32[]{:S(2)}, u32[]{:S(2)}) collective-permute-start(bf16[72,1024]{1,0:T(8,128)(2,1)S(1)} %get-tuple-element.67.refs_0_), channel_id=1, source_target_pairs={{0,4},{1,5},{4,8},{5,9},{8,12},{9,13},{12,14},{13,15},{14,10},{15,... | collective-permute-start | bytes 442376 | tf_op jit(solution)/shard_map/ppermute | solution.py:279
  10.6 2.6 %collective-permute-done.2.refs_1_ = bf16[72,1024]{1,0:T(8,128)(2,1)S(1)} collective-permute-done((bf16[72,1024]{1,0:T(8,128)(2,1)S(1)}, bf16[72,1024]{1,0:T(8,128)(2,1)S(1)}, u32[]{:S(2)}, u32[]{:S(2)}) %collective-permute-start.2) | collective-permute-done | bytes 147488 | tf_op jit(solution)/shard_map/ppermute | solution.py:279
  13.1 2.1 %collective-permute-start.4 = (bf16[72,1024]{1,0:T(8,128)(2,1)S(1)}, bf16[72,1024]{1,0:T(8,128)(2,1)S(1)}, u32[]{:S(2)}, u32[]{:S(2)}) collective-permute-start(bf16[72,1024]{1,0:T(8,128)(2,1)S(1)} %collective-permute-done.2.refs_1_), channel_id=1, source_target_pairs={{0,4},{1,5},{4,8},{5,9},{8,12},{9,13},{12,14},{13,15},{14,10},{15,... | collective-permute-start | bytes 442376 | tf_op jit(solution)/shard_map/ppermute | solution.py:279
  15.2 1.0 collective-permute-done.13.refs_1_
  16.3 2.1 %collective-permute-start.15 = (bf16[72,1024]{1,0:T(8,128)(2,1)S(1)}, bf16[72,1024]{1,0:T(8,128)(2,1)S(1)}, u32[]{:S(2)}, u32[]{:S(2)}) collective-permute-start(bf16[72,1024]{1,0:T(8,128)(2,1)S(1)} %collective-permute-done.13.refs_1_), channel_id=1, source_target_pairs={{0,4},{1,5},{4,8},{5,9},{8,12},{9,13},{12,14},{13,15},{14,10},{15,... | collective-permute-start | bytes 442376 | tf_op jit(solution)/shard_map/ppermute | solution.py:279
  18.7 2.0 %collective-permute-start.1 = (bf16[192,8,72]{2,0,1:T(8,128)(2,1)S(1)}, bf16[192,8,72]{2,0,1:T(8,128)(2,1)S(1)}, u32[]{:S(2)}, u32[]{:S(2)}) collective-permute-start(bf16[192,8,72]{2,0,1:T(8,128)(2,1)S(1)} %get-tuple-element.64), channel_id=1, source_target_pairs={{0,16},{16,0},{1,17},{17,1},{2,18},{18,2},{3,19},{19,3},{4,20},{20... | collective-permute-start | bytes 663560 | tf_op jit(solution)/shard_map/ppermute | solution.py:291
  20.7 1.6 %collective-permute-start.6 = (bf16[72,1024]{1,0:T(8,128)(2,1)S(1)}, bf16[72,1024]{1,0:T(8,128)(2,1)S(1)}, u32[]{:S(2)}, u32[]{:S(2)}) collective-permute-start(bf16[72,1024]{1,0:T(8,128)(2,1)S(1)} %collective-permute-done.4.refs_3_), channel_id=1, source_target_pairs={{0,4},{1,5},{4,8},{5,9},{8,12},{9,13},{12,14},{13,15},{14,10},{15,... | collective-permute-start | bytes 442376 | tf_op jit(solution)/shard_map/ppermute | solution.py:279
  23.0 2.1 %collective-permute-start.17 = (bf16[72,1024]{1,0:T(8,128)(2,1)S(1)}, bf16[72,1024]{1,0:T(8,128)(2,1)S(1)}, u32[]{:S(2)}, u32[]{:S(2)}) collective-permute-start(bf16[72,1024]{1,0:T(8,128)(2,1)S(1)} %collective-permute-done.15.refs_3_), channel_id=1, source_target_pairs={{0,4},{1,5},{4,8},{5,9},{8,12},{9,13},{12,14},{13,15},{14,10},{15,... | collective-permute-start | bytes 442376 | tf_op jit(solution)/shard_map/ppermute | solution.py:279
  25.1 1.8 %collective-permute-done.6.refs_5_ = bf16[72,1024]{1,0:T(8,128)(2,1)S(1)} collective-permute-done((bf16[72,1024]{1,0:T(8,128)(2,1)S(1)}, bf16[72,1024]{1,0:T(8,128)(2,1)S(1)}, u32[]{:S(2)}, u32[]{:S(2)}) %collective-permute-start.6) | collective-permute-done | bytes 147488 | tf_op jit(solution)/shard_map/ppermute | solution.py:279
  27.0 1.8 %collective-permute-start.8 = (bf16[40,1024]{1,0:T(8,128)(2,1)S(1)}, bf16[40,1024]{1,0:T(8,128)(2,1)S(1)}, u32[]{:S(2)}, u32[]{:S(2)}) collective-permute-start(bf16[40,1024]{1,0:T(8,128)(2,1)S(1)} %slice.48), channel_id=1, source_target_pairs={{0,4},{1,5},{4,8},{5,9},{8,12},{9,13},{12,14},{13,15},{14,10},{15,... | collective-permute-start | bytes 245768 | tf_op jit(solution)/shard_map/ppermute | solution.py:279
  29.4 1.8 %collective-permute-start.19 = (bf16[40,1024]{1,0:T(8,128)(2,1)S(1)}, bf16[40,1024]{1,0:T(8,128)(2,1)S(1)}, u32[]{:S(2)}, u32[]{:S(2)}) collective-permute-start(bf16[40,1024]{1,0:T(8,128)(2,1)S(1)} %slice.50), channel_id=1, source_target_pairs={{0,4},{1,5},{4,8},{5,9},{8,12},{9,13},{12,14},{13,15},{14,10},{15,... | collective-permute-start | bytes 245768 | tf_op jit(solution)/shard_map/ppermute | solution.py:279
  31.6 1.6 %shard_map.91.total_ref = f32[384,1024]{1,0:T(8,128)S(1)} custom-call(bf16[8,384,72]{2,1,0:T(8,128)(2,1)S(1)} %maximum_bitcast_fusion.act_ref, bf16[72,1024]{1,0:T(8,128)(2,1)S(1)} %get-tuple-element.68.refs_0_, bf16[72,1024]{1,0:T(8,128)(2,1)S(1)} %collective-permute-done.2.refs_1_, bf16[72,1024]{1,0:T(8,128)(2,1)S(1)} %collective-permute-done.3.refs_2_, ...), custom_call_target="tpu_custom_call" | custom-call | flops 452984832 | bytes 1572864 | tf_op jit(solution)/shard_map/pallas_call | solution.py:108
  33.2 1.6 %shard_map.94.total_ref = f32[384,1024]{1,0:T(8,128)S(1)} custom-call(bf16[8,384,72]{2,1,0:T(8,128)(2,1)S(1)} %maximum_bitcast_fusion.act_ref, bf16[72,1024]{1,0:T(8,128)(2,1)S(1)} %get-tuple-element.67.refs_0_, bf16[72,1024]{1,0:T(8,128)(2,1)S(1)} %collective-permute-done.13.refs_1_, bf16[72,1024]{1,0:T(8,128)(2,1)S(1)} %collective-permute-done.14.refs_2_, ...), custom_call_target="tpu_custom_call" | custom-call | flops 452984832 | bytes 1572864 | tf_op jit(solution)/shard_map/pallas_call | solution.py:108
  34.8 0.6 shard_map.92
  37.2 1.5 %collective-permute-start.12 = (bf16[96,1024]{1,0:T(8,128)(2,1)S(1)}, bf16[96,1024]{1,0:T(8,128)(2,1)S(1)}, u32[]{:S(2)}, u32[]{:S(2)}) collective-permute-start(bf16[96,1024]{1,0:T(8,128)(2,1)S(1)} %shard_map.93), channel_id=1, source_target_pairs={{0,16},{16,0},{1,17},{17,1},{2,18},{18,2},{3,19},{19,3},{4,20},{20... | collective-permute-start | bytes 589832 | tf_op jit(solution)/shard_map/ppermute | solution.py:324
  38.8 0.8 collective-permute-start.23
  39.7 5.3 %collective-permute-done.12.refs_2_ = bf16[96,1024]{1,0:T(8,128)(2,1)S(1)} collective-permute-done((bf16[96,1024]{1,0:T(8,128)(2,1)S(1)}, bf16[96,1024]{1,0:T(8,128)(2,1)S(1)}, u32[]{:S(2)}, u32[]{:S(2)}) %collective-permute-start.12) | collective-permute-done | bytes 196640 | tf_op jit(solution)/shard_map/ppermute | solution.py:324
  45.0 3.4 %collective-permute-done.23.refs_5_ = bf16[96,1024]{1,0:T(8,128)(2,1)S(1)} collective-permute-done((bf16[96,1024]{1,0:T(8,128)(2,1)S(1)}, bf16[96,1024]{1,0:T(8,128)(2,1)S(1)}, u32[]{:S(2)}, u32[]{:S(2)}) %collective-permute-start.23) | collective-permute-done | bytes 196640 | tf_op jit(solution)/shard_map/ppermute | solution.py:324
  48.7 1.9 %collective-permute-start.26 = (bf16[48,2176]{1,0:T(8,128)(2,1)S(1)}, bf16[48,2176]{1,0:T(8,128)(2,1)S(1)}, u32[]{:S(2)}, u32[]{:S(2)}) collective-permute-start(bf16[48,2176]{1,0:T(8,128)(2,1)S(1)} %get-tuple-element.43.refs_0_), channel_id=1, source_target_pairs={{0,4},{1,5},{4,8},{5,9},{8,12},{9,13},{12,14},{13,15},{14,10},{15,... | collective-permute-start | bytes 626696 | tf_op jit(solution)/shard_map/ppermute | solution.py:279
  50.8 1.7 %collective-permute-start.42 = (bf16[48,2176]{1,0:T(8,128)(2,1)S(1)}, bf16[48,2176]{1,0:T(8,128)(2,1)S(1)}, u32[]{:S(2)}, u32[]{:S(2)}) collective-permute-start(bf16[48,2176]{1,0:T(8,128)(2,1)S(1)} %get-tuple-element.52.refs_0_), channel_id=1, source_target_pairs={{0,2},{1,3},{4,0},{5,1},{8,4},{9,5},{12,8},{13,9},{14,12},{15,13},... | collective-permute-start | bytes 626696 | tf_op jit(solution)/shard_map/ppermute | solution.py:279
  52.8 3.9 %collective-permute-done.26.refs_0_ = bf16[48,2176]{1,0:T(8,128)(2,1)S(1)} collective-permute-done((bf16[48,2176]{1,0:T(8,128)(2,1)S(1)}, bf16[48,2176]{1,0:T(8,128)(2,1)S(1)}, u32[]{:S(2)}, u32[]{:S(2)}) %collective-permute-start.26) | collective-permute-done | bytes 208928 | tf_op jit(solution)/shard_map/ppermute | solution.py:279
  56.7 1.9 %collective-permute-start.31 = (bf16[48,2176]{1,0:T(8,128)(2,1)S(1)}, bf16[48,2176]{1,0:T(8,128)(2,1)S(1)}, u32[]{:S(2)}, u32[]{:S(2)}) collective-permute-start(bf16[48,2176]{1,0:T(8,128)(2,1)S(1)} %collective-permute-done.26.refs_0_), channel_id=1, source_target_pairs={{0,4},{1,5},{4,8},{5,9},{8,12},{9,13},{12,14},{13,15},{14,10},{15,... | collective-permute-start | bytes 626696 | tf_op jit(solution)/shard_map/ppermute | solution.py:279
  58.9 4.3 %collective-permute-done.42.refs_1_ = bf16[48,2176]{1,0:T(8,128)(2,1)S(1)} collective-permute-done((bf16[48,2176]{1,0:T(8,128)(2,1)S(1)}, bf16[48,2176]{1,0:T(8,128)(2,1)S(1)}, u32[]{:S(2)}, u32[]{:S(2)}) %collective-permute-start.42) | collective-permute-done | bytes 208928 | tf_op jit(solution)/shard_map/ppermute | solution.py:279
  63.3 1.8 %collective-permute-start.62 = (bf16[48,2176]{1,0:T(8,128)(2,1)S(1)}, bf16[48,2176]{1,0:T(8,128)(2,1)S(1)}, u32[]{:S(2)}, u32[]{:S(2)}) collective-permute-start(bf16[48,2176]{1,0:T(8,128)(2,1)S(1)} %collective-permute-done.58.refs_0_), channel_id=1, source_target_pairs={{0,4},{1,5},{4,8},{5,9},{8,12},{9,13},{12,14},{13,15},{14,10},{15,... | collective-permute-start | bytes 626696 | tf_op jit(solution)/shard_map/ppermute | solution.py:279
  65.2 2.4 %collective-permute-start.36 = (bf16[48,2176]{1,0:T(8,128)(2,1)S(1)}, bf16[48,2176]{1,0:T(8,128)(2,1)S(1)}, u32[]{:S(2)}, u32[]{:S(2)}) collective-permute-start(bf16[48,2176]{1,0:T(8,128)(2,1)S(1)} %collective-permute-done.31.refs_0_), channel_id=1, source_target_pairs={{0,4},{1,5},{4,8},{5,9},{8,12},{9,13},{12,14},{13,15},{14,10},{15,... | collective-permute-start | bytes 626696 | tf_op jit(solution)/shard_map/ppermute | solution.py:279
  67.8 4.3 %collective-permute-done.43.refs_1_ = bf16[48,2176]{1,0:T(8,128)(2,1)S(1)} collective-permute-done((bf16[48,2176]{1,0:T(8,128)(2,1)S(1)}, bf16[48,2176]{1,0:T(8,128)(2,1)S(1)}, u32[]{:S(2)}, u32[]{:S(2)}) %collective-permute-start.43) | collective-permute-done | bytes 208928 | tf_op jit(solution)/shard_map/ppermute | solution.py:279
  72.3 1.8 %collective-permute-start.66 = (bf16[48,2176]{1,0:T(8,128)(2,1)S(1)}, bf16[48,2176]{1,0:T(8,128)(2,1)S(1)}, u32[]{:S(2)}, u32[]{:S(2)}) collective-permute-start(bf16[48,2176]{1,0:T(8,128)(2,1)S(1)} %collective-permute-done.62.refs_0_), channel_id=1, source_target_pairs={{0,4},{1,5},{4,8},{5,9},{8,12},{9,13},{12,14},{13,15},{14,10},{15,... | collective-permute-start | bytes 626696 | tf_op jit(solution)/shard_map/ppermute | solution.py:279
  74.4 2.1 %collective-permute-done.37.refs_1_ = bf16[48,2176]{1,0:T(8,128)(2,1)S(1)} collective-permute-done((bf16[48,2176]{1,0:T(8,128)(2,1)S(1)}, bf16[48,2176]{1,0:T(8,128)(2,1)S(1)}, u32[]{:S(2)}, u32[]{:S(2)}) %collective-permute-start.37) | collective-permute-done | bytes 208928 | tf_op jit(solution)/shard_map/ppermute | solution.py:279
  76.6 1.6 %collective-permute-start.41 = (bf16[48,2176]{1,0:T(8,128)(2,1)S(1)}, bf16[48,2176]{1,0:T(8,128)(2,1)S(1)}, u32[]{:S(2)}, u32[]{:S(2)}) collective-permute-start(bf16[48,2176]{1,0:T(8,128)(2,1)S(1)} %collective-permute-done.36.refs_0_), channel_id=1, source_target_pairs={{0,4},{1,5},{4,8},{5,9},{8,12},{9,13},{12,14},{13,15},{14,10},{15,... | collective-permute-start | bytes 626696 | tf_op jit(solution)/shard_map/ppermute | solution.py:279
  78.1 0.9 collective-permute-done.44.refs_1_
  79.9 4.2 %collective-permute-done.41.refs_0_ = bf16[48,2176]{1,0:T(8,128)(2,1)S(1)} collective-permute-done((bf16[48,2176]{1,0:T(8,128)(2,1)S(1)}, bf16[48,2176]{1,0:T(8,128)(2,1)S(1)}, u32[]{:S(2)}, u32[]{:S(2)}) %collective-permute-start.41) | collective-permute-done | bytes 208928 | tf_op jit(solution)/shard_map/ppermute | solution.py:279
  84.1 1.3 collective-permute-done.45.refs_1_
  85.4 2.1 %shard_map.102 = (bf16[96,2048]{1,0:T(8,128)(2,1)S(1)}, bf16[96,2048]{1,0:T(8,128)(2,1)S(1)}) custom-call(bf16[48,2176]{1,0:T(8,128)(2,1)S(1)} %collective-permute-done.36.refs_0_, bf16[48,2176]{1,0:T(8,128)(2,1)S(1)} %collective-permute-done.37.refs_1_, bf16[48,2176]{1,0:T(8,128)(2,1)S(1)} %collective-permute-done.38.refs_2_, ...), custom_call_target="tpu_custom_call" | custom-call | flops 1811939328 | bytes 9437184 | tf_op jit(solution)/shard_map/pallas_call | solution.py:108
  87.6 0.6 collective-permute-start.29
  88.8 2.1 %shard_map.114 = (bf16[96,2048]{1,0:T(8,128)(2,1)S(1)}, bf16[96,2048]{1,0:T(8,128)(2,1)S(1)}) custom-call(bf16[48,2176]{1,0:T(8,128)(2,1)S(1)} %collective-permute-done.66.refs_0_, bf16[48,2176]{1,0:T(8,128)(2,1)S(1)} %collective-permute-done.44.refs_1_, bf16[48,2176]{1,0:T(8,128)(2,1)S(1)} %collective-permute-done.67.refs_2_, ...), custom_call_target="tpu_custom_call" | custom-call | flops 1811939328 | bytes 9437184 | tf_op jit(solution)/shard_map/pallas_call | solution.py:108
  91.4 2.1 %shard_map.103 = (bf16[96,2048]{1,0:T(8,128)(2,1)S(1)}, bf16[96,2048]{1,0:T(8,128)(2,1)S(1)}) custom-call(bf16[48,2176]{1,0:T(8,128)(2,1)S(1)} %collective-permute-done.41.refs_0_, bf16[48,2176]{1,0:T(8,128)(2,1)S(1)} %collective-permute-done.45.refs_1_, bf16[48,2176]{1,0:T(8,128)(2,1)S(1)} %collective-permute-done.46.refs_2_, ...), custom_call_target="tpu_custom_call" | custom-call | flops 1811939328 | bytes 9437184 | tf_op jit(solution)/shard_map/pallas_call | solution.py:108
  94.6 2.1 %shard_map.101 = (bf16[96,2048]{1,0:T(8,128)(2,1)S(1)}, bf16[96,2048]{1,0:T(8,128)(2,1)S(1)}) custom-call(bf16[48,2176]{1,0:T(8,128)(2,1)S(1)} %collective-permute-done.31.refs_0_, bf16[48,2176]{1,0:T(8,128)(2,1)S(1)} %collective-permute-done.32.refs_1_, bf16[48,2176]{1,0:T(8,128)(2,1)S(1)} %collective-permute-done.33.refs_2_, ...), custom_call_target="tpu_custom_call" | custom-call | flops 1811939328 | bytes 9437184 | tf_op jit(solution)/shard_map/pallas_call | solution.py:108
  96.9 2.1 %shard_map.113 = (bf16[96,2048]{1,0:T(8,128)(2,1)S(1)}, bf16[96,2048]{1,0:T(8,128)(2,1)S(1)}) custom-call(bf16[48,2176]{1,0:T(8,128)(2,1)S(1)} %collective-permute-done.62.refs_0_, bf16[48,2176]{1,0:T(8,128)(2,1)S(1)} %collective-permute-done.43.refs_1_, bf16[48,2176]{1,0:T(8,128)(2,1)S(1)} %collective-permute-done.63.refs_2_, ...), custom_call_target="tpu_custom_call" | custom-call | flops 1811939328 | bytes 9437184 | tf_op jit(solution)/shard_map/pallas_call | solution.py:108
  99.7 1.6 %collective-permute-start.49 = (bf16[48,2048]{1,0:T(8,128)(2,1)S(1)}, bf16[48,2048]{1,0:T(8,128)(2,1)S(1)}, u32[]{:S(2)}, u32[]{:S(2)}) collective-permute-start(bf16[48,2048]{1,0:T(8,128)(2,1)S(1)} %shard_map.104), channel_id=1, source_target_pairs={{0,4},{1,5},{4,8},{5,9},{8,12},{9,13},{12,14},{13,15},{14,10},{15,... | collective-permute-start | bytes 589832 | tf_op jit(solution)/shard_map/ppermute | solution.py:279
  101.9 2.1 %shard_map.100 = (bf16[96,2048]{1,0:T(8,128)(2,1)S(1)}, bf16[96,2048]{1,0:T(8,128)(2,1)S(1)}) custom-call(bf16[48,2176]{1,0:T(8,128)(2,1)S(1)} %collective-permute-done.26.refs_0_, bf16[48,2176]{1,0:T(8,128)(2,1)S(1)} %collective-permute-done.27.refs_1_, bf16[48,2176]{1,0:T(8,128)(2,1)S(1)} %collective-permute-done.28.refs_2_, ...), custom_call_target="tpu_custom_call" | custom-call | flops 1811939328 | bytes 9437184 | tf_op jit(solution)/shard_map/pallas_call | solution.py:108
  104.6 2.3 %collective-permute-done.49.refs_0_ = bf16[48,2048]{1,0:T(8,128)(2,1)S(1)} collective-permute-done((bf16[48,2048]{1,0:T(8,128)(2,1)S(1)}, bf16[48,2048]{1,0:T(8,128)(2,1)S(1)}, u32[]{:S(2)}, u32[]{:S(2)}) %collective-permute-start.49) | collective-permute-done | bytes 196640 | tf_op jit(solution)/shard_map/ppermute | solution.py:279
  107.0 1.6 %collective-permute-start.70 = (bf16[48,2048]{1,0:T(8,128)(2,1)S(1)}, bf16[48,2048]{1,0:T(8,128)(2,1)S(1)}, u32[]{:S(2)}, u32[]{:S(2)}) collective-permute-start(bf16[48,2048]{1,0:T(8,128)(2,1)S(1)} %shard_map.115), channel_id=1, source_target_pairs={{0,4},{1,5},{4,8},{5,9},{8,12},{9,13},{12,14},{13,15},{14,10},{15,... | collective-permute-start | bytes 589832 | tf_op jit(solution)/shard_map/ppermute | solution.py:279
  108.6 1.8 %collective-permute-start.50 = (bf16[48,2048]{1,0:T(8,128)(2,1)S(1)}, bf16[48,2048]{1,0:T(8,128)(2,1)S(1)}, u32[]{:S(2)}, u32[]{:S(2)}) collective-permute-start(bf16[48,2048]{1,0:T(8,128)(2,1)S(1)} %shard_map.105), channel_id=1, source_target_pairs={{0,4},{1,5},{4,8},{5,9},{8,12},{9,13},{12,14},{13,15},{14,10},{15,... | collective-permute-start | bytes 589832 | tf_op jit(solution)/shard_map/ppermute | solution.py:279
  110.4 2.1 %shard_map.112 = (bf16[96,2048]{1,0:T(8,128)(2,1)S(1)}, bf16[96,2048]{1,0:T(8,128)(2,1)S(1)}) custom-call(bf16[48,2176]{1,0:T(8,128)(2,1)S(1)} %collective-permute-done.58.refs_0_, bf16[48,2176]{1,0:T(8,128)(2,1)S(1)} %collective-permute-done.42.refs_1_, bf16[48,2176]{1,0:T(8,128)(2,1)S(1)} %collective-permute-done.59.refs_2_, ...), custom_call_target="tpu_custom_call" | custom-call | flops 1811939328 | bytes 9437184 | tf_op jit(solution)/shard_map/pallas_call | solution.py:108
  112.7 0.6 collective-permute-start.74
  113.4 1.3 collective-permute-done.70.refs_0_
  115.3 2.3 %collective-permute-done.50.refs_0_ = bf16[48,2048]{1,0:T(8,128)(2,1)S(1)} collective-permute-done((bf16[48,2048]{1,0:T(8,128)(2,1)S(1)}, bf16[48,2048]{1,0:T(8,128)(2,1)S(1)}, u32[]{:S(2)}, u32[]{:S(2)}) %collective-permute-start.50) | collective-permute-done | bytes 196640 | tf_op jit(solution)/shard_map/ppermute | solution.py:279
  117.6 1.6 %collective-permute-start.71 = (bf16[48,2048]{1,0:T(8,128)(2,1)S(1)}, bf16[48,2048]{1,0:T(8,128)(2,1)S(1)}, u32[]{:S(2)}, u32[]{:S(2)}) collective-permute-start(bf16[48,2048]{1,0:T(8,128)(2,1)S(1)} %shard_map.116), channel_id=1, source_target_pairs={{0,4},{1,5},{4,8},{5,9},{8,12},{9,13},{12,14},{13,15},{14,10},{15,... | collective-permute-start | bytes 589832 | tf_op jit(solution)/shard_map/ppermute | solution.py:279
  119.1 1.7 %shard_map.99 = (bf16[48,2048]{1,0:T(8,128)(2,1)S(1)}, bf16[48,2048]{1,0:T(8,128)(2,1)S(1)}) custom-call(bf16[48,2176]{1,0:T(8,128)(2,1)S(1)} %get-tuple-element.43.refs_0_, bf16[48,2176]{1,0:T(8,128)(2,1)S(1)} %collective-permute-done.24.refs_1_, bf16[2048,768]{1,0:T(8,128)(2,1)S(1)} %bitcast.25, bf16[2048,768]{1,0:T(8,128)(2,1)S(1)} %bitcast.34, ...), custom_call_target="tpu_custom_call" | custom-call | flops 905969664 | bytes 9437184 | tf_op jit(solution)/shard_map/pallas_call | solution.py:108
  120.9 1.6 %collective-permute-start.51 = (bf16[48,2048]{1,0:T(8,128)(2,1)S(1)}, bf16[48,2048]{1,0:T(8,128)(2,1)S(1)}, u32[]{:S(2)}, u32[]{:S(2)}) collective-permute-start(bf16[48,2048]{1,0:T(8,128)(2,1)S(1)} %shard_map.106), channel_id=1, source_target_pairs={{0,4},{1,5},{4,8},{5,9},{8,12},{9,13},{12,14},{13,15},{14,10},{15,... | collective-permute-start | bytes 589832 | tf_op jit(solution)/shard_map/ppermute | solution.py:279
  122.6 0.6 collective-permute-start.75
  123.1 1.6 %collective-permute-done.54.refs_0_ = bf16[48,2048]{1,0:T(8,128)(2,1)S(1)} collective-permute-done((bf16[48,2048]{1,0:T(8,128)(2,1)S(1)}, bf16[48,2048]{1,0:T(8,128)(2,1)S(1)}, u32[]{:S(2)}, u32[]{:S(2)}) %collective-permute-start.54) | collective-permute-done | bytes 196640 | tf_op jit(solution)/shard_map/ppermute | solution.py:279
  124.8 1.7 %shard_map.111 = (bf16[48,2048]{1,0:T(8,128)(2,1)S(1)}, bf16[48,2048]{1,0:T(8,128)(2,1)S(1)}) custom-call(bf16[48,2176]{1,0:T(8,128)(2,1)S(1)} %get-tuple-element.52.refs_0_, bf16[48,2176]{1,0:T(8,128)(2,1)S(1)} %collective-permute-done.56.refs_1_, bf16[2048,768]{1,0:T(8,128)(2,1)S(1)} %bitcast.26, bf16[2048,768]{1,0:T(8,128)(2,1)S(1)} %bitcast.35, ...), custom_call_target="tpu_custom_call" | custom-call | flops 905969664 | bytes 9437184 | tf_op jit(solution)/shard_map/pallas_call | solution.py:108
  126.6 0.6 collective-permute-start.57
  127.8 1.5 %collective-permute-start.72 = (bf16[48,2048]{1,0:T(8,128)(2,1)S(1)}, bf16[48,2048]{1,0:T(8,128)(2,1)S(1)}, u32[]{:S(2)}, u32[]{:S(2)}) collective-permute-start(bf16[48,2048]{1,0:T(8,128)(2,1)S(1)} %shard_map.117), channel_id=1, source_target_pairs={{0,4},{1,5},{4,8},{5,9},{8,12},{9,13},{12,14},{13,15},{14,10},{15,... | collective-permute-start | bytes 589832 | tf_op jit(solution)/shard_map/ppermute | solution.py:279
  129.4 1.4 collective-permute-start.52
  130.8 0.8 collective-permute-start.76
  131.6 3.3 %collective-permute-done.55.refs_3_ = bf16[48,2048]{1,0:T(8,128)(2,1)S(1)} collective-permute-done((bf16[48,2048]{1,0:T(8,128)(2,1)S(1)}, bf16[48,2048]{1,0:T(8,128)(2,1)S(1)}, u32[]{:S(2)}, u32[]{:S(2)}) %collective-permute-start.55) | collective-permute-done | bytes 196640 | tf_op jit(solution)/shard_map/ppermute | solution.py:279
  134.9 0.7 collective-permute-done.72.refs_6_
  135.6 3.0 %collective-permute-done.52.refs_2_ = bf16[48,2048]{1,0:T(8,128)(2,1)S(1)} collective-permute-done((bf16[48,2048]{1,0:T(8,128)(2,1)S(1)}, bf16[48,2048]{1,0:T(8,128)(2,1)S(1)}, u32[]{:S(2)}, u32[]{:S(2)}) %collective-permute-start.52) | collective-permute-done | bytes 196640 | tf_op jit(solution)/shard_map/ppermute | solution.py:279
  138.6 1.0 shard_map.122
  (151 shorter events, 14.3 us)
Async XLA Ops:
  4.5 13.9 %collective-permute-start = (bf16[96,8,2,72]{3,0,1,2:T(8,128)(2,1)S(1)}, bf16[96,8,2,72]{3,0,1,2:T(8,128)(2,1)S(1)}, u32[]{:S(2)}, u32[]{:S(2)}) collective-permute-start(bf16[96,8,2,72]{3,0,1,2:T(8,128)(2,1)S(1)} %get-tuple-element.66), channel_id=1, source_target_pairs={{0,1},{1,0},{2,3},{3,2},{4,5},{5,4},{6,7},{7,6},{8,9},{9,8},{10,11... | collective-permute-start | bytes 663560 | tf_op jit(solution)/shard_map/ppermute | solution.py:287
  5.4 7.7 %collective-permute-start.2 = (bf16[72,1024]{1,0:T(8,128)(2,1)S(1)}, bf16[72,1024]{1,0:T(8,128)(2,1)S(1)}, u32[]{:S(2)}, u32[]{:S(2)}) collective-permute-start(bf16[72,1024]{1,0:T(8,128)(2,1)S(1)} %get-tuple-element.68.refs_0_), channel_id=1, source_target_pairs={{0,4},{1,5},{4,8},{5,9},{8,12},{9,13},{12,14},{13,15},{14,10},{15,... | collective-permute-start | bytes 442376 | tf_op jit(solution)/shard_map/ppermute | solution.py:279
  8.5 6.7 %collective-permute-start.3 = (bf16[72,1024]{1,0:T(8,128)(2,1)S(1)}, bf16[72,1024]{1,0:T(8,128)(2,1)S(1)}, u32[]{:S(2)}, u32[]{:S(2)}) collective-permute-start(bf16[72,1024]{1,0:T(8,128)(2,1)S(1)} %get-tuple-element.68.refs_0_), channel_id=1, source_target_pairs={{0,2},{1,3},{4,0},{5,1},{8,4},{9,5},{12,8},{13,9},{14,12},{15,13},... | collective-permute-start | bytes 442376 | tf_op jit(solution)/shard_map/ppermute | solution.py:279
  8.5 7.8 %collective-permute-start.13 = (bf16[72,1024]{1,0:T(8,128)(2,1)S(1)}, bf16[72,1024]{1,0:T(8,128)(2,1)S(1)}, u32[]{:S(2)}, u32[]{:S(2)}) collective-permute-start(bf16[72,1024]{1,0:T(8,128)(2,1)S(1)} %get-tuple-element.67.refs_0_), channel_id=1, source_target_pairs={{0,4},{1,5},{4,8},{5,9},{8,12},{9,13},{12,14},{13,15},{14,10},{15,... | collective-permute-start | bytes 442376 | tf_op jit(solution)/shard_map/ppermute | solution.py:279
  10.6 7.9 %collective-permute-start.14 = (bf16[72,1024]{1,0:T(8,128)(2,1)S(1)}, bf16[72,1024]{1,0:T(8,128)(2,1)S(1)}, u32[]{:S(2)}, u32[]{:S(2)}) collective-permute-start(bf16[72,1024]{1,0:T(8,128)(2,1)S(1)} %get-tuple-element.67.refs_0_), channel_id=1, source_target_pairs={{0,2},{1,3},{4,0},{5,1},{8,4},{9,5},{12,8},{13,9},{14,12},{15,13},... | collective-permute-start | bytes 442376 | tf_op jit(solution)/shard_map/ppermute | solution.py:279
  13.1 7.6 %collective-permute-start.4 = (bf16[72,1024]{1,0:T(8,128)(2,1)S(1)}, bf16[72,1024]{1,0:T(8,128)(2,1)S(1)}, u32[]{:S(2)}, u32[]{:S(2)}) collective-permute-start(bf16[72,1024]{1,0:T(8,128)(2,1)S(1)} %collective-permute-done.2.refs_1_), channel_id=1, source_target_pairs={{0,4},{1,5},{4,8},{5,9},{8,12},{9,13},{12,14},{13,15},{14,10},{15,... | collective-permute-start | bytes 442376 | tf_op jit(solution)/shard_map/ppermute | solution.py:279
  15.2 7.0 %collective-permute-start.5 = (bf16[72,1024]{1,0:T(8,128)(2,1)S(1)}, bf16[72,1024]{1,0:T(8,128)(2,1)S(1)}, u32[]{:S(2)}, u32[]{:S(2)}) collective-permute-start(bf16[72,1024]{1,0:T(8,128)(2,1)S(1)} %collective-permute-done.3.refs_2_), channel_id=1, source_target_pairs={{0,2},{1,3},{4,0},{5,1},{8,4},{9,5},{12,8},{13,9},{14,12},{15,13},... | collective-permute-start | bytes 442376 | tf_op jit(solution)/shard_map/ppermute | solution.py:279
  16.3 6.7 %collective-permute-start.15 = (bf16[72,1024]{1,0:T(8,128)(2,1)S(1)}, bf16[72,1024]{1,0:T(8,128)(2,1)S(1)}, u32[]{:S(2)}, u32[]{:S(2)}) collective-permute-start(bf16[72,1024]{1,0:T(8,128)(2,1)S(1)} %collective-permute-done.13.refs_1_), channel_id=1, source_target_pairs={{0,4},{1,5},{4,8},{5,9},{8,12},{9,13},{12,14},{13,15},{14,10},{15,... | collective-permute-start | bytes 442376 | tf_op jit(solution)/shard_map/ppermute | solution.py:279
  18.4 6.7 %collective-permute-start.16 = (bf16[72,1024]{1,0:T(8,128)(2,1)S(1)}, bf16[72,1024]{1,0:T(8,128)(2,1)S(1)}, u32[]{:S(2)}, u32[]{:S(2)}) collective-permute-start(bf16[72,1024]{1,0:T(8,128)(2,1)S(1)} %collective-permute-done.14.refs_2_), channel_id=1, source_target_pairs={{0,2},{1,3},{4,0},{5,1},{8,4},{9,5},{12,8},{13,9},{14,12},{15,13},... | collective-permute-start | bytes 442376 | tf_op jit(solution)/shard_map/ppermute | solution.py:279
  18.7 12.8 %collective-permute-start.1 = (bf16[192,8,72]{2,0,1:T(8,128)(2,1)S(1)}, bf16[192,8,72]{2,0,1:T(8,128)(2,1)S(1)}, u32[]{:S(2)}, u32[]{:S(2)}) collective-permute-start(bf16[192,8,72]{2,0,1:T(8,128)(2,1)S(1)} %get-tuple-element.64), channel_id=1, source_target_pairs={{0,16},{16,0},{1,17},{17,1},{2,18},{18,2},{3,19},{19,3},{4,20},{20... | collective-permute-start | bytes 663560 | tf_op jit(solution)/shard_map/ppermute | solution.py:291
  20.7 6.3 %collective-permute-start.6 = (bf16[72,1024]{1,0:T(8,128)(2,1)S(1)}, bf16[72,1024]{1,0:T(8,128)(2,1)S(1)}, u32[]{:S(2)}, u32[]{:S(2)}) collective-permute-start(bf16[72,1024]{1,0:T(8,128)(2,1)S(1)} %collective-permute-done.4.refs_3_), channel_id=1, source_target_pairs={{0,4},{1,5},{4,8},{5,9},{8,12},{9,13},{12,14},{13,15},{14,10},{15,... | collective-permute-start | bytes 442376 | tf_op jit(solution)/shard_map/ppermute | solution.py:279
  22.3 6.5 %collective-permute-start.7 = (bf16[72,1024]{1,0:T(8,128)(2,1)S(1)}, bf16[72,1024]{1,0:T(8,128)(2,1)S(1)}, u32[]{:S(2)}, u32[]{:S(2)}) collective-permute-start(bf16[72,1024]{1,0:T(8,128)(2,1)S(1)} %collective-permute-done.5.refs_4_), channel_id=1, source_target_pairs={{0,2},{1,3},{4,0},{5,1},{8,4},{9,5},{12,8},{13,9},{14,12},{15,13},... | collective-permute-start | bytes 442376 | tf_op jit(solution)/shard_map/ppermute | solution.py:279
  23.0 6.4 %collective-permute-start.17 = (bf16[72,1024]{1,0:T(8,128)(2,1)S(1)}, bf16[72,1024]{1,0:T(8,128)(2,1)S(1)}, u32[]{:S(2)}, u32[]{:S(2)}) collective-permute-start(bf16[72,1024]{1,0:T(8,128)(2,1)S(1)} %collective-permute-done.15.refs_3_), channel_id=1, source_target_pairs={{0,4},{1,5},{4,8},{5,9},{8,12},{9,13},{12,14},{13,15},{14,10},{15,... | collective-permute-start | bytes 442376 | tf_op jit(solution)/shard_map/ppermute | solution.py:279
  25.1 6.1 %collective-permute-start.18 = (bf16[72,1024]{1,0:T(8,128)(2,1)S(1)}, bf16[72,1024]{1,0:T(8,128)(2,1)S(1)}, u32[]{:S(2)}, u32[]{:S(2)}) collective-permute-start(bf16[72,1024]{1,0:T(8,128)(2,1)S(1)} %collective-permute-done.16.refs_4_), channel_id=1, source_target_pairs={{0,2},{1,3},{4,0},{5,1},{8,4},{9,5},{12,8},{13,9},{14,12},{15,13},... | collective-permute-start | bytes 442376 | tf_op jit(solution)/shard_map/ppermute | solution.py:279
  27.0 7.9 %collective-permute-start.8 = (bf16[40,1024]{1,0:T(8,128)(2,1)S(1)}, bf16[40,1024]{1,0:T(8,128)(2,1)S(1)}, u32[]{:S(2)}, u32[]{:S(2)}) collective-permute-start(bf16[40,1024]{1,0:T(8,128)(2,1)S(1)} %slice.48), channel_id=1, source_target_pairs={{0,4},{1,5},{4,8},{5,9},{8,12},{9,13},{12,14},{13,15},{14,10},{15,... | collective-permute-start | bytes 245768 | tf_op jit(solution)/shard_map/ppermute | solution.py:279
  28.8 6.0 %collective-permute-start.9 = (bf16[32,1024]{1,0:T(8,128)(2,1)S(1)}, bf16[32,1024]{1,0:T(8,128)(2,1)S(1)}, u32[]{:S(2)}, u32[]{:S(2)}) collective-permute-start(bf16[32,1024]{1,0:T(8,128)(2,1)S(1)} %slice.49), channel_id=1, source_target_pairs={{0,2},{1,3},{4,0},{5,1},{8,4},{9,5},{12,8},{13,9},{14,12},{15,13},... | collective-permute-start | bytes 196616 | tf_op jit(solution)/shard_map/ppermute | solution.py:279
  29.4 6.2 %collective-permute-start.19 = (bf16[40,1024]{1,0:T(8,128)(2,1)S(1)}, bf16[40,1024]{1,0:T(8,128)(2,1)S(1)}, u32[]{:S(2)}, u32[]{:S(2)}) collective-permute-start(bf16[40,1024]{1,0:T(8,128)(2,1)S(1)} %slice.50), channel_id=1, source_target_pairs={{0,4},{1,5},{4,8},{5,9},{8,12},{9,13},{12,14},{13,15},{14,10},{15,... | collective-permute-start | bytes 245768 | tf_op jit(solution)/shard_map/ppermute | solution.py:279
  37.2 7.8 %collective-permute-start.12 = (bf16[96,1024]{1,0:T(8,128)(2,1)S(1)}, bf16[96,1024]{1,0:T(8,128)(2,1)S(1)}, u32[]{:S(2)}, u32[]{:S(2)}) collective-permute-start(bf16[96,1024]{1,0:T(8,128)(2,1)S(1)} %shard_map.93), channel_id=1, source_target_pairs={{0,16},{16,0},{1,17},{17,1},{2,18},{18,2},{3,19},{19,3},{4,20},{20... | collective-permute-start | bytes 589832 | tf_op jit(solution)/shard_map/ppermute | solution.py:324
  38.8 9.6 %collective-permute-start.23 = (bf16[96,1024]{1,0:T(8,128)(2,1)S(1)}, bf16[96,1024]{1,0:T(8,128)(2,1)S(1)}, u32[]{:S(2)}, u32[]{:S(2)}) collective-permute-start(bf16[96,1024]{1,0:T(8,128)(2,1)S(1)} %shard_map.96), channel_id=1, source_target_pairs={{0,16},{16,0},{1,17},{17,1},{2,18},{18,2},{3,19},{19,3},{4,20},{20... | collective-permute-start | bytes 589832 | tf_op jit(solution)/shard_map/ppermute | solution.py:324
  48.7 8.0 %collective-permute-start.26 = (bf16[48,2176]{1,0:T(8,128)(2,1)S(1)}, bf16[48,2176]{1,0:T(8,128)(2,1)S(1)}, u32[]{:S(2)}, u32[]{:S(2)}) collective-permute-start(bf16[48,2176]{1,0:T(8,128)(2,1)S(1)} %get-tuple-element.43.refs_0_), channel_id=1, source_target_pairs={{0,4},{1,5},{4,8},{5,9},{8,12},{9,13},{12,14},{13,15},{14,10},{15,... | collective-permute-start | bytes 626696 | tf_op jit(solution)/shard_map/ppermute | solution.py:279
  50.6 8.0 %collective-permute-start.27 = (bf16[48,2176]{1,0:T(8,128)(2,1)S(1)}, bf16[48,2176]{1,0:T(8,128)(2,1)S(1)}, u32[]{:S(2)}, u32[]{:S(2)}) collective-permute-start(bf16[48,2176]{1,0:T(8,128)(2,1)S(1)} %get-tuple-element.43.refs_0_), channel_id=1, source_target_pairs={{0,2},{1,3},{4,0},{5,1},{8,4},{9,5},{12,8},{13,9},{14,12},{15,13},... | collective-permute-start | bytes 626696 | tf_op jit(solution)/shard_map/ppermute | solution.py:279
  50.8 12.3 %collective-permute-start.42 = (bf16[48,2176]{1,0:T(8,128)(2,1)S(1)}, bf16[48,2176]{1,0:T(8,128)(2,1)S(1)}, u32[]{:S(2)}, u32[]{:S(2)}) collective-permute-start(bf16[48,2176]{1,0:T(8,128)(2,1)S(1)} %get-tuple-element.52.refs_0_), channel_id=1, source_target_pairs={{0,2},{1,3},{4,0},{5,1},{8,4},{9,5},{12,8},{13,9},{14,12},{15,13},... | collective-permute-start | bytes 626696 | tf_op jit(solution)/shard_map/ppermute | solution.py:279
  52.5 10.8 %collective-permute-start.58 = (bf16[48,2176]{1,0:T(8,128)(2,1)S(1)}, bf16[48,2176]{1,0:T(8,128)(2,1)S(1)}, u32[]{:S(2)}, u32[]{:S(2)}) collective-permute-start(bf16[48,2176]{1,0:T(8,128)(2,1)S(1)} %get-tuple-element.52.refs_0_), channel_id=1, source_target_pairs={{0,4},{1,5},{4,8},{5,9},{8,12},{9,13},{12,14},{13,15},{14,10},{15,... | collective-permute-start | bytes 626696 | tf_op jit(solution)/shard_map/ppermute | solution.py:279
  56.7 8.5 %collective-permute-start.31 = (bf16[48,2176]{1,0:T(8,128)(2,1)S(1)}, bf16[48,2176]{1,0:T(8,128)(2,1)S(1)}, u32[]{:S(2)}, u32[]{:S(2)}) collective-permute-start(bf16[48,2176]{1,0:T(8,128)(2,1)S(1)} %collective-permute-done.26.refs_0_), channel_id=1, source_target_pairs={{0,4},{1,5},{4,8},{5,9},{8,12},{9,13},{12,14},{13,15},{14,10},{15,... | collective-permute-start | bytes 626696 | tf_op jit(solution)/shard_map/ppermute | solution.py:279
  58.6 9.0 %collective-permute-start.32 = (bf16[48,2176]{1,0:T(8,128)(2,1)S(1)}, bf16[48,2176]{1,0:T(8,128)(2,1)S(1)}, u32[]{:S(2)}, u32[]{:S(2)}) collective-permute-start(bf16[48,2176]{1,0:T(8,128)(2,1)S(1)} %collective-permute-done.27.refs_1_), channel_id=1, source_target_pairs={{0,2},{1,3},{4,0},{5,1},{8,4},{9,5},{12,8},{13,9},{14,12},{15,13},... | collective-permute-start | bytes 626696 | tf_op jit(solution)/shard_map/ppermute | solution.py:279
  58.8 9.0 %collective-permute-start.24 = (bf16[48,2176]{1,0:T(8,128)(2,1)S(1)}, bf16[48,2176]{1,0:T(8,128)(2,1)S(1)}, u32[]{:S(2)}, u32[]{:S(2)}) collective-permute-start(bf16[48,2176]{1,0:T(8,128)(2,1)S(1)} %get-tuple-element.43.refs_0_), channel_id=1, source_target_pairs={{0,1},{1,0},{2,3},{3,2},{4,5},{5,4},{6,7},{7,6},{8,9},{9,8},{10,11... | collective-permute-start | bytes 626696 | tf_op jit(solution)/shard_map/ppermute | solution.py:341
  63.1 9.0 %collective-permute-start.43 = (bf16[48,2176]{1,0:T(8,128)(2,1)S(1)}, bf16[48,2176]{1,0:T(8,128)(2,1)S(1)}, u32[]{:S(2)}, u32[]{:S(2)}) collective-permute-start(bf16[48,2176]{1,0:T(8,128)(2,1)S(1)} %collective-permute-done.42.refs_1_), channel_id=1, source_target_pairs={{0,2},{1,3},{4,0},{5,1},{8,4},{9,5},{12,8},{13,9},{14,12},{15,13},... | collective-permute-start | bytes 626696 | tf_op jit(solution)/shard_map/ppermute | solution.py:279
  63.3 9.0 %collective-permute-start.62 = (bf16[48,2176]{1,0:T(8,128)(2,1)S(1)}, bf16[48,2176]{1,0:T(8,128)(2,1)S(1)}, u32[]{:S(2)}, u32[]{:S(2)}) collective-permute-start(bf16[48,2176]{1,0:T(8,128)(2,1)S(1)} %collective-permute-done.58.refs_0_), channel_id=1, source_target_pairs={{0,4},{1,5},{4,8},{5,9},{8,12},{9,13},{12,14},{13,15},{14,10},{15,... | collective-permute-start | bytes 626696 | tf_op jit(solution)/shard_map/ppermute | solution.py:279
  65.2 9.3 %collective-permute-start.36 = (bf16[48,2176]{1,0:T(8,128)(2,1)S(1)}, bf16[48,2176]{1,0:T(8,128)(2,1)S(1)}, u32[]{:S(2)}, u32[]{:S(2)}) collective-permute-start(bf16[48,2176]{1,0:T(8,128)(2,1)S(1)} %collective-permute-done.31.refs_0_), channel_id=1, source_target_pairs={{0,4},{1,5},{4,8},{5,9},{8,12},{9,13},{12,14},{13,15},{14,10},{15,... | collective-permute-start | bytes 626696 | tf_op jit(solution)/shard_map/ppermute | solution.py:279
  67.6 8.9 %collective-permute-start.37 = (bf16[48,2176]{1,0:T(8,128)(2,1)S(1)}, bf16[48,2176]{1,0:T(8,128)(2,1)S(1)}, u32[]{:S(2)}, u32[]{:S(2)}) collective-permute-start(bf16[48,2176]{1,0:T(8,128)(2,1)S(1)} %collective-permute-done.32.refs_1_), channel_id=1, source_target_pairs={{0,2},{1,3},{4,0},{5,1},{8,4},{9,5},{12,8},{13,9},{14,12},{15,13},... | collective-permute-start | bytes 626696 | tf_op jit(solution)/shard_map/ppermute | solution.py:279
  67.8 8.7 %collective-permute-start.56 = (bf16[48,2176]{1,0:T(8,128)(2,1)S(1)}, bf16[48,2176]{1,0:T(8,128)(2,1)S(1)}, u32[]{:S(2)}, u32[]{:S(2)}) collective-permute-start(bf16[48,2176]{1,0:T(8,128)(2,1)S(1)} %get-tuple-element.52.refs_0_), channel_id=1, source_target_pairs={{0,1},{1,0},{2,3},{3,2},{4,5},{5,4},{6,7},{7,6},{8,9},{9,8},{10,11... | collective-permute-start | bytes 626696 | tf_op jit(solution)/shard_map/ppermute | solution.py:341
  72.1 7.0 %collective-permute-start.44 = (bf16[48,2176]{1,0:T(8,128)(2,1)S(1)}, bf16[48,2176]{1,0:T(8,128)(2,1)S(1)}, u32[]{:S(2)}, u32[]{:S(2)}) collective-permute-start(bf16[48,2176]{1,0:T(8,128)(2,1)S(1)} %collective-permute-done.43.refs_1_), channel_id=1, source_target_pairs={{0,2},{1,3},{4,0},{5,1},{8,4},{9,5},{12,8},{13,9},{14,12},{15,13},... | collective-permute-start | bytes 626696 | tf_op jit(solution)/shard_map/ppermute | solution.py:279
  72.3 7.1 %collective-permute-start.66 = (bf16[48,2176]{1,0:T(8,128)(2,1)S(1)}, bf16[48,2176]{1,0:T(8,128)(2,1)S(1)}, u32[]{:S(2)}, u32[]{:S(2)}) collective-permute-start(bf16[48,2176]{1,0:T(8,128)(2,1)S(1)} %collective-permute-done.62.refs_0_), channel_id=1, source_target_pairs={{0,4},{1,5},{4,8},{5,9},{8,12},{9,13},{12,14},{13,15},{14,10},{15,... | collective-permute-start | bytes 626696 | tf_op jit(solution)/shard_map/ppermute | solution.py:279
  76.6 7.6 %collective-permute-start.41 = (bf16[48,2176]{1,0:T(8,128)(2,1)S(1)}, bf16[48,2176]{1,0:T(8,128)(2,1)S(1)}, u32[]{:S(2)}, u32[]{:S(2)}) collective-permute-start(bf16[48,2176]{1,0:T(8,128)(2,1)S(1)} %collective-permute-done.36.refs_0_), channel_id=1, source_target_pairs={{0,4},{1,5},{4,8},{5,9},{8,12},{9,13},{12,14},{13,15},{14,10},{15,... | collective-permute-start | bytes 626696 | tf_op jit(solution)/shard_map/ppermute | solution.py:279
  79.1 6.4 %collective-permute-start.45 = (bf16[48,2176]{1,0:T(8,128)(2,1)S(1)}, bf16[48,2176]{1,0:T(8,128)(2,1)S(1)}, u32[]{:S(2)}, u32[]{:S(2)}) collective-permute-start(bf16[48,2176]{1,0:T(8,128)(2,1)S(1)} %collective-permute-done.44.refs_1_), channel_id=1, source_target_pairs={{0,2},{1,3},{4,0},{5,1},{8,4},{9,5},{12,8},{13,9},{14,12},{15,13},... | collective-permute-start | bytes 626696 | tf_op jit(solution)/shard_map/ppermute | solution.py:279
  79.3 8.2 %collective-permute-start.28 = (bf16[48,2176]{1,0:T(8,128)(2,1)S(1)}, bf16[48,2176]{1,0:T(8,128)(2,1)S(1)}, u32[]{:S(2)}, u32[]{:S(2)}) collective-permute-start(bf16[48,2176]{1,0:T(8,128)(2,1)S(1)} %collective-permute-done.26.refs_0_), channel_id=1, source_target_pairs={{0,1},{1,0},{2,3},{3,2},{4,5},{5,4},{6,7},{7,6},{8,9},{9,8},{10,11... | collective-permute-start | bytes 626696 | tf_op jit(solution)/shard_map/ppermute | solution.py:341
  79.4 8.8 %collective-permute-start.67 = (bf16[48,2176]{1,0:T(8,128)(2,1)S(1)}, bf16[48,2176]{1,0:T(8,128)(2,1)S(1)}, u32[]{:S(2)}, u32[]{:S(2)}) collective-permute-start(bf16[48,2176]{1,0:T(8,128)(2,1)S(1)} %collective-permute-done.66.refs_0_), channel_id=1, source_target_pairs={{0,1},{1,0},{2,3},{3,2},{4,5},{5,4},{6,7},{7,6},{8,9},{9,8},{10,11... | collective-permute-start | bytes 626696 | tf_op jit(solution)/shard_map/ppermute | solution.py:341
  79.9 8.4 %collective-permute-start.68 = (bf16[48,2176]{1,0:T(8,128)(2,1)S(1)}, bf16[48,2176]{1,0:T(8,128)(2,1)S(1)}, u32[]{:S(2)}, u32[]{:S(2)}) collective-permute-start(bf16[48,2176]{1,0:T(8,128)(2,1)S(1)} %collective-permute-done.44.refs_1_), channel_id=1, source_target_pairs={{0,1},{1,0},{2,3},{3,2},{4,5},{5,4},{6,7},{7,6},{8,9},{9,8},{10,11... | collective-permute-start | bytes 626696 | tf_op jit(solution)/shard_map/ppermute | solution.py:341
  87.6 5.9 %collective-permute-start.29 = (bf16[48,2176]{1,0:T(8,128)(2,1)S(1)}, bf16[48,2176]{1,0:T(8,128)(2,1)S(1)}, u32[]{:S(2)}, u32[]{:S(2)}) collective-permute-start(bf16[48,2176]{1,0:T(8,128)(2,1)S(1)} %collective-permute-done.27.refs_1_), channel_id=1, source_target_pairs={{0,1},{1,0},{2,3},{3,2},{4,5},{5,4},{6,7},{7,6},{8,9},{9,8},{10,11... | collective-permute-start | bytes 626696 | tf_op jit(solution)/shard_map/ppermute | solution.py:341
  88.2 5.5 %collective-permute-start.33 = (bf16[48,2176]{1,0:T(8,128)(2,1)S(1)}, bf16[48,2176]{1,0:T(8,128)(2,1)S(1)}, u32[]{:S(2)}, u32[]{:S(2)}) collective-permute-start(bf16[48,2176]{1,0:T(8,128)(2,1)S(1)} %collective-permute-done.31.refs_0_), channel_id=1, source_target_pairs={{0,1},{1,0},{2,3},{3,2},{4,5},{5,4},{6,7},{7,6},{8,9},{9,8},{10,11... | collective-permute-start | bytes 626696 | tf_op jit(solution)/shard_map/ppermute | solution.py:341
  88.2 5.9 %collective-permute-start.34 = (bf16[48,2176]{1,0:T(8,128)(2,1)S(1)}, bf16[48,2176]{1,0:T(8,128)(2,1)S(1)}, u32[]{:S(2)}, u32[]{:S(2)}) collective-permute-start(bf16[48,2176]{1,0:T(8,128)(2,1)S(1)} %collective-permute-done.32.refs_1_), channel_id=1, source_target_pairs={{0,1},{1,0},{2,3},{3,2},{4,5},{5,4},{6,7},{7,6},{8,9},{9,8},{10,11... | collective-permute-start | bytes 626696 | tf_op jit(solution)/shard_map/ppermute | solution.py:341
  88.7 5.5 %collective-permute-start.63 = (bf16[48,2176]{1,0:T(8,128)(2,1)S(1)}, bf16[48,2176]{1,0:T(8,128)(2,1)S(1)}, u32[]{:S(2)}, u32[]{:S(2)}) collective-permute-start(bf16[48,2176]{1,0:T(8,128)(2,1)S(1)} %collective-permute-done.62.refs_0_), channel_id=1, source_target_pairs={{0,1},{1,0},{2,3},{3,2},{4,5},{5,4},{6,7},{7,6},{8,9},{9,8},{10,11... | collective-permute-start | bytes 626696 | tf_op jit(solution)/shard_map/ppermute | solution.py:341
  90.9 5.9 %collective-permute-start.64 = (bf16[48,2176]{1,0:T(8,128)(2,1)S(1)}, bf16[48,2176]{1,0:T(8,128)(2,1)S(1)}, u32[]{:S(2)}, u32[]{:S(2)}) collective-permute-start(bf16[48,2176]{1,0:T(8,128)(2,1)S(1)} %collective-permute-done.43.refs_1_), channel_id=1, source_target_pairs={{0,1},{1,0},{2,3},{3,2},{4,5},{5,4},{6,7},{7,6},{8,9},{9,8},{10,11... | collective-permute-start | bytes 626696 | tf_op jit(solution)/shard_map/ppermute | solution.py:341
  93.7 6.0 %collective-permute-start.40 = (bf16[96,2048]{1,0:T(8,128)(2,1)S(1)}, bf16[96,2048]{1,0:T(8,128)(2,1)S(1)}, u32[]{:S(2)}, u32[]{:S(2)}) collective-permute-start(bf16[96,2048]{1,0:T(8,128)(2,1)S(1)} %get-tuple-element.51), channel_id=1, source_target_pairs={{0,1},{1,0},{2,3},{3,2},{4,5},{5,4},{6,7},{7,6},{8,9},{9,8},{10,11... | collective-permute-start | bytes 1179656 | tf_op jit(solution)/shard_map/ppermute | solution.py:343
  94.1 7.3 %collective-permute-start.69 = (bf16[96,2048]{1,0:T(8,128)(2,1)S(1)}, bf16[96,2048]{1,0:T(8,128)(2,1)S(1)}, u32[]{:S(2)}, u32[]{:S(2)}) collective-permute-start(bf16[96,2048]{1,0:T(8,128)(2,1)S(1)} %get-tuple-element.62), channel_id=1, source_target_pairs={{0,1},{1,0},{2,3},{3,2},{4,5},{5,4},{6,7},{7,6},{8,9},{9,8},{10,11... | collective-permute-start | bytes 1179656 | tf_op jit(solution)/shard_map/ppermute | solution.py:343
  96.8 7.9 %collective-permute-start.35 = (bf16[96,2048]{1,0:T(8,128)(2,1)S(1)}, bf16[96,2048]{1,0:T(8,128)(2,1)S(1)}, u32[]{:S(2)}, u32[]{:S(2)}) collective-permute-start(bf16[96,2048]{1,0:T(8,128)(2,1)S(1)} %get-tuple-element.49), channel_id=1, source_target_pairs={{0,1},{1,0},{2,3},{3,2},{4,5},{5,4},{6,7},{7,6},{8,9},{9,8},{10,11... | collective-permute-start | bytes 1179656 | tf_op jit(solution)/shard_map/ppermute | solution.py:343
  99.0 9.6 %collective-permute-start.65 = (bf16[96,2048]{1,0:T(8,128)(2,1)S(1)}, bf16[96,2048]{1,0:T(8,128)(2,1)S(1)}, u32[]{:S(2)}, u32[]{:S(2)}) collective-permute-start(bf16[96,2048]{1,0:T(8,128)(2,1)S(1)} %get-tuple-element.60), channel_id=1, source_target_pairs={{0,1},{1,0},{2,3},{3,2},{4,5},{5,4},{6,7},{7,6},{8,9},{9,8},{10,11... | collective-permute-start | bytes 1179656 | tf_op jit(solution)/shard_map/ppermute | solution.py:343
  99.7 7.3 %collective-permute-start.49 = (bf16[48,2048]{1,0:T(8,128)(2,1)S(1)}, bf16[48,2048]{1,0:T(8,128)(2,1)S(1)}, u32[]{:S(2)}, u32[]{:S(2)}) collective-permute-start(bf16[48,2048]{1,0:T(8,128)(2,1)S(1)} %shard_map.104), channel_id=1, source_target_pairs={{0,4},{1,5},{4,8},{5,9},{8,12},{9,13},{12,14},{13,15},{14,10},{15,... | collective-permute-start | bytes 589832 | tf_op jit(solution)/shard_map/ppermute | solution.py:279
  101.4 11.2 %collective-permute-start.73 = (bf16[48,2048]{1,0:T(8,128)(2,1)S(1)}, bf16[48,2048]{1,0:T(8,128)(2,1)S(1)}, u32[]{:S(2)}, u32[]{:S(2)}) collective-permute-start(bf16[48,2048]{1,0:T(8,128)(2,1)S(1)} %shard_map.118), channel_id=1, source_target_pairs={{0,2},{1,3},{4,0},{5,1},{8,4},{9,5},{12,8},{13,9},{14,12},{15,13},... | collective-permute-start | bytes 589832 | tf_op jit(solution)/shard_map/ppermute | solution.py:279
  104.1 8.6 %collective-permute-start.53 = (bf16[48,2048]{1,0:T(8,128)(2,1)S(1)}, bf16[48,2048]{1,0:T(8,128)(2,1)S(1)}, u32[]{:S(2)}, u32[]{:S(2)}) collective-permute-start(bf16[48,2048]{1,0:T(8,128)(2,1)S(1)} %shard_map.108), channel_id=1, source_target_pairs={{0,2},{1,3},{4,0},{5,1},{8,4},{9,5},{12,8},{13,9},{14,12},{15,13},... | collective-permute-start | bytes 589832 | tf_op jit(solution)/shard_map/ppermute | solution.py:279
  104.6 17.9 %collective-permute-start.30 = (bf16[96,2048]{1,0:T(8,128)(2,1)S(1)}, bf16[96,2048]{1,0:T(8,128)(2,1)S(1)}, u32[]{:S(2)}, u32[]{:S(2)}) collective-permute-start(bf16[96,2048]{1,0:T(8,128)(2,1)S(1)} %get-tuple-element.47), channel_id=1, source_target_pairs={{0,1},{1,0},{2,3},{3,2},{4,5},{5,4},{6,7},{7,6},{8,9},{9,8},{10,11... | collective-permute-start | bytes 1179656 | tf_op jit(solution)/shard_map/ppermute | solution.py:343
  107.0 7.8 %collective-permute-start.70 = (bf16[48,2048]{1,0:T(8,128)(2,1)S(1)}, bf16[48,2048]{1,0:T(8,128)(2,1)S(1)}, u32[]{:S(2)}, u32[]{:S(2)}) collective-permute-start(bf16[48,2048]{1,0:T(8,128)(2,1)S(1)} %shard_map.115), channel_id=1, source_target_pairs={{0,4},{1,5},{4,8},{5,9},{8,12},{9,13},{12,14},{13,15},{14,10},{15,... | collective-permute-start | bytes 589832 | tf_op jit(solution)/shard_map/ppermute | solution.py:279
  108.6 8.9 %collective-permute-start.50 = (bf16[48,2048]{1,0:T(8,128)(2,1)S(1)}, bf16[48,2048]{1,0:T(8,128)(2,1)S(1)}, u32[]{:S(2)}, u32[]{:S(2)}) collective-permute-start(bf16[48,2048]{1,0:T(8,128)(2,1)S(1)} %shard_map.105), channel_id=1, source_target_pairs={{0,4},{1,5},{4,8},{5,9},{8,12},{9,13},{12,14},{13,15},{14,10},{15,... | collective-permute-start | bytes 589832 | tf_op jit(solution)/shard_map/ppermute | solution.py:279
  112.6 14.0 %collective-permute-start.61 = (bf16[96,2048]{1,0:T(8,128)(2,1)S(1)}, bf16[96,2048]{1,0:T(8,128)(2,1)S(1)}, u32[]{:S(2)}, u32[]{:S(2)}) collective-permute-start(bf16[96,2048]{1,0:T(8,128)(2,1)S(1)} %get-tuple-element.58), channel_id=1, source_target_pairs={{0,1},{1,0},{2,3},{3,2},{4,5},{5,4},{6,7},{7,6},{8,9},{9,8},{10,11... | collective-permute-start | bytes 1179656 | tf_op jit(solution)/shard_map/ppermute | solution.py:343
  112.7 8.2 %collective-permute-start.74 = (bf16[48,2048]{1,0:T(8,128)(2,1)S(1)}, bf16[48,2048]{1,0:T(8,128)(2,1)S(1)}, u32[]{:S(2)}, u32[]{:S(2)}) collective-permute-start(bf16[48,2048]{1,0:T(8,128)(2,1)S(1)} %shard_map.119), channel_id=1, source_target_pairs={{0,2},{1,3},{4,0},{5,1},{8,4},{9,5},{12,8},{13,9},{14,12},{15,13},... | collective-permute-start | bytes 589832 | tf_op jit(solution)/shard_map/ppermute | solution.py:279
  114.7 10.0 %collective-permute-start.54 = (bf16[48,2048]{1,0:T(8,128)(2,1)S(1)}, bf16[48,2048]{1,0:T(8,128)(2,1)S(1)}, u32[]{:S(2)}, u32[]{:S(2)}) collective-permute-start(bf16[48,2048]{1,0:T(8,128)(2,1)S(1)} %shard_map.109), channel_id=1, source_target_pairs={{0,2},{1,3},{4,0},{5,1},{8,4},{9,5},{12,8},{13,9},{14,12},{15,13},... | collective-permute-start | bytes 589832 | tf_op jit(solution)/shard_map/ppermute | solution.py:279
  117.6 9.6 %collective-permute-start.71 = (bf16[48,2048]{1,0:T(8,128)(2,1)S(1)}, bf16[48,2048]{1,0:T(8,128)(2,1)S(1)}, u32[]{:S(2)}, u32[]{:S(2)}) collective-permute-start(bf16[48,2048]{1,0:T(8,128)(2,1)S(1)} %shard_map.116), channel_id=1, source_target_pairs={{0,4},{1,5},{4,8},{5,9},{8,12},{9,13},{12,14},{13,15},{14,10},{15,... | collective-permute-start | bytes 589832 | tf_op jit(solution)/shard_map/ppermute | solution.py:279
  120.9 6.8 %collective-permute-start.51 = (bf16[48,2048]{1,0:T(8,128)(2,1)S(1)}, bf16[48,2048]{1,0:T(8,128)(2,1)S(1)}, u32[]{:S(2)}, u32[]{:S(2)}) collective-permute-start(bf16[48,2048]{1,0:T(8,128)(2,1)S(1)} %shard_map.106), channel_id=1, source_target_pairs={{0,4},{1,5},{4,8},{5,9},{8,12},{9,13},{12,14},{13,15},{14,10},{15,... | collective-permute-start | bytes 589832 | tf_op jit(solution)/shard_map/ppermute | solution.py:279
  122.6 6.8 %collective-permute-start.75 = (bf16[48,2048]{1,0:T(8,128)(2,1)S(1)}, bf16[48,2048]{1,0:T(8,128)(2,1)S(1)}, u32[]{:S(2)}, u32[]{:S(2)}) collective-permute-start(bf16[48,2048]{1,0:T(8,128)(2,1)S(1)} %shard_map.120), channel_id=1, source_target_pairs={{0,2},{1,3},{4,0},{5,1},{8,4},{9,5},{12,8},{13,9},{14,12},{15,13},... | collective-permute-start | bytes 589832 | tf_op jit(solution)/shard_map/ppermute | solution.py:279
  124.8 6.1 %collective-permute-start.25 = (bf16[48,2048]{1,0:T(8,128)(2,1)S(1)}, bf16[48,2048]{1,0:T(8,128)(2,1)S(1)}, u32[]{:S(2)}, u32[]{:S(2)}) collective-permute-start(bf16[48,2048]{1,0:T(8,128)(2,1)S(1)} %get-tuple-element.45), channel_id=1, source_target_pairs={{0,1},{1,0},{2,3},{3,2},{4,5},{5,4},{6,7},{7,6},{8,9},{9,8},{10,11... | collective-permute-start | bytes 589832 | tf_op jit(solution)/shard_map/ppermute | solution.py:343
  127.1 7.8 %collective-permute-start.55 = (bf16[48,2048]{1,0:T(8,128)(2,1)S(1)}, bf16[48,2048]{1,0:T(8,128)(2,1)S(1)}, u32[]{:S(2)}, u32[]{:S(2)}) collective-permute-start(bf16[48,2048]{1,0:T(8,128)(2,1)S(1)} %shard_map.110), channel_id=1, source_target_pairs={{0,2},{1,3},{4,0},{5,1},{8,4},{9,5},{12,8},{13,9},{14,12},{15,13},... | collective-permute-start | bytes 589832 | tf_op jit(solution)/shard_map/ppermute | solution.py:279
  127.8 7.8 %collective-permute-start.72 = (bf16[48,2048]{1,0:T(8,128)(2,1)S(1)}, bf16[48,2048]{1,0:T(8,128)(2,1)S(1)}, u32[]{:S(2)}, u32[]{:S(2)}) collective-permute-start(bf16[48,2048]{1,0:T(8,128)(2,1)S(1)} %shard_map.117), channel_id=1, source_target_pairs={{0,4},{1,5},{4,8},{5,9},{8,12},{9,13},{12,14},{13,15},{14,10},{15,... | collective-permute-start | bytes 589832 | tf_op jit(solution)/shard_map/ppermute | solution.py:279
  129.4 9.2 %collective-permute-start.52 = (bf16[48,2048]{1,0:T(8,128)(2,1)S(1)}, bf16[48,2048]{1,0:T(8,128)(2,1)S(1)}, u32[]{:S(2)}, u32[]{:S(2)}) collective-permute-start(bf16[48,2048]{1,0:T(8,128)(2,1)S(1)} %shard_map.107), channel_id=1, source_target_pairs={{0,4},{1,5},{4,8},{5,9},{8,12},{9,13},{12,14},{13,15},{14,10},{15,... | collective-permute-start | bytes 589832 | tf_op jit(solution)/shard_map/ppermute | solution.py:279
  130.8 7.8 %collective-permute-start.76 = (bf16[48,2048]{1,0:T(8,128)(2,1)S(1)}, bf16[48,2048]{1,0:T(8,128)(2,1)S(1)}, u32[]{:S(2)}, u32[]{:S(2)}) collective-permute-start(bf16[48,2048]{1,0:T(8,128)(2,1)S(1)} %shard_map.121), channel_id=1, source_target_pairs={{0,2},{1,3},{4,0},{5,1},{8,4},{9,5},{12,8},{13,9},{14,12},{15,13},... | collective-permute-start | bytes 589832 | tf_op jit(solution)/shard_map/ppermute | solution.py:279
  (21 other events, 236.5 us)
where the time goes:
time: 140 us
  starting transfers between devices  58.1 us (42%)
  waiting for transfers between devices  50.9 us (36%)
  Pallas kernels  24.9 us (18%)
  other arithmetic  3.07 us (2%)
  local copies, waits for them, and re-layouts  2.19 us (2%)
    ppermute x44, starting transfers between devices, hop(): return rings[way](array)  47.4 us
    ppermute x44, waiting for transfers between devices, hop(): return rings[way](array)  42.1 us
    pallas_call x32, Pallas kernels, kernel(): pl.pallas_call(body, out_shape=outs, in_specs=[VMEM] * len(ins), out_spec...  24.9 us
    ppermute x2, waiting for transfers between devices, dense(): theirs = cross(theirs)  8.72 us
  transfers between devices with their start and end apart: 77, of which 23 were waited for; matrix products, arithmetic and copies ran while one was open for 0% of the time, Pallas kernels for 17%

commit v1 on v0

--- a/solution.py
+++ b/solution.py
@@ -225,18 +225,24 @@
     refs[-1][...] = (refs[0][...] + refs[1][...]).astype(refs[-1].dtype)
 
 
-def add_body(at, own_ref, other_ref, *refs):
+def add_body(at, shift, own_ref, other_ref, *refs):
     out_ref = refs[-1]
     size = out_ref.shape[0]
     total = own_ref[at : at + size, :].astype(jnp.float32) + other_ref[at : at + size, :].astype(jnp.float32)
-    for ref in refs[:-1]:
-        total += ref[...].astype(jnp.float32)
-    out_ref[...] = total.astype(jnp.bfloat16)
-
-
-def add(own, other, at, size, total=None):
+    if len(refs) == 1:
+        out_ref[...] = total.astype(jnp.bfloat16)
+        return
+    to = shift + refs[0].shape[0]
+    out_ref[shift:to, :] = (total[shift:to] + refs[0][...].astype(jnp.float32)).astype(jnp.bfloat16)
+    if shift > 0:
+        out_ref[:shift, :] = total[:shift].astype(jnp.bfloat16)
+    if to < size:
+        out_ref[to:, :] = total[to:].astype(jnp.bfloat16)
+
+
+def add(own, other, at, size, total=None, shift=0):
     ins = [own, other] + ([] if total is None else [total])
-    return kernel(functools.partial(add_body, at), shaped(size, own.shape[1]), ins)
+    return kernel(functools.partial(add_body, at, shift), shaped(size, own.shape[1]), ins)
 
 
 def finish_body(merged_ref, *refs):
@@ -320,7 +326,8 @@
             flops=2 * size * half,
             moved=8 * size,
         )
-        theirs = kernel(plus_body, shaped(rows, share), [theirs, swap(theirs_other)])
+        theirs_other = swap(theirs_other)
+        theirs = kernel(plus_body, shaped(rows, share), [theirs, theirs_other])
         theirs = cross(theirs)
         streams += [own, swap(own_other), theirs]
     merged, *block = kernel(
@@ -335,7 +342,8 @@
     for _ in range(1, far):
         sides = [tuple(hop(way, side[way]) for way in (0, 1)) for side in sides]
         arrived.append(sides)
-    distant = hop(0, sides[0][0]), hop(1, sides[1][1])
+    short = cut // 2
+    arrived.append([(hop(0, side[0][:short]), hop(1, side[1][short:])) for side in sides])
 
     def served(ins):
         others = [swap(x) for x in ins]
@@ -343,19 +351,17 @@
         return own, swap(other)
 
     outs = [[served(ins) for ins in pair] for pair in arrived]
-    distant = served(distant)
-
-    def home(way, which, at, total):
+
+    def home(way, which):
+        total = add(*outs[far][which], way * short, short)
+        total = hop(way, total)
         for step in reversed(range(1, far)):
-            total = add(*outs[step][which], at, cut, total)
+            total = add(*outs[step][which], (1 - way) * cut, cut, total, way * short if step == far - 1 else 0)
             total = hop(way, total)
         return total
 
-    near = home(0, 1, cut, None), home(1, 0, 0, None)
-    top, bottom = (hop(way, add(*distant, way * cut, cut)) for way in (0, 1))
-    top, bottom = home(0, 0, cut, top), home(1, 1, 0, bottom)
-    ins = [merged, *outs[0][0], top, near[1], *outs[0][1], near[0], bottom]
-    return kernel(finish_body, shaped(rows, width), ins)
+    sums = [(*outs[0][which], home(0, which), home(1, which)) for which in (0, 1)]
+    return kernel(finish_body, shaped(rows, width), [merged, *sums[0], *sums[1]])
 
 
 def shards(*arrays):

time: 140 us -> 147 us (1.050)
  starting transfers between devices: 58.1 us -> 63.5 us
    ppermute x44 -> x48, starting transfers between devices: 47.4 us -> 52.6 us  [hop(): return rings[way](array)]
    pallas_call x32 -> x35, Pallas kernels: 24.9 us -> 26.1 us  [kernel(): pl.pallas_call(body, out_shape=outs, in_specs=[VMEM] * len(ins), out_spec...]
    ppermute x44 -> x48, waiting for transfers between devices: 42.1 us -> 42.8 us  [hop(): return rings[way](array)]
  transfers between devices with their start and end apart: 77 -> 84, of which waited for: 23 -> 30; matrix products, arithmetic and copies ran while one was open for 0% -> 0% of each run, Pallas kernels for 17% -> 17%
where the time goes in v1:
time: 147 us
  starting transfers between devices  63.5 us (43%)
  waiting for transfers between devices  51.6 us (35%)
  Pallas kernels  26.1 us (18%)
  other arithmetic  3.07 us (2%)
  local copies, waits for them, and re-layouts  2.23 us (2%)
    ppermute x48, starting transfers between devices, hop(): return rings[way](array)  52.6 us
    ppermute x48, waiting for transfers between devices, hop(): return rings[way](array)  42.8 us
    pallas_call x35, Pallas kernels, kernel(): pl.pallas_call(body, out_shape=outs, in_specs=[VMEM] * len(ins), out_spec...  26.1 us
    ppermute x2, waiting for transfers between devices, dense(): theirs = cross(theirs)  8.71 us
  transfers between devices with their start and end apart: 84, of which 30 were waited for; matrix products, arithmetic and copies ran while one was open for 0% of the time, Pallas kernels for 17%

profile of v1, /device:TPU:0, one launch (start us, length us, event | category | flops | bytes accessed | tf_op | source)
XLA Modules:
  0.0 147.0 jit_solution(4133585365251061460)
XLA Ops:
  0.0 1.3 copy.10
  1.3 2.6 %fusion.1 = bf16[96,2304]{0,1:T(8,128)(2,1)S(1)} fusion(bf16[96,2304]{0,1:T(8,128)(2,1)S(1)} %copy.10), kind=kLoop, calls=%fused_computation.4 | loop fusion | flops 14598144 | bytes 884736 | tf_op jit(solution)/shard_map/convert_element_type | solution.py:289
  5.4 3.1 %collective-permute-start.2 = (bf16[72,1024]{1,0:T(8,128)(2,1)S(1)}, bf16[72,1024]{1,0:T(8,128)(2,1)S(1)}, u32[]{:S(2)}, u32[]{:S(2)}) collective-permute-start(bf16[72,1024]{1,0:T(8,128)(2,1)S(1)} %get-tuple-element.72.refs_0_), channel_id=1, source_target_pairs={{0,4},{1,5},{4,8},{5,9},{8,12},{9,13},{12,14},{13,15},{14,10},{15,... | collective-permute-start | bytes 442376 | tf_op jit(solution)/shard_map/ppermute | solution.py:285
  8.5 2.0 %collective-permute-start.13 = (bf16[72,1024]{1,0:T(8,128)(2,1)S(1)}, bf16[72,1024]{1,0:T(8,128)(2,1)S(1)}, u32[]{:S(2)}, u32[]{:S(2)}) collective-permute-start(bf16[72,1024]{1,0:T(8,128)(2,1)S(1)} %get-tuple-element.71.refs_0_), channel_id=1, source_target_pairs={{0,4},{1,5},{4,8},{5,9},{8,12},{9,13},{12,14},{13,15},{14,10},{15,... | collective-permute-start | bytes 442376 | tf_op jit(solution)/shard_map/ppermute | solution.py:285
  10.6 2.6 %collective-permute-done.2.refs_1_ = bf16[72,1024]{1,0:T(8,128)(2,1)S(1)} collective-permute-done((bf16[72,1024]{1,0:T(8,128)(2,1)S(1)}, bf16[72,1024]{1,0:T(8,128)(2,1)S(1)}, u32[]{:S(2)}, u32[]{:S(2)}) %collective-permute-start.2) | collective-permute-done | bytes 147488 | tf_op jit(solution)/shard_map/ppermute | solution.py:285
  13.1 2.1 %collective-permute-start.4 = (bf16[72,1024]{1,0:T(8,128)(2,1)S(1)}, bf16[72,1024]{1,0:T(8,128)(2,1)S(1)}, u32[]{:S(2)}, u32[]{:S(2)}) collective-permute-start(bf16[72,1024]{1,0:T(8,128)(2,1)S(1)} %collective-permute-done.2.refs_1_), channel_id=1, source_target_pairs={{0,4},{1,5},{4,8},{5,9},{8,12},{9,13},{12,14},{13,15},{14,10},{15,... | collective-permute-start | bytes 442376 | tf_op jit(solution)/shard_map/ppermute | solution.py:285
  15.2 1.0 collective-permute-done.13.refs_1_
  16.3 2.1 %collective-permute-start.15 = (bf16[72,1024]{1,0:T(8,128)(2,1)S(1)}, bf16[72,1024]{1,0:T(8,128)(2,1)S(1)}, u32[]{:S(2)}, u32[]{:S(2)}) collective-permute-start(bf16[72,1024]{1,0:T(8,128)(2,1)S(1)} %collective-permute-done.13.refs_1_), channel_id=1, source_target_pairs={{0,4},{1,5},{4,8},{5,9},{8,12},{9,13},{12,14},{13,15},{14,10},{15,... | collective-permute-start | bytes 442376 | tf_op jit(solution)/shard_map/ppermute | solution.py:285
  18.7 2.0 %collective-permute-start.1 = (bf16[192,8,72]{2,0,1:T(8,128)(2,1)S(1)}, bf16[192,8,72]{2,0,1:T(8,128)(2,1)S(1)}, u32[]{:S(2)}, u32[]{:S(2)}) collective-permute-start(bf16[192,8,72]{2,0,1:T(8,128)(2,1)S(1)} %get-tuple-element.68), channel_id=1, source_target_pairs={{0,16},{16,0},{1,17},{17,1},{2,18},{18,2},{3,19},{19,3},{4,20},{20... | collective-permute-start | bytes 663560 | tf_op jit(solution)/shard_map/ppermute | solution.py:297
  20.7 1.6 %collective-permute-start.6 = (bf16[72,1024]{1,0:T(8,128)(2,1)S(1)}, bf16[72,1024]{1,0:T(8,128)(2,1)S(1)}, u32[]{:S(2)}, u32[]{:S(2)}) collective-permute-start(bf16[72,1024]{1,0:T(8,128)(2,1)S(1)} %collective-permute-done.4.refs_3_), channel_id=1, source_target_pairs={{0,4},{1,5},{4,8},{5,9},{8,12},{9,13},{12,14},{13,15},{14,10},{15,... | collective-permute-start | bytes 442376 | tf_op jit(solution)/shard_map/ppermute | solution.py:285
  23.0 2.1 %collective-permute-start.17 = (bf16[72,1024]{1,0:T(8,128)(2,1)S(1)}, bf16[72,1024]{1,0:T(8,128)(2,1)S(1)}, u32[]{:S(2)}, u32[]{:S(2)}) collective-permute-start(bf16[72,1024]{1,0:T(8,128)(2,1)S(1)} %collective-permute-done.15.refs_3_), channel_id=1, source_target_pairs={{0,4},{1,5},{4,8},{5,9},{8,12},{9,13},{12,14},{13,15},{14,10},{15,... | collective-permute-start | bytes 442376 | tf_op jit(solution)/shard_map/ppermute | solution.py:285
  25.1 1.8 %collective-permute-done.6.refs_5_ = bf16[72,1024]{1,0:T(8,128)(2,1)S(1)} collective-permute-done((bf16[72,1024]{1,0:T(8,128)(2,1)S(1)}, bf16[72,1024]{1,0:T(8,128)(2,1)S(1)}, u32[]{:S(2)}, u32[]{:S(2)}) %collective-permute-start.6) | collective-permute-done | bytes 147488 | tf_op jit(solution)/shard_map/ppermute | solution.py:285
  27.0 1.8 %collective-permute-start.8 = (bf16[40,1024]{1,0:T(8,128)(2,1)S(1)}, bf16[40,1024]{1,0:T(8,128)(2,1)S(1)}, u32[]{:S(2)}, u32[]{:S(2)}) collective-permute-start(bf16[40,1024]{1,0:T(8,128)(2,1)S(1)} %slice.64), channel_id=1, source_target_pairs={{0,4},{1,5},{4,8},{5,9},{8,12},{9,13},{12,14},{13,15},{14,10},{15,... | collective-permute-start | bytes 245768 | tf_op jit(solution)/shard_map/ppermute | solution.py:285
  29.4 1.8 %collective-permute-start.19 = (bf16[40,1024]{1,0:T(8,128)(2,1)S(1)}, bf16[40,1024]{1,0:T(8,128)(2,1)S(1)}, u32[]{:S(2)}, u32[]{:S(2)}) collective-permute-start(bf16[40,1024]{1,0:T(8,128)(2,1)S(1)} %slice.66), channel_id=1, source_target_pairs={{0,4},{1,5},{4,8},{5,9},{8,12},{9,13},{12,14},{13,15},{14,10},{15,... | collective-permute-start | bytes 245768 | tf_op jit(solution)/shard_map/ppermute | solution.py:285
  31.6 1.6 %shard_map.91.total_ref = f32[384,1024]{1,0:T(8,128)S(1)} custom-call(bf16[8,384,72]{2,1,0:T(8,128)(2,1)S(1)} %maximum_bitcast_fusion.act_ref, bf16[72,1024]{1,0:T(8,128)(2,1)S(1)} %get-tuple-element.72.refs_0_, bf16[72,1024]{1,0:T(8,128)(2,1)S(1)} %collective-permute-done.2.refs_1_, bf16[72,1024]{1,0:T(8,128)(2,1)S(1)} %collective-permute-done.3.refs_2_, ...), custom_call_target="tpu_custom_call" | custom-call | flops 452984832 | bytes 1572864 | tf_op jit(solution)/shard_map/pallas_call | solution.py:108
  33.2 1.6 %shard_map.94.total_ref = f32[384,1024]{1,0:T(8,128)S(1)} custom-call(bf16[8,384,72]{2,1,0:T(8,128)(2,1)S(1)} %maximum_bitcast_fusion.act_ref, bf16[72,1024]{1,0:T(8,128)(2,1)S(1)} %get-tuple-element.71.refs_0_, bf16[72,1024]{1,0:T(8,128)(2,1)S(1)} %collective-permute-done.13.refs_1_, bf16[72,1024]{1,0:T(8,128)(2,1)S(1)} %collective-permute-done.14.refs_2_, ...), custom_call_target="tpu_custom_call" | custom-call | flops 452984832 | bytes 1572864 | tf_op jit(solution)/shard_map/pallas_call | solution.py:108
  37.2 1.5 %collective-permute-start.12 = (bf16[96,1024]{1,0:T(8,128)(2,1)S(1)}, bf16[96,1024]{1,0:T(8,128)(2,1)S(1)}, u32[]{:S(2)}, u32[]{:S(2)}) collective-permute-start(bf16[96,1024]{1,0:T(8,128)(2,1)S(1)} %shard_map.93), channel_id=1, source_target_pairs={{0,16},{16,0},{1,17},{17,1},{2,18},{18,2},{3,19},{19,3},{4,20},{20... | collective-permute-start | bytes 589832 | tf_op jit(solution)/shard_map/ppermute | solution.py:331
  39.7 5.3 %collective-permute-done.12.refs_2_ = bf16[96,1024]{1,0:T(8,128)(2,1)S(1)} collective-permute-done((bf16[96,1024]{1,0:T(8,128)(2,1)S(1)}, bf16[96,1024]{1,0:T(8,128)(2,1)S(1)}, u32[]{:S(2)}, u32[]{:S(2)}) %collective-permute-start.12) | collective-permute-done | bytes 196640 | tf_op jit(solution)/shard_map/ppermute | solution.py:331
  45.0 3.4 %collective-permute-done.23.refs_5_ = bf16[96,1024]{1,0:T(8,128)(2,1)S(1)} collective-permute-done((bf16[96,1024]{1,0:T(8,128)(2,1)S(1)}, bf16[96,1024]{1,0:T(8,128)(2,1)S(1)}, u32[]{:S(2)}, u32[]{:S(2)}) %collective-permute-start.23) | collective-permute-done | bytes 196640 | tf_op jit(solution)/shard_map/ppermute | solution.py:331
  48.7 1.9 %collective-permute-start.26 = (bf16[48,2176]{1,0:T(8,128)(2,1)S(1)}, bf16[48,2176]{1,0:T(8,128)(2,1)S(1)}, u32[]{:S(2)}, u32[]{:S(2)}) collective-permute-start(bf16[48,2176]{1,0:T(8,128)(2,1)S(1)} %get-tuple-element.45.refs_0_), channel_id=1, source_target_pairs={{0,4},{1,5},{4,8},{5,9},{8,12},{9,13},{12,14},{13,15},{14,10},{15,... | collective-permute-start | bytes 626696 | tf_op jit(solution)/shard_map/ppermute | solution.py:285
  50.8 1.8 %collective-permute-start.56 = (bf16[48,2176]{1,0:T(8,128)(2,1)S(1)}, bf16[48,2176]{1,0:T(8,128)(2,1)S(1)}, u32[]{:S(2)}, u32[]{:S(2)}) collective-permute-start(bf16[48,2176]{1,0:T(8,128)(2,1)S(1)} %get-tuple-element.56.refs_0_), channel_id=1, source_target_pairs={{0,4},{1,5},{4,8},{5,9},{8,12},{9,13},{12,14},{13,15},{14,10},{15,... | collective-permute-start | bytes 626696 | tf_op jit(solution)/shard_map/ppermute | solution.py:285
  52.8 4.0 %collective-permute-done.26.refs_0_ = bf16[48,2176]{1,0:T(8,128)(2,1)S(1)} collective-permute-done((bf16[48,2176]{1,0:T(8,128)(2,1)S(1)}, bf16[48,2176]{1,0:T(8,128)(2,1)S(1)}, u32[]{:S(2)}, u32[]{:S(2)}) %collective-permute-start.26) | collective-permute-done | bytes 208928 | tf_op jit(solution)/shard_map/ppermute | solution.py:285
  56.8 1.8 %collective-permute-start.31 = (bf16[48,2176]{1,0:T(8,128)(2,1)S(1)}, bf16[48,2176]{1,0:T(8,128)(2,1)S(1)}, u32[]{:S(2)}, u32[]{:S(2)}) collective-permute-start(bf16[48,2176]{1,0:T(8,128)(2,1)S(1)} %collective-permute-done.26.refs_0_), channel_id=1, source_target_pairs={{0,4},{1,5},{4,8},{5,9},{8,12},{9,13},{12,14},{13,15},{14,10},{15,... | collective-permute-start | bytes 626696 | tf_op jit(solution)/shard_map/ppermute | solution.py:285
  58.8 2.4 %collective-permute-done.56.refs_0_ = bf16[48,2176]{1,0:T(8,128)(2,1)S(1)} collective-permute-done((bf16[48,2176]{1,0:T(8,128)(2,1)S(1)}, bf16[48,2176]{1,0:T(8,128)(2,1)S(1)}, u32[]{:S(2)}, u32[]{:S(2)}) %collective-permute-start.56) | collective-permute-done | bytes 208928 | tf_op jit(solution)/shard_map/ppermute | solution.py:285
  61.3 1.8 %collective-permute-start.61 = (bf16[48,2176]{1,0:T(8,128)(2,1)S(1)}, bf16[48,2176]{1,0:T(8,128)(2,1)S(1)}, u32[]{:S(2)}, u32[]{:S(2)}) collective-permute-start(bf16[48,2176]{1,0:T(8,128)(2,1)S(1)} %collective-permute-done.56.refs_0_), channel_id=1, source_target_pairs={{0,4},{1,5},{4,8},{5,9},{8,12},{9,13},{12,14},{13,15},{14,10},{15,... | collective-permute-start | bytes 626696 | tf_op jit(solution)/shard_map/ppermute | solution.py:285
  63.3 2.4 %collective-permute-done.31.refs_0_ = bf16[48,2176]{1,0:T(8,128)(2,1)S(1)} collective-permute-done((bf16[48,2176]{1,0:T(8,128)(2,1)S(1)}, bf16[48,2176]{1,0:T(8,128)(2,1)S(1)}, u32[]{:S(2)}, u32[]{:S(2)}) %collective-permute-start.31) | collective-permute-done | bytes 208928 | tf_op jit(solution)/shard_map/ppermute | solution.py:285
  65.8 1.8 %collective-permute-start.36 = (bf16[48,2176]{1,0:T(8,128)(2,1)S(1)}, bf16[48,2176]{1,0:T(8,128)(2,1)S(1)}, u32[]{:S(2)}, u32[]{:S(2)}) collective-permute-start(bf16[48,2176]{1,0:T(8,128)(2,1)S(1)} %collective-permute-done.31.refs_0_), channel_id=1, source_target_pairs={{0,4},{1,5},{4,8},{5,9},{8,12},{9,13},{12,14},{13,15},{14,10},{15,... | collective-permute-start | bytes 626696 | tf_op jit(solution)/shard_map/ppermute | solution.py:285
  67.9 2.4 %collective-permute-done.61.refs_0_ = bf16[48,2176]{1,0:T(8,128)(2,1)S(1)} collective-permute-done((bf16[48,2176]{1,0:T(8,128)(2,1)S(1)}, bf16[48,2176]{1,0:T(8,128)(2,1)S(1)}, u32[]{:S(2)}, u32[]{:S(2)}) %collective-permute-start.61) | collective-permute-done | bytes 208928 | tf_op jit(solution)/shard_map/ppermute | solution.py:285
  70.7 1.6 %collective-permute-start.66 = (bf16[48,2176]{1,0:T(8,128)(2,1)S(1)}, bf16[48,2176]{1,0:T(8,128)(2,1)S(1)}, u32[]{:S(2)}, u32[]{:S(2)}) collective-permute-start(bf16[48,2176]{1,0:T(8,128)(2,1)S(1)} %collective-permute-done.61.refs_0_), channel_id=1, source_target_pairs={{0,4},{1,5},{4,8},{5,9},{8,12},{9,13},{12,14},{13,15},{14,10},{15,... | collective-permute-start | bytes 626696 | tf_op jit(solution)/shard_map/ppermute | solution.py:285
  73.0 1.7 %collective-permute-start.67 = (bf16[48,2176]{1,0:T(8,128)(2,1)S(1)}, bf16[48,2176]{1,0:T(8,128)(2,1)S(1)}, u32[]{:S(2)}, u32[]{:S(2)}) collective-permute-start(bf16[48,2176]{1,0:T(8,128)(2,1)S(1)} %collective-permute-done.62.refs_1_), channel_id=1, source_target_pairs={{0,2},{1,3},{4,0},{5,1},{8,4},{9,5},{12,8},{13,9},{14,12},{15,13},... | collective-permute-start | bytes 626696 | tf_op jit(solution)/shard_map/ppermute | solution.py:285
  75.4 1.6 %collective-permute-start.41 = (bf16[24,2176]{1,0:T(8,128)(2,1)S(1)}, bf16[24,2176]{1,0:T(8,128)(2,1)S(1)}, u32[]{:S(2)}, u32[]{:S(2)}) collective-permute-start(bf16[24,2176]{1,0:T(8,128)(2,1)S(1)} %slice.68), channel_id=1, source_target_pairs={{0,4},{1,5},{4,8},{5,9},{8,12},{9,13},{12,14},{13,15},{14,10},{15,... | collective-permute-start | bytes 313352 | tf_op jit(solution)/shard_map/ppermute | solution.py:285
  77.5 2.7 %collective-permute-done.41.refs_0_ = bf16[24,2176]{1,0:T(8,128)(2,1)S(1)} collective-permute-done((bf16[24,2176]{1,0:T(8,128)(2,1)S(1)}, bf16[24,2176]{1,0:T(8,128)(2,1)S(1)}, u32[]{:S(2)}, u32[]{:S(2)}) %collective-permute-start.41) | collective-permute-done | bytes 104480 | tf_op jit(solution)/shard_map/ppermute | solution.py:285
  80.8 1.1 collective-permute-done.42.refs_1_
  81.9 1.6 %collective-permute-start.71 = (bf16[24,2176]{1,0:T(8,128)(2,1)S(1)}, bf16[24,2176]{1,0:T(8,128)(2,1)S(1)}, u32[]{:S(2)}, u32[]{:S(2)}) collective-permute-start(bf16[24,2176]{1,0:T(8,128)(2,1)S(1)} %slice.70), channel_id=1, source_target_pairs={{0,4},{1,5},{4,8},{5,9},{8,12},{9,13},{12,14},{13,15},{14,10},{15,... | collective-permute-start | bytes 313352 | tf_op jit(solution)/shard_map/ppermute | solution.py:285
  84.0 1.7 %shard_map.103 = (bf16[48,2048]{1,0:T(8,128)(2,1)S(1)}, bf16[48,2048]{1,0:T(8,128)(2,1)S(1)}) custom-call(bf16[24,2176]{1,0:T(8,128)(2,1)S(1)} %collective-permute-done.41.refs_0_, bf16[24,2176]{1,0:T(8,128)(2,1)S(1)} %collective-permute-done.42.refs_1_, bf16[24,2176]{1,0:T(8,128)(2,1)S(1)} %collective-permute-done.43.refs_2_, ...), custom_call_target="tpu_custom_call" | custom-call | flops 905969664 | bytes 9437184 | tf_op jit(solution)/shard_map/pallas_call | solution.py:108
  85.7 1.6 %collective-permute-done.71.refs_0_ = bf16[24,2176]{1,0:T(8,128)(2,1)S(1)} collective-permute-done((bf16[24,2176]{1,0:T(8,128)(2,1)S(1)}, bf16[24,2176]{1,0:T(8,128)(2,1)S(1)}, u32[]{:S(2)}, u32[]{:S(2)}) %collective-permute-start.71) | collective-permute-done | bytes 104480 | tf_op jit(solution)/shard_map/ppermute | solution.py:285
  87.3 1.3 collective-permute-done.72.refs_1_
  89.2 2.1 %shard_map.102 = (bf16[96,2048]{1,0:T(8,128)(2,1)S(1)}, bf16[96,2048]{1,0:T(8,128)(2,1)S(1)}) custom-call(bf16[48,2176]{1,0:T(8,128)(2,1)S(1)} %collective-permute-done.36.refs_0_, bf16[48,2176]{1,0:T(8,128)(2,1)S(1)} %collective-permute-done.37.refs_1_, bf16[48,2176]{1,0:T(8,128)(2,1)S(1)} %collective-permute-done.38.refs_2_, ...), custom_call_target="tpu_custom_call" | custom-call | flops 1811939328 | bytes 9437184 | tf_op jit(solution)/shard_map/pallas_call | solution.py:108
  92.3 1.7 %shard_map.116 = (bf16[48,2048]{1,0:T(8,128)(2,1)S(1)}, bf16[48,2048]{1,0:T(8,128)(2,1)S(1)}) custom-call(bf16[24,2176]{1,0:T(8,128)(2,1)S(1)} %collective-permute-done.71.refs_0_, bf16[24,2176]{1,0:T(8,128)(2,1)S(1)} %collective-permute-done.72.refs_1_, bf16[24,2176]{1,0:T(8,128)(2,1)S(1)} %collective-permute-done.73.refs_2_, ...), custom_call_target="tpu_custom_call" | custom-call | flops 905969664 | bytes 9437184 | tf_op jit(solution)/shard_map/pallas_call | solution.py:108
  94.6 2.1 %shard_map.115 = (bf16[96,2048]{1,0:T(8,128)(2,1)S(1)}, bf16[96,2048]{1,0:T(8,128)(2,1)S(1)}) custom-call(bf16[48,2176]{1,0:T(8,128)(2,1)S(1)} %collective-permute-done.66.refs_0_, bf16[48,2176]{1,0:T(8,128)(2,1)S(1)} %collective-permute-done.67.refs_1_, bf16[48,2176]{1,0:T(8,128)(2,1)S(1)} %collective-permute-done.68.refs_2_, ...), custom_call_target="tpu_custom_call" | custom-call | flops 1811939328 | bytes 9437184 | tf_op jit(solution)/shard_map/pallas_call | solution.py:108
  97.4 1.6 %collective-permute-start.46 = (bf16[24,2048]{1,0:T(8,128)(2,1)S(1)}, bf16[24,2048]{1,0:T(8,128)(2,1)S(1)}, u32[]{:S(2)}, u32[]{:S(2)}) collective-permute-start(bf16[24,2048]{1,0:T(8,128)(2,1)S(1)} %shard_map.104), channel_id=1, source_target_pairs={{0,4},{1,5},{4,8},{5,9},{8,12},{9,13},{12,14},{13,15},{14,10},{15,... | collective-permute-start | bytes 294920 | tf_op jit(solution)/shard_map/ppermute | solution.py:285
  99.0 2.1 %shard_map.101 = (bf16[96,2048]{1,0:T(8,128)(2,1)S(1)}, bf16[96,2048]{1,0:T(8,128)(2,1)S(1)}) custom-call(bf16[48,2176]{1,0:T(8,128)(2,1)S(1)} %collective-permute-done.31.refs_0_, bf16[48,2176]{1,0:T(8,128)(2,1)S(1)} %collective-permute-done.32.refs_1_, bf16[48,2176]{1,0:T(8,128)(2,1)S(1)} %collective-permute-done.33.refs_2_, ...), custom_call_target="tpu_custom_call" | custom-call | flops 1811939328 | bytes 9437184 | tf_op jit(solution)/shard_map/pallas_call | solution.py:108
  102.6 2.1 %shard_map.114 = (bf16[96,2048]{1,0:T(8,128)(2,1)S(1)}, bf16[96,2048]{1,0:T(8,128)(2,1)S(1)}) custom-call(bf16[48,2176]{1,0:T(8,128)(2,1)S(1)} %collective-permute-done.61.refs_0_, bf16[48,2176]{1,0:T(8,128)(2,1)S(1)} %collective-permute-done.62.refs_1_, bf16[48,2176]{1,0:T(8,128)(2,1)S(1)} %collective-permute-done.63.refs_2_, ...), custom_call_target="tpu_custom_call" | custom-call | flops 1811939328 | bytes 9437184 | tf_op jit(solution)/shard_map/pallas_call | solution.py:108
  104.8 2.0 %collective-permute-done.50.refs_0_ = bf16[24,2048]{1,0:T(8,128)(2,1)S(1)} collective-permute-done((bf16[24,2048]{1,0:T(8,128)(2,1)S(1)}, bf16[24,2048]{1,0:T(8,128)(2,1)S(1)}, u32[]{:S(2)}, u32[]{:S(2)}) %collective-permute-start.50) | collective-permute-done | bytes 98336 | tf_op jit(solution)/shard_map/ppermute | solution.py:285
  106.8 1.6 %collective-permute-start.76 = (bf16[24,2048]{1,0:T(8,128)(2,1)S(1)}, bf16[24,2048]{1,0:T(8,128)(2,1)S(1)}, u32[]{:S(2)}, u32[]{:S(2)}) collective-permute-start(bf16[24,2048]{1,0:T(8,128)(2,1)S(1)} %shard_map.117), channel_id=1, source_target_pairs={{0,4},{1,5},{4,8},{5,9},{8,12},{9,13},{12,14},{13,15},{14,10},{15,... | collective-permute-start | bytes 294920 | tf_op jit(solution)/shard_map/ppermute | solution.py:285
  108.6 1.6 %collective-permute-start.47 = (bf16[48,2048]{1,0:T(8,128)(2,1)S(1)}, bf16[48,2048]{1,0:T(8,128)(2,1)S(1)}, u32[]{:S(2)}, u32[]{:S(2)}) collective-permute-start(bf16[48,2048]{1,0:T(8,128)(2,1)S(1)} %shard_map.105), channel_id=1, source_target_pairs={{0,4},{1,5},{4,8},{5,9},{8,12},{9,13},{12,14},{13,15},{14,10},{15,... | collective-permute-start | bytes 589832 | tf_op jit(solution)/shard_map/ppermute | solution.py:285
  110.2 2.4 %collective-permute-done.76.refs_0_ = bf16[24,2048]{1,0:T(8,128)(2,1)S(1)} collective-permute-done((bf16[24,2048]{1,0:T(8,128)(2,1)S(1)}, bf16[24,2048]{1,0:T(8,128)(2,1)S(1)}, u32[]{:S(2)}, u32[]{:S(2)}) %collective-permute-start.76) | collective-permute-done | bytes 98336 | tf_op jit(solution)/shard_map/ppermute | solution.py:285
  113.0 1.2 collective-permute-start.51
  114.2 2.1 %shard_map.100 = (bf16[96,2048]{1,0:T(8,128)(2,1)S(1)}, bf16[96,2048]{1,0:T(8,128)(2,1)S(1)}) custom-call(bf16[48,2176]{1,0:T(8,128)(2,1)S(1)} %collective-permute-done.26.refs_0_, bf16[48,2176]{1,0:T(8,128)(2,1)S(1)} %collective-permute-done.27.refs_1_, bf16[48,2176]{1,0:T(8,128)(2,1)S(1)} %collective-permute-done.28.refs_2_, ...), custom_call_target="tpu_custom_call" | custom-call | flops 1811939328 | bytes 9437184 | tf_op jit(solution)/shard_map/pallas_call | solution.py:108
  116.5 1.8 %collective-permute-done.80.refs_0_ = bf16[24,2048]{1,0:T(8,128)(2,1)S(1)} collective-permute-done((bf16[24,2048]{1,0:T(8,128)(2,1)S(1)}, bf16[24,2048]{1,0:T(8,128)(2,1)S(1)}, u32[]{:S(2)}, u32[]{:S(2)}) %collective-permute-start.80) | collective-permute-done | bytes 98336 | tf_op jit(solution)/shard_map/ppermute | solution.py:285
  118.2 1.6 %collective-permute-start.77 = (bf16[48,2048]{1,0:T(8,128)(2,1)S(1)}, bf16[48,2048]{1,0:T(8,128)(2,1)S(1)}, u32[]{:S(2)}, u32[]{:S(2)}) collective-permute-start(bf16[48,2048]{1,0:T(8,128)(2,1)S(1)} %shard_map.118), channel_id=1, source_target_pairs={{0,4},{1,5},{4,8},{5,9},{8,12},{9,13},{12,14},{13,15},{14,10},{15,... | collective-permute-start | bytes 589832 | tf_op jit(solution)/shard_map/ppermute | solution.py:285
  120.5 2.1 %shard_map.113 = (bf16[96,2048]{1,0:T(8,128)(2,1)S(1)}, bf16[96,2048]{1,0:T(8,128)(2,1)S(1)}) custom-call(bf16[48,2176]{1,0:T(8,128)(2,1)S(1)} %collective-permute-done.56.refs_0_, bf16[48,2176]{1,0:T(8,128)(2,1)S(1)} %collective-permute-done.57.refs_1_, bf16[48,2176]{1,0:T(8,128)(2,1)S(1)} %collective-permute-done.58.refs_2_, ...), custom_call_target="tpu_custom_call" | custom-call | flops 1811939328 | bytes 9437184 | tf_op jit(solution)/shard_map/pallas_call | solution.py:108
  123.9 1.6 %collective-permute-start.48 = (bf16[48,2048]{1,0:T(8,128)(2,1)S(1)}, bf16[48,2048]{1,0:T(8,128)(2,1)S(1)}, u32[]{:S(2)}, u32[]{:S(2)}) collective-permute-start(bf16[48,2048]{1,0:T(8,128)(2,1)S(1)} %shard_map.106), channel_id=1, source_target_pairs={{0,4},{1,5},{4,8},{5,9},{8,12},{9,13},{12,14},{13,15},{14,10},{15,... | collective-permute-start | bytes 589832 | tf_op jit(solution)/shard_map/ppermute | solution.py:285
  126.1 1.1 collective-permute-done.81.refs_0_
  127.3 1.5 %collective-permute-start.78 = (bf16[48,2048]{1,0:T(8,128)(2,1)S(1)}, bf16[48,2048]{1,0:T(8,128)(2,1)S(1)}, u32[]{:S(2)}, u32[]{:S(2)}) collective-permute-start(bf16[48,2048]{1,0:T(8,128)(2,1)S(1)} %shard_map.119), channel_id=1, source_target_pairs={{0,4},{1,5},{4,8},{5,9},{8,12},{9,13},{12,14},{13,15},{14,10},{15,... | collective-permute-start | bytes 589832 | tf_op jit(solution)/shard_map/ppermute | solution.py:285
  128.8 1.7 %shard_map.99 = (bf16[48,2048]{1,0:T(8,128)(2,1)S(1)}, bf16[48,2048]{1,0:T(8,128)(2,1)S(1)}) custom-call(bf16[48,2176]{1,0:T(8,128)(2,1)S(1)} %get-tuple-element.45.refs_0_, bf16[48,2176]{1,0:T(8,128)(2,1)S(1)} %collective-permute-done.24.refs_1_, bf16[2048,768]{1,0:T(8,128)(2,1)S(1)} %bitcast.26, bf16[2048,768]{1,0:T(8,128)(2,1)S(1)} %bitcast.36, ...), custom_call_target="tpu_custom_call" | custom-call | flops 905969664 | bytes 9437184 | tf_op jit(solution)/shard_map/pallas_call | solution.py:108
  131.1 1.7 %shard_map.112 = (bf16[48,2048]{1,0:T(8,128)(2,1)S(1)}, bf16[48,2048]{1,0:T(8,128)(2,1)S(1)}) custom-call(bf16[48,2176]{1,0:T(8,128)(2,1)S(1)} %get-tuple-element.56.refs_0_, bf16[48,2176]{1,0:T(8,128)(2,1)S(1)} %collective-permute-done.54.refs_1_, bf16[2048,768]{1,0:T(8,128)(2,1)S(1)} %bitcast.27, bf16[2048,768]{1,0:T(8,128)(2,1)S(1)} %bitcast.37, ...), custom_call_target="tpu_custom_call" | custom-call | flops 905969664 | bytes 9437184 | tf_op jit(solution)/shard_map/pallas_call | solution.py:108
  133.5 1.6 %collective-permute-start.49 = (bf16[48,2048]{1,0:T(8,128)(2,1)S(1)}, bf16[48,2048]{1,0:T(8,128)(2,1)S(1)}, u32[]{:S(2)}, u32[]{:S(2)}) collective-permute-start(bf16[48,2048]{1,0:T(8,128)(2,1)S(1)} %shard_map.107), channel_id=1, source_target_pairs={{0,4},{1,5},{4,8},{5,9},{8,12},{9,13},{12,14},{13,15},{14,10},{15,... | collective-permute-start | bytes 589832 | tf_op jit(solution)/shard_map/ppermute | solution.py:285
  135.7 1.0 collective-permute-done.82.refs_0_
  137.8 1.1 collective-permute-start.83
  138.9 2.5 %collective-permute-done.49.refs_2_ = bf16[48,2048]{1,0:T(8,128)(2,1)S(1)} collective-permute-done((bf16[48,2048]{1,0:T(8,128)(2,1)S(1)}, bf16[48,2048]{1,0:T(8,128)(2,1)S(1)}, u32[]{:S(2)}, u32[]{:S(2)}) %collective-permute-start.49) | collective-permute-done | bytes 196640 | tf_op jit(solution)/shard_map/ppermute | solution.py:285
  141.4 1.5 %collective-permute-done.53.refs_3_ = bf16[48,2048]{1,0:T(8,128)(2,1)S(1)} collective-permute-done((bf16[48,2048]{1,0:T(8,128)(2,1)S(1)}, bf16[48,2048]{1,0:T(8,128)(2,1)S(1)}, u32[]{:S(2)}, u32[]{:S(2)}) %collective-permute-start.53) | collective-permute-done | bytes 196640 | tf_op jit(solution)/shard_map/ppermute | solution.py:285
  142.9 1.7 %collective-permute-done.79.refs_6_ = bf16[48,2048]{1,0:T(8,128)(2,1)S(1)} collective-permute-done((bf16[48,2048]{1,0:T(8,128)(2,1)S(1)}, bf16[48,2048]{1,0:T(8,128)(2,1)S(1)}, u32[]{:S(2)}, u32[]{:S(2)}) %collective-permute-start.79) | collective-permute-done | bytes 196640 | tf_op jit(solution)/shard_map/ppermute | solution.py:285
  144.6 1.4 collective-permute-done.83.refs_7_
  (172 shorter events, 23.3 us)
Async XLA Ops:
  4.5 13.9 %collective-permute-start = (bf16[96,8,2,72]{3,0,1,2:T(8,128)(2,1)S(1)}, bf16[96,8,2,72]{3,0,1,2:T(8,128)(2,1)S(1)}, u32[]{:S(2)}, u32[]{:S(2)}) collective-permute-start(bf16[96,8,2,72]{3,0,1,2:T(8,128)(2,1)S(1)} %get-tuple-element.70), channel_id=1, source_target_pairs={{0,1},{1,0},{2,3},{3,2},{4,5},{5,4},{6,7},{7,6},{8,9},{9,8},{10,11... | collective-permute-start | bytes 663560 | tf_op jit(solution)/shard_map/ppermute | solution.py:293
  5.4 7.7 %collective-permute-start.2 = (bf16[72,1024]{1,0:T(8,128)(2,1)S(1)}, bf16[72,1024]{1,0:T(8,128)(2,1)S(1)}, u32[]{:S(2)}, u32[]{:S(2)}) collective-permute-start(bf16[72,1024]{1,0:T(8,128)(2,1)S(1)} %get-tuple-element.72.refs_0_), channel_id=1, source_target_pairs={{0,4},{1,5},{4,8},{5,9},{8,12},{9,13},{12,14},{13,15},{14,10},{15,... | collective-permute-start | bytes 442376 | tf_op jit(solution)/shard_map/ppermute | solution.py:285
  8.5 6.7 %collective-permute-start.3 = (bf16[72,1024]{1,0:T(8,128)(2,1)S(1)}, bf16[72,1024]{1,0:T(8,128)(2,1)S(1)}, u32[]{:S(2)}, u32[]{:S(2)}) collective-permute-start(bf16[72,1024]{1,0:T(8,128)(2,1)S(1)} %get-tuple-element.72.refs_0_), channel_id=1, source_target_pairs={{0,2},{1,3},{4,0},{5,1},{8,4},{9,5},{12,8},{13,9},{14,12},{15,13},... | collective-permute-start | bytes 442376 | tf_op jit(solution)/shard_map/ppermute | solution.py:285
  8.5 7.8 %collective-permute-start.13 = (bf16[72,1024]{1,0:T(8,128)(2,1)S(1)}, bf16[72,1024]{1,0:T(8,128)(2,1)S(1)}, u32[]{:S(2)}, u32[]{:S(2)}) collective-permute-start(bf16[72,1024]{1,0:T(8,128)(2,1)S(1)} %get-tuple-element.71.refs_0_), channel_id=1, source_target_pairs={{0,4},{1,5},{4,8},{5,9},{8,12},{9,13},{12,14},{13,15},{14,10},{15,... | collective-permute-start | bytes 442376 | tf_op jit(solution)/shard_map/ppermute | solution.py:285
  10.6 7.9 %collective-permute-start.14 = (bf16[72,1024]{1,0:T(8,128)(2,1)S(1)}, bf16[72,1024]{1,0:T(8,128)(2,1)S(1)}, u32[]{:S(2)}, u32[]{:S(2)}) collective-permute-start(bf16[72,1024]{1,0:T(8,128)(2,1)S(1)} %get-tuple-element.71.refs_0_), channel_id=1, source_target_pairs={{0,2},{1,3},{4,0},{5,1},{8,4},{9,5},{12,8},{13,9},{14,12},{15,13},... | collective-permute-start | bytes 442376 | tf_op jit(solution)/shard_map/ppermute | solution.py:285
  13.1 7.6 %collective-permute-start.4 = (bf16[72,1024]{1,0:T(8,128)(2,1)S(1)}, bf16[72,1024]{1,0:T(8,128)(2,1)S(1)}, u32[]{:S(2)}, u32[]{:S(2)}) collective-permute-start(bf16[72,1024]{1,0:T(8,128)(2,1)S(1)} %collective-permute-done.2.refs_1_), channel_id=1, source_target_pairs={{0,4},{1,5},{4,8},{5,9},{8,12},{9,13},{12,14},{13,15},{14,10},{15,... | collective-permute-start | bytes 442376 | tf_op jit(solution)/shard_map/ppermute | solution.py:285
  15.2 7.0 %collective-permute-start.5 = (bf16[72,1024]{1,0:T(8,128)(2,1)S(1)}, bf16[72,1024]{1,0:T(8,128)(2,1)S(1)}, u32[]{:S(2)}, u32[]{:S(2)}) collective-permute-start(bf16[72,1024]{1,0:T(8,128)(2,1)S(1)} %collective-permute-done.3.refs_2_), channel_id=1, source_target_pairs={{0,2},{1,3},{4,0},{5,1},{8,4},{9,5},{12,8},{13,9},{14,12},{15,13},... | collective-permute-start | bytes 442376 | tf_op jit(solution)/shard_map/ppermute | solution.py:285
  16.3 6.7 %collective-permute-start.15 = (bf16[72,1024]{1,0:T(8,128)(2,1)S(1)}, bf16[72,1024]{1,0:T(8,128)(2,1)S(1)}, u32[]{:S(2)}, u32[]{:S(2)}) collective-permute-start(bf16[72,1024]{1,0:T(8,128)(2,1)S(1)} %collective-permute-done.13.refs_1_), channel_id=1, source_target_pairs={{0,4},{1,5},{4,8},{5,9},{8,12},{9,13},{12,14},{13,15},{14,10},{15,... | collective-permute-start | bytes 442376 | tf_op jit(solution)/shard_map/ppermute | solution.py:285
  18.4 6.7 %collective-permute-start.16 = (bf16[72,1024]{1,0:T(8,128)(2,1)S(1)}, bf16[72,1024]{1,0:T(8,128)(2,1)S(1)}, u32[]{:S(2)}, u32[]{:S(2)}) collective-permute-start(bf16[72,1024]{1,0:T(8,128)(2,1)S(1)} %collective-permute-done.14.refs_2_), channel_id=1, source_target_pairs={{0,2},{1,3},{4,0},{5,1},{8,4},{9,5},{12,8},{13,9},{14,12},{15,13},... | collective-permute-start | bytes 442376 | tf_op jit(solution)/shard_map/ppermute | solution.py:285
  18.7 12.8 %collective-permute-start.1 = (bf16[192,8,72]{2,0,1:T(8,128)(2,1)S(1)}, bf16[192,8,72]{2,0,1:T(8,128)(2,1)S(1)}, u32[]{:S(2)}, u32[]{:S(2)}) collective-permute-start(bf16[192,8,72]{2,0,1:T(8,128)(2,1)S(1)} %get-tuple-element.68), channel_id=1, source_target_pairs={{0,16},{16,0},{1,17},{17,1},{2,18},{18,2},{3,19},{19,3},{4,20},{20... | collective-permute-start | bytes 663560 | tf_op jit(solution)/shard_map/ppermute | solution.py:297
  20.7 6.3 %collective-permute-start.6 = (bf16[72,1024]{1,0:T(8,128)(2,1)S(1)}, bf16[72,1024]{1,0:T(8,128)(2,1)S(1)}, u32[]{:S(2)}, u32[]{:S(2)}) collective-permute-start(bf16[72,1024]{1,0:T(8,128)(2,1)S(1)} %collective-permute-done.4.refs_3_), channel_id=1, source_target_pairs={{0,4},{1,5},{4,8},{5,9},{8,12},{9,13},{12,14},{13,15},{14,10},{15,... | collective-permute-start | bytes 442376 | tf_op jit(solution)/shard_map/ppermute | solution.py:285
  22.3 6.5 %collective-permute-start.7 = (bf16[72,1024]{1,0:T(8,128)(2,1)S(1)}, bf16[72,1024]{1,0:T(8,128)(2,1)S(1)}, u32[]{:S(2)}, u32[]{:S(2)}) collective-permute-start(bf16[72,1024]{1,0:T(8,128)(2,1)S(1)} %collective-permute-done.5.refs_4_), channel_id=1, source_target_pairs={{0,2},{1,3},{4,0},{5,1},{8,4},{9,5},{12,8},{13,9},{14,12},{15,13},... | collective-permute-start | bytes 442376 | tf_op jit(solution)/shard_map/ppermute | solution.py:285
  23.0 6.4 %collective-permute-start.17 = (bf16[72,1024]{1,0:T(8,128)(2,1)S(1)}, bf16[72,1024]{1,0:T(8,128)(2,1)S(1)}, u32[]{:S(2)}, u32[]{:S(2)}) collective-permute-start(bf16[72,1024]{1,0:T(8,128)(2,1)S(1)} %collective-permute-done.15.refs_3_), channel_id=1, source_target_pairs={{0,4},{1,5},{4,8},{5,9},{8,12},{9,13},{12,14},{13,15},{14,10},{15,... | collective-permute-start | bytes 442376 | tf_op jit(solution)/shard_map/ppermute | solution.py:285
  25.1 6.1 %collective-permute-start.18 = (bf16[72,1024]{1,0:T(8,128)(2,1)S(1)}, bf16[72,1024]{1,0:T(8,128)(2,1)S(1)}, u32[]{:S(2)}, u32[]{:S(2)}) collective-permute-start(bf16[72,1024]{1,0:T(8,128)(2,1)S(1)} %collective-permute-done.16.refs_4_), channel_id=1, source_target_pairs={{0,2},{1,3},{4,0},{5,1},{8,4},{9,5},{12,8},{13,9},{14,12},{15,13},... | collective-permute-start | bytes 442376 | tf_op jit(solution)/shard_map/ppermute | solution.py:285
  27.0 7.8 %collective-permute-start.8 = (bf16[40,1024]{1,0:T(8,128)(2,1)S(1)}, bf16[40,1024]{1,0:T(8,128)(2,1)S(1)}, u32[]{:S(2)}, u32[]{:S(2)}) collective-permute-start(bf16[40,1024]{1,0:T(8,128)(2,1)S(1)} %slice.64), channel_id=1, source_target_pairs={{0,4},{1,5},{4,8},{5,9},{8,12},{9,13},{12,14},{13,15},{14,10},{15,... | collective-permute-start | bytes 245768 | tf_op jit(solution)/shard_map/ppermute | solution.py:285
  28.8 6.0 %collective-permute-start.9 = (bf16[32,1024]{1,0:T(8,128)(2,1)S(1)}, bf16[32,1024]{1,0:T(8,128)(2,1)S(1)}, u32[]{:S(2)}, u32[]{:S(2)}) collective-permute-start(bf16[32,1024]{1,0:T(8,128)(2,1)S(1)} %slice.65), channel_id=1, source_target_pairs={{0,2},{1,3},{4,0},{5,1},{8,4},{9,5},{12,8},{13,9},{14,12},{15,13},... | collective-permute-start | bytes 196616 | tf_op jit(solution)/shard_map/ppermute | solution.py:285
  29.4 6.2 %collective-permute-start.19 = (bf16[40,1024]{1,0:T(8,128)(2,1)S(1)}, bf16[40,1024]{1,0:T(8,128)(2,1)S(1)}, u32[]{:S(2)}, u32[]{:S(2)}) collective-permute-start(bf16[40,1024]{1,0:T(8,128)(2,1)S(1)} %slice.66), channel_id=1, source_target_pairs={{0,4},{1,5},{4,8},{5,9},{8,12},{9,13},{12,14},{13,15},{14,10},{15,... | collective-permute-start | bytes 245768 | tf_op jit(solution)/shard_map/ppermute | solution.py:285
  37.2 7.8 %collective-permute-start.12 = (bf16[96,1024]{1,0:T(8,128)(2,1)S(1)}, bf16[96,1024]{1,0:T(8,128)(2,1)S(1)}, u32[]{:S(2)}, u32[]{:S(2)}) collective-permute-start(bf16[96,1024]{1,0:T(8,128)(2,1)S(1)} %shard_map.93), channel_id=1, source_target_pairs={{0,16},{16,0},{1,17},{17,1},{2,18},{18,2},{3,19},{19,3},{4,20},{20... | collective-permute-start | bytes 589832 | tf_op jit(solution)/shard_map/ppermute | solution.py:331
  38.8 9.6 %collective-permute-start.23 = (bf16[96,1024]{1,0:T(8,128)(2,1)S(1)}, bf16[96,1024]{1,0:T(8,128)(2,1)S(1)}, u32[]{:S(2)}, u32[]{:S(2)}) collective-permute-start(bf16[96,1024]{1,0:T(8,128)(2,1)S(1)} %shard_map.96), channel_id=1, source_target_pairs={{0,16},{16,0},{1,17},{17,1},{2,18},{18,2},{3,19},{19,3},{4,20},{20... | collective-permute-start | bytes 589832 | tf_op jit(solution)/shard_map/ppermute | solution.py:331
  48.7 8.1 %collective-permute-start.26 = (bf16[48,2176]{1,0:T(8,128)(2,1)S(1)}, bf16[48,2176]{1,0:T(8,128)(2,1)S(1)}, u32[]{:S(2)}, u32[]{:S(2)}) collective-permute-start(bf16[48,2176]{1,0:T(8,128)(2,1)S(1)} %get-tuple-element.45.refs_0_), channel_id=1, source_target_pairs={{0,4},{1,5},{4,8},{5,9},{8,12},{9,13},{12,14},{13,15},{14,10},{15,... | collective-permute-start | bytes 626696 | tf_op jit(solution)/shard_map/ppermute | solution.py:285
  50.6 8.0 %collective-permute-start.27 = (bf16[48,2176]{1,0:T(8,128)(2,1)S(1)}, bf16[48,2176]{1,0:T(8,128)(2,1)S(1)}, u32[]{:S(2)}, u32[]{:S(2)}) collective-permute-start(bf16[48,2176]{1,0:T(8,128)(2,1)S(1)} %get-tuple-element.45.refs_0_), channel_id=1, source_target_pairs={{0,2},{1,3},{4,0},{5,1},{8,4},{9,5},{12,8},{13,9},{14,12},{15,13},... | collective-permute-start | bytes 626696 | tf_op jit(solution)/shard_map/ppermute | solution.py:285
  50.8 10.5 %collective-permute-start.56 = (bf16[48,2176]{1,0:T(8,128)(2,1)S(1)}, bf16[48,2176]{1,0:T(8,128)(2,1)S(1)}, u32[]{:S(2)}, u32[]{:S(2)}) collective-permute-start(bf16[48,2176]{1,0:T(8,128)(2,1)S(1)} %get-tuple-element.56.refs_0_), channel_id=1, source_target_pairs={{0,4},{1,5},{4,8},{5,9},{8,12},{9,13},{12,14},{13,15},{14,10},{15,... | collective-permute-start | bytes 626696 | tf_op jit(solution)/shard_map/ppermute | solution.py:285
  52.6 10.5 %collective-permute-start.57 = (bf16[48,2176]{1,0:T(8,128)(2,1)S(1)}, bf16[48,2176]{1,0:T(8,128)(2,1)S(1)}, u32[]{:S(2)}, u32[]{:S(2)}) collective-permute-start(bf16[48,2176]{1,0:T(8,128)(2,1)S(1)} %get-tuple-element.56.refs_0_), channel_id=1, source_target_pairs={{0,2},{1,3},{4,0},{5,1},{8,4},{9,5},{12,8},{13,9},{14,12},{15,13},... | collective-permute-start | bytes 626696 | tf_op jit(solution)/shard_map/ppermute | solution.py:285
  56.8 9.0 %collective-permute-start.31 = (bf16[48,2176]{1,0:T(8,128)(2,1)S(1)}, bf16[48,2176]{1,0:T(8,128)(2,1)S(1)}, u32[]{:S(2)}, u32[]{:S(2)}) collective-permute-start(bf16[48,2176]{1,0:T(8,128)(2,1)S(1)} %collective-permute-done.26.refs_0_), channel_id=1, source_target_pairs={{0,4},{1,5},{4,8},{5,9},{8,12},{9,13},{12,14},{13,15},{14,10},{15,... | collective-permute-start | bytes 626696 | tf_op jit(solution)/shard_map/ppermute | solution.py:285
  58.6 9.0 %collective-permute-start.24 = (bf16[48,2176]{1,0:T(8,128)(2,1)S(1)}, bf16[48,2176]{1,0:T(8,128)(2,1)S(1)}, u32[]{:S(2)}, u32[]{:S(2)}) collective-permute-start(bf16[48,2176]{1,0:T(8,128)(2,1)S(1)} %get-tuple-element.45.refs_0_), channel_id=1, source_target_pairs={{0,1},{1,0},{2,3},{3,2},{4,5},{5,4},{6,7},{7,6},{8,9},{9,8},{10,11... | collective-permute-start | bytes 626696 | tf_op jit(solution)/shard_map/ppermute | solution.py:349
  58.6 9.0 %collective-permute-start.32 = (bf16[48,2176]{1,0:T(8,128)(2,1)S(1)}, bf16[48,2176]{1,0:T(8,128)(2,1)S(1)}, u32[]{:S(2)}, u32[]{:S(2)}) collective-permute-start(bf16[48,2176]{1,0:T(8,128)(2,1)S(1)} %collective-permute-done.27.refs_1_), channel_id=1, source_target_pairs={{0,2},{1,3},{4,0},{5,1},{8,4},{9,5},{12,8},{13,9},{14,12},{15,13},... | collective-permute-start | bytes 626696 | tf_op jit(solution)/shard_map/ppermute | solution.py:285
  61.3 9.0 %collective-permute-start.61 = (bf16[48,2176]{1,0:T(8,128)(2,1)S(1)}, bf16[48,2176]{1,0:T(8,128)(2,1)S(1)}, u32[]{:S(2)}, u32[]{:S(2)}) collective-permute-start(bf16[48,2176]{1,0:T(8,128)(2,1)S(1)} %collective-permute-done.56.refs_0_), channel_id=1, source_target_pairs={{0,4},{1,5},{4,8},{5,9},{8,12},{9,13},{12,14},{13,15},{14,10},{15,... | collective-permute-start | bytes 626696 | tf_op jit(solution)/shard_map/ppermute | solution.py:285
  63.1 7.6 %collective-permute-start.62 = (bf16[48,2176]{1,0:T(8,128)(2,1)S(1)}, bf16[48,2176]{1,0:T(8,128)(2,1)S(1)}, u32[]{:S(2)}, u32[]{:S(2)}) collective-permute-start(bf16[48,2176]{1,0:T(8,128)(2,1)S(1)} %collective-permute-done.57.refs_1_), channel_id=1, source_target_pairs={{0,2},{1,3},{4,0},{5,1},{8,4},{9,5},{12,8},{13,9},{14,12},{15,13},... | collective-permute-start | bytes 626696 | tf_op jit(solution)/shard_map/ppermute | solution.py:285
  65.8 7.3 %collective-permute-start.36 = (bf16[48,2176]{1,0:T(8,128)(2,1)S(1)}, bf16[48,2176]{1,0:T(8,128)(2,1)S(1)}, u32[]{:S(2)}, u32[]{:S(2)}) collective-permute-start(bf16[48,2176]{1,0:T(8,128)(2,1)S(1)} %collective-permute-done.31.refs_0_), channel_id=1, source_target_pairs={{0,4},{1,5},{4,8},{5,9},{8,12},{9,13},{12,14},{13,15},{14,10},{15,... | collective-permute-start | bytes 626696 | tf_op jit(solution)/shard_map/ppermute | solution.py:285
  67.6 7.2 %collective-permute-start.28 = (bf16[48,2176]{1,0:T(8,128)(2,1)S(1)}, bf16[48,2176]{1,0:T(8,128)(2,1)S(1)}, u32[]{:S(2)}, u32[]{:S(2)}) collective-permute-start(bf16[48,2176]{1,0:T(8,128)(2,1)S(1)} %collective-permute-done.26.refs_0_), channel_id=1, source_target_pairs={{0,1},{1,0},{2,3},{3,2},{4,5},{5,4},{6,7},{7,6},{8,9},{9,8},{10,11... | collective-permute-start | bytes 626696 | tf_op jit(solution)/shard_map/ppermute | solution.py:349
  67.6 7.8 %collective-permute-start.37 = (bf16[48,2176]{1,0:T(8,128)(2,1)S(1)}, bf16[48,2176]{1,0:T(8,128)(2,1)S(1)}, u32[]{:S(2)}, u32[]{:S(2)}) collective-permute-start(bf16[48,2176]{1,0:T(8,128)(2,1)S(1)} %collective-permute-done.32.refs_1_), channel_id=1, source_target_pairs={{0,2},{1,3},{4,0},{5,1},{8,4},{9,5},{12,8},{13,9},{14,12},{15,13},... | collective-permute-start | bytes 626696 | tf_op jit(solution)/shard_map/ppermute | solution.py:285
  70.2 6.8 %collective-permute-start.29 = (bf16[48,2176]{1,0:T(8,128)(2,1)S(1)}, bf16[48,2176]{1,0:T(8,128)(2,1)S(1)}, u32[]{:S(2)}, u32[]{:S(2)}) collective-permute-start(bf16[48,2176]{1,0:T(8,128)(2,1)S(1)} %collective-permute-done.27.refs_1_), channel_id=1, source_target_pairs={{0,1},{1,0},{2,3},{3,2},{4,5},{5,4},{6,7},{7,6},{8,9},{9,8},{10,11... | collective-permute-start | bytes 626696 | tf_op jit(solution)/shard_map/ppermute | solution.py:349
  70.7 9.5 %collective-permute-start.66 = (bf16[48,2176]{1,0:T(8,128)(2,1)S(1)}, bf16[48,2176]{1,0:T(8,128)(2,1)S(1)}, u32[]{:S(2)}, u32[]{:S(2)}) collective-permute-start(bf16[48,2176]{1,0:T(8,128)(2,1)S(1)} %collective-permute-done.61.refs_0_), channel_id=1, source_target_pairs={{0,4},{1,5},{4,8},{5,9},{8,12},{9,13},{12,14},{13,15},{14,10},{15,... | collective-permute-start | bytes 626696 | tf_op jit(solution)/shard_map/ppermute | solution.py:285
  73.0 7.7 %collective-permute-start.67 = (bf16[48,2176]{1,0:T(8,128)(2,1)S(1)}, bf16[48,2176]{1,0:T(8,128)(2,1)S(1)}, u32[]{:S(2)}, u32[]{:S(2)}) collective-permute-start(bf16[48,2176]{1,0:T(8,128)(2,1)S(1)} %collective-permute-done.62.refs_1_), channel_id=1, source_target_pairs={{0,2},{1,3},{4,0},{5,1},{8,4},{9,5},{12,8},{13,9},{14,12},{15,13},... | collective-permute-start | bytes 626696 | tf_op jit(solution)/shard_map/ppermute | solution.py:285
  74.8 7.1 %collective-permute-start.58 = (bf16[48,2176]{1,0:T(8,128)(2,1)S(1)}, bf16[48,2176]{1,0:T(8,128)(2,1)S(1)}, u32[]{:S(2)}, u32[]{:S(2)}) collective-permute-start(bf16[48,2176]{1,0:T(8,128)(2,1)S(1)} %collective-permute-done.56.refs_0_), channel_id=1, source_target_pairs={{0,1},{1,0},{2,3},{3,2},{4,5},{5,4},{6,7},{7,6},{8,9},{9,8},{10,11... | collective-permute-start | bytes 626696 | tf_op jit(solution)/shard_map/ppermute | solution.py:349
  80.2 8.4 %collective-permute-start.38 = (bf16[48,2176]{1,0:T(8,128)(2,1)S(1)}, bf16[48,2176]{1,0:T(8,128)(2,1)S(1)}, u32[]{:S(2)}, u32[]{:S(2)}) collective-permute-start(bf16[48,2176]{1,0:T(8,128)(2,1)S(1)} %collective-permute-done.36.refs_0_), channel_id=1, source_target_pairs={{0,1},{1,0},{2,3},{3,2},{4,5},{5,4},{6,7},{7,6},{8,9},{9,8},{10,11... | collective-permute-start | bytes 626696 | tf_op jit(solution)/shard_map/ppermute | solution.py:349
  80.7 8.4 %collective-permute-start.39 = (bf16[48,2176]{1,0:T(8,128)(2,1)S(1)}, bf16[48,2176]{1,0:T(8,128)(2,1)S(1)}, u32[]{:S(2)}, u32[]{:S(2)}) collective-permute-start(bf16[48,2176]{1,0:T(8,128)(2,1)S(1)} %collective-permute-done.37.refs_1_), channel_id=1, source_target_pairs={{0,1},{1,0},{2,3},{3,2},{4,5},{5,4},{6,7},{7,6},{8,9},{9,8},{10,11... | collective-permute-start | bytes 626696 | tf_op jit(solution)/shard_map/ppermute | solution.py:349
  84.0 7.3 %collective-permute-start.68 = (bf16[48,2176]{1,0:T(8,128)(2,1)S(1)}, bf16[48,2176]{1,0:T(8,128)(2,1)S(1)}, u32[]{:S(2)}, u32[]{:S(2)}) collective-permute-start(bf16[48,2176]{1,0:T(8,128)(2,1)S(1)} %collective-permute-done.66.refs_0_), channel_id=1, source_target_pairs={{0,1},{1,0},{2,3},{3,2},{4,5},{5,4},{6,7},{7,6},{8,9},{9,8},{10,11... | collective-permute-start | bytes 626696 | tf_op jit(solution)/shard_map/ppermute | solution.py:349
  87.3 6.7 %collective-permute-start.69 = (bf16[48,2176]{1,0:T(8,128)(2,1)S(1)}, bf16[48,2176]{1,0:T(8,128)(2,1)S(1)}, u32[]{:S(2)}, u32[]{:S(2)}) collective-permute-start(bf16[48,2176]{1,0:T(8,128)(2,1)S(1)} %collective-permute-done.67.refs_1_), channel_id=1, source_target_pairs={{0,1},{1,0},{2,3},{3,2},{4,5},{5,4},{6,7},{7,6},{8,9},{9,8},{10,11... | collective-permute-start | bytes 626696 | tf_op jit(solution)/shard_map/ppermute | solution.py:349
  94.0 7.1 %collective-permute-start.64 = (bf16[48,2176]{1,0:T(8,128)(2,1)S(1)}, bf16[48,2176]{1,0:T(8,128)(2,1)S(1)}, u32[]{:S(2)}, u32[]{:S(2)}) collective-permute-start(bf16[48,2176]{1,0:T(8,128)(2,1)S(1)} %collective-permute-done.62.refs_1_), channel_id=1, source_target_pairs={{0,1},{1,0},{2,3},{3,2},{4,5},{5,4},{6,7},{7,6},{8,9},{9,8},{10,11... | collective-permute-start | bytes 626696 | tf_op jit(solution)/shard_map/ppermute | solution.py:349
  94.2 7.0 %collective-permute-start.75 = (bf16[48,2048]{1,0:T(8,128)(2,1)S(1)}, bf16[48,2048]{1,0:T(8,128)(2,1)S(1)}, u32[]{:S(2)}, u32[]{:S(2)}) collective-permute-start(bf16[48,2048]{1,0:T(8,128)(2,1)S(1)} %get-tuple-element.66), channel_id=1, source_target_pairs={{0,1},{1,0},{2,3},{3,2},{4,5},{5,4},{6,7},{7,6},{8,9},{9,8},{10,11... | collective-permute-start | bytes 589832 | tf_op jit(solution)/shard_map/ppermute | solution.py:351
  96.8 10.0 %collective-permute-start.40 = (bf16[96,2048]{1,0:T(8,128)(2,1)S(1)}, bf16[96,2048]{1,0:T(8,128)(2,1)S(1)}, u32[]{:S(2)}, u32[]{:S(2)}) collective-permute-start(bf16[96,2048]{1,0:T(8,128)(2,1)S(1)} %get-tuple-element.53), channel_id=1, source_target_pairs={{0,1},{1,0},{2,3},{3,2},{4,5},{5,4},{6,7},{7,6},{8,9},{9,8},{10,11... | collective-permute-start | bytes 1179656 | tf_op jit(solution)/shard_map/ppermute | solution.py:351
  97.0 16.1 %collective-permute-start.70 = (bf16[96,2048]{1,0:T(8,128)(2,1)S(1)}, bf16[96,2048]{1,0:T(8,128)(2,1)S(1)}, u32[]{:S(2)}, u32[]{:S(2)}) collective-permute-start(bf16[96,2048]{1,0:T(8,128)(2,1)S(1)} %get-tuple-element.64), channel_id=1, source_target_pairs={{0,1},{1,0},{2,3},{3,2},{4,5},{5,4},{6,7},{7,6},{8,9},{9,8},{10,11... | collective-permute-start | bytes 1179656 | tf_op jit(solution)/shard_map/ppermute | solution.py:351
  101.1 7.5 %collective-permute-start.59 = (bf16[48,2176]{1,0:T(8,128)(2,1)S(1)}, bf16[48,2176]{1,0:T(8,128)(2,1)S(1)}, u32[]{:S(2)}, u32[]{:S(2)}) collective-permute-start(bf16[48,2176]{1,0:T(8,128)(2,1)S(1)} %collective-permute-done.57.refs_1_), channel_id=1, source_target_pairs={{0,1},{1,0},{2,3},{3,2},{4,5},{5,4},{6,7},{7,6},{8,9},{9,8},{10,11... | collective-permute-start | bytes 626696 | tf_op jit(solution)/shard_map/ppermute | solution.py:349
  101.2 15.2 %collective-permute-start.35 = (bf16[96,2048]{1,0:T(8,128)(2,1)S(1)}, bf16[96,2048]{1,0:T(8,128)(2,1)S(1)}, u32[]{:S(2)}, u32[]{:S(2)}) collective-permute-start(bf16[96,2048]{1,0:T(8,128)(2,1)S(1)} %get-tuple-element.51), channel_id=1, source_target_pairs={{0,1},{1,0},{2,3},{3,2},{4,5},{5,4},{6,7},{7,6},{8,9},{9,8},{10,11... | collective-permute-start | bytes 1179656 | tf_op jit(solution)/shard_map/ppermute | solution.py:351
  106.8 13.1 %collective-permute-start.65 = (bf16[96,2048]{1,0:T(8,128)(2,1)S(1)}, bf16[96,2048]{1,0:T(8,128)(2,1)S(1)}, u32[]{:S(2)}, u32[]{:S(2)}) collective-permute-start(bf16[96,2048]{1,0:T(8,128)(2,1)S(1)} %get-tuple-element.62), channel_id=1, source_target_pairs={{0,1},{1,0},{2,3},{3,2},{4,5},{5,4},{6,7},{7,6},{8,9},{9,8},{10,11... | collective-permute-start | bytes 1179656 | tf_op jit(solution)/shard_map/ppermute | solution.py:351
  106.8 5.7 %collective-permute-start.76 = (bf16[24,2048]{1,0:T(8,128)(2,1)S(1)}, bf16[24,2048]{1,0:T(8,128)(2,1)S(1)}, u32[]{:S(2)}, u32[]{:S(2)}) collective-permute-start(bf16[24,2048]{1,0:T(8,128)(2,1)S(1)} %shard_map.117), channel_id=1, source_target_pairs={{0,4},{1,5},{4,8},{5,9},{8,12},{9,13},{12,14},{13,15},{14,10},{15,... | collective-permute-start | bytes 294920 | tf_op jit(solution)/shard_map/ppermute | solution.py:285
  108.6 11.3 %collective-permute-start.47 = (bf16[48,2048]{1,0:T(8,128)(2,1)S(1)}, bf16[48,2048]{1,0:T(8,128)(2,1)S(1)}, u32[]{:S(2)}, u32[]{:S(2)}) collective-permute-start(bf16[48,2048]{1,0:T(8,128)(2,1)S(1)} %shard_map.105), channel_id=1, source_target_pairs={{0,4},{1,5},{4,8},{5,9},{8,12},{9,13},{12,14},{13,15},{14,10},{15,... | collective-permute-start | bytes 589832 | tf_op jit(solution)/shard_map/ppermute | solution.py:285
  113.0 9.6 %collective-permute-start.51 = (bf16[48,2048]{1,0:T(8,128)(2,1)S(1)}, bf16[48,2048]{1,0:T(8,128)(2,1)S(1)}, u32[]{:S(2)}, u32[]{:S(2)}) collective-permute-start(bf16[48,2048]{1,0:T(8,128)(2,1)S(1)} %shard_map.109), channel_id=1, source_target_pairs={{0,2},{1,3},{4,0},{5,1},{8,4},{9,5},{12,8},{13,9},{14,12},{15,13},... | collective-permute-start | bytes 589832 | tf_op jit(solution)/shard_map/ppermute | solution.py:285
  116.4 14.1 %collective-permute-start.30 = (bf16[96,2048]{1,0:T(8,128)(2,1)S(1)}, bf16[96,2048]{1,0:T(8,128)(2,1)S(1)}, u32[]{:S(2)}, u32[]{:S(2)}) collective-permute-start(bf16[96,2048]{1,0:T(8,128)(2,1)S(1)} %get-tuple-element.49), channel_id=1, source_target_pairs={{0,1},{1,0},{2,3},{3,2},{4,5},{5,4},{6,7},{7,6},{8,9},{9,8},{10,11... | collective-permute-start | bytes 1179656 | tf_op jit(solution)/shard_map/ppermute | solution.py:351
  118.2 5.7 %collective-permute-start.77 = (bf16[48,2048]{1,0:T(8,128)(2,1)S(1)}, bf16[48,2048]{1,0:T(8,128)(2,1)S(1)}, u32[]{:S(2)}, u32[]{:S(2)}) collective-permute-start(bf16[48,2048]{1,0:T(8,128)(2,1)S(1)} %shard_map.118), channel_id=1, source_target_pairs={{0,4},{1,5},{4,8},{5,9},{8,12},{9,13},{12,14},{13,15},{14,10},{15,... | collective-permute-start | bytes 589832 | tf_op jit(solution)/shard_map/ppermute | solution.py:285
  119.9 5.8 %collective-permute-start.54 = (bf16[48,2176]{1,0:T(8,128)(2,1)S(1)}, bf16[48,2176]{1,0:T(8,128)(2,1)S(1)}, u32[]{:S(2)}, u32[]{:S(2)}) collective-permute-start(bf16[48,2176]{1,0:T(8,128)(2,1)S(1)} %get-tuple-element.56.refs_0_), channel_id=1, source_target_pairs={{0,1},{1,0},{2,3},{3,2},{4,5},{5,4},{6,7},{7,6},{8,9},{9,8},{10,11... | collective-permute-start | bytes 626696 | tf_op jit(solution)/shard_map/ppermute | solution.py:349
  120.0 7.3 %collective-permute-start.81 = (bf16[48,2048]{1,0:T(8,128)(2,1)S(1)}, bf16[48,2048]{1,0:T(8,128)(2,1)S(1)}, u32[]{:S(2)}, u32[]{:S(2)}) collective-permute-start(bf16[48,2048]{1,0:T(8,128)(2,1)S(1)} %shard_map.122), channel_id=1, source_target_pairs={{0,2},{1,3},{4,0},{5,1},{8,4},{9,5},{12,8},{13,9},{14,12},{15,13},... | collective-permute-start | bytes 589832 | tf_op jit(solution)/shard_map/ppermute | solution.py:285
  122.6 10.9 %collective-permute-start.60 = (bf16[96,2048]{1,0:T(8,128)(2,1)S(1)}, bf16[96,2048]{1,0:T(8,128)(2,1)S(1)}, u32[]{:S(2)}, u32[]{:S(2)}) collective-permute-start(bf16[96,2048]{1,0:T(8,128)(2,1)S(1)} %get-tuple-element.60), channel_id=1, source_target_pairs={{0,1},{1,0},{2,3},{3,2},{4,5},{5,4},{6,7},{7,6},{8,9},{9,8},{10,11... | collective-permute-start | bytes 1179656 | tf_op jit(solution)/shard_map/ppermute | solution.py:351
  123.9 7.2 %collective-permute-start.48 = (bf16[48,2048]{1,0:T(8,128)(2,1)S(1)}, bf16[48,2048]{1,0:T(8,128)(2,1)S(1)}, u32[]{:S(2)}, u32[]{:S(2)}) collective-permute-start(bf16[48,2048]{1,0:T(8,128)(2,1)S(1)} %shard_map.106), channel_id=1, source_target_pairs={{0,4},{1,5},{4,8},{5,9},{8,12},{9,13},{12,14},{13,15},{14,10},{15,... | collective-permute-start | bytes 589832 | tf_op jit(solution)/shard_map/ppermute | solution.py:285
  125.6 7.2 %collective-permute-start.52 = (bf16[48,2048]{1,0:T(8,128)(2,1)S(1)}, bf16[48,2048]{1,0:T(8,128)(2,1)S(1)}, u32[]{:S(2)}, u32[]{:S(2)}) collective-permute-start(bf16[48,2048]{1,0:T(8,128)(2,1)S(1)} %shard_map.110), channel_id=1, source_target_pairs={{0,2},{1,3},{4,0},{5,1},{8,4},{9,5},{12,8},{13,9},{14,12},{15,13},... | collective-permute-start | bytes 589832 | tf_op jit(solution)/shard_map/ppermute | solution.py:285
  127.3 7.9 %collective-permute-start.78 = (bf16[48,2048]{1,0:T(8,128)(2,1)S(1)}, bf16[48,2048]{1,0:T(8,128)(2,1)S(1)}, u32[]{:S(2)}, u32[]{:S(2)}) collective-permute-start(bf16[48,2048]{1,0:T(8,128)(2,1)S(1)} %shard_map.119), channel_id=1, source_target_pairs={{0,4},{1,5},{4,8},{5,9},{8,12},{9,13},{12,14},{13,15},{14,10},{15,... | collective-permute-start | bytes 589832 | tf_op jit(solution)/shard_map/ppermute | solution.py:285
  130.5 6.2 %collective-permute-start.82 = (bf16[48,2048]{1,0:T(8,128)(2,1)S(1)}, bf16[48,2048]{1,0:T(8,128)(2,1)S(1)}, u32[]{:S(2)}, u32[]{:S(2)}) collective-permute-start(bf16[48,2048]{1,0:T(8,128)(2,1)S(1)} %shard_map.123), channel_id=1, source_target_pairs={{0,2},{1,3},{4,0},{5,1},{8,4},{9,5},{12,8},{13,9},{14,12},{15,13},... | collective-permute-start | bytes 589832 | tf_op jit(solution)/shard_map/ppermute | solution.py:285
  131.1 6.7 %collective-permute-start.25 = (bf16[48,2048]{1,0:T(8,128)(2,1)S(1)}, bf16[48,2048]{1,0:T(8,128)(2,1)S(1)}, u32[]{:S(2)}, u32[]{:S(2)}) collective-permute-start(bf16[48,2048]{1,0:T(8,128)(2,1)S(1)} %get-tuple-element.47), channel_id=1, source_target_pairs={{0,1},{1,0},{2,3},{3,2},{4,5},{5,4},{6,7},{7,6},{8,9},{9,8},{10,11... | collective-permute-start | bytes 589832 | tf_op jit(solution)/shard_map/ppermute | solution.py:351
  132.9 6.0 %collective-permute-start.55 = (bf16[48,2048]{1,0:T(8,128)(2,1)S(1)}, bf16[48,2048]{1,0:T(8,128)(2,1)S(1)}, u32[]{:S(2)}, u32[]{:S(2)}) collective-permute-start(bf16[48,2048]{1,0:T(8,128)(2,1)S(1)} %get-tuple-element.58), channel_id=1, source_target_pairs={{0,1},{1,0},{2,3},{3,2},{4,5},{5,4},{6,7},{7,6},{8,9},{9,8},{10,11... | collective-permute-start | bytes 589832 | tf_op jit(solution)/shard_map/ppermute | solution.py:351
  133.5 7.8 %collective-permute-start.49 = (bf16[48,2048]{1,0:T(8,128)(2,1)S(1)}, bf16[48,2048]{1,0:T(8,128)(2,1)S(1)}, u32[]{:S(2)}, u32[]{:S(2)}) collective-permute-start(bf16[48,2048]{1,0:T(8,128)(2,1)S(1)} %shard_map.107), channel_id=1, source_target_pairs={{0,4},{1,5},{4,8},{5,9},{8,12},{9,13},{12,14},{13,15},{14,10},{15,... | collective-permute-start | bytes 589832 | tf_op jit(solution)/shard_map/ppermute | solution.py:285
  135.1 7.8 %collective-permute-start.53 = (bf16[48,2048]{1,0:T(8,128)(2,1)S(1)}, bf16[48,2048]{1,0:T(8,128)(2,1)S(1)}, u32[]{:S(2)}, u32[]{:S(2)}) collective-permute-start(bf16[48,2048]{1,0:T(8,128)(2,1)S(1)} %shard_map.111), channel_id=1, source_target_pairs={{0,2},{1,3},{4,0},{5,1},{8,4},{9,5},{12,8},{13,9},{14,12},{15,13},... | collective-permute-start | bytes 589832 | tf_op jit(solution)/shard_map/ppermute | solution.py:285
  136.7 7.9 %collective-permute-start.79 = (bf16[48,2048]{1,0:T(8,128)(2,1)S(1)}, bf16[48,2048]{1,0:T(8,128)(2,1)S(1)}, u32[]{:S(2)}, u32[]{:S(2)}) collective-permute-start(bf16[48,2048]{1,0:T(8,128)(2,1)S(1)} %shard_map.120), channel_id=1, source_target_pairs={{0,4},{1,5},{4,8},{5,9},{8,12},{9,13},{12,14},{13,15},{14,10},{15,... | collective-permute-start | bytes 589832 | tf_op jit(solution)/shard_map/ppermute | solution.py:285
  137.8 8.3 %collective-permute-start.83 = (bf16[48,2048]{1,0:T(8,128)(2,1)S(1)}, bf16[48,2048]{1,0:T(8,128)(2,1)S(1)}, u32[]{:S(2)}, u32[]{:S(2)}) collective-permute-start(bf16[48,2048]{1,0:T(8,128)(2,1)S(1)} %shard_map.124), channel_id=1, source_target_pairs={{0,2},{1,3},{4,0},{5,1},{8,4},{9,5},{12,8},{13,9},{14,12},{15,13},... | collective-permute-start | bytes 589832 | tf_op jit(solution)/shard_map/ppermute | solution.py:285
  (28 other events, 258.6 us)

commit v2 on v1

--- a/solution.py
+++ b/solution.py
@@ -120,20 +120,20 @@
     return jax.ShapeDtypeStruct((rows, width), dtype)
 
 
-def serve_body(blocks, *refs):
-    ins = refs[:blocks]
-    gate_ref, up_ref, down_ref, own_ref, other_ref, x_ref, h_ref = refs[blocks:]
+def serve_body(blocks, which, experts, *refs):
+    ins, tagged = refs[:blocks], refs[: blocks * (which + 1)][-blocks:]
+    gate_ref, up_ref, down_ref, own_ref, other_ref, x_ref, h_ref = refs[blocks * (which + 1) :]
     width, wide = gate_ref.shape
-    expert = lax.axis_index(DP)
     start = 0
     share = []
-    for ref in ins:
+    for ref, tag in zip(ins, tagged):
         size = ref.shape[0]
         x_ref[start : start + size, :] = ref[:, :width]
-        tags = ref[:, width:].astype(jnp.float32)
-        mine = lax.broadcasted_iota(jnp.int32, tags.shape, 1) == expert
-        chosen = jnp.sum(jnp.where(mine, tags, 0.0), axis=1, keepdims=True)
-        share.append(chosen / jnp.sum(tags, axis=1, keepdims=True))
+        tags = tag[:, width:].astype(jnp.float32)
+        lane = lax.broadcasted_iota(jnp.int32, tags.shape, 1) - which * experts
+        chosen = jnp.sum(jnp.where(lane == lax.axis_index(DP), tags, 0.0), axis=1, keepdims=True)
+        whole = jnp.sum(jnp.where((lane >= 0) & (lane < experts), tags, 0.0), axis=1, keepdims=True)
+        share.append(chosen / whole)
         start += size
     share = jnp.concatenate(share, axis=0)
     tile = tile_of(wide, 256)
@@ -150,13 +150,13 @@
         other_ref[:, at : at + tile] = out[half:].astype(jnp.bfloat16)
 
 
-def serve(ins, experts):
+def serve(which, ins, tagged, weights):
     rows = sum(x.shape[0] for x in ins)
-    width, wide = experts[0].shape
+    width, wide = weights[0].shape
     return kernel(
-        functools.partial(serve_body, len(ins)),
+        functools.partial(serve_body, len(ins), which, lax.axis_size(DP)),
         [shaped(rows // 2, width)] * 2,
-        [*ins, *experts],
+        [*ins, *tagged, *weights],
         [pltpu.VMEM((rows, width), jnp.bfloat16), pltpu.VMEM((rows, wide), jnp.bfloat16)],
         24 * MIB,
         6 * rows * width * wide,
@@ -164,13 +164,17 @@
     )
 
 
-def tag_body(ids_ref, counts_ref, out_ref):
-    rows, lanes = out_ref.shape
-    expert = lax.broadcasted_iota(jnp.int32, (lanes, rows), 0)
-    total = jnp.zeros((lanes, rows), jnp.float32)
+def tag_body(experts, ids_ref, counts_ref, out_ref):
+    cut, lanes = out_ref.shape
+    lane = lax.broadcasted_iota(jnp.int32, (lanes, ids_ref.shape[1]), 0)
+    total = jnp.zeros(lane.shape, jnp.float32)
     for k in range(ids_ref.shape[0]):
-        total += jnp.where(expert == ids_ref[k : k + 1, :], counts_ref[k : k + 1, :].astype(jnp.float32), 0.0)
-    out_ref[...] = total.T.astype(jnp.bfloat16)
+        counts = counts_ref[k : k + 1, :].astype(jnp.float32)
+        total += jnp.where(lane % experts == ids_ref[k : k + 1, :], counts, 0.0)
+    total = total.T
+    lane = lax.broadcasted_iota(jnp.int32, (cut, lanes), 1)
+    total = jnp.where(lane < experts, total[:cut], jnp.where(lane < 2 * experts, total[cut:], 0.0))
+    out_ref[...] = total.astype(jnp.bfloat16)
 
 
 def bulk_body(chips, offsets, act_ref, *refs):
@@ -205,8 +209,7 @@
     bias_ref, gain_ref, tags_ref, merged_ref, low_ref, high_ref = refs[3 * parts :]
     width = merged_ref.shape[1]
     cut = low_ref.shape[0]
-    low_ref[:, width:] = tags_ref[:cut, :]
-    high_ref[:, width:] = tags_ref[cut:, :]
+    low_ref[:, width:] = tags_ref[...]
     at = 0
     square = 0.0
     for index in range(parts):
@@ -218,7 +221,7 @@
         at = to
     scale = lax.rsqrt(square / width + 1e-06)
     low_ref[:, :width] = (merged_ref[:cut, :] * scale[:cut] * gain_ref[...]).astype(jnp.bfloat16)
-    high_ref[:, :width] = (merged_ref[cut:, :] * scale[cut:] * gain_ref[...]).astype(jnp.bfloat16)
+    high_ref[...] = (merged_ref[cut:, :] * scale[cut:] * gain_ref[...]).astype(jnp.bfloat16)
 
 
 def plus_body(*refs):
@@ -284,8 +287,7 @@
     def hop(way, array):
         return rings[way](array)
 
-    zero = jnp.uint32(0)
-    weight = lax.dynamic_slice(merger_weight, (lax.axis_index(GROUPS).astype(jnp.uint32) * half, zero), (half, width))
+    first = lax.axis_index(GROUPS).astype(jnp.uint32) * half
     act = jax.nn.gelu(merger_input.astype(jnp.float32), approximate=False).astype(jnp.bfloat16)
     act = act.reshape(rows, chips, 2, 2, half)
     kept = jnp.where(first_core, act[:, :, 0], act[:, :, 1])
@@ -297,14 +299,15 @@
     given = cross(given)
     act = jnp.concatenate([kept, given], axis=0).transpose(1, 0, 2)
 
-    lanes = -(-n // LANES) * LANES
-    tags = kernel(tag_body, shaped(rows, lanes), [expert_ids.T, combine_ints.T])
+    lanes = -(-2 * n // LANES) * LANES
+    tags = kernel(functools.partial(tag_body, n), shaped(cut, lanes), [expert_ids.T, combine_ints.T])
 
     mid = (half + 15) // 16 * 8
     share = width // PARTS
     streams = []
     for part in range(PARTS):
-        left = right = weight[:, part * share : (part + 1) * share]
+        weight = merger_weight if part == 0 else lax.optimization_barrier(merger_weight)
+        left = right = lax.dynamic_slice(weight, (first, jnp.uint32(part * share)), (half, share))
         offsets, pieces = [0], [left]
         for step in range(1, far):
             left, right = hop(0, left), hop(1, right)
@@ -332,7 +335,7 @@
         streams += [own, swap(own_other), theirs]
     merged, *block = kernel(
         functools.partial(norm_body, PARTS),
-        [shaped(rows, width, jnp.float32)] + [shaped(cut, width + lanes)] * 2,
+        [shaped(rows, width, jnp.float32), shaped(cut, width + lanes), shaped(cut, width)],
         [*streams, merger_bias[None], norm_gain[None], tags],
     )
 
@@ -345,12 +348,15 @@
     short = cut // 2
     arrived.append([(hop(0, side[0][:short]), hop(1, side[1][short:])) for side in sides])
 
-    def served(ins):
-        others = [swap(x) for x in ins]
-        own, other = serve([*ins, *others], experts)
-        return own, swap(other)
-
-    outs = [[served(ins) for ins in pair] for pair in arrived]
+    outs = []
+    for step, pair in enumerate(arrived):
+        tagged = []
+        outs.append([])
+        for which, ins in enumerate(pair):
+            ins = [*ins, *(swap(x) for x in ins)]
+            own, other = serve(which, ins, tagged, experts)
+            tagged = ins
+            outs[step].append((own, swap(other)))
 
     def home(way, which):
         total = add(*outs[far][which], way * short, short)

time: 147 us -> 148 us (level)
  transfers between devices with their start and end apart: 84 -> 84, of which waited for: 30 -> 31; matrix products, arithmetic and copies ran while one was open for 0% -> 3% of each run, Pallas kernels for 17% -> 17%
where the time goes in v2:
time: 148 us
  starting transfers between devices  62.7 us (42%)
  waiting for transfers between devices  52.5 us (35%)
  Pallas kernels  26 us (18%)
  other arithmetic  3.07 us (2%)
  local copies, waits for them, and re-layouts  3 us (2%)
    ppermute x48, starting transfers between devices, hop(): return rings[way](array)  51.1 us
    ppermute x48, waiting for transfers between devices, hop(): return rings[way](array)  42.7 us
    pallas_call x35, Pallas kernels, kernel(): pl.pallas_call(body, out_shape=outs, in_specs=[VMEM] * len(ins), out_spec...  26 us
    ppermute x2, waiting for transfers between devices, dense(): theirs = cross(theirs)  8.75 us
    ppermute x18, starting transfers between devices, dense(): ins = [*ins, *(swap(x) for x in ins)]  3.78 us
  transfers between devices with their start and end apart: 84, of which 31 were waited for; matrix products, arithmetic and copies ran while one was open for 3% of the time, Pallas kernels for 17%

profile of v2, /device:TPU:0, one launch (start us, length us, event | category | flops | bytes accessed | tf_op | source)
XLA Modules:
  0.0 147.9 jit_solution(1551627133136848517)
XLA Ops:
  0.0 1.1 copy-done
  1.1 3.0 %collective-permute-start.3 = (bf16[72,1024]{1,0:T(8,128)(2,1)S(1)}, bf16[72,1024]{1,0:T(8,128)(2,1)S(1)}, u32[]{:S(2)}, u32[]{:S(2)}) collective-permute-start(bf16[72,1024]{1,0:T(8,128)(2,1)S(1)} %constant_dynamic-slice_fusion.1.refs_0_), channel_id=1, source_target_pairs={{0,2},{1,3},{4,0},{5,1},{8,4},{9,5},{12,8},{13,9},{14,12},{15,13},... | collective-permute-start | bytes 442376 | tf_op jit(solution)/shard_map/ppermute | solution.py:288
  4.2 1.3 copy.10
  5.6 2.6 %fusion.1 = bf16[96,2304]{0,1:T(8,128)(2,1)S(1)} fusion(bf16[96,2304]{0,1:T(8,128)(2,1)S(1)} %copy.10), kind=kLoop, calls=%fused_computation.4 | loop fusion | flops 14598144 | bytes 884736 | tf_op jit(solution)/shard_map/convert_element_type | solution.py:291
  8.9 1.9 %collective-permute-start.14 = (bf16[72,1024]{1,0:T(8,128)(2,1)S(1)}, bf16[72,1024]{1,0:T(8,128)(2,1)S(1)}, u32[]{:S(2)}, u32[]{:S(2)}) collective-permute-start(bf16[72,1024]{1,0:T(8,128)(2,1)S(1)} %constant_dynamic-slice_fusion.refs_0_), channel_id=1, source_target_pairs={{0,2},{1,3},{4,0},{5,1},{8,4},{9,5},{12,8},{13,9},{14,12},{15,13},... | collective-permute-start | bytes 442376 | tf_op jit(solution)/shard_map/ppermute | solution.py:288
  11.0 1.9 %collective-permute-start.5 = (bf16[72,1024]{1,0:T(8,128)(2,1)S(1)}, bf16[72,1024]{1,0:T(8,128)(2,1)S(1)}, u32[]{:S(2)}, u32[]{:S(2)}) collective-permute-start(bf16[72,1024]{1,0:T(8,128)(2,1)S(1)} %collective-permute-done.3.refs_2_), channel_id=1, source_target_pairs={{0,2},{1,3},{4,0},{5,1},{8,4},{9,5},{12,8},{13,9},{14,12},{15,13},... | collective-permute-start | bytes 442376 | tf_op jit(solution)/shard_map/ppermute | solution.py:288
  13.0 2.7 %collective-permute-done.14.refs_2_ = bf16[72,1024]{1,0:T(8,128)(2,1)S(1)} collective-permute-done((bf16[72,1024]{1,0:T(8,128)(2,1)S(1)}, bf16[72,1024]{1,0:T(8,128)(2,1)S(1)}, u32[]{:S(2)}, u32[]{:S(2)}) %collective-permute-start.14) | collective-permute-done | bytes 147488 | tf_op jit(solution)/shard_map/ppermute | solution.py:288
  15.6 1.9 %collective-permute-start.16 = (bf16[72,1024]{1,0:T(8,128)(2,1)S(1)}, bf16[72,1024]{1,0:T(8,128)(2,1)S(1)}, u32[]{:S(2)}, u32[]{:S(2)}) collective-permute-start(bf16[72,1024]{1,0:T(8,128)(2,1)S(1)} %collective-permute-done.14.refs_2_), channel_id=1, source_target_pairs={{0,2},{1,3},{4,0},{5,1},{8,4},{9,5},{12,8},{13,9},{14,12},{15,13},... | collective-permute-start | bytes 442376 | tf_op jit(solution)/shard_map/ppermute | solution.py:288
  17.9 2.0 %collective-permute-start.1 = (bf16[192,8,72]{2,0,1:T(8,128)(2,1)S(1)}, bf16[192,8,72]{2,0,1:T(8,128)(2,1)S(1)}, u32[]{:S(2)}, u32[]{:S(2)}) collective-permute-start(bf16[192,8,72]{2,0,1:T(8,128)(2,1)S(1)} %get-tuple-element.68), channel_id=1, source_target_pairs={{0,16},{16,0},{1,17},{17,1},{2,18},{18,2},{3,19},{19,3},{4,20},{20... | collective-permute-start | bytes 663560 | tf_op jit(solution)/shard_map/ppermute | solution.py:299
  19.9 1.5 %collective-permute-start.7 = (bf16[72,1024]{1,0:T(8,128)(2,1)S(1)}, bf16[72,1024]{1,0:T(8,128)(2,1)S(1)}, u32[]{:S(2)}, u32[]{:S(2)}) collective-permute-start(bf16[72,1024]{1,0:T(8,128)(2,1)S(1)} %collective-permute-done.5.refs_4_), channel_id=1, source_target_pairs={{0,2},{1,3},{4,0},{5,1},{8,4},{9,5},{12,8},{13,9},{14,12},{15,13},... | collective-permute-start | bytes 442376 | tf_op jit(solution)/shard_map/ppermute | solution.py:288
  22.4 1.9 %collective-permute-start.18 = (bf16[72,1024]{1,0:T(8,128)(2,1)S(1)}, bf16[72,1024]{1,0:T(8,128)(2,1)S(1)}, u32[]{:S(2)}, u32[]{:S(2)}) collective-permute-start(bf16[72,1024]{1,0:T(8,128)(2,1)S(1)} %collective-permute-done.16.refs_4_), channel_id=1, source_target_pairs={{0,2},{1,3},{4,0},{5,1},{8,4},{9,5},{12,8},{13,9},{14,12},{15,13},... | collective-permute-start | bytes 442376 | tf_op jit(solution)/shard_map/ppermute | solution.py:288
  24.4 1.9 %collective-permute-done.7.refs_6_ = bf16[72,1024]{1,0:T(8,128)(2,1)S(1)} collective-permute-done((bf16[72,1024]{1,0:T(8,128)(2,1)S(1)}, bf16[72,1024]{1,0:T(8,128)(2,1)S(1)}, u32[]{:S(2)}, u32[]{:S(2)}) %collective-permute-start.7) | collective-permute-done | bytes 147488 | tf_op jit(solution)/shard_map/ppermute | solution.py:288
  26.3 1.6 %collective-permute-start.9 = (bf16[32,1024]{1,0:T(8,128)(2,1)S(1)}, bf16[32,1024]{1,0:T(8,128)(2,1)S(1)}, u32[]{:S(2)}, u32[]{:S(2)}) collective-permute-start(bf16[32,1024]{1,0:T(8,128)(2,1)S(1)} %slice.57), channel_id=1, source_target_pairs={{0,2},{1,3},{4,0},{5,1},{8,4},{9,5},{12,8},{13,9},{14,12},{15,13},... | collective-permute-start | bytes 196616 | tf_op jit(solution)/shard_map/ppermute | solution.py:288
  28.9 1.5 %collective-permute-start.20 = (bf16[32,1024]{1,0:T(8,128)(2,1)S(1)}, bf16[32,1024]{1,0:T(8,128)(2,1)S(1)}, u32[]{:S(2)}, u32[]{:S(2)}) collective-permute-start(bf16[32,1024]{1,0:T(8,128)(2,1)S(1)} %slice.59), channel_id=1, source_target_pairs={{0,2},{1,3},{4,0},{5,1},{8,4},{9,5},{12,8},{13,9},{14,12},{15,13},... | collective-permute-start | bytes 196616 | tf_op jit(solution)/shard_map/ppermute | solution.py:288
  31.3 1.6 %shard_map.94.total_ref = f32[384,1024]{1,0:T(8,128)S(1)} custom-call(bf16[8,384,72]{2,1,0:T(8,128)(2,1)S(1)} %maximum_bitcast_fusion.act_ref, bf16[72,1024]{1,0:T(8,128)(2,1)S(1)} %constant_dynamic-slice_fusion.refs_0_, bf16[72,1024]{1,0:T(8,128)(2,1)S(1)} %collective-permute-done.13.refs_1_, bf16[72,1024]{1,0:T(8,128)(2,1)S(1)} %collective-permute-done.14.refs_2_, ...), custom_call_target="tpu_custom_call" | custom-call | flops 452984832 | bytes 1572864 | tf_op jit(solution)/shard_map/pallas_call | solution.py:108
  32.9 1.6 %shard_map.91.total_ref = f32[384,1024]{1,0:T(8,128)S(1)} custom-call(bf16[8,384,72]{2,1,0:T(8,128)(2,1)S(1)} %maximum_bitcast_fusion.act_ref, bf16[72,1024]{1,0:T(8,128)(2,1)S(1)} %constant_dynamic-slice_fusion.1.refs_0_, bf16[72,1024]{1,0:T(8,128)(2,1)S(1)} %collective-permute-done.2.refs_1_, bf16[72,1024]{1,0:T(8,128)(2,1)S(1)} %collective-permute-done.3.refs_2_, ...), custom_call_target="tpu_custom_call" | custom-call | flops 452984832 | bytes 1572864 | tf_op jit(solution)/shard_map/pallas_call | solution.py:108
  37.4 1.5 %collective-permute-start.23 = (bf16[96,1024]{1,0:T(8,128)(2,1)S(1)}, bf16[96,1024]{1,0:T(8,128)(2,1)S(1)}, u32[]{:S(2)}, u32[]{:S(2)}) collective-permute-start(bf16[96,1024]{1,0:T(8,128)(2,1)S(1)} %shard_map.96), channel_id=1, source_target_pairs={{0,16},{16,0},{1,17},{17,1},{2,18},{18,2},{3,19},{19,3},{4,20},{20... | collective-permute-start | bytes 589832 | tf_op jit(solution)/shard_map/ppermute | solution.py:334
  39.9 5.4 %collective-permute-done.23.refs_5_ = bf16[96,1024]{1,0:T(8,128)(2,1)S(1)} collective-permute-done((bf16[96,1024]{1,0:T(8,128)(2,1)S(1)}, bf16[96,1024]{1,0:T(8,128)(2,1)S(1)}, u32[]{:S(2)}, u32[]{:S(2)}) %collective-permute-start.23) | collective-permute-done | bytes 196640 | tf_op jit(solution)/shard_map/ppermute | solution.py:334
  45.2 3.4 %collective-permute-done.12.refs_2_ = bf16[96,1024]{1,0:T(8,128)(2,1)S(1)} collective-permute-done((bf16[96,1024]{1,0:T(8,128)(2,1)S(1)}, bf16[96,1024]{1,0:T(8,128)(2,1)S(1)}, u32[]{:S(2)}, u32[]{:S(2)}) %collective-permute-start.12) | collective-permute-done | bytes 196640 | tf_op jit(solution)/shard_map/ppermute | solution.py:334
  48.9 1.6 %collective-permute-start.57 = (bf16[48,2048]{1,0:T(8,128)(2,1)S(1)}, bf16[48,2048]{1,0:T(8,128)(2,1)S(1)}, u32[]{:S(2)}, u32[]{:S(2)}) collective-permute-start(bf16[48,2048]{1,0:T(8,128)(2,1)S(1)} %get-tuple-element.56.refs_0_), channel_id=1, source_target_pairs={{0,2},{1,3},{4,0},{5,1},{8,4},{9,5},{12,8},{13,9},{14,12},{15,13},... | collective-permute-start | bytes 589832 | tf_op jit(solution)/shard_map/ppermute | solution.py:288
  51.0 1.6 %collective-permute-start.27 = (bf16[48,2176]{1,0:T(8,128)(2,1)S(1)}, bf16[48,2176]{1,0:T(8,128)(2,1)S(1)}, u32[]{:S(2)}, u32[]{:S(2)}) collective-permute-start(bf16[48,2176]{1,0:T(8,128)(2,1)S(1)} %get-tuple-element.45.refs_0_.refs_2_), channel_id=1, source_target_pairs={{0,2},{1,3},{4,0},{5,1},{8,4},{9,5},{12,8},{13,9},{14,12},{15,13},... | collective-permute-start | bytes 626696 | tf_op jit(solution)/shard_map/ppermute | solution.py:288
  53.0 3.7 %collective-permute-done.57.refs_1_ = bf16[48,2048]{1,0:T(8,128)(2,1)S(1)} collective-permute-done((bf16[48,2048]{1,0:T(8,128)(2,1)S(1)}, bf16[48,2048]{1,0:T(8,128)(2,1)S(1)}, u32[]{:S(2)}, u32[]{:S(2)}) %collective-permute-start.57) | collective-permute-done | bytes 196640 | tf_op jit(solution)/shard_map/ppermute | solution.py:288
  56.7 1.6 %collective-permute-start.62 = (bf16[48,2048]{1,0:T(8,128)(2,1)S(1)}, bf16[48,2048]{1,0:T(8,128)(2,1)S(1)}, u32[]{:S(2)}, u32[]{:S(2)}) collective-permute-start(bf16[48,2048]{1,0:T(8,128)(2,1)S(1)} %collective-permute-done.57.refs_1_), channel_id=1, source_target_pairs={{0,2},{1,3},{4,0},{5,1},{8,4},{9,5},{12,8},{13,9},{14,12},{15,13},... | collective-permute-start | bytes 589832 | tf_op jit(solution)/shard_map/ppermute | solution.py:288
  58.8 2.4 %collective-permute-done.27.refs_1_.refs_5_ = bf16[48,2176]{1,0:T(8,128)(2,1)S(1)} collective-permute-done((bf16[48,2176]{1,0:T(8,128)(2,1)S(1)}, bf16[48,2176]{1,0:T(8,128)(2,1)S(1)}, u32[]{:S(2)}, u32[]{:S(2)}) %collective-permute-start.27) | collective-permute-done | bytes 208928 | tf_op jit(solution)/shard_map/ppermute | solution.py:288
  61.2 1.6 %collective-permute-start.32 = (bf16[48,2176]{1,0:T(8,128)(2,1)S(1)}, bf16[48,2176]{1,0:T(8,128)(2,1)S(1)}, u32[]{:S(2)}, u32[]{:S(2)}) collective-permute-start(bf16[48,2176]{1,0:T(8,128)(2,1)S(1)} %collective-permute-done.27.refs_1_.refs_5_), channel_id=1, source_target_pairs={{0,2},{1,3},{4,0},{5,1},{8,4},{9,5},{12,8},{13,9},{14,12},{15,13},... | collective-permute-start | bytes 626696 | tf_op jit(solution)/shard_map/ppermute | solution.py:288
  63.2 2.2 %collective-permute-done.62.refs_1_ = bf16[48,2048]{1,0:T(8,128)(2,1)S(1)} collective-permute-done((bf16[48,2048]{1,0:T(8,128)(2,1)S(1)}, bf16[48,2048]{1,0:T(8,128)(2,1)S(1)}, u32[]{:S(2)}, u32[]{:S(2)}) %collective-permute-start.62) | collective-permute-done | bytes 196640 | tf_op jit(solution)/shard_map/ppermute | solution.py:288
  65.4 1.6 %collective-permute-start.67 = (bf16[48,2048]{1,0:T(8,128)(2,1)S(1)}, bf16[48,2048]{1,0:T(8,128)(2,1)S(1)}, u32[]{:S(2)}, u32[]{:S(2)}) collective-permute-start(bf16[48,2048]{1,0:T(8,128)(2,1)S(1)} %collective-permute-done.62.refs_1_), channel_id=1, source_target_pairs={{0,2},{1,3},{4,0},{5,1},{8,4},{9,5},{12,8},{13,9},{14,12},{15,13},... | collective-permute-start | bytes 589832 | tf_op jit(solution)/shard_map/ppermute | solution.py:288
  67.5 2.4 %collective-permute-done.32.refs_1_.refs_5_ = bf16[48,2176]{1,0:T(8,128)(2,1)S(1)} collective-permute-done((bf16[48,2176]{1,0:T(8,128)(2,1)S(1)}, bf16[48,2176]{1,0:T(8,128)(2,1)S(1)}, u32[]{:S(2)}, u32[]{:S(2)}) %collective-permute-start.32) | collective-permute-done | bytes 208928 | tf_op jit(solution)/shard_map/ppermute | solution.py:288
  69.9 1.6 %collective-permute-start.37 = (bf16[48,2176]{1,0:T(8,128)(2,1)S(1)}, bf16[48,2176]{1,0:T(8,128)(2,1)S(1)}, u32[]{:S(2)}, u32[]{:S(2)}) collective-permute-start(bf16[48,2176]{1,0:T(8,128)(2,1)S(1)} %collective-permute-done.32.refs_1_.refs_5_), channel_id=1, source_target_pairs={{0,2},{1,3},{4,0},{5,1},{8,4},{9,5},{12,8},{13,9},{14,12},{15,13},... | collective-permute-start | bytes 626696 | tf_op jit(solution)/shard_map/ppermute | solution.py:288
  71.9 2.2 %collective-permute-done.67.refs_1_ = bf16[48,2048]{1,0:T(8,128)(2,1)S(1)} collective-permute-done((bf16[48,2048]{1,0:T(8,128)(2,1)S(1)}, bf16[48,2048]{1,0:T(8,128)(2,1)S(1)}, u32[]{:S(2)}, u32[]{:S(2)}) %collective-permute-start.67) | collective-permute-done | bytes 196640 | tf_op jit(solution)/shard_map/ppermute | solution.py:288
  74.1 1.6 %collective-permute-done.66.refs_0_ = bf16[48,2048]{1,0:T(8,128)(2,1)S(1)} collective-permute-done((bf16[48,2048]{1,0:T(8,128)(2,1)S(1)}, bf16[48,2048]{1,0:T(8,128)(2,1)S(1)}, u32[]{:S(2)}, u32[]{:S(2)}) %collective-permute-start.66) | collective-permute-done | bytes 196640 | tf_op jit(solution)/shard_map/ppermute | solution.py:288
  75.7 1.6 %collective-permute-start.72 = (bf16[24,2048]{1,0:T(8,128)(2,1)S(1)}, bf16[24,2048]{1,0:T(8,128)(2,1)S(1)}, u32[]{:S(2)}, u32[]{:S(2)}) collective-permute-start(bf16[24,2048]{1,0:T(8,128)(2,1)S(1)} %slice.63), channel_id=1, source_target_pairs={{0,2},{1,3},{4,0},{5,1},{8,4},{9,5},{12,8},{13,9},{14,12},{15,13},... | collective-permute-start | bytes 294920 | tf_op jit(solution)/shard_map/ppermute | solution.py:288
  78.2 1.6 %collective-permute-start.42 = (bf16[24,2176]{1,0:T(8,128)(2,1)S(1)}, bf16[24,2176]{1,0:T(8,128)(2,1)S(1)}, u32[]{:S(2)}, u32[]{:S(2)}) collective-permute-start(bf16[24,2176]{1,0:T(8,128)(2,1)S(1)} %slice.61), channel_id=1, source_target_pairs={{0,2},{1,3},{4,0},{5,1},{8,4},{9,5},{12,8},{13,9},{14,12},{15,13},... | collective-permute-start | bytes 313352 | tf_op jit(solution)/shard_map/ppermute | solution.py:288
  81.6 1.0 collective-permute-done.71.refs_0_
  83.2 1.5 %collective-permute-done.41.refs_0_.refs_4_ = bf16[24,2176]{1,0:T(8,128)(2,1)S(1)} collective-permute-done((bf16[24,2176]{1,0:T(8,128)(2,1)S(1)}, bf16[24,2176]{1,0:T(8,128)(2,1)S(1)}, u32[]{:S(2)}, u32[]{:S(2)}) %collective-permute-start.41) | collective-permute-done | bytes 104480 | tf_op jit(solution)/shard_map/ppermute | solution.py:288
  87.1 1.7 %shard_map.116 = (bf16[48,2048]{1,0:T(8,128)(2,1)S(1)}, bf16[48,2048]{1,0:T(8,128)(2,1)S(1)}) custom-call(bf16[24,2048]{1,0:T(8,128)(2,1)S(1)} %collective-permute-done.71.refs_0_, bf16[24,2048]{1,0:T(8,128)(2,1)S(1)} %collective-permute-done.72.refs_1_, bf16[24,2048]{1,0:T(8,128)(2,1)S(1)} %collective-permute-done.73.refs_2_, ...), custom_call_target="tpu_custom_call" | custom-call | flops 905969664 | bytes 9437184 | tf_op jit(solution)/shard_map/pallas_call | solution.py:108
  89.3 2.1 %shard_map.102 = (bf16[96,2048]{1,0:T(8,128)(2,1)S(1)}, bf16[96,2048]{1,0:T(8,128)(2,1)S(1)}) custom-call(bf16[48,2176]{1,0:T(8,128)(2,1)S(1)} %collective-permute-done.36.refs_0_.refs_4_, bf16[48,2176]{1,0:T(8,128)(2,1)S(1)} %collective-permute-done.37.refs_1_.refs_5_, bf16[48,2176]{1,0:T(8,128)(2,1)S(1)} %collective-permute-done.38.refs_2_.refs_6_, ...), custom_call_target="tpu_custom_call" | custom-call | flops 1811939328 | bytes 9437184 | tf_op jit(solution)/shard_map/pallas_call | solution.py:108
  92.2 1.7 %shard_map.103 = (bf16[48,2048]{1,0:T(8,128)(2,1)S(1)}, bf16[48,2048]{1,0:T(8,128)(2,1)S(1)}) custom-call(bf16[24,2176]{1,0:T(8,128)(2,1)S(1)} %collective-permute-done.41.refs_0_.refs_4_, bf16[24,2176]{1,0:T(8,128)(2,1)S(1)} %collective-permute-done.42.refs_1_.refs_5_, bf16[24,2176]{1,0:T(8,128)(2,1)S(1)} %collective-permute-done.43.refs_2_.refs_6_, ...), custom_call_target="tpu_custom_call" | custom-call | flops 905969664 | bytes 9437184 | tf_op jit(solution)/shard_map/pallas_call | solution.py:108
  94.5 2.1 %shard_map.115 = (bf16[96,2048]{1,0:T(8,128)(2,1)S(1)}, bf16[96,2048]{1,0:T(8,128)(2,1)S(1)}) custom-call(bf16[48,2048]{1,0:T(8,128)(2,1)S(1)} %collective-permute-done.66.refs_0_, bf16[48,2048]{1,0:T(8,128)(2,1)S(1)} %collective-permute-done.67.refs_1_, bf16[48,2048]{1,0:T(8,128)(2,1)S(1)} %collective-permute-done.68.refs_2_, ...), custom_call_target="tpu_custom_call" | custom-call | flops 1811939328 | bytes 9437184 | tf_op jit(solution)/shard_map/pallas_call | solution.py:108
  97.7 2.1 %shard_map.114 = (bf16[96,2048]{1,0:T(8,128)(2,1)S(1)}, bf16[96,2048]{1,0:T(8,128)(2,1)S(1)}) custom-call(bf16[48,2048]{1,0:T(8,128)(2,1)S(1)} %collective-permute-done.61.refs_0_, bf16[48,2048]{1,0:T(8,128)(2,1)S(1)} %collective-permute-done.62.refs_1_, bf16[48,2048]{1,0:T(8,128)(2,1)S(1)} %collective-permute-done.63.refs_2_, ...), custom_call_target="tpu_custom_call" | custom-call | flops 1811939328 | bytes 9437184 | tf_op jit(solution)/shard_map/pallas_call | solution.py:108
  100.4 1.9 %collective-permute-done.76.refs_0_ = bf16[24,2048]{1,0:T(8,128)(2,1)S(1)} collective-permute-done((bf16[24,2048]{1,0:T(8,128)(2,1)S(1)}, bf16[24,2048]{1,0:T(8,128)(2,1)S(1)}, u32[]{:S(2)}, u32[]{:S(2)}) %collective-permute-start.76) | collective-permute-done | bytes 98336 | tf_op jit(solution)/shard_map/ppermute | solution.py:288
  102.3 1.6 %collective-permute-start.80 = (bf16[24,2048]{1,0:T(8,128)(2,1)S(1)}, bf16[24,2048]{1,0:T(8,128)(2,1)S(1)}, u32[]{:S(2)}, u32[]{:S(2)}) collective-permute-start(bf16[24,2048]{1,0:T(8,128)(2,1)S(1)} %shard_map.121), channel_id=1, source_target_pairs={{0,2},{1,3},{4,0},{5,1},{8,4},{9,5},{12,8},{13,9},{14,12},{15,13},... | collective-permute-start | bytes 294920 | tf_op jit(solution)/shard_map/ppermute | solution.py:288
  103.9 2.1 %shard_map.101 = (bf16[96,2048]{1,0:T(8,128)(2,1)S(1)}, bf16[96,2048]{1,0:T(8,128)(2,1)S(1)}) custom-call(bf16[48,2176]{1,0:T(8,128)(2,1)S(1)} %collective-permute-done.31.refs_0_.refs_4_, bf16[48,2176]{1,0:T(8,128)(2,1)S(1)} %collective-permute-done.32.refs_1_.refs_5_, bf16[48,2176]{1,0:T(8,128)(2,1)S(1)} %collective-permute-done.33.refs_2_.refs_6_, ...), custom_call_target="tpu_custom_call" | custom-call | flops 1811939328 | bytes 9437184 | tf_op jit(solution)/shard_map/pallas_call | solution.py:108
  107.6 1.4 collective-permute-start.77
  109.0 3.6 %collective-permute-done.46.refs_0_ = bf16[24,2048]{1,0:T(8,128)(2,1)S(1)} collective-permute-done((bf16[24,2048]{1,0:T(8,128)(2,1)S(1)}, bf16[24,2048]{1,0:T(8,128)(2,1)S(1)}, u32[]{:S(2)}, u32[]{:S(2)}) %collective-permute-start.46) | collective-permute-done | bytes 98336 | tf_op jit(solution)/shard_map/ppermute | solution.py:288
  112.7 1.6 %collective-permute-start.50 = (bf16[24,2048]{1,0:T(8,128)(2,1)S(1)}, bf16[24,2048]{1,0:T(8,128)(2,1)S(1)}, u32[]{:S(2)}, u32[]{:S(2)}) collective-permute-start(bf16[24,2048]{1,0:T(8,128)(2,1)S(1)} %shard_map.108), channel_id=1, source_target_pairs={{0,2},{1,3},{4,0},{5,1},{8,4},{9,5},{12,8},{13,9},{14,12},{15,13},... | collective-permute-start | bytes 294920 | tf_op jit(solution)/shard_map/ppermute | solution.py:288
  115.2 2.1 %shard_map.113 = (bf16[96,2048]{1,0:T(8,128)(2,1)S(1)}, bf16[96,2048]{1,0:T(8,128)(2,1)S(1)}) custom-call(bf16[48,2048]{1,0:T(8,128)(2,1)S(1)} %collective-permute-done.56.refs_0_, bf16[48,2048]{1,0:T(8,128)(2,1)S(1)} %collective-permute-done.57.refs_1_, bf16[48,2048]{1,0:T(8,128)(2,1)S(1)} %collective-permute-done.58.refs_2_, ...), custom_call_target="tpu_custom_call" | custom-call | flops 1811939328 | bytes 9437184 | tf_op jit(solution)/shard_map/pallas_call | solution.py:108
  118.9 1.6 %collective-permute-start.51 = (bf16[48,2048]{1,0:T(8,128)(2,1)S(1)}, bf16[48,2048]{1,0:T(8,128)(2,1)S(1)}, u32[]{:S(2)}, u32[]{:S(2)}) collective-permute-start(bf16[48,2048]{1,0:T(8,128)(2,1)S(1)} %shard_map.109), channel_id=1, source_target_pairs={{0,2},{1,3},{4,0},{5,1},{8,4},{9,5},{12,8},{13,9},{14,12},{15,13},... | collective-permute-start | bytes 589832 | tf_op jit(solution)/shard_map/ppermute | solution.py:288
  120.6 2.1 %shard_map.100 = (bf16[96,2048]{1,0:T(8,128)(2,1)S(1)}, bf16[96,2048]{1,0:T(8,128)(2,1)S(1)}) custom-call(bf16[48,2176]{1,0:T(8,128)(2,1)S(1)} %collective-permute-done.26.refs_0_.refs_4_, bf16[48,2176]{1,0:T(8,128)(2,1)S(1)} %collective-permute-done.27.refs_1_.refs_5_, bf16[48,2176]{1,0:T(8,128)(2,1)S(1)} %collective-permute-done.28.refs_2_.refs_6_, ...), custom_call_target="tpu_custom_call" | custom-call | flops 1811939328 | bytes 9437184 | tf_op jit(solution)/shard_map/pallas_call | solution.py:108
  123.0 1.7 %collective-permute-done.47.refs_0_ = bf16[48,2048]{1,0:T(8,128)(2,1)S(1)} collective-permute-done((bf16[48,2048]{1,0:T(8,128)(2,1)S(1)}, bf16[48,2048]{1,0:T(8,128)(2,1)S(1)}, u32[]{:S(2)}, u32[]{:S(2)}) %collective-permute-start.47) | collective-permute-done | bytes 196640 | tf_op jit(solution)/shard_map/ppermute | solution.py:288
  124.7 1.1 collective-permute-start.78
  126.0 1.0 collective-permute-start.82
  127.0 1.1 collective-permute-start.48
  128.1 1.7 %shard_map.112 = (bf16[48,2048]{1,0:T(8,128)(2,1)S(1)}, bf16[48,2048]{1,0:T(8,128)(2,1)S(1)}) custom-call(bf16[48,2048]{1,0:T(8,128)(2,1)S(1)} %get-tuple-element.56.refs_0_, bf16[48,2048]{1,0:T(8,128)(2,1)S(1)} %collective-permute-done.54.refs_1_, bf16[48,2176]{1,0:T(8,128)(2,1)S(1)} %get-tuple-element.45.refs_0_.refs_2_, ...), custom_call_target="tpu_custom_call" | custom-call | flops 905969664 | bytes 9437184 | tf_op jit(solution)/shard_map/pallas_call | solution.py:108
  129.9 1.0 collective-permute-start.52
  130.8 1.6 %collective-permute-done.78.refs_0_ = bf16[48,2048]{1,0:T(8,128)(2,1)S(1)} collective-permute-done((bf16[48,2048]{1,0:T(8,128)(2,1)S(1)}, bf16[48,2048]{1,0:T(8,128)(2,1)S(1)}, u32[]{:S(2)}, u32[]{:S(2)}) %collective-permute-start.78) | collective-permute-done | bytes 196640 | tf_op jit(solution)/shard_map/ppermute | solution.py:288
  132.4 1.7 %shard_map.99 = (bf16[48,2048]{1,0:T(8,128)(2,1)S(1)}, bf16[48,2048]{1,0:T(8,128)(2,1)S(1)}) custom-call(bf16[48,2176]{1,0:T(8,128)(2,1)S(1)} %get-tuple-element.45.refs_0_.refs_2_, bf16[48,2176]{1,0:T(8,128)(2,1)S(1)} %collective-permute-done.24.refs_1_.refs_3_, bf16[2048,768]{1,0:T(8,128)(2,1)S(1)} %bitcast.27, bf16[2048,768]{1,0:T(8,128)(2,1)S(1)} %bitcast.37, ...), custom_call_target="tpu_custom_call" | custom-call | flops 905969664 | bytes 9437184 | tf_op jit(solution)/shard_map/pallas_call | solution.py:108
  134.8 1.3 collective-permute-start.79
  137.0 1.3 collective-permute-start.49
  139.2 3.4 %collective-permute-done.79.refs_6_ = bf16[48,2048]{1,0:T(8,128)(2,1)S(1)} collective-permute-done((bf16[48,2048]{1,0:T(8,128)(2,1)S(1)}, bf16[48,2048]{1,0:T(8,128)(2,1)S(1)}, u32[]{:S(2)}, u32[]{:S(2)}) %collective-permute-start.79) | collective-permute-done | bytes 196640 | tf_op jit(solution)/shard_map/ppermute | solution.py:288
  142.7 1.2 collective-permute-done.83.refs_7_
  143.9 2.0 %collective-permute-done.49.refs_2_ = bf16[48,2048]{1,0:T(8,128)(2,1)S(1)} collective-permute-done((bf16[48,2048]{1,0:T(8,128)(2,1)S(1)}, bf16[48,2048]{1,0:T(8,128)(2,1)S(1)}, u32[]{:S(2)}, u32[]{:S(2)}) %collective-permute-start.49) | collective-permute-done | bytes 196640 | tf_op jit(solution)/shard_map/ppermute | solution.py:288
  145.9 1.0 collective-permute-done.53.refs_3_
  146.9 1.0 shard_map.125
  (173 shorter events, 27.7 us)
Async XLA Ops:
  1.1 9.9 %collective-permute-start.3 = (bf16[72,1024]{1,0:T(8,128)(2,1)S(1)}, bf16[72,1024]{1,0:T(8,128)(2,1)S(1)}, u32[]{:S(2)}, u32[]{:S(2)}) collective-permute-start(bf16[72,1024]{1,0:T(8,128)(2,1)S(1)} %constant_dynamic-slice_fusion.1.refs_0_), channel_id=1, source_target_pairs={{0,2},{1,3},{4,0},{5,1},{8,4},{9,5},{12,8},{13,9},{14,12},{15,13},... | collective-permute-start | bytes 442376 | tf_op jit(solution)/shard_map/ppermute | solution.py:288
  4.1 8.7 %collective-permute-start.2 = (bf16[72,1024]{1,0:T(8,128)(2,1)S(1)}, bf16[72,1024]{1,0:T(8,128)(2,1)S(1)}, u32[]{:S(2)}, u32[]{:S(2)}) collective-permute-start(bf16[72,1024]{1,0:T(8,128)(2,1)S(1)} %constant_dynamic-slice_fusion.1.refs_0_), channel_id=1, source_target_pairs={{0,4},{1,5},{4,8},{5,9},{8,12},{9,13},{12,14},{13,15},{14,10},{15,... | collective-permute-start | bytes 442376 | tf_op jit(solution)/shard_map/ppermute | solution.py:288
  8.8 8.9 %collective-permute-start = (bf16[96,8,2,72]{3,0,1,2:T(8,128)(2,1)S(1)}, bf16[96,8,2,72]{3,0,1,2:T(8,128)(2,1)S(1)}, u32[]{:S(2)}, u32[]{:S(2)}) collective-permute-start(bf16[96,8,2,72]{3,0,1,2:T(8,128)(2,1)S(1)} %get-tuple-element.70), channel_id=1, source_target_pairs={{0,1},{1,0},{2,3},{3,2},{4,5},{5,4},{6,7},{7,6},{8,9},{9,8},{10,11... | collective-permute-start | bytes 663560 | tf_op jit(solution)/shard_map/ppermute | solution.py:295
  8.9 6.8 %collective-permute-start.14 = (bf16[72,1024]{1,0:T(8,128)(2,1)S(1)}, bf16[72,1024]{1,0:T(8,128)(2,1)S(1)}, u32[]{:S(2)}, u32[]{:S(2)}) collective-permute-start(bf16[72,1024]{1,0:T(8,128)(2,1)S(1)} %constant_dynamic-slice_fusion.refs_0_), channel_id=1, source_target_pairs={{0,2},{1,3},{4,0},{5,1},{8,4},{9,5},{12,8},{13,9},{14,12},{15,13},... | collective-permute-start | bytes 442376 | tf_op jit(solution)/shard_map/ppermute | solution.py:288
  10.8 6.7 %collective-permute-start.13 = (bf16[72,1024]{1,0:T(8,128)(2,1)S(1)}, bf16[72,1024]{1,0:T(8,128)(2,1)S(1)}, u32[]{:S(2)}, u32[]{:S(2)}) collective-permute-start(bf16[72,1024]{1,0:T(8,128)(2,1)S(1)} %constant_dynamic-slice_fusion.refs_0_), channel_id=1, source_target_pairs={{0,4},{1,5},{4,8},{5,9},{8,12},{9,13},{12,14},{13,15},{14,10},{15,... | collective-permute-start | bytes 442376 | tf_op jit(solution)/shard_map/ppermute | solution.py:288
  11.0 8.9 %collective-permute-start.5 = (bf16[72,1024]{1,0:T(8,128)(2,1)S(1)}, bf16[72,1024]{1,0:T(8,128)(2,1)S(1)}, u32[]{:S(2)}, u32[]{:S(2)}) collective-permute-start(bf16[72,1024]{1,0:T(8,128)(2,1)S(1)} %collective-permute-done.3.refs_2_), channel_id=1, source_target_pairs={{0,2},{1,3},{4,0},{5,1},{8,4},{9,5},{12,8},{13,9},{14,12},{15,13},... | collective-permute-start | bytes 442376 | tf_op jit(solution)/shard_map/ppermute | solution.py:288
  12.8 8.6 %collective-permute-start.4 = (bf16[72,1024]{1,0:T(8,128)(2,1)S(1)}, bf16[72,1024]{1,0:T(8,128)(2,1)S(1)}, u32[]{:S(2)}, u32[]{:S(2)}) collective-permute-start(bf16[72,1024]{1,0:T(8,128)(2,1)S(1)} %collective-permute-done.2.refs_1_), channel_id=1, source_target_pairs={{0,4},{1,5},{4,8},{5,9},{8,12},{9,13},{12,14},{13,15},{14,10},{15,... | collective-permute-start | bytes 442376 | tf_op jit(solution)/shard_map/ppermute | solution.py:288
  15.6 6.7 %collective-permute-start.16 = (bf16[72,1024]{1,0:T(8,128)(2,1)S(1)}, bf16[72,1024]{1,0:T(8,128)(2,1)S(1)}, u32[]{:S(2)}, u32[]{:S(2)}) collective-permute-start(bf16[72,1024]{1,0:T(8,128)(2,1)S(1)} %collective-permute-done.14.refs_2_), channel_id=1, source_target_pairs={{0,2},{1,3},{4,0},{5,1},{8,4},{9,5},{12,8},{13,9},{14,12},{15,13},... | collective-permute-start | bytes 442376 | tf_op jit(solution)/shard_map/ppermute | solution.py:288
  17.5 6.7 %collective-permute-start.15 = (bf16[72,1024]{1,0:T(8,128)(2,1)S(1)}, bf16[72,1024]{1,0:T(8,128)(2,1)S(1)}, u32[]{:S(2)}, u32[]{:S(2)}) collective-permute-start(bf16[72,1024]{1,0:T(8,128)(2,1)S(1)} %collective-permute-done.13.refs_1_), channel_id=1, source_target_pairs={{0,4},{1,5},{4,8},{5,9},{8,12},{9,13},{12,14},{13,15},{14,10},{15,... | collective-permute-start | bytes 442376 | tf_op jit(solution)/shard_map/ppermute | solution.py:288
  17.9 13.2 %collective-permute-start.1 = (bf16[192,8,72]{2,0,1:T(8,128)(2,1)S(1)}, bf16[192,8,72]{2,0,1:T(8,128)(2,1)S(1)}, u32[]{:S(2)}, u32[]{:S(2)}) collective-permute-start(bf16[192,8,72]{2,0,1:T(8,128)(2,1)S(1)} %get-tuple-element.68), channel_id=1, source_target_pairs={{0,16},{16,0},{1,17},{17,1},{2,18},{18,2},{3,19},{19,3},{4,20},{20... | collective-permute-start | bytes 663560 | tf_op jit(solution)/shard_map/ppermute | solution.py:299
  19.9 6.4 %collective-permute-start.7 = (bf16[72,1024]{1,0:T(8,128)(2,1)S(1)}, bf16[72,1024]{1,0:T(8,128)(2,1)S(1)}, u32[]{:S(2)}, u32[]{:S(2)}) collective-permute-start(bf16[72,1024]{1,0:T(8,128)(2,1)S(1)} %collective-permute-done.5.refs_4_), channel_id=1, source_target_pairs={{0,2},{1,3},{4,0},{5,1},{8,4},{9,5},{12,8},{13,9},{14,12},{15,13},... | collective-permute-start | bytes 442376 | tf_op jit(solution)/shard_map/ppermute | solution.py:288
  21.4 6.7 %collective-permute-start.6 = (bf16[72,1024]{1,0:T(8,128)(2,1)S(1)}, bf16[72,1024]{1,0:T(8,128)(2,1)S(1)}, u32[]{:S(2)}, u32[]{:S(2)}) collective-permute-start(bf16[72,1024]{1,0:T(8,128)(2,1)S(1)} %collective-permute-done.4.refs_3_), channel_id=1, source_target_pairs={{0,4},{1,5},{4,8},{5,9},{8,12},{9,13},{12,14},{13,15},{14,10},{15,... | collective-permute-start | bytes 442376 | tf_op jit(solution)/shard_map/ppermute | solution.py:288
  22.4 6.5 %collective-permute-start.18 = (bf16[72,1024]{1,0:T(8,128)(2,1)S(1)}, bf16[72,1024]{1,0:T(8,128)(2,1)S(1)}, u32[]{:S(2)}, u32[]{:S(2)}) collective-permute-start(bf16[72,1024]{1,0:T(8,128)(2,1)S(1)} %collective-permute-done.16.refs_4_), channel_id=1, source_target_pairs={{0,2},{1,3},{4,0},{5,1},{8,4},{9,5},{12,8},{13,9},{14,12},{15,13},... | collective-permute-start | bytes 442376 | tf_op jit(solution)/shard_map/ppermute | solution.py:288
  24.2 6.3 %collective-permute-start.17 = (bf16[72,1024]{1,0:T(8,128)(2,1)S(1)}, bf16[72,1024]{1,0:T(8,128)(2,1)S(1)}, u32[]{:S(2)}, u32[]{:S(2)}) collective-permute-start(bf16[72,1024]{1,0:T(8,128)(2,1)S(1)} %collective-permute-done.15.refs_3_), channel_id=1, source_target_pairs={{0,4},{1,5},{4,8},{5,9},{8,12},{9,13},{12,14},{13,15},{14,10},{15,... | collective-permute-start | bytes 442376 | tf_op jit(solution)/shard_map/ppermute | solution.py:288
  26.3 9.3 %collective-permute-start.9 = (bf16[32,1024]{1,0:T(8,128)(2,1)S(1)}, bf16[32,1024]{1,0:T(8,128)(2,1)S(1)}, u32[]{:S(2)}, u32[]{:S(2)}) collective-permute-start(bf16[32,1024]{1,0:T(8,128)(2,1)S(1)} %slice.57), channel_id=1, source_target_pairs={{0,2},{1,3},{4,0},{5,1},{8,4},{9,5},{12,8},{13,9},{14,12},{15,13},... | collective-permute-start | bytes 196616 | tf_op jit(solution)/shard_map/ppermute | solution.py:288
  28.1 7.5 %collective-permute-start.8 = (bf16[40,1024]{1,0:T(8,128)(2,1)S(1)}, bf16[40,1024]{1,0:T(8,128)(2,1)S(1)}, u32[]{:S(2)}, u32[]{:S(2)}) collective-permute-start(bf16[40,1024]{1,0:T(8,128)(2,1)S(1)} %slice.56), channel_id=1, source_target_pairs={{0,4},{1,5},{4,8},{5,9},{8,12},{9,13},{12,14},{13,15},{14,10},{15,... | collective-permute-start | bytes 245768 | tf_op jit(solution)/shard_map/ppermute | solution.py:288
  28.9 5.5 %collective-permute-start.20 = (bf16[32,1024]{1,0:T(8,128)(2,1)S(1)}, bf16[32,1024]{1,0:T(8,128)(2,1)S(1)}, u32[]{:S(2)}, u32[]{:S(2)}) collective-permute-start(bf16[32,1024]{1,0:T(8,128)(2,1)S(1)} %slice.59), channel_id=1, source_target_pairs={{0,2},{1,3},{4,0},{5,1},{8,4},{9,5},{12,8},{13,9},{14,12},{15,13},... | collective-permute-start | bytes 196616 | tf_op jit(solution)/shard_map/ppermute | solution.py:288
  37.4 7.8 %collective-permute-start.23 = (bf16[96,1024]{1,0:T(8,128)(2,1)S(1)}, bf16[96,1024]{1,0:T(8,128)(2,1)S(1)}, u32[]{:S(2)}, u32[]{:S(2)}) collective-permute-start(bf16[96,1024]{1,0:T(8,128)(2,1)S(1)} %shard_map.96), channel_id=1, source_target_pairs={{0,16},{16,0},{1,17},{17,1},{2,18},{18,2},{3,19},{19,3},{4,20},{20... | collective-permute-start | bytes 589832 | tf_op jit(solution)/shard_map/ppermute | solution.py:334
  38.9 9.7 %collective-permute-start.12 = (bf16[96,1024]{1,0:T(8,128)(2,1)S(1)}, bf16[96,1024]{1,0:T(8,128)(2,1)S(1)}, u32[]{:S(2)}, u32[]{:S(2)}) collective-permute-start(bf16[96,1024]{1,0:T(8,128)(2,1)S(1)} %shard_map.93), channel_id=1, source_target_pairs={{0,16},{16,0},{1,17},{17,1},{2,18},{18,2},{3,19},{19,3},{4,20},{20... | collective-permute-start | bytes 589832 | tf_op jit(solution)/shard_map/ppermute | solution.py:334
  48.9 7.8 %collective-permute-start.57 = (bf16[48,2048]{1,0:T(8,128)(2,1)S(1)}, bf16[48,2048]{1,0:T(8,128)(2,1)S(1)}, u32[]{:S(2)}, u32[]{:S(2)}) collective-permute-start(bf16[48,2048]{1,0:T(8,128)(2,1)S(1)} %get-tuple-element.56.refs_0_), channel_id=1, source_target_pairs={{0,2},{1,3},{4,0},{5,1},{8,4},{9,5},{12,8},{13,9},{14,12},{15,13},... | collective-permute-start | bytes 589832 | tf_op jit(solution)/shard_map/ppermute | solution.py:288
  50.5 7.8 %collective-permute-start.56 = (bf16[48,2048]{1,0:T(8,128)(2,1)S(1)}, bf16[48,2048]{1,0:T(8,128)(2,1)S(1)}, u32[]{:S(2)}, u32[]{:S(2)}) collective-permute-start(bf16[48,2048]{1,0:T(8,128)(2,1)S(1)} %get-tuple-element.56.refs_0_), channel_id=1, source_target_pairs={{0,4},{1,5},{4,8},{5,9},{8,12},{9,13},{12,14},{13,15},{14,10},{15,... | collective-permute-start | bytes 589832 | tf_op jit(solution)/shard_map/ppermute | solution.py:288
  51.0 10.2 %collective-permute-start.27 = (bf16[48,2176]{1,0:T(8,128)(2,1)S(1)}, bf16[48,2176]{1,0:T(8,128)(2,1)S(1)}, u32[]{:S(2)}, u32[]{:S(2)}) collective-permute-start(bf16[48,2176]{1,0:T(8,128)(2,1)S(1)} %get-tuple-element.45.refs_0_.refs_2_), channel_id=1, source_target_pairs={{0,2},{1,3},{4,0},{5,1},{8,4},{9,5},{12,8},{13,9},{14,12},{15,13},... | collective-permute-start | bytes 626696 | tf_op jit(solution)/shard_map/ppermute | solution.py:288
  52.6 10.2 %collective-permute-start.26 = (bf16[48,2176]{1,0:T(8,128)(2,1)S(1)}, bf16[48,2176]{1,0:T(8,128)(2,1)S(1)}, u32[]{:S(2)}, u32[]{:S(2)}) collective-permute-start(bf16[48,2176]{1,0:T(8,128)(2,1)S(1)} %get-tuple-element.45.refs_0_.refs_2_), channel_id=1, source_target_pairs={{0,4},{1,5},{4,8},{5,9},{8,12},{9,13},{12,14},{13,15},{14,10},{15,... | collective-permute-start | bytes 626696 | tf_op jit(solution)/shard_map/ppermute | solution.py:288
  56.7 8.7 %collective-permute-start.62 = (bf16[48,2048]{1,0:T(8,128)(2,1)S(1)}, bf16[48,2048]{1,0:T(8,128)(2,1)S(1)}, u32[]{:S(2)}, u32[]{:S(2)}) collective-permute-start(bf16[48,2048]{1,0:T(8,128)(2,1)S(1)} %collective-permute-done.57.refs_1_), channel_id=1, source_target_pairs={{0,2},{1,3},{4,0},{5,1},{8,4},{9,5},{12,8},{13,9},{14,12},{15,13},... | collective-permute-start | bytes 589832 | tf_op jit(solution)/shard_map/ppermute | solution.py:288
  58.3 8.7 %collective-permute-start.61 = (bf16[48,2048]{1,0:T(8,128)(2,1)S(1)}, bf16[48,2048]{1,0:T(8,128)(2,1)S(1)}, u32[]{:S(2)}, u32[]{:S(2)}) collective-permute-start(bf16[48,2048]{1,0:T(8,128)(2,1)S(1)} %collective-permute-done.56.refs_0_), channel_id=1, source_target_pairs={{0,4},{1,5},{4,8},{5,9},{8,12},{9,13},{12,14},{13,15},{14,10},{15,... | collective-permute-start | bytes 589832 | tf_op jit(solution)/shard_map/ppermute | solution.py:288
  61.2 8.7 %collective-permute-start.32 = (bf16[48,2176]{1,0:T(8,128)(2,1)S(1)}, bf16[48,2176]{1,0:T(8,128)(2,1)S(1)}, u32[]{:S(2)}, u32[]{:S(2)}) collective-permute-start(bf16[48,2176]{1,0:T(8,128)(2,1)S(1)} %collective-permute-done.27.refs_1_.refs_5_), channel_id=1, source_target_pairs={{0,2},{1,3},{4,0},{5,1},{8,4},{9,5},{12,8},{13,9},{14,12},{15,13},... | collective-permute-start | bytes 626696 | tf_op jit(solution)/shard_map/ppermute | solution.py:288
  62.8 8.7 %collective-permute-start.31 = (bf16[48,2176]{1,0:T(8,128)(2,1)S(1)}, bf16[48,2176]{1,0:T(8,128)(2,1)S(1)}, u32[]{:S(2)}, u32[]{:S(2)}) collective-permute-start(bf16[48,2176]{1,0:T(8,128)(2,1)S(1)} %collective-permute-done.26.refs_0_.refs_4_), channel_id=1, source_target_pairs={{0,4},{1,5},{4,8},{5,9},{8,12},{9,13},{12,14},{13,15},{14,10},{15,... | collective-permute-start | bytes 626696 | tf_op jit(solution)/shard_map/ppermute | solution.py:288
  65.4 8.7 %collective-permute-start.67 = (bf16[48,2048]{1,0:T(8,128)(2,1)S(1)}, bf16[48,2048]{1,0:T(8,128)(2,1)S(1)}, u32[]{:S(2)}, u32[]{:S(2)}) collective-permute-start(bf16[48,2048]{1,0:T(8,128)(2,1)S(1)} %collective-permute-done.62.refs_1_), channel_id=1, source_target_pairs={{0,2},{1,3},{4,0},{5,1},{8,4},{9,5},{12,8},{13,9},{14,12},{15,13},... | collective-permute-start | bytes 589832 | tf_op jit(solution)/shard_map/ppermute | solution.py:288
  67.0 8.7 %collective-permute-start.66 = (bf16[48,2048]{1,0:T(8,128)(2,1)S(1)}, bf16[48,2048]{1,0:T(8,128)(2,1)S(1)}, u32[]{:S(2)}, u32[]{:S(2)}) collective-permute-start(bf16[48,2048]{1,0:T(8,128)(2,1)S(1)} %collective-permute-done.61.refs_0_), channel_id=1, source_target_pairs={{0,4},{1,5},{4,8},{5,9},{8,12},{9,13},{12,14},{13,15},{14,10},{15,... | collective-permute-start | bytes 589832 | tf_op jit(solution)/shard_map/ppermute | solution.py:288
  69.9 7.4 %collective-permute-start.37 = (bf16[48,2176]{1,0:T(8,128)(2,1)S(1)}, bf16[48,2176]{1,0:T(8,128)(2,1)S(1)}, u32[]{:S(2)}, u32[]{:S(2)}) collective-permute-start(bf16[48,2176]{1,0:T(8,128)(2,1)S(1)} %collective-permute-done.32.refs_1_.refs_5_), channel_id=1, source_target_pairs={{0,2},{1,3},{4,0},{5,1},{8,4},{9,5},{12,8},{13,9},{14,12},{15,13},... | collective-permute-start | bytes 626696 | tf_op jit(solution)/shard_map/ppermute | solution.py:288
  71.5 6.7 %collective-permute-start.36 = (bf16[48,2176]{1,0:T(8,128)(2,1)S(1)}, bf16[48,2176]{1,0:T(8,128)(2,1)S(1)}, u32[]{:S(2)}, u32[]{:S(2)}) collective-permute-start(bf16[48,2176]{1,0:T(8,128)(2,1)S(1)} %collective-permute-done.31.refs_0_.refs_4_), channel_id=1, source_target_pairs={{0,4},{1,5},{4,8},{5,9},{8,12},{9,13},{12,14},{13,15},{14,10},{15,... | collective-permute-start | bytes 626696 | tf_op jit(solution)/shard_map/ppermute | solution.py:288
  71.9 7.9 %collective-permute-start.54 = (bf16[48,2048]{1,0:T(8,128)(2,1)S(1)}, bf16[48,2048]{1,0:T(8,128)(2,1)S(1)}, u32[]{:S(2)}, u32[]{:S(2)}) collective-permute-start(bf16[48,2048]{1,0:T(8,128)(2,1)S(1)} %get-tuple-element.56.refs_0_), channel_id=1, source_target_pairs={{0,1},{1,0},{2,3},{3,2},{4,5},{5,4},{6,7},{7,6},{8,9},{9,8},{10,11... | collective-permute-start | bytes 589832 | tf_op jit(solution)/shard_map/ppermute | solution.py:356
  74.1 7.0 %collective-permute-start.59 = (bf16[48,2048]{1,0:T(8,128)(2,1)S(1)}, bf16[48,2048]{1,0:T(8,128)(2,1)S(1)}, u32[]{:S(2)}, u32[]{:S(2)}) collective-permute-start(bf16[48,2048]{1,0:T(8,128)(2,1)S(1)} %collective-permute-done.57.refs_1_), channel_id=1, source_target_pairs={{0,1},{1,0},{2,3},{3,2},{4,5},{5,4},{6,7},{7,6},{8,9},{9,8},{10,11... | collective-permute-start | bytes 589832 | tf_op jit(solution)/shard_map/ppermute | solution.py:356
  75.7 5.4 %collective-permute-start.72 = (bf16[24,2048]{1,0:T(8,128)(2,1)S(1)}, bf16[24,2048]{1,0:T(8,128)(2,1)S(1)}, u32[]{:S(2)}, u32[]{:S(2)}) collective-permute-start(bf16[24,2048]{1,0:T(8,128)(2,1)S(1)} %slice.63), channel_id=1, source_target_pairs={{0,2},{1,3},{4,0},{5,1},{8,4},{9,5},{12,8},{13,9},{14,12},{15,13},... | collective-permute-start | bytes 294920 | tf_op jit(solution)/shard_map/ppermute | solution.py:288
  77.3 5.4 %collective-permute-start.71 = (bf16[24,2048]{1,0:T(8,128)(2,1)S(1)}, bf16[24,2048]{1,0:T(8,128)(2,1)S(1)}, u32[]{:S(2)}, u32[]{:S(2)}) collective-permute-start(bf16[24,2048]{1,0:T(8,128)(2,1)S(1)} %slice.62), channel_id=1, source_target_pairs={{0,4},{1,5},{4,8},{5,9},{8,12},{9,13},{12,14},{13,15},{14,10},{15,... | collective-permute-start | bytes 294920 | tf_op jit(solution)/shard_map/ppermute | solution.py:288
  81.1 7.6 %collective-permute-start.39 = (bf16[48,2176]{1,0:T(8,128)(2,1)S(1)}, bf16[48,2176]{1,0:T(8,128)(2,1)S(1)}, u32[]{:S(2)}, u32[]{:S(2)}) collective-permute-start(bf16[48,2176]{1,0:T(8,128)(2,1)S(1)} %collective-permute-done.37.refs_1_.refs_5_), channel_id=1, source_target_pairs={{0,1},{1,0},{2,3},{3,2},{4,5},{5,4},{6,7},{7,6},{8,9},{9,8},{10,11... | collective-permute-start | bytes 626696 | tf_op jit(solution)/shard_map/ppermute | solution.py:356
  82.7 6.3 %collective-permute-start.38 = (bf16[48,2176]{1,0:T(8,128)(2,1)S(1)}, bf16[48,2176]{1,0:T(8,128)(2,1)S(1)}, u32[]{:S(2)}, u32[]{:S(2)}) collective-permute-start(bf16[48,2176]{1,0:T(8,128)(2,1)S(1)} %collective-permute-done.36.refs_0_.refs_4_), channel_id=1, source_target_pairs={{0,1},{1,0},{2,3},{3,2},{4,5},{5,4},{6,7},{7,6},{8,9},{9,8},{10,11... | collective-permute-start | bytes 626696 | tf_op jit(solution)/shard_map/ppermute | solution.py:356
  89.0 5.3 %collective-permute-start.75 = (bf16[48,2048]{1,0:T(8,128)(2,1)S(1)}, bf16[48,2048]{1,0:T(8,128)(2,1)S(1)}, u32[]{:S(2)}, u32[]{:S(2)}) collective-permute-start(bf16[48,2048]{1,0:T(8,128)(2,1)S(1)} %get-tuple-element.66), channel_id=1, source_target_pairs={{0,1},{1,0},{2,3},{3,2},{4,5},{5,4},{6,7},{7,6},{8,9},{9,8},{10,11... | collective-permute-start | bytes 589832 | tf_op jit(solution)/shard_map/ppermute | solution.py:359
  91.7 5.4 %collective-permute-start.34 = (bf16[48,2176]{1,0:T(8,128)(2,1)S(1)}, bf16[48,2176]{1,0:T(8,128)(2,1)S(1)}, u32[]{:S(2)}, u32[]{:S(2)}) collective-permute-start(bf16[48,2176]{1,0:T(8,128)(2,1)S(1)} %collective-permute-done.32.refs_1_.refs_5_), channel_id=1, source_target_pairs={{0,1},{1,0},{2,3},{3,2},{4,5},{5,4},{6,7},{7,6},{8,9},{9,8},{10,11... | collective-permute-start | bytes 626696 | tf_op jit(solution)/shard_map/ppermute | solution.py:356
  93.9 5.9 %collective-permute-start.29 = (bf16[48,2176]{1,0:T(8,128)(2,1)S(1)}, bf16[48,2176]{1,0:T(8,128)(2,1)S(1)}, u32[]{:S(2)}, u32[]{:S(2)}) collective-permute-start(bf16[48,2176]{1,0:T(8,128)(2,1)S(1)} %collective-permute-done.27.refs_1_.refs_5_), channel_id=1, source_target_pairs={{0,1},{1,0},{2,3},{3,2},{4,5},{5,4},{6,7},{7,6},{8,9},{9,8},{10,11... | collective-permute-start | bytes 626696 | tf_op jit(solution)/shard_map/ppermute | solution.py:356
  94.3 5.6 %collective-permute-start.45 = (bf16[48,2048]{1,0:T(8,128)(2,1)S(1)}, bf16[48,2048]{1,0:T(8,128)(2,1)S(1)}, u32[]{:S(2)}, u32[]{:S(2)}) collective-permute-start(bf16[48,2048]{1,0:T(8,128)(2,1)S(1)} %get-tuple-element.55), channel_id=1, source_target_pairs={{0,1},{1,0},{2,3},{3,2},{4,5},{5,4},{6,7},{7,6},{8,9},{9,8},{10,11... | collective-permute-start | bytes 589832 | tf_op jit(solution)/shard_map/ppermute | solution.py:359
  96.6 10.3 %collective-permute-start.70 = (bf16[96,2048]{1,0:T(8,128)(2,1)S(1)}, bf16[96,2048]{1,0:T(8,128)(2,1)S(1)}, u32[]{:S(2)}, u32[]{:S(2)}) collective-permute-start(bf16[96,2048]{1,0:T(8,128)(2,1)S(1)} %get-tuple-element.64), channel_id=1, source_target_pairs={{0,1},{1,0},{2,3},{3,2},{4,5},{5,4},{6,7},{7,6},{8,9},{9,8},{10,11... | collective-permute-start | bytes 1179656 | tf_op jit(solution)/shard_map/ppermute | solution.py:359
  97.1 17.2 %collective-permute-start.40 = (bf16[96,2048]{1,0:T(8,128)(2,1)S(1)}, bf16[96,2048]{1,0:T(8,128)(2,1)S(1)}, u32[]{:S(2)}, u32[]{:S(2)}) collective-permute-start(bf16[96,2048]{1,0:T(8,128)(2,1)S(1)} %get-tuple-element.53), channel_id=1, source_target_pairs={{0,1},{1,0},{2,3},{3,2},{4,5},{5,4},{6,7},{7,6},{8,9},{9,8},{10,11... | collective-permute-start | bytes 1179656 | tf_op jit(solution)/shard_map/ppermute | solution.py:359
  99.8 7.8 %collective-permute-start.28 = (bf16[48,2176]{1,0:T(8,128)(2,1)S(1)}, bf16[48,2176]{1,0:T(8,128)(2,1)S(1)}, u32[]{:S(2)}, u32[]{:S(2)}) collective-permute-start(bf16[48,2176]{1,0:T(8,128)(2,1)S(1)} %collective-permute-done.26.refs_0_.refs_4_), channel_id=1, source_target_pairs={{0,1},{1,0},{2,3},{3,2},{4,5},{5,4},{6,7},{7,6},{8,9},{9,8},{10,11... | collective-permute-start | bytes 626696 | tf_op jit(solution)/shard_map/ppermute | solution.py:356
  100.0 17.4 %collective-permute-start.65 = (bf16[96,2048]{1,0:T(8,128)(2,1)S(1)}, bf16[96,2048]{1,0:T(8,128)(2,1)S(1)}, u32[]{:S(2)}, u32[]{:S(2)}) collective-permute-start(bf16[96,2048]{1,0:T(8,128)(2,1)S(1)} %get-tuple-element.62), channel_id=1, source_target_pairs={{0,1},{1,0},{2,3},{3,2},{4,5},{5,4},{6,7},{7,6},{8,9},{9,8},{10,11... | collective-permute-start | bytes 1179656 | tf_op jit(solution)/shard_map/ppermute | solution.py:359
  106.9 11.9 %collective-permute-start.35 = (bf16[96,2048]{1,0:T(8,128)(2,1)S(1)}, bf16[96,2048]{1,0:T(8,128)(2,1)S(1)}, u32[]{:S(2)}, u32[]{:S(2)}) collective-permute-start(bf16[96,2048]{1,0:T(8,128)(2,1)S(1)} %get-tuple-element.51), channel_id=1, source_target_pairs={{0,1},{1,0},{2,3},{3,2},{4,5},{5,4},{6,7},{7,6},{8,9},{9,8},{10,11... | collective-permute-start | bytes 1179656 | tf_op jit(solution)/shard_map/ppermute | solution.py:359
  106.9 5.7 %collective-permute-start.46 = (bf16[24,2048]{1,0:T(8,128)(2,1)S(1)}, bf16[24,2048]{1,0:T(8,128)(2,1)S(1)}, u32[]{:S(2)}, u32[]{:S(2)}) collective-permute-start(bf16[24,2048]{1,0:T(8,128)(2,1)S(1)} %shard_map.104), channel_id=1, source_target_pairs={{0,4},{1,5},{4,8},{5,9},{8,12},{9,13},{12,14},{13,15},{14,10},{15,... | collective-permute-start | bytes 294920 | tf_op jit(solution)/shard_map/ppermute | solution.py:288
  107.6 11.3 %collective-permute-start.77 = (bf16[48,2048]{1,0:T(8,128)(2,1)S(1)}, bf16[48,2048]{1,0:T(8,128)(2,1)S(1)}, u32[]{:S(2)}, u32[]{:S(2)}) collective-permute-start(bf16[48,2048]{1,0:T(8,128)(2,1)S(1)} %shard_map.118), channel_id=1, source_target_pairs={{0,4},{1,5},{4,8},{5,9},{8,12},{9,13},{12,14},{13,15},{14,10},{15,... | collective-permute-start | bytes 589832 | tf_op jit(solution)/shard_map/ppermute | solution.py:288
  112.7 5.7 %collective-permute-start.50 = (bf16[24,2048]{1,0:T(8,128)(2,1)S(1)}, bf16[24,2048]{1,0:T(8,128)(2,1)S(1)}, u32[]{:S(2)}, u32[]{:S(2)}) collective-permute-start(bf16[24,2048]{1,0:T(8,128)(2,1)S(1)} %shard_map.108), channel_id=1, source_target_pairs={{0,2},{1,3},{4,0},{5,1},{8,4},{9,5},{12,8},{13,9},{14,12},{15,13},... | collective-permute-start | bytes 294920 | tf_op jit(solution)/shard_map/ppermute | solution.py:288
  114.2 8.4 %collective-permute-start.81 = (bf16[48,2048]{1,0:T(8,128)(2,1)S(1)}, bf16[48,2048]{1,0:T(8,128)(2,1)S(1)}, u32[]{:S(2)}, u32[]{:S(2)}) collective-permute-start(bf16[48,2048]{1,0:T(8,128)(2,1)S(1)} %shard_map.122), channel_id=1, source_target_pairs={{0,2},{1,3},{4,0},{5,1},{8,4},{9,5},{12,8},{13,9},{14,12},{15,13},... | collective-permute-start | bytes 589832 | tf_op jit(solution)/shard_map/ppermute | solution.py:288
  117.3 12.5 %collective-permute-start.60 = (bf16[96,2048]{1,0:T(8,128)(2,1)S(1)}, bf16[96,2048]{1,0:T(8,128)(2,1)S(1)}, u32[]{:S(2)}, u32[]{:S(2)}) collective-permute-start(bf16[96,2048]{1,0:T(8,128)(2,1)S(1)} %get-tuple-element.60), channel_id=1, source_target_pairs={{0,1},{1,0},{2,3},{3,2},{4,5},{5,4},{6,7},{7,6},{8,9},{9,8},{10,11... | collective-permute-start | bytes 1179656 | tf_op jit(solution)/shard_map/ppermute | solution.py:359
  118.3 6.4 %collective-permute-start.47 = (bf16[48,2048]{1,0:T(8,128)(2,1)S(1)}, bf16[48,2048]{1,0:T(8,128)(2,1)S(1)}, u32[]{:S(2)}, u32[]{:S(2)}) collective-permute-start(bf16[48,2048]{1,0:T(8,128)(2,1)S(1)} %shard_map.105), channel_id=1, source_target_pairs={{0,4},{1,5},{4,8},{5,9},{8,12},{9,13},{12,14},{13,15},{14,10},{15,... | collective-permute-start | bytes 589832 | tf_op jit(solution)/shard_map/ppermute | solution.py:288
  118.9 7.2 %collective-permute-start.24 = (bf16[48,2176]{1,0:T(8,128)(2,1)S(1)}, bf16[48,2176]{1,0:T(8,128)(2,1)S(1)}, u32[]{:S(2)}, u32[]{:S(2)}) collective-permute-start(bf16[48,2176]{1,0:T(8,128)(2,1)S(1)} %get-tuple-element.45.refs_0_.refs_2_), channel_id=1, source_target_pairs={{0,1},{1,0},{2,3},{3,2},{4,5},{5,4},{6,7},{7,6},{8,9},{9,8},{10,11... | collective-permute-start | bytes 626696 | tf_op jit(solution)/shard_map/ppermute | solution.py:356
  118.9 8.0 %collective-permute-start.51 = (bf16[48,2048]{1,0:T(8,128)(2,1)S(1)}, bf16[48,2048]{1,0:T(8,128)(2,1)S(1)}, u32[]{:S(2)}, u32[]{:S(2)}) collective-permute-start(bf16[48,2048]{1,0:T(8,128)(2,1)S(1)} %shard_map.109), channel_id=1, source_target_pairs={{0,2},{1,3},{4,0},{5,1},{8,4},{9,5},{12,8},{13,9},{14,12},{15,13},... | collective-permute-start | bytes 589832 | tf_op jit(solution)/shard_map/ppermute | solution.py:288
  122.7 12.1 %collective-permute-start.30 = (bf16[96,2048]{1,0:T(8,128)(2,1)S(1)}, bf16[96,2048]{1,0:T(8,128)(2,1)S(1)}, u32[]{:S(2)}, u32[]{:S(2)}) collective-permute-start(bf16[96,2048]{1,0:T(8,128)(2,1)S(1)} %get-tuple-element.49), channel_id=1, source_target_pairs={{0,1},{1,0},{2,3},{3,2},{4,5},{5,4},{6,7},{7,6},{8,9},{9,8},{10,11... | collective-permute-start | bytes 1179656 | tf_op jit(solution)/shard_map/ppermute | solution.py:359
  124.7 7.7 %collective-permute-start.78 = (bf16[48,2048]{1,0:T(8,128)(2,1)S(1)}, bf16[48,2048]{1,0:T(8,128)(2,1)S(1)}, u32[]{:S(2)}, u32[]{:S(2)}) collective-permute-start(bf16[48,2048]{1,0:T(8,128)(2,1)S(1)} %shard_map.119), channel_id=1, source_target_pairs={{0,4},{1,5},{4,8},{5,9},{8,12},{9,13},{12,14},{13,15},{14,10},{15,... | collective-permute-start | bytes 589832 | tf_op jit(solution)/shard_map/ppermute | solution.py:288
  126.0 8.1 %collective-permute-start.82 = (bf16[48,2048]{1,0:T(8,128)(2,1)S(1)}, bf16[48,2048]{1,0:T(8,128)(2,1)S(1)}, u32[]{:S(2)}, u32[]{:S(2)}) collective-permute-start(bf16[48,2048]{1,0:T(8,128)(2,1)S(1)} %shard_map.123), channel_id=1, source_target_pairs={{0,2},{1,3},{4,0},{5,1},{8,4},{9,5},{12,8},{13,9},{14,12},{15,13},... | collective-permute-start | bytes 589832 | tf_op jit(solution)/shard_map/ppermute | solution.py:288
  127.0 9.1 %collective-permute-start.48 = (bf16[48,2048]{1,0:T(8,128)(2,1)S(1)}, bf16[48,2048]{1,0:T(8,128)(2,1)S(1)}, u32[]{:S(2)}, u32[]{:S(2)}) collective-permute-start(bf16[48,2048]{1,0:T(8,128)(2,1)S(1)} %shard_map.106), channel_id=1, source_target_pairs={{0,4},{1,5},{4,8},{5,9},{8,12},{9,13},{12,14},{13,15},{14,10},{15,... | collective-permute-start | bytes 589832 | tf_op jit(solution)/shard_map/ppermute | solution.py:288
  129.9 7.1 %collective-permute-start.52 = (bf16[48,2048]{1,0:T(8,128)(2,1)S(1)}, bf16[48,2048]{1,0:T(8,128)(2,1)S(1)}, u32[]{:S(2)}, u32[]{:S(2)}) collective-permute-start(bf16[48,2048]{1,0:T(8,128)(2,1)S(1)} %shard_map.110), channel_id=1, source_target_pairs={{0,2},{1,3},{4,0},{5,1},{8,4},{9,5},{12,8},{13,9},{14,12},{15,13},... | collective-permute-start | bytes 589832 | tf_op jit(solution)/shard_map/ppermute | solution.py:288
  132.4 6.0 %collective-permute-start.55 = (bf16[48,2048]{1,0:T(8,128)(2,1)S(1)}, bf16[48,2048]{1,0:T(8,128)(2,1)S(1)}, u32[]{:S(2)}, u32[]{:S(2)}) collective-permute-start(bf16[48,2048]{1,0:T(8,128)(2,1)S(1)} %get-tuple-element.58), channel_id=1, source_target_pairs={{0,1},{1,0},{2,3},{3,2},{4,5},{5,4},{6,7},{7,6},{8,9},{9,8},{10,11... | collective-permute-start | bytes 589832 | tf_op jit(solution)/shard_map/ppermute | solution.py:359
  134.8 7.8 %collective-permute-start.79 = (bf16[48,2048]{1,0:T(8,128)(2,1)S(1)}, bf16[48,2048]{1,0:T(8,128)(2,1)S(1)}, u32[]{:S(2)}, u32[]{:S(2)}) collective-permute-start(bf16[48,2048]{1,0:T(8,128)(2,1)S(1)} %shard_map.120), channel_id=1, source_target_pairs={{0,4},{1,5},{4,8},{5,9},{8,12},{9,13},{12,14},{13,15},{14,10},{15,... | collective-permute-start | bytes 589832 | tf_op jit(solution)/shard_map/ppermute | solution.py:288
  136.1 7.8 %collective-permute-start.83 = (bf16[48,2048]{1,0:T(8,128)(2,1)S(1)}, bf16[48,2048]{1,0:T(8,128)(2,1)S(1)}, u32[]{:S(2)}, u32[]{:S(2)}) collective-permute-start(bf16[48,2048]{1,0:T(8,128)(2,1)S(1)} %shard_map.124), channel_id=1, source_target_pairs={{0,2},{1,3},{4,0},{5,1},{8,4},{9,5},{12,8},{13,9},{14,12},{15,13},... | collective-permute-start | bytes 589832 | tf_op jit(solution)/shard_map/ppermute | solution.py:288
  137.0 8.9 %collective-permute-start.49 = (bf16[48,2048]{1,0:T(8,128)(2,1)S(1)}, bf16[48,2048]{1,0:T(8,128)(2,1)S(1)}, u32[]{:S(2)}, u32[]{:S(2)}) collective-permute-start(bf16[48,2048]{1,0:T(8,128)(2,1)S(1)} %shard_map.107), channel_id=1, source_target_pairs={{0,4},{1,5},{4,8},{5,9},{8,12},{9,13},{12,14},{13,15},{14,10},{15,... | collective-permute-start | bytes 589832 | tf_op jit(solution)/shard_map/ppermute | solution.py:288
  138.4 8.5 %collective-permute-start.53 = (bf16[48,2048]{1,0:T(8,128)(2,1)S(1)}, bf16[48,2048]{1,0:T(8,128)(2,1)S(1)}, u32[]{:S(2)}, u32[]{:S(2)}) collective-permute-start(bf16[48,2048]{1,0:T(8,128)(2,1)S(1)} %shard_map.111), channel_id=1, source_target_pairs={{0,2},{1,3},{4,0},{5,1},{8,4},{9,5},{12,8},{13,9},{14,12},{15,13},... | collective-permute-start | bytes 589832 | tf_op jit(solution)/shard_map/ppermute | solution.py:288
  (28 other events, 265.4 us)

commit v3 on v2

--- a/solution.py
+++ b/solution.py
@@ -1,7 +1,9 @@
 import functools
+import math
 
 import jax
 import jax.numpy as jnp
+import numpy as np
 from jax import lax
 from jax.experimental import pallas as pl
 from jax.experimental.pallas import tpu as pltpu
@@ -177,25 +179,45 @@
     out_ref[...] = total.astype(jnp.bfloat16)
 
 
-def bulk_body(chips, offsets, act_ref, *refs):
-    pieces, out_ref = refs[:-1], refs[-1]
+def gelu_body(chips, in_ref, mine_ref, given_ref):
+    half = mine_ref.shape[3]
+    first_core = lax.axis_index(DP) % 2 == 0
+    first_group = lax.axis_index(GROUPS) == 0
+    for chip in range(chips):
+        x = in_ref[:, chip * 4 * half : (chip + 1) * 4 * half].astype(jnp.float32)
+        act = 0.5 * x * (1.0 + lax.erf(x * np.float32(math.sqrt(0.5))))
+        cuts = [act[:, at * half : (at + 1) * half] for at in range(4)]
+        for ref, near, away in ((mine_ref, 0, 2), (given_ref, 2, 0)):
+            low = jnp.where(first_core, cuts[near], cuts[away])
+            high = jnp.where(first_core, cuts[near + 1], cuts[away + 1])
+            ref[0, chip] = jnp.where(first_group, low, high).astype(jnp.bfloat16)
+            ref[1, chip] = jnp.where(first_group, high, low).astype(jnp.bfloat16)
+
+
+def rows_of(refs, chip):
+    mine_ref, given_ref, theirs_ref = refs
+    return jnp.concatenate([mine_ref[0, chip], given_ref[0, chip], theirs_ref[0, chip], theirs_ref[1, chip]], axis=0)
+
+
+def bulk_body(chips, offsets, *refs):
+    pieces, out_ref = refs[3:-1], refs[-1]
     width = out_ref.shape[1]
     tile = tile_of(width, 512)
     for at in range(0, width, tile):
         total = None
         for offset, piece in zip(offsets, pieces):
-            act = act_ref[chip_at(chips, offset)]
+            act = rows_of(refs[:3], chip_at(chips, offset))
             part = jnp.dot(act, piece[:, at : at + tile], preferred_element_type=jnp.float32)
             total = part if total is None else total + part
         out_ref[:, at : at + tile] = total
 
 
-def last_body(chips, act_ref, total_ref, top_ref, bottom_ref, *outs):
+def last_body(chips, mine_ref, given_ref, theirs_ref, total_ref, top_ref, bottom_ref, *outs):
     width = total_ref.shape[1]
     mid = top_ref.shape[0]
     rows = outs[0].shape[0]
     tile = tile_of(width, 512)
-    act = act_ref[chip_at(chips, chips // 2)]
+    act = rows_of((mine_ref, given_ref, theirs_ref), chip_at(chips, chips // 2))
     for at in range(0, width, tile):
         to = at + tile
         total = total_ref[:, at:to]
@@ -277,8 +299,6 @@
     depth, width = merger_weight.shape
     half = depth // 2
     cut = rows // 2
-    first_core = lax.axis_index(DP) % 2 == 0
-    first_group = lax.axis_index(GROUPS) == 0
 
     swap = functools.partial(lax.ppermute, axis_name=DP, perm=swap_pairs(n))
     cross = functools.partial(lax.ppermute, axis_name=GROUPS, perm=swap_pairs(2))
@@ -288,16 +308,12 @@
         return rings[way](array)
 
     first = lax.axis_index(GROUPS).astype(jnp.uint32) * half
-    act = jax.nn.gelu(merger_input.astype(jnp.float32), approximate=False).astype(jnp.bfloat16)
-    act = act.reshape(rows, chips, 2, 2, half)
-    kept = jnp.where(first_core, act[:, :, 0], act[:, :, 1])
-    given = jnp.where(first_core, act[:, :, 1], act[:, :, 0])
+    weight = lax.dynamic_slice(merger_weight, (first, jnp.uint32(0)), (half, width))
+    block = jax.ShapeDtypeStruct((2, chips, rows, half), jnp.bfloat16)
+    mine, given = kernel(functools.partial(gelu_body, chips), [block, block], [merger_input])
     given = swap(given)
-    act = jnp.concatenate([kept, given], axis=0)
-    kept = jnp.where(first_group, act[:, :, 0], act[:, :, 1])
-    given = jnp.where(first_group, act[:, :, 1], act[:, :, 0])
-    given = cross(given)
-    act = jnp.concatenate([kept, given], axis=0).transpose(1, 0, 2)
+    crossed = jnp.stack([mine[1], given[1]])
+    crossed = cross(crossed)
 
     lanes = -(-2 * n // LANES) * LANES
     tags = kernel(functools.partial(tag_body, n), shaped(cut, lanes), [expert_ids.T, combine_ints.T])
@@ -306,8 +322,7 @@
     share = width // PARTS
     streams = []
     for part in range(PARTS):
-        weight = merger_weight if part == 0 else lax.optimization_barrier(merger_weight)
-        left = right = lax.dynamic_slice(weight, (first, jnp.uint32(part * share)), (half, share))
+        left = right = weight[:, part * share : (part + 1) * share]
         offsets, pieces = [0], [left]
         for step in range(1, far):
             left, right = hop(0, left), hop(1, right)
@@ -318,14 +333,14 @@
         total = kernel(
             functools.partial(bulk_body, chips, offsets),
             shaped(4 * rows, share, jnp.float32),
-            [act, *pieces],
+            [mine, given, crossed, *pieces],
             flops=2 * size * half * chips,
             moved=4 * size,
         )
         own, own_other, theirs, theirs_other = kernel(
             functools.partial(last_body, chips),
             [shaped(rows, share, jnp.float32)] * 4,
-            [act, total, top, bottom],
+            [mine, given, crossed, total, top, bottom],
             flops=2 * size * half,
             moved=8 * size,
         )

time: 148 us -> 148 us (level)
  Pallas kernels: 26 us -> 29.2 us
  other arithmetic: 3.07 us -> 0.09 us
  starting transfers between devices: 62.7 us -> 65.2 us
  waiting for transfers between devices: 52.5 us -> 50.4 us
    pallas_call x35 -> x36, Pallas kernels: 26 us -> 29.2 us  [kernel(): pl.pallas_call(body, out_shape=outs, in_specs=[VMEM] * len(ins), out_spec...]
    convert_element_type x1 -> x0, other arithmetic: 2.62 us -> none  [dense(): jax.nn.gelu(merger_input.astype(jnp.float32), approximate=False)]
    ppermute x48, starting transfers between devices: 51.1 us -> 53.4 us  [hop(): return rings[way](array)]
    ppermute x48, waiting for transfers between devices: 42.7 us -> 40.6 us  [hop(): return rings[way](array)]
    unnamed x19 -> x16, local copies, waits for them, and re-layouts: 2.87 us -> 1.06 us
  transfers between devices with their start and end apart: 84 -> 84, of which waited for: 31 -> 30; matrix products, arithmetic and copies ran while one was open for 3% -> 1% of each run, Pallas kernels for 17% -> 17%
where the time goes in v3:
time: 148 us
  starting transfers between devices  65.2 us (44%)
  waiting for transfers between devices  50.4 us (34%)
  Pallas kernels  29.2 us (20%)
  local copies, waits for them, and re-layouts  2.24 us (2%)
    ppermute x48, starting transfers between devices, hop(): return rings[way](array)  53.4 us
    ppermute x48, waiting for transfers between devices, hop(): return rings[way](array)  40.6 us
    pallas_call x36, Pallas kernels, kernel(): pl.pallas_call(body, out_shape=outs, in_specs=[VMEM] * len(ins), out_spec...  29.2 us
    ppermute x2, waiting for transfers between devices, dense(): theirs = cross(theirs)  8.72 us
    ppermute x18, starting transfers between devices, dense(): ins = [*ins, *(swap(x) for x in ins)]  3.47 us
  transfers between devices with their start and end apart: 84, of which 30 were waited for; matrix products, arithmetic and copies ran while one was open for 1% of the time, Pallas kernels for 17%

profile of v3, /device:TPU:0, one launch (start us, length us, event | category | flops | bytes accessed | tf_op | source)
XLA Modules:
  0.0 147.8 jit_solution(3497927480594174314)
XLA Ops:
  0.0 1.0 copy-done.3
  1.0 3.2 %shard_map.91 = (bf16[2,8,96,72]{3,2,1,0:T(8,128)(2,1)S(1)}, bf16[2,8,96,72]{3,2,1,0:T(8,128)(2,1)S(1)}) custom-call(bf16[96,2304]{1,0:T(8,128)(2,1)S(1)} %copy-done.3), custom_call_target="tpu_custom_call" | custom-call | tf_op jit(solution)/shard_map/pallas_call | solution.py:110
  4.8 1.1 fusion
  5.9 2.6 %collective-permute-start.14 = (bf16[72,1024]{1,0:T(8,128)(2,1)S(1)}, bf16[72,1024]{1,0:T(8,128)(2,1)S(1)}, u32[]{:S(2)}, u32[]{:S(2)}) collective-permute-start(bf16[72,1024]{1,0:T(8,128)(2,1)S(1)} %get-tuple-element.71.refs_3_), channel_id=1, source_target_pairs={{0,2},{1,3},{4,0},{5,1},{8,4},{9,5},{12,8},{13,9},{14,12},{15,13},... | collective-permute-start | bytes 442376 | tf_op jit(solution)/shard_map/ppermute | solution.py:308
  8.6 1.9 %collective-permute-start.3 = (bf16[72,1024]{1,0:T(8,128)(2,1)S(1)}, bf16[72,1024]{1,0:T(8,128)(2,1)S(1)}, u32[]{:S(2)}, u32[]{:S(2)}) collective-permute-start(bf16[72,1024]{1,0:T(8,128)(2,1)S(1)} %get-tuple-element.72.refs_3_), channel_id=1, source_target_pairs={{0,2},{1,3},{4,0},{5,1},{8,4},{9,5},{12,8},{13,9},{14,12},{15,13},... | collective-permute-start | bytes 442376 | tf_op jit(solution)/shard_map/ppermute | solution.py:308
  10.6 2.6 %collective-permute-done.14.refs_5_ = bf16[72,1024]{1,0:T(8,128)(2,1)S(1)} collective-permute-done((bf16[72,1024]{1,0:T(8,128)(2,1)S(1)}, bf16[72,1024]{1,0:T(8,128)(2,1)S(1)}, u32[]{:S(2)}, u32[]{:S(2)}) %collective-permute-start.14) | collective-permute-done | bytes 147488 | tf_op jit(solution)/shard_map/ppermute | solution.py:308
  13.2 1.9 %collective-permute-start.16 = (bf16[72,1024]{1,0:T(8,128)(2,1)S(1)}, bf16[72,1024]{1,0:T(8,128)(2,1)S(1)}, u32[]{:S(2)}, u32[]{:S(2)}) collective-permute-start(bf16[72,1024]{1,0:T(8,128)(2,1)S(1)} %collective-permute-done.14.refs_5_), channel_id=1, source_target_pairs={{0,2},{1,3},{4,0},{5,1},{8,4},{9,5},{12,8},{13,9},{14,12},{15,13},... | collective-permute-start | bytes 442376 | tf_op jit(solution)/shard_map/ppermute | solution.py:308
  15.3 1.1 collective-permute-done.3.refs_5_
  16.4 1.9 %collective-permute-start.5 = (bf16[72,1024]{1,0:T(8,128)(2,1)S(1)}, bf16[72,1024]{1,0:T(8,128)(2,1)S(1)}, u32[]{:S(2)}, u32[]{:S(2)}) collective-permute-start(bf16[72,1024]{1,0:T(8,128)(2,1)S(1)} %collective-permute-done.3.refs_5_), channel_id=1, source_target_pairs={{0,2},{1,3},{4,0},{5,1},{8,4},{9,5},{12,8},{13,9},{14,12},{15,13},... | collective-permute-start | bytes 442376 | tf_op jit(solution)/shard_map/ppermute | solution.py:308
  18.6 2.0 %collective-permute-start.1 = (bf16[2,8,96,72]{3,2,1,0:T(8,128)(2,1)S(1)}, bf16[2,8,96,72]{3,2,1,0:T(8,128)(2,1)S(1)}, u32[]{:S(2)}, u32[]{:S(2)}) collective-permute-start(bf16[2,8,96,72]{3,2,1,0:T(8,128)(2,1)S(1)} %pad_maximum_fusion), channel_id=1, source_target_pairs={{0,16},{16,0},{1,17},{17,1},{2,18},{18,2},{3,19},{19,3},{4,20},{20... | collective-permute-start | bytes 663560 | tf_op jit(solution)/shard_map/ppermute | solution.py:316
  20.6 1.5 %collective-permute-start.18 = (bf16[72,1024]{1,0:T(8,128)(2,1)S(1)}, bf16[72,1024]{1,0:T(8,128)(2,1)S(1)}, u32[]{:S(2)}, u32[]{:S(2)}) collective-permute-start(bf16[72,1024]{1,0:T(8,128)(2,1)S(1)} %collective-permute-done.16.refs_7_), channel_id=1, source_target_pairs={{0,2},{1,3},{4,0},{5,1},{8,4},{9,5},{12,8},{13,9},{14,12},{15,13},... | collective-permute-start | bytes 442376 | tf_op jit(solution)/shard_map/ppermute | solution.py:308
  23.1 1.9 %collective-permute-start.7 = (bf16[72,1024]{1,0:T(8,128)(2,1)S(1)}, bf16[72,1024]{1,0:T(8,128)(2,1)S(1)}, u32[]{:S(2)}, u32[]{:S(2)}) collective-permute-start(bf16[72,1024]{1,0:T(8,128)(2,1)S(1)} %collective-permute-done.5.refs_7_), channel_id=1, source_target_pairs={{0,2},{1,3},{4,0},{5,1},{8,4},{9,5},{12,8},{13,9},{14,12},{15,13},... | collective-permute-start | bytes 442376 | tf_op jit(solution)/shard_map/ppermute | solution.py:308
  25.2 1.6 %collective-permute-done.18.refs_9_ = bf16[72,1024]{1,0:T(8,128)(2,1)S(1)} collective-permute-done((bf16[72,1024]{1,0:T(8,128)(2,1)S(1)}, bf16[72,1024]{1,0:T(8,128)(2,1)S(1)}, u32[]{:S(2)}, u32[]{:S(2)}) %collective-permute-start.18) | collective-permute-done | bytes 147488 | tf_op jit(solution)/shard_map/ppermute | solution.py:308
  26.8 1.8 %collective-permute-start.20 = (bf16[32,1024]{1,0:T(8,128)(2,1)S(1)}, bf16[32,1024]{1,0:T(8,128)(2,1)S(1)}, u32[]{:S(2)}, u32[]{:S(2)}) collective-permute-start(bf16[32,1024]{1,0:T(8,128)(2,1)S(1)} %slice.52), channel_id=1, source_target_pairs={{0,2},{1,3},{4,0},{5,1},{8,4},{9,5},{12,8},{13,9},{14,12},{15,13},... | collective-permute-start | bytes 196616 | tf_op jit(solution)/shard_map/ppermute | solution.py:308
  29.6 1.6 %collective-permute-start.9 = (bf16[32,1024]{1,0:T(8,128)(2,1)S(1)}, bf16[32,1024]{1,0:T(8,128)(2,1)S(1)}, u32[]{:S(2)}, u32[]{:S(2)}) collective-permute-start(bf16[32,1024]{1,0:T(8,128)(2,1)S(1)} %slice.50), channel_id=1, source_target_pairs={{0,2},{1,3},{4,0},{5,1},{8,4},{9,5},{12,8},{13,9},{14,12},{15,13},... | collective-permute-start | bytes 196616 | tf_op jit(solution)/shard_map/ppermute | solution.py:308
  31.8 1.6 %shard_map.95.total_ref = f32[384,1024]{1,0:T(8,128)S(1)} custom-call(bf16[2,8,96,72]{3,2,1,0:T(8,128)(2,1)S(1)} %get-tuple-element.38.refs_0_.mine_ref, bf16[2,8,96,72]{3,2,1,0:T(8,128)(2,1)S(1)} %collective-permute-done.refs_1_.given_ref, bf16[2,8,96,72]{3,2,1,0:T(8,128)(2,1)S(1)} %collective-permute-done.1.refs_2_.theirs_ref, ...), custom_call_target="tpu_custom_call" | custom-call | flops 452984832 | bytes 1572864 | tf_op jit(solution)/shard_map/pallas_call | solution.py:110
  33.4 1.6 %shard_map.92.total_ref = f32[384,1024]{1,0:T(8,128)S(1)} custom-call(bf16[2,8,96,72]{3,2,1,0:T(8,128)(2,1)S(1)} %get-tuple-element.38.refs_0_.mine_ref, bf16[2,8,96,72]{3,2,1,0:T(8,128)(2,1)S(1)} %collective-permute-done.refs_1_.given_ref, bf16[2,8,96,72]{3,2,1,0:T(8,128)(2,1)S(1)} %collective-permute-done.1.refs_2_.theirs_ref, ...), custom_call_target="tpu_custom_call" | custom-call | flops 452984832 | bytes 1572864 | tf_op jit(solution)/shard_map/pallas_call | solution.py:110
  37.5 1.6 %collective-permute-start.23 = (bf16[96,1024]{1,0:T(8,128)(2,1)S(1)}, bf16[96,1024]{1,0:T(8,128)(2,1)S(1)}, u32[]{:S(2)}, u32[]{:S(2)}) collective-permute-start(bf16[96,1024]{1,0:T(8,128)(2,1)S(1)} %shard_map.97), channel_id=1, source_target_pairs={{0,16},{16,0},{1,17},{17,1},{2,18},{18,2},{3,19},{19,3},{4,20},{20... | collective-permute-start | bytes 589832 | tf_op jit(solution)/shard_map/ppermute | solution.py:349
  40.0 5.3 %collective-permute-done.23.refs_5_ = bf16[96,1024]{1,0:T(8,128)(2,1)S(1)} collective-permute-done((bf16[96,1024]{1,0:T(8,128)(2,1)S(1)}, bf16[96,1024]{1,0:T(8,128)(2,1)S(1)}, u32[]{:S(2)}, u32[]{:S(2)}) %collective-permute-start.23) | collective-permute-done | bytes 196640 | tf_op jit(solution)/shard_map/ppermute | solution.py:349
  45.3 3.4 %collective-permute-done.12.refs_2_ = bf16[96,1024]{1,0:T(8,128)(2,1)S(1)} collective-permute-done((bf16[96,1024]{1,0:T(8,128)(2,1)S(1)}, bf16[96,1024]{1,0:T(8,128)(2,1)S(1)}, u32[]{:S(2)}, u32[]{:S(2)}) %collective-permute-start.12) | collective-permute-done | bytes 196640 | tf_op jit(solution)/shard_map/ppermute | solution.py:349
  49.0 1.6 %collective-permute-start.57 = (bf16[48,2048]{1,0:T(8,128)(2,1)S(1)}, bf16[48,2048]{1,0:T(8,128)(2,1)S(1)}, u32[]{:S(2)}, u32[]{:S(2)}) collective-permute-start(bf16[48,2048]{1,0:T(8,128)(2,1)S(1)} %get-tuple-element.60.refs_0_), channel_id=1, source_target_pairs={{0,2},{1,3},{4,0},{5,1},{8,4},{9,5},{12,8},{13,9},{14,12},{15,13},... | collective-permute-start | bytes 589832 | tf_op jit(solution)/shard_map/ppermute | solution.py:308
  51.1 1.5 %collective-permute-start.27 = (bf16[48,2176]{1,0:T(8,128)(2,1)S(1)}, bf16[48,2176]{1,0:T(8,128)(2,1)S(1)}, u32[]{:S(2)}, u32[]{:S(2)}) collective-permute-start(bf16[48,2176]{1,0:T(8,128)(2,1)S(1)} %get-tuple-element.49.refs_0_.refs_2_), channel_id=1, source_target_pairs={{0,2},{1,3},{4,0},{5,1},{8,4},{9,5},{12,8},{13,9},{14,12},{15,13},... | collective-permute-start | bytes 626696 | tf_op jit(solution)/shard_map/ppermute | solution.py:308
  53.1 3.7 %collective-permute-done.57.refs_1_ = bf16[48,2048]{1,0:T(8,128)(2,1)S(1)} collective-permute-done((bf16[48,2048]{1,0:T(8,128)(2,1)S(1)}, bf16[48,2048]{1,0:T(8,128)(2,1)S(1)}, u32[]{:S(2)}, u32[]{:S(2)}) %collective-permute-start.57) | collective-permute-done | bytes 196640 | tf_op jit(solution)/shard_map/ppermute | solution.py:308
  56.8 1.5 %collective-permute-start.62 = (bf16[48,2048]{1,0:T(8,128)(2,1)S(1)}, bf16[48,2048]{1,0:T(8,128)(2,1)S(1)}, u32[]{:S(2)}, u32[]{:S(2)}) collective-permute-start(bf16[48,2048]{1,0:T(8,128)(2,1)S(1)} %collective-permute-done.57.refs_1_), channel_id=1, source_target_pairs={{0,2},{1,3},{4,0},{5,1},{8,4},{9,5},{12,8},{13,9},{14,12},{15,13},... | collective-permute-start | bytes 589832 | tf_op jit(solution)/shard_map/ppermute | solution.py:308
  58.8 2.4 %collective-permute-done.27.refs_1_.refs_5_ = bf16[48,2176]{1,0:T(8,128)(2,1)S(1)} collective-permute-done((bf16[48,2176]{1,0:T(8,128)(2,1)S(1)}, bf16[48,2176]{1,0:T(8,128)(2,1)S(1)}, u32[]{:S(2)}, u32[]{:S(2)}) %collective-permute-start.27) | collective-permute-done | bytes 208928 | tf_op jit(solution)/shard_map/ppermute | solution.py:308
  61.3 1.5 %collective-permute-start.32 = (bf16[48,2176]{1,0:T(8,128)(2,1)S(1)}, bf16[48,2176]{1,0:T(8,128)(2,1)S(1)}, u32[]{:S(2)}, u32[]{:S(2)}) collective-permute-start(bf16[48,2176]{1,0:T(8,128)(2,1)S(1)} %collective-permute-done.27.refs_1_.refs_5_), channel_id=1, source_target_pairs={{0,2},{1,3},{4,0},{5,1},{8,4},{9,5},{12,8},{13,9},{14,12},{15,13},... | collective-permute-start | bytes 626696 | tf_op jit(solution)/shard_map/ppermute | solution.py:308
  63.3 2.2 %collective-permute-done.62.refs_1_ = bf16[48,2048]{1,0:T(8,128)(2,1)S(1)} collective-permute-done((bf16[48,2048]{1,0:T(8,128)(2,1)S(1)}, bf16[48,2048]{1,0:T(8,128)(2,1)S(1)}, u32[]{:S(2)}, u32[]{:S(2)}) %collective-permute-start.62) | collective-permute-done | bytes 196640 | tf_op jit(solution)/shard_map/ppermute | solution.py:308
  65.5 1.5 %collective-permute-start.67 = (bf16[48,2048]{1,0:T(8,128)(2,1)S(1)}, bf16[48,2048]{1,0:T(8,128)(2,1)S(1)}, u32[]{:S(2)}, u32[]{:S(2)}) collective-permute-start(bf16[48,2048]{1,0:T(8,128)(2,1)S(1)} %collective-permute-done.62.refs_1_), channel_id=1, source_target_pairs={{0,2},{1,3},{4,0},{5,1},{8,4},{9,5},{12,8},{13,9},{14,12},{15,13},... | collective-permute-start | bytes 589832 | tf_op jit(solution)/shard_map/ppermute | solution.py:308
  67.5 2.4 %collective-permute-done.32.refs_1_.refs_5_ = bf16[48,2176]{1,0:T(8,128)(2,1)S(1)} collective-permute-done((bf16[48,2176]{1,0:T(8,128)(2,1)S(1)}, bf16[48,2176]{1,0:T(8,128)(2,1)S(1)}, u32[]{:S(2)}, u32[]{:S(2)}) %collective-permute-start.32) | collective-permute-done | bytes 208928 | tf_op jit(solution)/shard_map/ppermute | solution.py:308
  70.0 1.5 %collective-permute-start.37 = (bf16[48,2176]{1,0:T(8,128)(2,1)S(1)}, bf16[48,2176]{1,0:T(8,128)(2,1)S(1)}, u32[]{:S(2)}, u32[]{:S(2)}) collective-permute-start(bf16[48,2176]{1,0:T(8,128)(2,1)S(1)} %collective-permute-done.32.refs_1_.refs_5_), channel_id=1, source_target_pairs={{0,2},{1,3},{4,0},{5,1},{8,4},{9,5},{12,8},{13,9},{14,12},{15,13},... | collective-permute-start | bytes 626696 | tf_op jit(solution)/shard_map/ppermute | solution.py:308
  72.0 2.2 %collective-permute-done.67.refs_1_ = bf16[48,2048]{1,0:T(8,128)(2,1)S(1)} collective-permute-done((bf16[48,2048]{1,0:T(8,128)(2,1)S(1)}, bf16[48,2048]{1,0:T(8,128)(2,1)S(1)}, u32[]{:S(2)}, u32[]{:S(2)}) %collective-permute-start.67) | collective-permute-done | bytes 196640 | tf_op jit(solution)/shard_map/ppermute | solution.py:308
  74.2 1.5 %collective-permute-done.66.refs_0_ = bf16[48,2048]{1,0:T(8,128)(2,1)S(1)} collective-permute-done((bf16[48,2048]{1,0:T(8,128)(2,1)S(1)}, bf16[48,2048]{1,0:T(8,128)(2,1)S(1)}, u32[]{:S(2)}, u32[]{:S(2)}) %collective-permute-start.66) | collective-permute-done | bytes 196640 | tf_op jit(solution)/shard_map/ppermute | solution.py:308
  75.7 1.6 %collective-permute-start.72 = (bf16[24,2048]{1,0:T(8,128)(2,1)S(1)}, bf16[24,2048]{1,0:T(8,128)(2,1)S(1)}, u32[]{:S(2)}, u32[]{:S(2)}) collective-permute-start(bf16[24,2048]{1,0:T(8,128)(2,1)S(1)} %slice.56), channel_id=1, source_target_pairs={{0,2},{1,3},{4,0},{5,1},{8,4},{9,5},{12,8},{13,9},{14,12},{15,13},... | collective-permute-start | bytes 294920 | tf_op jit(solution)/shard_map/ppermute | solution.py:308
  77.3 1.3 collective-permute-start.71
  78.6 1.2 collective-permute-start.42
  79.8 1.1 collective-permute-start.41
  83.3 1.4 collective-permute-done.41.refs_0_.refs_4_
  85.2 0.9 collective-permute-done.73.refs_2_
  87.1 1.7 %shard_map.117 = (bf16[48,2048]{1,0:T(8,128)(2,1)S(1)}, bf16[48,2048]{1,0:T(8,128)(2,1)S(1)}) custom-call(bf16[24,2048]{1,0:T(8,128)(2,1)S(1)} %collective-permute-done.71.refs_0_, bf16[24,2048]{1,0:T(8,128)(2,1)S(1)} %collective-permute-done.72.refs_1_, bf16[24,2048]{1,0:T(8,128)(2,1)S(1)} %collective-permute-done.73.refs_2_, ...), custom_call_target="tpu_custom_call" | custom-call | flops 905969664 | bytes 9437184 | tf_op jit(solution)/shard_map/pallas_call | solution.py:110
  89.3 2.1 %shard_map.103 = (bf16[96,2048]{1,0:T(8,128)(2,1)S(1)}, bf16[96,2048]{1,0:T(8,128)(2,1)S(1)}) custom-call(bf16[48,2176]{1,0:T(8,128)(2,1)S(1)} %collective-permute-done.36.refs_0_.refs_4_, bf16[48,2176]{1,0:T(8,128)(2,1)S(1)} %collective-permute-done.37.refs_1_.refs_5_, bf16[48,2176]{1,0:T(8,128)(2,1)S(1)} %collective-permute-done.38.refs_2_.refs_6_, ...), custom_call_target="tpu_custom_call" | custom-call | flops 1811939328 | bytes 9437184 | tf_op jit(solution)/shard_map/pallas_call | solution.py:110
  92.2 1.7 %shard_map.104 = (bf16[48,2048]{1,0:T(8,128)(2,1)S(1)}, bf16[48,2048]{1,0:T(8,128)(2,1)S(1)}) custom-call(bf16[24,2176]{1,0:T(8,128)(2,1)S(1)} %collective-permute-done.41.refs_0_.refs_4_, bf16[24,2176]{1,0:T(8,128)(2,1)S(1)} %collective-permute-done.42.refs_1_.refs_5_, bf16[24,2176]{1,0:T(8,128)(2,1)S(1)} %collective-permute-done.43.refs_2_.refs_6_, ...), custom_call_target="tpu_custom_call" | custom-call | flops 905969664 | bytes 9437184 | tf_op jit(solution)/shard_map/pallas_call | solution.py:110
  94.5 2.1 %shard_map.116 = (bf16[96,2048]{1,0:T(8,128)(2,1)S(1)}, bf16[96,2048]{1,0:T(8,128)(2,1)S(1)}) custom-call(bf16[48,2048]{1,0:T(8,128)(2,1)S(1)} %collective-permute-done.66.refs_0_, bf16[48,2048]{1,0:T(8,128)(2,1)S(1)} %collective-permute-done.67.refs_1_, bf16[48,2048]{1,0:T(8,128)(2,1)S(1)} %collective-permute-done.68.refs_2_, ...), custom_call_target="tpu_custom_call" | custom-call | flops 1811939328 | bytes 9437184 | tf_op jit(solution)/shard_map/pallas_call | solution.py:110
  98.1 2.1 %shard_map.115 = (bf16[96,2048]{1,0:T(8,128)(2,1)S(1)}, bf16[96,2048]{1,0:T(8,128)(2,1)S(1)}) custom-call(bf16[48,2048]{1,0:T(8,128)(2,1)S(1)} %collective-permute-done.61.refs_0_, bf16[48,2048]{1,0:T(8,128)(2,1)S(1)} %collective-permute-done.62.refs_1_, bf16[48,2048]{1,0:T(8,128)(2,1)S(1)} %collective-permute-done.63.refs_2_, ...), custom_call_target="tpu_custom_call" | custom-call | flops 1811939328 | bytes 9437184 | tf_op jit(solution)/shard_map/pallas_call | solution.py:110
  100.8 1.4 collective-permute-done.76.refs_0_
  102.3 1.6 %collective-permute-start.80 = (bf16[24,2048]{1,0:T(8,128)(2,1)S(1)}, bf16[24,2048]{1,0:T(8,128)(2,1)S(1)}, u32[]{:S(2)}, u32[]{:S(2)}) collective-permute-start(bf16[24,2048]{1,0:T(8,128)(2,1)S(1)} %shard_map.122), channel_id=1, source_target_pairs={{0,2},{1,3},{4,0},{5,1},{8,4},{9,5},{12,8},{13,9},{14,12},{15,13},... | collective-permute-start | bytes 294920 | tf_op jit(solution)/shard_map/ppermute | solution.py:308
  103.9 2.1 %shard_map.102 = (bf16[96,2048]{1,0:T(8,128)(2,1)S(1)}, bf16[96,2048]{1,0:T(8,128)(2,1)S(1)}) custom-call(bf16[48,2176]{1,0:T(8,128)(2,1)S(1)} %collective-permute-done.31.refs_0_.refs_4_, bf16[48,2176]{1,0:T(8,128)(2,1)S(1)} %collective-permute-done.32.refs_1_.refs_5_, bf16[48,2176]{1,0:T(8,128)(2,1)S(1)} %collective-permute-done.33.refs_2_.refs_6_, ...), custom_call_target="tpu_custom_call" | custom-call | flops 1811939328 | bytes 9437184 | tf_op jit(solution)/shard_map/pallas_call | solution.py:110
  108.1 1.6 %collective-permute-start.77 = (bf16[48,2048]{1,0:T(8,128)(2,1)S(1)}, bf16[48,2048]{1,0:T(8,128)(2,1)S(1)}, u32[]{:S(2)}, u32[]{:S(2)}) collective-permute-start(bf16[48,2048]{1,0:T(8,128)(2,1)S(1)} %shard_map.119), channel_id=1, source_target_pairs={{0,4},{1,5},{4,8},{5,9},{8,12},{9,13},{12,14},{13,15},{14,10},{15,... | collective-permute-start | bytes 589832 | tf_op jit(solution)/shard_map/ppermute | solution.py:308
  109.7 3.0 %collective-permute-done.46.refs_0_ = bf16[24,2048]{1,0:T(8,128)(2,1)S(1)} collective-permute-done((bf16[24,2048]{1,0:T(8,128)(2,1)S(1)}, bf16[24,2048]{1,0:T(8,128)(2,1)S(1)}, u32[]{:S(2)}, u32[]{:S(2)}) %collective-permute-start.46) | collective-permute-done | bytes 98336 | tf_op jit(solution)/shard_map/ppermute | solution.py:308
  112.7 1.6 %collective-permute-start.50 = (bf16[24,2048]{1,0:T(8,128)(2,1)S(1)}, bf16[24,2048]{1,0:T(8,128)(2,1)S(1)}, u32[]{:S(2)}, u32[]{:S(2)}) collective-permute-start(bf16[24,2048]{1,0:T(8,128)(2,1)S(1)} %shard_map.109), channel_id=1, source_target_pairs={{0,2},{1,3},{4,0},{5,1},{8,4},{9,5},{12,8},{13,9},{14,12},{15,13},... | collective-permute-start | bytes 294920 | tf_op jit(solution)/shard_map/ppermute | solution.py:308
  114.2 1.6 %collective-permute-start.81 = (bf16[48,2048]{1,0:T(8,128)(2,1)S(1)}, bf16[48,2048]{1,0:T(8,128)(2,1)S(1)}, u32[]{:S(2)}, u32[]{:S(2)}) collective-permute-start(bf16[48,2048]{1,0:T(8,128)(2,1)S(1)} %shard_map.123), channel_id=1, source_target_pairs={{0,2},{1,3},{4,0},{5,1},{8,4},{9,5},{12,8},{13,9},{14,12},{15,13},... | collective-permute-start | bytes 589832 | tf_op jit(solution)/shard_map/ppermute | solution.py:308
  115.8 2.1 %shard_map.114 = (bf16[96,2048]{1,0:T(8,128)(2,1)S(1)}, bf16[96,2048]{1,0:T(8,128)(2,1)S(1)}) custom-call(bf16[48,2048]{1,0:T(8,128)(2,1)S(1)} %collective-permute-done.56.refs_0_, bf16[48,2048]{1,0:T(8,128)(2,1)S(1)} %collective-permute-done.57.refs_1_, bf16[48,2048]{1,0:T(8,128)(2,1)S(1)} %collective-permute-done.58.refs_2_, ...), custom_call_target="tpu_custom_call" | custom-call | flops 1811939328 | bytes 9437184 | tf_op jit(solution)/shard_map/pallas_call | solution.py:110
  119.4 1.2 collective-permute-start.51
  120.6 2.1 %shard_map.101 = (bf16[96,2048]{1,0:T(8,128)(2,1)S(1)}, bf16[96,2048]{1,0:T(8,128)(2,1)S(1)}) custom-call(bf16[48,2176]{1,0:T(8,128)(2,1)S(1)} %collective-permute-done.26.refs_0_.refs_4_, bf16[48,2176]{1,0:T(8,128)(2,1)S(1)} %collective-permute-done.27.refs_1_.refs_5_, bf16[48,2176]{1,0:T(8,128)(2,1)S(1)} %collective-permute-done.28.refs_2_.refs_6_, ...), custom_call_target="tpu_custom_call" | custom-call | flops 1811939328 | bytes 9437184 | tf_op jit(solution)/shard_map/pallas_call | solution.py:110
  123.0 2.4 %collective-permute-done.47.refs_0_ = bf16[48,2048]{1,0:T(8,128)(2,1)S(1)} collective-permute-done((bf16[48,2048]{1,0:T(8,128)(2,1)S(1)}, bf16[48,2048]{1,0:T(8,128)(2,1)S(1)}, u32[]{:S(2)}, u32[]{:S(2)}) %collective-permute-start.47) | collective-permute-done | bytes 196640 | tf_op jit(solution)/shard_map/ppermute | solution.py:308
  126.0 1.6 %collective-permute-start.82 = (bf16[48,2048]{1,0:T(8,128)(2,1)S(1)}, bf16[48,2048]{1,0:T(8,128)(2,1)S(1)}, u32[]{:S(2)}, u32[]{:S(2)}) collective-permute-start(bf16[48,2048]{1,0:T(8,128)(2,1)S(1)} %shard_map.124), channel_id=1, source_target_pairs={{0,2},{1,3},{4,0},{5,1},{8,4},{9,5},{12,8},{13,9},{14,12},{15,13},... | collective-permute-start | bytes 589832 | tf_op jit(solution)/shard_map/ppermute | solution.py:308
  128.3 1.7 %shard_map.113 = (bf16[48,2048]{1,0:T(8,128)(2,1)S(1)}, bf16[48,2048]{1,0:T(8,128)(2,1)S(1)}) custom-call(bf16[48,2048]{1,0:T(8,128)(2,1)S(1)} %get-tuple-element.60.refs_0_, bf16[48,2048]{1,0:T(8,128)(2,1)S(1)} %collective-permute-done.54.refs_1_, bf16[48,2176]{1,0:T(8,128)(2,1)S(1)} %get-tuple-element.49.refs_0_.refs_2_, ...), custom_call_target="tpu_custom_call" | custom-call | flops 905969664 | bytes 9437184 | tf_op jit(solution)/shard_map/pallas_call | solution.py:110
  130.0 1.5 collective-permute-start.52
  131.5 1.7 %collective-permute-done.78.refs_0_ = bf16[48,2048]{1,0:T(8,128)(2,1)S(1)} collective-permute-done((bf16[48,2048]{1,0:T(8,128)(2,1)S(1)}, bf16[48,2048]{1,0:T(8,128)(2,1)S(1)}, u32[]{:S(2)}, u32[]{:S(2)}) %collective-permute-start.78) | collective-permute-done | bytes 196640 | tf_op jit(solution)/shard_map/ppermute | solution.py:308
  133.2 1.7 %shard_map.100 = (bf16[48,2048]{1,0:T(8,128)(2,1)S(1)}, bf16[48,2048]{1,0:T(8,128)(2,1)S(1)}) custom-call(bf16[48,2176]{1,0:T(8,128)(2,1)S(1)} %get-tuple-element.49.refs_0_.refs_2_, bf16[48,2176]{1,0:T(8,128)(2,1)S(1)} %collective-permute-done.24.refs_1_.refs_3_, bf16[2048,768]{1,0:T(8,128)(2,1)S(1)} %bitcast.16, bf16[2048,768]{1,0:T(8,128)(2,1)S(1)} %bitcast.26, ...), custom_call_target="tpu_custom_call" | custom-call | flops 905969664 | bytes 9437184 | tf_op jit(solution)/shard_map/pallas_call | solution.py:110
  135.8 1.9 %collective-permute-start.83 = (bf16[48,2048]{1,0:T(8,128)(2,1)S(1)}, bf16[48,2048]{1,0:T(8,128)(2,1)S(1)}, u32[]{:S(2)}, u32[]{:S(2)}) collective-permute-start(bf16[48,2048]{1,0:T(8,128)(2,1)S(1)} %shard_map.125), channel_id=1, source_target_pairs={{0,2},{1,3},{4,0},{5,1},{8,4},{9,5},{12,8},{13,9},{14,12},{15,13},... | collective-permute-start | bytes 589832 | tf_op jit(solution)/shard_map/ppermute | solution.py:308
  138.1 1.9 %collective-permute-start.53 = (bf16[48,2048]{1,0:T(8,128)(2,1)S(1)}, bf16[48,2048]{1,0:T(8,128)(2,1)S(1)}, u32[]{:S(2)}, u32[]{:S(2)}) collective-permute-start(bf16[48,2048]{1,0:T(8,128)(2,1)S(1)} %shard_map.112), channel_id=1, source_target_pairs={{0,2},{1,3},{4,0},{5,1},{8,4},{9,5},{12,8},{13,9},{14,12},{15,13},... | collective-permute-start | bytes 589832 | tf_op jit(solution)/shard_map/ppermute | solution.py:308
  140.0 3.4 %collective-permute-done.79.refs_6_ = bf16[48,2048]{1,0:T(8,128)(2,1)S(1)} collective-permute-done((bf16[48,2048]{1,0:T(8,128)(2,1)S(1)}, bf16[48,2048]{1,0:T(8,128)(2,1)S(1)}, u32[]{:S(2)}, u32[]{:S(2)}) %collective-permute-start.79) | collective-permute-done | bytes 196640 | tf_op jit(solution)/shard_map/ppermute | solution.py:308
  143.6 3.1 %collective-permute-done.49.refs_2_ = bf16[48,2048]{1,0:T(8,128)(2,1)S(1)} collective-permute-done((bf16[48,2048]{1,0:T(8,128)(2,1)S(1)}, bf16[48,2048]{1,0:T(8,128)(2,1)S(1)}, u32[]{:S(2)}, u32[]{:S(2)}) %collective-permute-start.49) | collective-permute-done | bytes 196640 | tf_op jit(solution)/shard_map/ppermute | solution.py:308
  146.8 1.0 shard_map.126
  (168 shorter events, 25.1 us)
Async XLA Ops:
  4.2 14.2 %collective-permute-start = (bf16[2,8,96,72]{3,2,1,0:T(8,128)(2,1)S(1)}, bf16[2,8,96,72]{3,2,1,0:T(8,128)(2,1)S(1)}, u32[]{:S(2)}, u32[]{:S(2)}) collective-permute-start(bf16[2,8,96,72]{3,2,1,0:T(8,128)(2,1)S(1)} %get-tuple-element.39), channel_id=1, source_target_pairs={{0,1},{1,0},{2,3},{3,2},{4,5},{5,4},{6,7},{7,6},{8,9},{9,8},{10,11... | collective-permute-start | bytes 663560 | tf_op jit(solution)/shard_map/ppermute | solution.py:314
  5.9 7.3 %collective-permute-start.14 = (bf16[72,1024]{1,0:T(8,128)(2,1)S(1)}, bf16[72,1024]{1,0:T(8,128)(2,1)S(1)}, u32[]{:S(2)}, u32[]{:S(2)}) collective-permute-start(bf16[72,1024]{1,0:T(8,128)(2,1)S(1)} %get-tuple-element.71.refs_3_), channel_id=1, source_target_pairs={{0,2},{1,3},{4,0},{5,1},{8,4},{9,5},{12,8},{13,9},{14,12},{15,13},... | collective-permute-start | bytes 442376 | tf_op jit(solution)/shard_map/ppermute | solution.py:308
  8.5 6.7 %collective-permute-start.13 = (bf16[72,1024]{1,0:T(8,128)(2,1)S(1)}, bf16[72,1024]{1,0:T(8,128)(2,1)S(1)}, u32[]{:S(2)}, u32[]{:S(2)}) collective-permute-start(bf16[72,1024]{1,0:T(8,128)(2,1)S(1)} %get-tuple-element.71.refs_3_), channel_id=1, source_target_pairs={{0,4},{1,5},{4,8},{5,9},{8,12},{9,13},{12,14},{13,15},{14,10},{15,... | collective-permute-start | bytes 442376 | tf_op jit(solution)/shard_map/ppermute | solution.py:308
  8.6 7.8 %collective-permute-start.3 = (bf16[72,1024]{1,0:T(8,128)(2,1)S(1)}, bf16[72,1024]{1,0:T(8,128)(2,1)S(1)}, u32[]{:S(2)}, u32[]{:S(2)}) collective-permute-start(bf16[72,1024]{1,0:T(8,128)(2,1)S(1)} %get-tuple-element.72.refs_3_), channel_id=1, source_target_pairs={{0,2},{1,3},{4,0},{5,1},{8,4},{9,5},{12,8},{13,9},{14,12},{15,13},... | collective-permute-start | bytes 442376 | tf_op jit(solution)/shard_map/ppermute | solution.py:308
  10.5 7.9 %collective-permute-start.2 = (bf16[72,1024]{1,0:T(8,128)(2,1)S(1)}, bf16[72,1024]{1,0:T(8,128)(2,1)S(1)}, u32[]{:S(2)}, u32[]{:S(2)}) collective-permute-start(bf16[72,1024]{1,0:T(8,128)(2,1)S(1)} %get-tuple-element.72.refs_3_), channel_id=1, source_target_pairs={{0,4},{1,5},{4,8},{5,9},{8,12},{9,13},{12,14},{13,15},{14,10},{15,... | collective-permute-start | bytes 442376 | tf_op jit(solution)/shard_map/ppermute | solution.py:308
  13.2 7.3 %collective-permute-start.16 = (bf16[72,1024]{1,0:T(8,128)(2,1)S(1)}, bf16[72,1024]{1,0:T(8,128)(2,1)S(1)}, u32[]{:S(2)}, u32[]{:S(2)}) collective-permute-start(bf16[72,1024]{1,0:T(8,128)(2,1)S(1)} %collective-permute-done.14.refs_5_), channel_id=1, source_target_pairs={{0,2},{1,3},{4,0},{5,1},{8,4},{9,5},{12,8},{13,9},{14,12},{15,13},... | collective-permute-start | bytes 442376 | tf_op jit(solution)/shard_map/ppermute | solution.py:308
  15.2 6.9 %collective-permute-start.15 = (bf16[72,1024]{1,0:T(8,128)(2,1)S(1)}, bf16[72,1024]{1,0:T(8,128)(2,1)S(1)}, u32[]{:S(2)}, u32[]{:S(2)}) collective-permute-start(bf16[72,1024]{1,0:T(8,128)(2,1)S(1)} %collective-permute-done.13.refs_4_), channel_id=1, source_target_pairs={{0,4},{1,5},{4,8},{5,9},{8,12},{9,13},{12,14},{13,15},{14,10},{15,... | collective-permute-start | bytes 442376 | tf_op jit(solution)/shard_map/ppermute | solution.py:308
  16.4 6.7 %collective-permute-start.5 = (bf16[72,1024]{1,0:T(8,128)(2,1)S(1)}, bf16[72,1024]{1,0:T(8,128)(2,1)S(1)}, u32[]{:S(2)}, u32[]{:S(2)}) collective-permute-start(bf16[72,1024]{1,0:T(8,128)(2,1)S(1)} %collective-permute-done.3.refs_5_), channel_id=1, source_target_pairs={{0,2},{1,3},{4,0},{5,1},{8,4},{9,5},{12,8},{13,9},{14,12},{15,13},... | collective-permute-start | bytes 442376 | tf_op jit(solution)/shard_map/ppermute | solution.py:308
  18.3 6.7 %collective-permute-start.4 = (bf16[72,1024]{1,0:T(8,128)(2,1)S(1)}, bf16[72,1024]{1,0:T(8,128)(2,1)S(1)}, u32[]{:S(2)}, u32[]{:S(2)}) collective-permute-start(bf16[72,1024]{1,0:T(8,128)(2,1)S(1)} %collective-permute-done.2.refs_4_), channel_id=1, source_target_pairs={{0,4},{1,5},{4,8},{5,9},{8,12},{9,13},{12,14},{13,15},{14,10},{15,... | collective-permute-start | bytes 442376 | tf_op jit(solution)/shard_map/ppermute | solution.py:308
  18.6 13.2 %collective-permute-start.1 = (bf16[2,8,96,72]{3,2,1,0:T(8,128)(2,1)S(1)}, bf16[2,8,96,72]{3,2,1,0:T(8,128)(2,1)S(1)}, u32[]{:S(2)}, u32[]{:S(2)}) collective-permute-start(bf16[2,8,96,72]{3,2,1,0:T(8,128)(2,1)S(1)} %pad_maximum_fusion), channel_id=1, source_target_pairs={{0,16},{16,0},{1,17},{17,1},{2,18},{18,2},{3,19},{19,3},{4,20},{20... | collective-permute-start | bytes 663560 | tf_op jit(solution)/shard_map/ppermute | solution.py:316
  20.6 6.2 %collective-permute-start.18 = (bf16[72,1024]{1,0:T(8,128)(2,1)S(1)}, bf16[72,1024]{1,0:T(8,128)(2,1)S(1)}, u32[]{:S(2)}, u32[]{:S(2)}) collective-permute-start(bf16[72,1024]{1,0:T(8,128)(2,1)S(1)} %collective-permute-done.16.refs_7_), channel_id=1, source_target_pairs={{0,2},{1,3},{4,0},{5,1},{8,4},{9,5},{12,8},{13,9},{14,12},{15,13},... | collective-permute-start | bytes 442376 | tf_op jit(solution)/shard_map/ppermute | solution.py:308
  22.1 6.6 %collective-permute-start.17 = (bf16[72,1024]{1,0:T(8,128)(2,1)S(1)}, bf16[72,1024]{1,0:T(8,128)(2,1)S(1)}, u32[]{:S(2)}, u32[]{:S(2)}) collective-permute-start(bf16[72,1024]{1,0:T(8,128)(2,1)S(1)} %collective-permute-done.15.refs_6_), channel_id=1, source_target_pairs={{0,4},{1,5},{4,8},{5,9},{8,12},{9,13},{12,14},{13,15},{14,10},{15,... | collective-permute-start | bytes 442376 | tf_op jit(solution)/shard_map/ppermute | solution.py:308
  23.1 6.5 %collective-permute-start.7 = (bf16[72,1024]{1,0:T(8,128)(2,1)S(1)}, bf16[72,1024]{1,0:T(8,128)(2,1)S(1)}, u32[]{:S(2)}, u32[]{:S(2)}) collective-permute-start(bf16[72,1024]{1,0:T(8,128)(2,1)S(1)} %collective-permute-done.5.refs_7_), channel_id=1, source_target_pairs={{0,2},{1,3},{4,0},{5,1},{8,4},{9,5},{12,8},{13,9},{14,12},{15,13},... | collective-permute-start | bytes 442376 | tf_op jit(solution)/shard_map/ppermute | solution.py:308
  25.1 6.2 %collective-permute-start.6 = (bf16[72,1024]{1,0:T(8,128)(2,1)S(1)}, bf16[72,1024]{1,0:T(8,128)(2,1)S(1)}, u32[]{:S(2)}, u32[]{:S(2)}) collective-permute-start(bf16[72,1024]{1,0:T(8,128)(2,1)S(1)} %collective-permute-done.4.refs_6_), channel_id=1, source_target_pairs={{0,4},{1,5},{4,8},{5,9},{8,12},{9,13},{12,14},{13,15},{14,10},{15,... | collective-permute-start | bytes 442376 | tf_op jit(solution)/shard_map/ppermute | solution.py:308
  26.8 8.1 %collective-permute-start.20 = (bf16[32,1024]{1,0:T(8,128)(2,1)S(1)}, bf16[32,1024]{1,0:T(8,128)(2,1)S(1)}, u32[]{:S(2)}, u32[]{:S(2)}) collective-permute-start(bf16[32,1024]{1,0:T(8,128)(2,1)S(1)} %slice.52), channel_id=1, source_target_pairs={{0,2},{1,3},{4,0},{5,1},{8,4},{9,5},{12,8},{13,9},{14,12},{15,13},... | collective-permute-start | bytes 196616 | tf_op jit(solution)/shard_map/ppermute | solution.py:308
  28.7 6.2 %collective-permute-start.19 = (bf16[40,1024]{1,0:T(8,128)(2,1)S(1)}, bf16[40,1024]{1,0:T(8,128)(2,1)S(1)}, u32[]{:S(2)}, u32[]{:S(2)}) collective-permute-start(bf16[40,1024]{1,0:T(8,128)(2,1)S(1)} %slice.51), channel_id=1, source_target_pairs={{0,4},{1,5},{4,8},{5,9},{8,12},{9,13},{12,14},{13,15},{14,10},{15,... | collective-permute-start | bytes 245768 | tf_op jit(solution)/shard_map/ppermute | solution.py:308
  29.6 6.1 %collective-permute-start.9 = (bf16[32,1024]{1,0:T(8,128)(2,1)S(1)}, bf16[32,1024]{1,0:T(8,128)(2,1)S(1)}, u32[]{:S(2)}, u32[]{:S(2)}) collective-permute-start(bf16[32,1024]{1,0:T(8,128)(2,1)S(1)} %slice.50), channel_id=1, source_target_pairs={{0,2},{1,3},{4,0},{5,1},{8,4},{9,5},{12,8},{13,9},{14,12},{15,13},... | collective-permute-start | bytes 196616 | tf_op jit(solution)/shard_map/ppermute | solution.py:308
  37.5 7.8 %collective-permute-start.23 = (bf16[96,1024]{1,0:T(8,128)(2,1)S(1)}, bf16[96,1024]{1,0:T(8,128)(2,1)S(1)}, u32[]{:S(2)}, u32[]{:S(2)}) collective-permute-start(bf16[96,1024]{1,0:T(8,128)(2,1)S(1)} %shard_map.97), channel_id=1, source_target_pairs={{0,16},{16,0},{1,17},{17,1},{2,18},{18,2},{3,19},{19,3},{4,20},{20... | collective-permute-start | bytes 589832 | tf_op jit(solution)/shard_map/ppermute | solution.py:349
  39.1 9.6 %collective-permute-start.12 = (bf16[96,1024]{1,0:T(8,128)(2,1)S(1)}, bf16[96,1024]{1,0:T(8,128)(2,1)S(1)}, u32[]{:S(2)}, u32[]{:S(2)}) collective-permute-start(bf16[96,1024]{1,0:T(8,128)(2,1)S(1)} %shard_map.94), channel_id=1, source_target_pairs={{0,16},{16,0},{1,17},{17,1},{2,18},{18,2},{3,19},{19,3},{4,20},{20... | collective-permute-start | bytes 589832 | tf_op jit(solution)/shard_map/ppermute | solution.py:349
  49.0 7.8 %collective-permute-start.57 = (bf16[48,2048]{1,0:T(8,128)(2,1)S(1)}, bf16[48,2048]{1,0:T(8,128)(2,1)S(1)}, u32[]{:S(2)}, u32[]{:S(2)}) collective-permute-start(bf16[48,2048]{1,0:T(8,128)(2,1)S(1)} %get-tuple-element.60.refs_0_), channel_id=1, source_target_pairs={{0,2},{1,3},{4,0},{5,1},{8,4},{9,5},{12,8},{13,9},{14,12},{15,13},... | collective-permute-start | bytes 589832 | tf_op jit(solution)/shard_map/ppermute | solution.py:308
  50.5 7.8 %collective-permute-start.56 = (bf16[48,2048]{1,0:T(8,128)(2,1)S(1)}, bf16[48,2048]{1,0:T(8,128)(2,1)S(1)}, u32[]{:S(2)}, u32[]{:S(2)}) collective-permute-start(bf16[48,2048]{1,0:T(8,128)(2,1)S(1)} %get-tuple-element.60.refs_0_), channel_id=1, source_target_pairs={{0,4},{1,5},{4,8},{5,9},{8,12},{9,13},{12,14},{13,15},{14,10},{15,... | collective-permute-start | bytes 589832 | tf_op jit(solution)/shard_map/ppermute | solution.py:308
  51.1 10.2 %collective-permute-start.27 = (bf16[48,2176]{1,0:T(8,128)(2,1)S(1)}, bf16[48,2176]{1,0:T(8,128)(2,1)S(1)}, u32[]{:S(2)}, u32[]{:S(2)}) collective-permute-start(bf16[48,2176]{1,0:T(8,128)(2,1)S(1)} %get-tuple-element.49.refs_0_.refs_2_), channel_id=1, source_target_pairs={{0,2},{1,3},{4,0},{5,1},{8,4},{9,5},{12,8},{13,9},{14,12},{15,13},... | collective-permute-start | bytes 626696 | tf_op jit(solution)/shard_map/ppermute | solution.py:308
  52.6 10.2 %collective-permute-start.26 = (bf16[48,2176]{1,0:T(8,128)(2,1)S(1)}, bf16[48,2176]{1,0:T(8,128)(2,1)S(1)}, u32[]{:S(2)}, u32[]{:S(2)}) collective-permute-start(bf16[48,2176]{1,0:T(8,128)(2,1)S(1)} %get-tuple-element.49.refs_0_.refs_2_), channel_id=1, source_target_pairs={{0,4},{1,5},{4,8},{5,9},{8,12},{9,13},{12,14},{13,15},{14,10},{15,... | collective-permute-start | bytes 626696 | tf_op jit(solution)/shard_map/ppermute | solution.py:308
  56.8 8.7 %collective-permute-start.62 = (bf16[48,2048]{1,0:T(8,128)(2,1)S(1)}, bf16[48,2048]{1,0:T(8,128)(2,1)S(1)}, u32[]{:S(2)}, u32[]{:S(2)}) collective-permute-start(bf16[48,2048]{1,0:T(8,128)(2,1)S(1)} %collective-permute-done.57.refs_1_), channel_id=1, source_target_pairs={{0,2},{1,3},{4,0},{5,1},{8,4},{9,5},{12,8},{13,9},{14,12},{15,13},... | collective-permute-start | bytes 589832 | tf_op jit(solution)/shard_map/ppermute | solution.py:308
  58.3 8.7 %collective-permute-start.61 = (bf16[48,2048]{1,0:T(8,128)(2,1)S(1)}, bf16[48,2048]{1,0:T(8,128)(2,1)S(1)}, u32[]{:S(2)}, u32[]{:S(2)}) collective-permute-start(bf16[48,2048]{1,0:T(8,128)(2,1)S(1)} %collective-permute-done.56.refs_0_), channel_id=1, source_target_pairs={{0,4},{1,5},{4,8},{5,9},{8,12},{9,13},{12,14},{13,15},{14,10},{15,... | collective-permute-start | bytes 589832 | tf_op jit(solution)/shard_map/ppermute | solution.py:308
  61.3 8.7 %collective-permute-start.32 = (bf16[48,2176]{1,0:T(8,128)(2,1)S(1)}, bf16[48,2176]{1,0:T(8,128)(2,1)S(1)}, u32[]{:S(2)}, u32[]{:S(2)}) collective-permute-start(bf16[48,2176]{1,0:T(8,128)(2,1)S(1)} %collective-permute-done.27.refs_1_.refs_5_), channel_id=1, source_target_pairs={{0,2},{1,3},{4,0},{5,1},{8,4},{9,5},{12,8},{13,9},{14,12},{15,13},... | collective-permute-start | bytes 626696 | tf_op jit(solution)/shard_map/ppermute | solution.py:308
  62.8 8.7 %collective-permute-start.31 = (bf16[48,2176]{1,0:T(8,128)(2,1)S(1)}, bf16[48,2176]{1,0:T(8,128)(2,1)S(1)}, u32[]{:S(2)}, u32[]{:S(2)}) collective-permute-start(bf16[48,2176]{1,0:T(8,128)(2,1)S(1)} %collective-permute-done.26.refs_0_.refs_4_), channel_id=1, source_target_pairs={{0,4},{1,5},{4,8},{5,9},{8,12},{9,13},{12,14},{13,15},{14,10},{15,... | collective-permute-start | bytes 626696 | tf_op jit(solution)/shard_map/ppermute | solution.py:308
  65.5 8.7 %collective-permute-start.67 = (bf16[48,2048]{1,0:T(8,128)(2,1)S(1)}, bf16[48,2048]{1,0:T(8,128)(2,1)S(1)}, u32[]{:S(2)}, u32[]{:S(2)}) collective-permute-start(bf16[48,2048]{1,0:T(8,128)(2,1)S(1)} %collective-permute-done.62.refs_1_), channel_id=1, source_target_pairs={{0,2},{1,3},{4,0},{5,1},{8,4},{9,5},{12,8},{13,9},{14,12},{15,13},... | collective-permute-start | bytes 589832 | tf_op jit(solution)/shard_map/ppermute | solution.py:308
  67.0 8.7 %collective-permute-start.66 = (bf16[48,2048]{1,0:T(8,128)(2,1)S(1)}, bf16[48,2048]{1,0:T(8,128)(2,1)S(1)}, u32[]{:S(2)}, u32[]{:S(2)}) collective-permute-start(bf16[48,2048]{1,0:T(8,128)(2,1)S(1)} %collective-permute-done.61.refs_0_), channel_id=1, source_target_pairs={{0,4},{1,5},{4,8},{5,9},{8,12},{9,13},{12,14},{13,15},{14,10},{15,... | collective-permute-start | bytes 589832 | tf_op jit(solution)/shard_map/ppermute | solution.py:308
  70.0 7.3 %collective-permute-start.37 = (bf16[48,2176]{1,0:T(8,128)(2,1)S(1)}, bf16[48,2176]{1,0:T(8,128)(2,1)S(1)}, u32[]{:S(2)}, u32[]{:S(2)}) collective-permute-start(bf16[48,2176]{1,0:T(8,128)(2,1)S(1)} %collective-permute-done.32.refs_1_.refs_5_), channel_id=1, source_target_pairs={{0,2},{1,3},{4,0},{5,1},{8,4},{9,5},{12,8},{13,9},{14,12},{15,13},... | collective-permute-start | bytes 626696 | tf_op jit(solution)/shard_map/ppermute | solution.py:308
  71.5 7.1 %collective-permute-start.36 = (bf16[48,2176]{1,0:T(8,128)(2,1)S(1)}, bf16[48,2176]{1,0:T(8,128)(2,1)S(1)}, u32[]{:S(2)}, u32[]{:S(2)}) collective-permute-start(bf16[48,2176]{1,0:T(8,128)(2,1)S(1)} %collective-permute-done.31.refs_0_.refs_4_), channel_id=1, source_target_pairs={{0,4},{1,5},{4,8},{5,9},{8,12},{9,13},{12,14},{13,15},{14,10},{15,... | collective-permute-start | bytes 626696 | tf_op jit(solution)/shard_map/ppermute | solution.py:308
  72.0 7.8 %collective-permute-start.54 = (bf16[48,2048]{1,0:T(8,128)(2,1)S(1)}, bf16[48,2048]{1,0:T(8,128)(2,1)S(1)}, u32[]{:S(2)}, u32[]{:S(2)}) collective-permute-start(bf16[48,2048]{1,0:T(8,128)(2,1)S(1)} %get-tuple-element.60.refs_0_), channel_id=1, source_target_pairs={{0,1},{1,0},{2,3},{3,2},{4,5},{5,4},{6,7},{7,6},{8,9},{9,8},{10,11... | collective-permute-start | bytes 589832 | tf_op jit(solution)/shard_map/ppermute | solution.py:371
  74.2 7.1 %collective-permute-start.59 = (bf16[48,2048]{1,0:T(8,128)(2,1)S(1)}, bf16[48,2048]{1,0:T(8,128)(2,1)S(1)}, u32[]{:S(2)}, u32[]{:S(2)}) collective-permute-start(bf16[48,2048]{1,0:T(8,128)(2,1)S(1)} %collective-permute-done.57.refs_1_), channel_id=1, source_target_pairs={{0,1},{1,0},{2,3},{3,2},{4,5},{5,4},{6,7},{7,6},{8,9},{9,8},{10,11... | collective-permute-start | bytes 589832 | tf_op jit(solution)/shard_map/ppermute | solution.py:371
  75.7 5.5 %collective-permute-start.72 = (bf16[24,2048]{1,0:T(8,128)(2,1)S(1)}, bf16[24,2048]{1,0:T(8,128)(2,1)S(1)}, u32[]{:S(2)}, u32[]{:S(2)}) collective-permute-start(bf16[24,2048]{1,0:T(8,128)(2,1)S(1)} %slice.56), channel_id=1, source_target_pairs={{0,2},{1,3},{4,0},{5,1},{8,4},{9,5},{12,8},{13,9},{14,12},{15,13},... | collective-permute-start | bytes 294920 | tf_op jit(solution)/shard_map/ppermute | solution.py:308
  77.3 5.4 %collective-permute-start.71 = (bf16[24,2048]{1,0:T(8,128)(2,1)S(1)}, bf16[24,2048]{1,0:T(8,128)(2,1)S(1)}, u32[]{:S(2)}, u32[]{:S(2)}) collective-permute-start(bf16[24,2048]{1,0:T(8,128)(2,1)S(1)} %slice.55), channel_id=1, source_target_pairs={{0,4},{1,5},{4,8},{5,9},{8,12},{9,13},{12,14},{13,15},{14,10},{15,... | collective-permute-start | bytes 294920 | tf_op jit(solution)/shard_map/ppermute | solution.py:308
  81.2 7.5 %collective-permute-start.39 = (bf16[48,2176]{1,0:T(8,128)(2,1)S(1)}, bf16[48,2176]{1,0:T(8,128)(2,1)S(1)}, u32[]{:S(2)}, u32[]{:S(2)}) collective-permute-start(bf16[48,2176]{1,0:T(8,128)(2,1)S(1)} %collective-permute-done.37.refs_1_.refs_5_), channel_id=1, source_target_pairs={{0,1},{1,0},{2,3},{3,2},{4,5},{5,4},{6,7},{7,6},{8,9},{9,8},{10,11... | collective-permute-start | bytes 626696 | tf_op jit(solution)/shard_map/ppermute | solution.py:371
  82.7 6.3 %collective-permute-start.38 = (bf16[48,2176]{1,0:T(8,128)(2,1)S(1)}, bf16[48,2176]{1,0:T(8,128)(2,1)S(1)}, u32[]{:S(2)}, u32[]{:S(2)}) collective-permute-start(bf16[48,2176]{1,0:T(8,128)(2,1)S(1)} %collective-permute-done.36.refs_0_.refs_4_), channel_id=1, source_target_pairs={{0,1},{1,0},{2,3},{3,2},{4,5},{5,4},{6,7},{7,6},{8,9},{9,8},{10,11... | collective-permute-start | bytes 626696 | tf_op jit(solution)/shard_map/ppermute | solution.py:371
  86.7 5.3 %collective-permute-start.69 = (bf16[48,2048]{1,0:T(8,128)(2,1)S(1)}, bf16[48,2048]{1,0:T(8,128)(2,1)S(1)}, u32[]{:S(2)}, u32[]{:S(2)}) collective-permute-start(bf16[48,2048]{1,0:T(8,128)(2,1)S(1)} %collective-permute-done.67.refs_1_), channel_id=1, source_target_pairs={{0,1},{1,0},{2,3},{3,2},{4,5},{5,4},{6,7},{7,6},{8,9},{9,8},{10,11... | collective-permute-start | bytes 589832 | tf_op jit(solution)/shard_map/ppermute | solution.py:371
  89.0 5.4 %collective-permute-start.75 = (bf16[48,2048]{1,0:T(8,128)(2,1)S(1)}, bf16[48,2048]{1,0:T(8,128)(2,1)S(1)}, u32[]{:S(2)}, u32[]{:S(2)}) collective-permute-start(bf16[48,2048]{1,0:T(8,128)(2,1)S(1)} %get-tuple-element.70), channel_id=1, source_target_pairs={{0,1},{1,0},{2,3},{3,2},{4,5},{5,4},{6,7},{7,6},{8,9},{9,8},{10,11... | collective-permute-start | bytes 589832 | tf_op jit(solution)/shard_map/ppermute | solution.py:374
  91.7 5.4 %collective-permute-start.34 = (bf16[48,2176]{1,0:T(8,128)(2,1)S(1)}, bf16[48,2176]{1,0:T(8,128)(2,1)S(1)}, u32[]{:S(2)}, u32[]{:S(2)}) collective-permute-start(bf16[48,2176]{1,0:T(8,128)(2,1)S(1)} %collective-permute-done.32.refs_1_.refs_5_), channel_id=1, source_target_pairs={{0,1},{1,0},{2,3},{3,2},{4,5},{5,4},{6,7},{7,6},{8,9},{9,8},{10,11... | collective-permute-start | bytes 626696 | tf_op jit(solution)/shard_map/ppermute | solution.py:371
  93.9 6.4 %collective-permute-start.29 = (bf16[48,2176]{1,0:T(8,128)(2,1)S(1)}, bf16[48,2176]{1,0:T(8,128)(2,1)S(1)}, u32[]{:S(2)}, u32[]{:S(2)}) collective-permute-start(bf16[48,2176]{1,0:T(8,128)(2,1)S(1)} %collective-permute-done.27.refs_1_.refs_5_), channel_id=1, source_target_pairs={{0,1},{1,0},{2,3},{3,2},{4,5},{5,4},{6,7},{7,6},{8,9},{9,8},{10,11... | collective-permute-start | bytes 626696 | tf_op jit(solution)/shard_map/ppermute | solution.py:371
  94.3 6.1 %collective-permute-start.45 = (bf16[48,2048]{1,0:T(8,128)(2,1)S(1)}, bf16[48,2048]{1,0:T(8,128)(2,1)S(1)}, u32[]{:S(2)}, u32[]{:S(2)}) collective-permute-start(bf16[48,2048]{1,0:T(8,128)(2,1)S(1)} %get-tuple-element.59), channel_id=1, source_target_pairs={{0,1},{1,0},{2,3},{3,2},{4,5},{5,4},{6,7},{7,6},{8,9},{9,8},{10,11... | collective-permute-start | bytes 589832 | tf_op jit(solution)/shard_map/ppermute | solution.py:374
  96.6 10.3 %collective-permute-start.70 = (bf16[96,2048]{1,0:T(8,128)(2,1)S(1)}, bf16[96,2048]{1,0:T(8,128)(2,1)S(1)}, u32[]{:S(2)}, u32[]{:S(2)}) collective-permute-start(bf16[96,2048]{1,0:T(8,128)(2,1)S(1)} %get-tuple-element.68), channel_id=1, source_target_pairs={{0,1},{1,0},{2,3},{3,2},{4,5},{5,4},{6,7},{7,6},{8,9},{9,8},{10,11... | collective-permute-start | bytes 1179656 | tf_op jit(solution)/shard_map/ppermute | solution.py:374
  97.1 17.2 %collective-permute-start.40 = (bf16[96,2048]{1,0:T(8,128)(2,1)S(1)}, bf16[96,2048]{1,0:T(8,128)(2,1)S(1)}, u32[]{:S(2)}, u32[]{:S(2)}) collective-permute-start(bf16[96,2048]{1,0:T(8,128)(2,1)S(1)} %get-tuple-element.57), channel_id=1, source_target_pairs={{0,1},{1,0},{2,3},{3,2},{4,5},{5,4},{6,7},{7,6},{8,9},{9,8},{10,11... | collective-permute-start | bytes 1179656 | tf_op jit(solution)/shard_map/ppermute | solution.py:374
  100.3 7.8 %collective-permute-start.28 = (bf16[48,2176]{1,0:T(8,128)(2,1)S(1)}, bf16[48,2176]{1,0:T(8,128)(2,1)S(1)}, u32[]{:S(2)}, u32[]{:S(2)}) collective-permute-start(bf16[48,2176]{1,0:T(8,128)(2,1)S(1)} %collective-permute-done.26.refs_0_.refs_4_), channel_id=1, source_target_pairs={{0,1},{1,0},{2,3},{3,2},{4,5},{5,4},{6,7},{7,6},{8,9},{9,8},{10,11... | collective-permute-start | bytes 626696 | tf_op jit(solution)/shard_map/ppermute | solution.py:371
  100.4 17.6 %collective-permute-start.65 = (bf16[96,2048]{1,0:T(8,128)(2,1)S(1)}, bf16[96,2048]{1,0:T(8,128)(2,1)S(1)}, u32[]{:S(2)}, u32[]{:S(2)}) collective-permute-start(bf16[96,2048]{1,0:T(8,128)(2,1)S(1)} %get-tuple-element.66), channel_id=1, source_target_pairs={{0,1},{1,0},{2,3},{3,2},{4,5},{5,4},{6,7},{7,6},{8,9},{9,8},{10,11... | collective-permute-start | bytes 1179656 | tf_op jit(solution)/shard_map/ppermute | solution.py:374
  106.9 12.4 %collective-permute-start.35 = (bf16[96,2048]{1,0:T(8,128)(2,1)S(1)}, bf16[96,2048]{1,0:T(8,128)(2,1)S(1)}, u32[]{:S(2)}, u32[]{:S(2)}) collective-permute-start(bf16[96,2048]{1,0:T(8,128)(2,1)S(1)} %get-tuple-element.55), channel_id=1, source_target_pairs={{0,1},{1,0},{2,3},{3,2},{4,5},{5,4},{6,7},{7,6},{8,9},{9,8},{10,11... | collective-permute-start | bytes 1179656 | tf_op jit(solution)/shard_map/ppermute | solution.py:374
  107.0 5.7 %collective-permute-start.46 = (bf16[24,2048]{1,0:T(8,128)(2,1)S(1)}, bf16[24,2048]{1,0:T(8,128)(2,1)S(1)}, u32[]{:S(2)}, u32[]{:S(2)}) collective-permute-start(bf16[24,2048]{1,0:T(8,128)(2,1)S(1)} %shard_map.105), channel_id=1, source_target_pairs={{0,4},{1,5},{4,8},{5,9},{8,12},{9,13},{12,14},{13,15},{14,10},{15,... | collective-permute-start | bytes 294920 | tf_op jit(solution)/shard_map/ppermute | solution.py:308
  108.1 11.3 %collective-permute-start.77 = (bf16[48,2048]{1,0:T(8,128)(2,1)S(1)}, bf16[48,2048]{1,0:T(8,128)(2,1)S(1)}, u32[]{:S(2)}, u32[]{:S(2)}) collective-permute-start(bf16[48,2048]{1,0:T(8,128)(2,1)S(1)} %shard_map.119), channel_id=1, source_target_pairs={{0,4},{1,5},{4,8},{5,9},{8,12},{9,13},{12,14},{13,15},{14,10},{15,... | collective-permute-start | bytes 589832 | tf_op jit(solution)/shard_map/ppermute | solution.py:308
  112.7 5.7 %collective-permute-start.50 = (bf16[24,2048]{1,0:T(8,128)(2,1)S(1)}, bf16[24,2048]{1,0:T(8,128)(2,1)S(1)}, u32[]{:S(2)}, u32[]{:S(2)}) collective-permute-start(bf16[24,2048]{1,0:T(8,128)(2,1)S(1)} %shard_map.109), channel_id=1, source_target_pairs={{0,2},{1,3},{4,0},{5,1},{8,4},{9,5},{12,8},{13,9},{14,12},{15,13},... | collective-permute-start | bytes 294920 | tf_op jit(solution)/shard_map/ppermute | solution.py:308
  114.2 8.4 %collective-permute-start.81 = (bf16[48,2048]{1,0:T(8,128)(2,1)S(1)}, bf16[48,2048]{1,0:T(8,128)(2,1)S(1)}, u32[]{:S(2)}, u32[]{:S(2)}) collective-permute-start(bf16[48,2048]{1,0:T(8,128)(2,1)S(1)} %shard_map.123), channel_id=1, source_target_pairs={{0,2},{1,3},{4,0},{5,1},{8,4},{9,5},{12,8},{13,9},{14,12},{15,13},... | collective-permute-start | bytes 589832 | tf_op jit(solution)/shard_map/ppermute | solution.py:308
  118.0 12.0 %collective-permute-start.60 = (bf16[96,2048]{1,0:T(8,128)(2,1)S(1)}, bf16[96,2048]{1,0:T(8,128)(2,1)S(1)}, u32[]{:S(2)}, u32[]{:S(2)}) collective-permute-start(bf16[96,2048]{1,0:T(8,128)(2,1)S(1)} %get-tuple-element.64), channel_id=1, source_target_pairs={{0,1},{1,0},{2,3},{3,2},{4,5},{5,4},{6,7},{7,6},{8,9},{9,8},{10,11... | collective-permute-start | bytes 1179656 | tf_op jit(solution)/shard_map/ppermute | solution.py:374
  118.3 7.1 %collective-permute-start.47 = (bf16[48,2048]{1,0:T(8,128)(2,1)S(1)}, bf16[48,2048]{1,0:T(8,128)(2,1)S(1)}, u32[]{:S(2)}, u32[]{:S(2)}) collective-permute-start(bf16[48,2048]{1,0:T(8,128)(2,1)S(1)} %shard_map.106), channel_id=1, source_target_pairs={{0,4},{1,5},{4,8},{5,9},{8,12},{9,13},{12,14},{13,15},{14,10},{15,... | collective-permute-start | bytes 589832 | tf_op jit(solution)/shard_map/ppermute | solution.py:308
  119.3 6.7 %collective-permute-start.24 = (bf16[48,2176]{1,0:T(8,128)(2,1)S(1)}, bf16[48,2176]{1,0:T(8,128)(2,1)S(1)}, u32[]{:S(2)}, u32[]{:S(2)}) collective-permute-start(bf16[48,2176]{1,0:T(8,128)(2,1)S(1)} %get-tuple-element.49.refs_0_.refs_2_), channel_id=1, source_target_pairs={{0,1},{1,0},{2,3},{3,2},{4,5},{5,4},{6,7},{7,6},{8,9},{9,8},{10,11... | collective-permute-start | bytes 626696 | tf_op jit(solution)/shard_map/ppermute | solution.py:371
  119.4 8.3 %collective-permute-start.51 = (bf16[48,2048]{1,0:T(8,128)(2,1)S(1)}, bf16[48,2048]{1,0:T(8,128)(2,1)S(1)}, u32[]{:S(2)}, u32[]{:S(2)}) collective-permute-start(bf16[48,2048]{1,0:T(8,128)(2,1)S(1)} %shard_map.110), channel_id=1, source_target_pairs={{0,2},{1,3},{4,0},{5,1},{8,4},{9,5},{12,8},{13,9},{14,12},{15,13},... | collective-permute-start | bytes 589832 | tf_op jit(solution)/shard_map/ppermute | solution.py:308
  122.7 12.9 %collective-permute-start.30 = (bf16[96,2048]{1,0:T(8,128)(2,1)S(1)}, bf16[96,2048]{1,0:T(8,128)(2,1)S(1)}, u32[]{:S(2)}, u32[]{:S(2)}) collective-permute-start(bf16[96,2048]{1,0:T(8,128)(2,1)S(1)} %get-tuple-element.53), channel_id=1, source_target_pairs={{0,1},{1,0},{2,3},{3,2},{4,5},{5,4},{6,7},{7,6},{8,9},{9,8},{10,11... | collective-permute-start | bytes 1179656 | tf_op jit(solution)/shard_map/ppermute | solution.py:374
  125.4 7.8 %collective-permute-start.78 = (bf16[48,2048]{1,0:T(8,128)(2,1)S(1)}, bf16[48,2048]{1,0:T(8,128)(2,1)S(1)}, u32[]{:S(2)}, u32[]{:S(2)}) collective-permute-start(bf16[48,2048]{1,0:T(8,128)(2,1)S(1)} %shard_map.120), channel_id=1, source_target_pairs={{0,4},{1,5},{4,8},{5,9},{8,12},{9,13},{12,14},{13,15},{14,10},{15,... | collective-permute-start | bytes 589832 | tf_op jit(solution)/shard_map/ppermute | solution.py:308
  126.0 8.9 %collective-permute-start.82 = (bf16[48,2048]{1,0:T(8,128)(2,1)S(1)}, bf16[48,2048]{1,0:T(8,128)(2,1)S(1)}, u32[]{:S(2)}, u32[]{:S(2)}) collective-permute-start(bf16[48,2048]{1,0:T(8,128)(2,1)S(1)} %shard_map.124), channel_id=1, source_target_pairs={{0,2},{1,3},{4,0},{5,1},{8,4},{9,5},{12,8},{13,9},{14,12},{15,13},... | collective-permute-start | bytes 589832 | tf_op jit(solution)/shard_map/ppermute | solution.py:308
  127.6 8.2 %collective-permute-start.48 = (bf16[48,2048]{1,0:T(8,128)(2,1)S(1)}, bf16[48,2048]{1,0:T(8,128)(2,1)S(1)}, u32[]{:S(2)}, u32[]{:S(2)}) collective-permute-start(bf16[48,2048]{1,0:T(8,128)(2,1)S(1)} %shard_map.107), channel_id=1, source_target_pairs={{0,4},{1,5},{4,8},{5,9},{8,12},{9,13},{12,14},{13,15},{14,10},{15,... | collective-permute-start | bytes 589832 | tf_op jit(solution)/shard_map/ppermute | solution.py:308
  130.0 7.7 %collective-permute-start.52 = (bf16[48,2048]{1,0:T(8,128)(2,1)S(1)}, bf16[48,2048]{1,0:T(8,128)(2,1)S(1)}, u32[]{:S(2)}, u32[]{:S(2)}) collective-permute-start(bf16[48,2048]{1,0:T(8,128)(2,1)S(1)} %shard_map.111), channel_id=1, source_target_pairs={{0,2},{1,3},{4,0},{5,1},{8,4},{9,5},{12,8},{13,9},{14,12},{15,13},... | collective-permute-start | bytes 589832 | tf_op jit(solution)/shard_map/ppermute | solution.py:308
  135.6 7.8 %collective-permute-start.79 = (bf16[48,2048]{1,0:T(8,128)(2,1)S(1)}, bf16[48,2048]{1,0:T(8,128)(2,1)S(1)}, u32[]{:S(2)}, u32[]{:S(2)}) collective-permute-start(bf16[48,2048]{1,0:T(8,128)(2,1)S(1)} %shard_map.121), channel_id=1, source_target_pairs={{0,4},{1,5},{4,8},{5,9},{8,12},{9,13},{12,14},{13,15},{14,10},{15,... | collective-permute-start | bytes 589832 | tf_op jit(solution)/shard_map/ppermute | solution.py:308
  135.8 7.8 %collective-permute-start.83 = (bf16[48,2048]{1,0:T(8,128)(2,1)S(1)}, bf16[48,2048]{1,0:T(8,128)(2,1)S(1)}, u32[]{:S(2)}, u32[]{:S(2)}) collective-permute-start(bf16[48,2048]{1,0:T(8,128)(2,1)S(1)} %shard_map.125), channel_id=1, source_target_pairs={{0,2},{1,3},{4,0},{5,1},{8,4},{9,5},{12,8},{13,9},{14,12},{15,13},... | collective-permute-start | bytes 589832 | tf_op jit(solution)/shard_map/ppermute | solution.py:308
  137.8 8.9 %collective-permute-start.49 = (bf16[48,2048]{1,0:T(8,128)(2,1)S(1)}, bf16[48,2048]{1,0:T(8,128)(2,1)S(1)}, u32[]{:S(2)}, u32[]{:S(2)}) collective-permute-start(bf16[48,2048]{1,0:T(8,128)(2,1)S(1)} %shard_map.108), channel_id=1, source_target_pairs={{0,4},{1,5},{4,8},{5,9},{8,12},{9,13},{12,14},{13,15},{14,10},{15,... | collective-permute-start | bytes 589832 | tf_op jit(solution)/shard_map/ppermute | solution.py:308
  138.1 8.7 %collective-permute-start.53 = (bf16[48,2048]{1,0:T(8,128)(2,1)S(1)}, bf16[48,2048]{1,0:T(8,128)(2,1)S(1)}, u32[]{:S(2)}, u32[]{:S(2)}) collective-permute-start(bf16[48,2048]{1,0:T(8,128)(2,1)S(1)} %shard_map.112), channel_id=1, source_target_pairs={{0,2},{1,3},{4,0},{5,1},{8,4},{9,5},{12,8},{13,9},{14,12},{15,13},... | collective-permute-start | bytes 589832 | tf_op jit(solution)/shard_map/ppermute | solution.py:308
  (28 other events, 271.1 us)

commit v4 on v3

--- a/solution.py
+++ b/solution.py
@@ -138,12 +138,12 @@
         share.append(chosen / whole)
         start += size
     share = jnp.concatenate(share, axis=0)
-    tile = tile_of(wide, 256)
+    tile = tile_of(wide, 384)
     for at in range(0, wide, tile):
         x = x_ref[...]
         gate = jnp.dot(x, gate_ref[:, at : at + tile], preferred_element_type=jnp.float32)
         up = jnp.dot(x, up_ref[:, at : at + tile], preferred_element_type=jnp.float32)
-        h_ref[:, at : at + tile] = (gate * (1.0 / (1.0 + jnp.exp(-gate))) * up * share).astype(jnp.bfloat16)
+        h_ref[:, at : at + tile] = (gate * lax.logistic(gate) * up * share).astype(jnp.bfloat16)
     half = start // 2
     tile = tile_of(width, 512)
     for at in range(0, width, tile):
@@ -185,13 +185,13 @@
     first_group = lax.axis_index(GROUPS) == 0
     for chip in range(chips):
         x = in_ref[:, chip * 4 * half : (chip + 1) * 4 * half].astype(jnp.float32)
-        act = 0.5 * x * (1.0 + lax.erf(x * np.float32(math.sqrt(0.5))))
+        act = (0.5 * x * (1.0 + lax.erf(x * np.float32(math.sqrt(0.5))))).astype(jnp.bfloat16)
         cuts = [act[:, at * half : (at + 1) * half] for at in range(4)]
         for ref, near, away in ((mine_ref, 0, 2), (given_ref, 2, 0)):
             low = jnp.where(first_core, cuts[near], cuts[away])
             high = jnp.where(first_core, cuts[near + 1], cuts[away + 1])
-            ref[0, chip] = jnp.where(first_group, low, high).astype(jnp.bfloat16)
-            ref[1, chip] = jnp.where(first_group, high, low).astype(jnp.bfloat16)
+            ref[0, chip] = jnp.where(first_group, low, high)
+            ref[1, chip] = jnp.where(first_group, high, low)
 
 
 def rows_of(refs, chip):

time: 148 us -> 149 us (level)
  Pallas kernels: 29.2 us -> 32 us
  waiting for transfers between devices: 50.4 us -> 48.8 us
    pallas_call x36, Pallas kernels: 29.2 us -> 32 us  [kernel(): pl.pallas_call(body, out_shape=outs, in_specs=[VMEM] * len(ins), out_spec...]
    ppermute x48, waiting for transfers between devices: 40.6 us -> 39 us  [hop(): return rings[way](array)]
  transfers between devices with their start and end apart: 84 -> 84, of which waited for: 30 -> 29; matrix products, arithmetic and copies ran while one was open for 1% -> 1% of each run, Pallas kernels for 17% -> 19%
where the time goes in v4:
time: 149 us
  starting transfers between devices  65.6 us (44%)
  waiting for transfers between devices  48.8 us (33%)
  Pallas kernels  32 us (21%)
  local copies, waits for them, and re-layouts  2.24 us (2%)
    ppermute x48, starting transfers between devices, hop(): return rings[way](array)  53.9 us
    ppermute x48, waiting for transfers between devices, hop(): return rings[way](array)  39 us
    pallas_call x36, Pallas kernels, kernel(): pl.pallas_call(body, out_shape=outs, in_specs=[VMEM] * len(ins), out_spec...  32 us
    ppermute x2, waiting for transfers between devices, dense(): theirs = cross(theirs)  8.71 us
    ppermute x18, starting transfers between devices, dense(): ins = [*ins, *(swap(x) for x in ins)]  3.5 us
  transfers between devices with their start and end apart: 84, of which 29 were waited for; matrix products, arithmetic and copies ran while one was open for 1% of the time, Pallas kernels for 19%

profile of v4, /device:TPU:0, one launch (start us, length us, event | category | flops | bytes accessed | tf_op | source)
XLA Modules:
  0.0 149.3 jit_solution(10956094891220238654)
XLA Ops:
  0.0 1.0 copy-done.3
  1.0 3.1 %shard_map.91 = (bf16[2,8,96,72]{3,2,1,0:T(8,128)(2,1)S(1)}, bf16[2,8,96,72]{3,2,1,0:T(8,128)(2,1)S(1)}) custom-call(bf16[96,2304]{1,0:T(8,128)(2,1)S(1)} %copy-done.3), custom_call_target="tpu_custom_call" | custom-call | tf_op jit(solution)/shard_map/pallas_call | solution.py:110
  4.7 1.1 fusion
  5.8 2.6 %collective-permute-start.14 = (bf16[72,1024]{1,0:T(8,128)(2,1)S(1)}, bf16[72,1024]{1,0:T(8,128)(2,1)S(1)}, u32[]{:S(2)}, u32[]{:S(2)}) collective-permute-start(bf16[72,1024]{1,0:T(8,128)(2,1)S(1)} %get-tuple-element.71.refs_3_), channel_id=1, source_target_pairs={{0,2},{1,3},{4,0},{5,1},{8,4},{9,5},{12,8},{13,9},{14,12},{15,13},... | collective-permute-start | bytes 442376 | tf_op jit(solution)/shard_map/ppermute | solution.py:308
  8.5 1.9 %collective-permute-start.3 = (bf16[72,1024]{1,0:T(8,128)(2,1)S(1)}, bf16[72,1024]{1,0:T(8,128)(2,1)S(1)}, u32[]{:S(2)}, u32[]{:S(2)}) collective-permute-start(bf16[72,1024]{1,0:T(8,128)(2,1)S(1)} %get-tuple-element.72.refs_3_), channel_id=1, source_target_pairs={{0,2},{1,3},{4,0},{5,1},{8,4},{9,5},{12,8},{13,9},{14,12},{15,13},... | collective-permute-start | bytes 442376 | tf_op jit(solution)/shard_map/ppermute | solution.py:308
  10.5 2.6 %collective-permute-done.14.refs_5_ = bf16[72,1024]{1,0:T(8,128)(2,1)S(1)} collective-permute-done((bf16[72,1024]{1,0:T(8,128)(2,1)S(1)}, bf16[72,1024]{1,0:T(8,128)(2,1)S(1)}, u32[]{:S(2)}, u32[]{:S(2)}) %collective-permute-start.14) | collective-permute-done | bytes 147488 | tf_op jit(solution)/shard_map/ppermute | solution.py:308
  13.1 1.9 %collective-permute-start.16 = (bf16[72,1024]{1,0:T(8,128)(2,1)S(1)}, bf16[72,1024]{1,0:T(8,128)(2,1)S(1)}, u32[]{:S(2)}, u32[]{:S(2)}) collective-permute-start(bf16[72,1024]{1,0:T(8,128)(2,1)S(1)} %collective-permute-done.14.refs_5_), channel_id=1, source_target_pairs={{0,2},{1,3},{4,0},{5,1},{8,4},{9,5},{12,8},{13,9},{14,12},{15,13},... | collective-permute-start | bytes 442376 | tf_op jit(solution)/shard_map/ppermute | solution.py:308
  15.2 1.1 collective-permute-done.3.refs_5_
  16.3 1.9 %collective-permute-start.5 = (bf16[72,1024]{1,0:T(8,128)(2,1)S(1)}, bf16[72,1024]{1,0:T(8,128)(2,1)S(1)}, u32[]{:S(2)}, u32[]{:S(2)}) collective-permute-start(bf16[72,1024]{1,0:T(8,128)(2,1)S(1)} %collective-permute-done.3.refs_5_), channel_id=1, source_target_pairs={{0,2},{1,3},{4,0},{5,1},{8,4},{9,5},{12,8},{13,9},{14,12},{15,13},... | collective-permute-start | bytes 442376 | tf_op jit(solution)/shard_map/ppermute | solution.py:308
  18.5 2.0 %collective-permute-start.1 = (bf16[2,8,96,72]{3,2,1,0:T(8,128)(2,1)S(1)}, bf16[2,8,96,72]{3,2,1,0:T(8,128)(2,1)S(1)}, u32[]{:S(2)}, u32[]{:S(2)}) collective-permute-start(bf16[2,8,96,72]{3,2,1,0:T(8,128)(2,1)S(1)} %pad_maximum_fusion), channel_id=1, source_target_pairs={{0,16},{16,0},{1,17},{17,1},{2,18},{18,2},{3,19},{19,3},{4,20},{20... | collective-permute-start | bytes 663560 | tf_op jit(solution)/shard_map/ppermute | solution.py:316
  20.4 1.5 collective-permute-start.18
  23.0 1.9 %collective-permute-start.7 = (bf16[72,1024]{1,0:T(8,128)(2,1)S(1)}, bf16[72,1024]{1,0:T(8,128)(2,1)S(1)}, u32[]{:S(2)}, u32[]{:S(2)}) collective-permute-start(bf16[72,1024]{1,0:T(8,128)(2,1)S(1)} %collective-permute-done.5.refs_7_), channel_id=1, source_target_pairs={{0,2},{1,3},{4,0},{5,1},{8,4},{9,5},{12,8},{13,9},{14,12},{15,13},... | collective-permute-start | bytes 442376 | tf_op jit(solution)/shard_map/ppermute | solution.py:308
  25.1 1.6 %collective-permute-done.18.refs_9_ = bf16[72,1024]{1,0:T(8,128)(2,1)S(1)} collective-permute-done((bf16[72,1024]{1,0:T(8,128)(2,1)S(1)}, bf16[72,1024]{1,0:T(8,128)(2,1)S(1)}, u32[]{:S(2)}, u32[]{:S(2)}) %collective-permute-start.18) | collective-permute-done | bytes 147488 | tf_op jit(solution)/shard_map/ppermute | solution.py:308
  26.7 1.8 %collective-permute-start.20 = (bf16[32,1024]{1,0:T(8,128)(2,1)S(1)}, bf16[32,1024]{1,0:T(8,128)(2,1)S(1)}, u32[]{:S(2)}, u32[]{:S(2)}) collective-permute-start(bf16[32,1024]{1,0:T(8,128)(2,1)S(1)} %slice.52), channel_id=1, source_target_pairs={{0,2},{1,3},{4,0},{5,1},{8,4},{9,5},{12,8},{13,9},{14,12},{15,13},... | collective-permute-start | bytes 196616 | tf_op jit(solution)/shard_map/ppermute | solution.py:308
  29.4 1.6 %collective-permute-start.9 = (bf16[32,1024]{1,0:T(8,128)(2,1)S(1)}, bf16[32,1024]{1,0:T(8,128)(2,1)S(1)}, u32[]{:S(2)}, u32[]{:S(2)}) collective-permute-start(bf16[32,1024]{1,0:T(8,128)(2,1)S(1)} %slice.50), channel_id=1, source_target_pairs={{0,2},{1,3},{4,0},{5,1},{8,4},{9,5},{12,8},{13,9},{14,12},{15,13},... | collective-permute-start | bytes 196616 | tf_op jit(solution)/shard_map/ppermute | solution.py:308
  31.7 1.6 %shard_map.95.total_ref = f32[384,1024]{1,0:T(8,128)S(1)} custom-call(bf16[2,8,96,72]{3,2,1,0:T(8,128)(2,1)S(1)} %get-tuple-element.38.refs_0_.mine_ref, bf16[2,8,96,72]{3,2,1,0:T(8,128)(2,1)S(1)} %collective-permute-done.refs_1_.given_ref, bf16[2,8,96,72]{3,2,1,0:T(8,128)(2,1)S(1)} %collective-permute-done.1.refs_2_.theirs_ref, ...), custom_call_target="tpu_custom_call" | custom-call | flops 452984832 | bytes 1572864 | tf_op jit(solution)/shard_map/pallas_call | solution.py:110
  33.2 1.6 %shard_map.92.total_ref = f32[384,1024]{1,0:T(8,128)S(1)} custom-call(bf16[2,8,96,72]{3,2,1,0:T(8,128)(2,1)S(1)} %get-tuple-element.38.refs_0_.mine_ref, bf16[2,8,96,72]{3,2,1,0:T(8,128)(2,1)S(1)} %collective-permute-done.refs_1_.given_ref, bf16[2,8,96,72]{3,2,1,0:T(8,128)(2,1)S(1)} %collective-permute-done.1.refs_2_.theirs_ref, ...), custom_call_target="tpu_custom_call" | custom-call | flops 452984832 | bytes 1572864 | tf_op jit(solution)/shard_map/pallas_call | solution.py:110
  37.3 1.6 %collective-permute-start.23 = (bf16[96,1024]{1,0:T(8,128)(2,1)S(1)}, bf16[96,1024]{1,0:T(8,128)(2,1)S(1)}, u32[]{:S(2)}, u32[]{:S(2)}) collective-permute-start(bf16[96,1024]{1,0:T(8,128)(2,1)S(1)} %shard_map.97), channel_id=1, source_target_pairs={{0,16},{16,0},{1,17},{17,1},{2,18},{18,2},{3,19},{19,3},{4,20},{20... | collective-permute-start | bytes 589832 | tf_op jit(solution)/shard_map/ppermute | solution.py:349
  39.8 5.3 %collective-permute-done.23.refs_5_ = bf16[96,1024]{1,0:T(8,128)(2,1)S(1)} collective-permute-done((bf16[96,1024]{1,0:T(8,128)(2,1)S(1)}, bf16[96,1024]{1,0:T(8,128)(2,1)S(1)}, u32[]{:S(2)}, u32[]{:S(2)}) %collective-permute-start.23) | collective-permute-done | bytes 196640 | tf_op jit(solution)/shard_map/ppermute | solution.py:349
  45.1 3.4 %collective-permute-done.12.refs_2_ = bf16[96,1024]{1,0:T(8,128)(2,1)S(1)} collective-permute-done((bf16[96,1024]{1,0:T(8,128)(2,1)S(1)}, bf16[96,1024]{1,0:T(8,128)(2,1)S(1)}, u32[]{:S(2)}, u32[]{:S(2)}) %collective-permute-start.12) | collective-permute-done | bytes 196640 | tf_op jit(solution)/shard_map/ppermute | solution.py:349
  48.8 1.6 %collective-permute-start.57 = (bf16[48,2048]{1,0:T(8,128)(2,1)S(1)}, bf16[48,2048]{1,0:T(8,128)(2,1)S(1)}, u32[]{:S(2)}, u32[]{:S(2)}) collective-permute-start(bf16[48,2048]{1,0:T(8,128)(2,1)S(1)} %get-tuple-element.60.refs_0_), channel_id=1, source_target_pairs={{0,2},{1,3},{4,0},{5,1},{8,4},{9,5},{12,8},{13,9},{14,12},{15,13},... | collective-permute-start | bytes 589832 | tf_op jit(solution)/shard_map/ppermute | solution.py:308
  50.9 1.5 %collective-permute-start.27 = (bf16[48,2176]{1,0:T(8,128)(2,1)S(1)}, bf16[48,2176]{1,0:T(8,128)(2,1)S(1)}, u32[]{:S(2)}, u32[]{:S(2)}) collective-permute-start(bf16[48,2176]{1,0:T(8,128)(2,1)S(1)} %get-tuple-element.49.refs_0_.refs_2_), channel_id=1, source_target_pairs={{0,2},{1,3},{4,0},{5,1},{8,4},{9,5},{12,8},{13,9},{14,12},{15,13},... | collective-permute-start | bytes 626696 | tf_op jit(solution)/shard_map/ppermute | solution.py:308
  52.9 3.7 %collective-permute-done.57.refs_1_ = bf16[48,2048]{1,0:T(8,128)(2,1)S(1)} collective-permute-done((bf16[48,2048]{1,0:T(8,128)(2,1)S(1)}, bf16[48,2048]{1,0:T(8,128)(2,1)S(1)}, u32[]{:S(2)}, u32[]{:S(2)}) %collective-permute-start.57) | collective-permute-done | bytes 196640 | tf_op jit(solution)/shard_map/ppermute | solution.py:308
  56.7 1.5 %collective-permute-start.62 = (bf16[48,2048]{1,0:T(8,128)(2,1)S(1)}, bf16[48,2048]{1,0:T(8,128)(2,1)S(1)}, u32[]{:S(2)}, u32[]{:S(2)}) collective-permute-start(bf16[48,2048]{1,0:T(8,128)(2,1)S(1)} %collective-permute-done.57.refs_1_), channel_id=1, source_target_pairs={{0,2},{1,3},{4,0},{5,1},{8,4},{9,5},{12,8},{13,9},{14,12},{15,13},... | collective-permute-start | bytes 589832 | tf_op jit(solution)/shard_map/ppermute | solution.py:308
  58.7 2.4 %collective-permute-done.27.refs_1_.refs_5_ = bf16[48,2176]{1,0:T(8,128)(2,1)S(1)} collective-permute-done((bf16[48,2176]{1,0:T(8,128)(2,1)S(1)}, bf16[48,2176]{1,0:T(8,128)(2,1)S(1)}, u32[]{:S(2)}, u32[]{:S(2)}) %collective-permute-start.27) | collective-permute-done | bytes 208928 | tf_op jit(solution)/shard_map/ppermute | solution.py:308
  61.1 1.5 %collective-permute-start.32 = (bf16[48,2176]{1,0:T(8,128)(2,1)S(1)}, bf16[48,2176]{1,0:T(8,128)(2,1)S(1)}, u32[]{:S(2)}, u32[]{:S(2)}) collective-permute-start(bf16[48,2176]{1,0:T(8,128)(2,1)S(1)} %collective-permute-done.27.refs_1_.refs_5_), channel_id=1, source_target_pairs={{0,2},{1,3},{4,0},{5,1},{8,4},{9,5},{12,8},{13,9},{14,12},{15,13},... | collective-permute-start | bytes 626696 | tf_op jit(solution)/shard_map/ppermute | solution.py:308
  63.2 2.2 %collective-permute-done.62.refs_1_ = bf16[48,2048]{1,0:T(8,128)(2,1)S(1)} collective-permute-done((bf16[48,2048]{1,0:T(8,128)(2,1)S(1)}, bf16[48,2048]{1,0:T(8,128)(2,1)S(1)}, u32[]{:S(2)}, u32[]{:S(2)}) %collective-permute-start.62) | collective-permute-done | bytes 196640 | tf_op jit(solution)/shard_map/ppermute | solution.py:308
  65.3 1.5 %collective-permute-start.67 = (bf16[48,2048]{1,0:T(8,128)(2,1)S(1)}, bf16[48,2048]{1,0:T(8,128)(2,1)S(1)}, u32[]{:S(2)}, u32[]{:S(2)}) collective-permute-start(bf16[48,2048]{1,0:T(8,128)(2,1)S(1)} %collective-permute-done.62.refs_1_), channel_id=1, source_target_pairs={{0,2},{1,3},{4,0},{5,1},{8,4},{9,5},{12,8},{13,9},{14,12},{15,13},... | collective-permute-start | bytes 589832 | tf_op jit(solution)/shard_map/ppermute | solution.py:308
  67.4 2.4 %collective-permute-done.32.refs_1_.refs_5_ = bf16[48,2176]{1,0:T(8,128)(2,1)S(1)} collective-permute-done((bf16[48,2176]{1,0:T(8,128)(2,1)S(1)}, bf16[48,2176]{1,0:T(8,128)(2,1)S(1)}, u32[]{:S(2)}, u32[]{:S(2)}) %collective-permute-start.32) | collective-permute-done | bytes 208928 | tf_op jit(solution)/shard_map/ppermute | solution.py:308
  69.8 1.5 %collective-permute-start.37 = (bf16[48,2176]{1,0:T(8,128)(2,1)S(1)}, bf16[48,2176]{1,0:T(8,128)(2,1)S(1)}, u32[]{:S(2)}, u32[]{:S(2)}) collective-permute-start(bf16[48,2176]{1,0:T(8,128)(2,1)S(1)} %collective-permute-done.32.refs_1_.refs_5_), channel_id=1, source_target_pairs={{0,2},{1,3},{4,0},{5,1},{8,4},{9,5},{12,8},{13,9},{14,12},{15,13},... | collective-permute-start | bytes 626696 | tf_op jit(solution)/shard_map/ppermute | solution.py:308
  71.9 2.2 %collective-permute-done.67.refs_1_ = bf16[48,2048]{1,0:T(8,128)(2,1)S(1)} collective-permute-done((bf16[48,2048]{1,0:T(8,128)(2,1)S(1)}, bf16[48,2048]{1,0:T(8,128)(2,1)S(1)}, u32[]{:S(2)}, u32[]{:S(2)}) %collective-permute-start.67) | collective-permute-done | bytes 196640 | tf_op jit(solution)/shard_map/ppermute | solution.py:308
  74.1 1.5 %collective-permute-done.66.refs_0_ = bf16[48,2048]{1,0:T(8,128)(2,1)S(1)} collective-permute-done((bf16[48,2048]{1,0:T(8,128)(2,1)S(1)}, bf16[48,2048]{1,0:T(8,128)(2,1)S(1)}, u32[]{:S(2)}, u32[]{:S(2)}) %collective-permute-start.66) | collective-permute-done | bytes 196640 | tf_op jit(solution)/shard_map/ppermute | solution.py:308
  75.6 1.6 %collective-permute-start.72 = (bf16[24,2048]{1,0:T(8,128)(2,1)S(1)}, bf16[24,2048]{1,0:T(8,128)(2,1)S(1)}, u32[]{:S(2)}, u32[]{:S(2)}) collective-permute-start(bf16[24,2048]{1,0:T(8,128)(2,1)S(1)} %slice.56), channel_id=1, source_target_pairs={{0,2},{1,3},{4,0},{5,1},{8,4},{9,5},{12,8},{13,9},{14,12},{15,13},... | collective-permute-start | bytes 294920 | tf_op jit(solution)/shard_map/ppermute | solution.py:308
  77.2 1.3 collective-permute-start.71
  78.5 1.2 collective-permute-start.42
  79.7 1.1 collective-permute-start.41
  83.2 1.4 collective-permute-done.41.refs_0_.refs_4_
  86.9 1.8 %shard_map.117 = (bf16[48,2048]{1,0:T(8,128)(2,1)S(1)}, bf16[48,2048]{1,0:T(8,128)(2,1)S(1)}) custom-call(bf16[24,2048]{1,0:T(8,128)(2,1)S(1)} %collective-permute-done.71.refs_0_, bf16[24,2048]{1,0:T(8,128)(2,1)S(1)} %collective-permute-done.72.refs_1_, bf16[24,2048]{1,0:T(8,128)(2,1)S(1)} %collective-permute-done.73.refs_2_, ...), custom_call_target="tpu_custom_call" | custom-call | flops 905969664 | bytes 9437184 | tf_op jit(solution)/shard_map/pallas_call | solution.py:110
  89.3 2.5 %shard_map.103 = (bf16[96,2048]{1,0:T(8,128)(2,1)S(1)}, bf16[96,2048]{1,0:T(8,128)(2,1)S(1)}) custom-call(bf16[48,2176]{1,0:T(8,128)(2,1)S(1)} %collective-permute-done.36.refs_0_.refs_4_, bf16[48,2176]{1,0:T(8,128)(2,1)S(1)} %collective-permute-done.37.refs_1_.refs_5_, bf16[48,2176]{1,0:T(8,128)(2,1)S(1)} %collective-permute-done.38.refs_2_.refs_6_, ...), custom_call_target="tpu_custom_call" | custom-call | flops 1811939328 | bytes 9437184 | tf_op jit(solution)/shard_map/pallas_call | solution.py:110
  92.6 1.8 %shard_map.104 = (bf16[48,2048]{1,0:T(8,128)(2,1)S(1)}, bf16[48,2048]{1,0:T(8,128)(2,1)S(1)}) custom-call(bf16[24,2176]{1,0:T(8,128)(2,1)S(1)} %collective-permute-done.41.refs_0_.refs_4_, bf16[24,2176]{1,0:T(8,128)(2,1)S(1)} %collective-permute-done.42.refs_1_.refs_5_, bf16[24,2176]{1,0:T(8,128)(2,1)S(1)} %collective-permute-done.43.refs_2_.refs_6_, ...), custom_call_target="tpu_custom_call" | custom-call | flops 905969664 | bytes 9437184 | tf_op jit(solution)/shard_map/pallas_call | solution.py:110
  94.9 2.5 %shard_map.116 = (bf16[96,2048]{1,0:T(8,128)(2,1)S(1)}, bf16[96,2048]{1,0:T(8,128)(2,1)S(1)}) custom-call(bf16[48,2048]{1,0:T(8,128)(2,1)S(1)} %collective-permute-done.66.refs_0_, bf16[48,2048]{1,0:T(8,128)(2,1)S(1)} %collective-permute-done.67.refs_1_, bf16[48,2048]{1,0:T(8,128)(2,1)S(1)} %collective-permute-done.68.refs_2_, ...), custom_call_target="tpu_custom_call" | custom-call | flops 1811939328 | bytes 9437184 | tf_op jit(solution)/shard_map/pallas_call | solution.py:110
  99.0 2.5 %shard_map.115 = (bf16[96,2048]{1,0:T(8,128)(2,1)S(1)}, bf16[96,2048]{1,0:T(8,128)(2,1)S(1)}) custom-call(bf16[48,2048]{1,0:T(8,128)(2,1)S(1)} %collective-permute-done.61.refs_0_, bf16[48,2048]{1,0:T(8,128)(2,1)S(1)} %collective-permute-done.62.refs_1_, bf16[48,2048]{1,0:T(8,128)(2,1)S(1)} %collective-permute-done.63.refs_2_, ...), custom_call_target="tpu_custom_call" | custom-call | flops 1811939328 | bytes 9437184 | tf_op jit(solution)/shard_map/pallas_call | solution.py:110
  102.1 1.0 collective-permute-done.76.refs_0_
  103.2 1.6 %collective-permute-start.80 = (bf16[24,2048]{1,0:T(8,128)(2,1)S(1)}, bf16[24,2048]{1,0:T(8,128)(2,1)S(1)}, u32[]{:S(2)}, u32[]{:S(2)}) collective-permute-start(bf16[24,2048]{1,0:T(8,128)(2,1)S(1)} %shard_map.122), channel_id=1, source_target_pairs={{0,2},{1,3},{4,0},{5,1},{8,4},{9,5},{12,8},{13,9},{14,12},{15,13},... | collective-permute-start | bytes 294920 | tf_op jit(solution)/shard_map/ppermute | solution.py:308
  104.7 2.6 %shard_map.102 = (bf16[96,2048]{1,0:T(8,128)(2,1)S(1)}, bf16[96,2048]{1,0:T(8,128)(2,1)S(1)}) custom-call(bf16[48,2176]{1,0:T(8,128)(2,1)S(1)} %collective-permute-done.31.refs_0_.refs_4_, bf16[48,2176]{1,0:T(8,128)(2,1)S(1)} %collective-permute-done.32.refs_1_.refs_5_, bf16[48,2176]{1,0:T(8,128)(2,1)S(1)} %collective-permute-done.33.refs_2_.refs_6_, ...), custom_call_target="tpu_custom_call" | custom-call | flops 1811939328 | bytes 9437184 | tf_op jit(solution)/shard_map/pallas_call | solution.py:110
  107.8 1.0 collective-permute-start.46
  109.0 1.6 %collective-permute-start.77 = (bf16[48,2048]{1,0:T(8,128)(2,1)S(1)}, bf16[48,2048]{1,0:T(8,128)(2,1)S(1)}, u32[]{:S(2)}, u32[]{:S(2)}) collective-permute-start(bf16[48,2048]{1,0:T(8,128)(2,1)S(1)} %shard_map.119), channel_id=1, source_target_pairs={{0,4},{1,5},{4,8},{5,9},{8,12},{9,13},{12,14},{13,15},{14,10},{15,... | collective-permute-start | bytes 589832 | tf_op jit(solution)/shard_map/ppermute | solution.py:308
  110.6 2.9 %collective-permute-done.46.refs_0_ = bf16[24,2048]{1,0:T(8,128)(2,1)S(1)} collective-permute-done((bf16[24,2048]{1,0:T(8,128)(2,1)S(1)}, bf16[24,2048]{1,0:T(8,128)(2,1)S(1)}, u32[]{:S(2)}, u32[]{:S(2)}) %collective-permute-start.46) | collective-permute-done | bytes 98336 | tf_op jit(solution)/shard_map/ppermute | solution.py:308
  113.5 1.6 %collective-permute-start.50 = (bf16[24,2048]{1,0:T(8,128)(2,1)S(1)}, bf16[24,2048]{1,0:T(8,128)(2,1)S(1)}, u32[]{:S(2)}, u32[]{:S(2)}) collective-permute-start(bf16[24,2048]{1,0:T(8,128)(2,1)S(1)} %shard_map.109), channel_id=1, source_target_pairs={{0,2},{1,3},{4,0},{5,1},{8,4},{9,5},{12,8},{13,9},{14,12},{15,13},... | collective-permute-start | bytes 294920 | tf_op jit(solution)/shard_map/ppermute | solution.py:308
  115.1 1.6 %collective-permute-start.81 = (bf16[48,2048]{1,0:T(8,128)(2,1)S(1)}, bf16[48,2048]{1,0:T(8,128)(2,1)S(1)}, u32[]{:S(2)}, u32[]{:S(2)}) collective-permute-start(bf16[48,2048]{1,0:T(8,128)(2,1)S(1)} %shard_map.123), channel_id=1, source_target_pairs={{0,2},{1,3},{4,0},{5,1},{8,4},{9,5},{12,8},{13,9},{14,12},{15,13},... | collective-permute-start | bytes 589832 | tf_op jit(solution)/shard_map/ppermute | solution.py:308
  116.7 2.5 %shard_map.114 = (bf16[96,2048]{1,0:T(8,128)(2,1)S(1)}, bf16[96,2048]{1,0:T(8,128)(2,1)S(1)}) custom-call(bf16[48,2048]{1,0:T(8,128)(2,1)S(1)} %collective-permute-done.56.refs_0_, bf16[48,2048]{1,0:T(8,128)(2,1)S(1)} %collective-permute-done.57.refs_1_, bf16[48,2048]{1,0:T(8,128)(2,1)S(1)} %collective-permute-done.58.refs_2_, ...), custom_call_target="tpu_custom_call" | custom-call | flops 1811939328 | bytes 9437184 | tf_op jit(solution)/shard_map/pallas_call | solution.py:110
  120.3 1.5 collective-permute-start.51
  121.8 2.5 %shard_map.101 = (bf16[96,2048]{1,0:T(8,128)(2,1)S(1)}, bf16[96,2048]{1,0:T(8,128)(2,1)S(1)}) custom-call(bf16[48,2176]{1,0:T(8,128)(2,1)S(1)} %collective-permute-done.26.refs_0_.refs_4_, bf16[48,2176]{1,0:T(8,128)(2,1)S(1)} %collective-permute-done.27.refs_1_.refs_5_, bf16[48,2176]{1,0:T(8,128)(2,1)S(1)} %collective-permute-done.28.refs_2_.refs_6_, ...), custom_call_target="tpu_custom_call" | custom-call | flops 1811939328 | bytes 9437184 | tf_op jit(solution)/shard_map/pallas_call | solution.py:110
  124.5 2.2 %collective-permute-done.47.refs_0_ = bf16[48,2048]{1,0:T(8,128)(2,1)S(1)} collective-permute-done((bf16[48,2048]{1,0:T(8,128)(2,1)S(1)}, bf16[48,2048]{1,0:T(8,128)(2,1)S(1)}, u32[]{:S(2)}, u32[]{:S(2)}) %collective-permute-start.47) | collective-permute-done | bytes 196640 | tf_op jit(solution)/shard_map/ppermute | solution.py:308
  127.3 1.6 %collective-permute-start.82 = (bf16[48,2048]{1,0:T(8,128)(2,1)S(1)}, bf16[48,2048]{1,0:T(8,128)(2,1)S(1)}, u32[]{:S(2)}, u32[]{:S(2)}) collective-permute-start(bf16[48,2048]{1,0:T(8,128)(2,1)S(1)} %shard_map.124), channel_id=1, source_target_pairs={{0,2},{1,3},{4,0},{5,1},{8,4},{9,5},{12,8},{13,9},{14,12},{15,13},... | collective-permute-start | bytes 589832 | tf_op jit(solution)/shard_map/ppermute | solution.py:308
  129.4 1.7 %shard_map.113 = (bf16[48,2048]{1,0:T(8,128)(2,1)S(1)}, bf16[48,2048]{1,0:T(8,128)(2,1)S(1)}) custom-call(bf16[48,2048]{1,0:T(8,128)(2,1)S(1)} %get-tuple-element.60.refs_0_, bf16[48,2048]{1,0:T(8,128)(2,1)S(1)} %collective-permute-done.54.refs_1_, bf16[48,2176]{1,0:T(8,128)(2,1)S(1)} %get-tuple-element.49.refs_0_.refs_2_, ...), custom_call_target="tpu_custom_call" | custom-call | flops 905969664 | bytes 9437184 | tf_op jit(solution)/shard_map/pallas_call | solution.py:110
  131.2 1.9 %collective-permute-start.52 = (bf16[48,2048]{1,0:T(8,128)(2,1)S(1)}, bf16[48,2048]{1,0:T(8,128)(2,1)S(1)}, u32[]{:S(2)}, u32[]{:S(2)}) collective-permute-start(bf16[48,2048]{1,0:T(8,128)(2,1)S(1)} %shard_map.111), channel_id=1, source_target_pairs={{0,2},{1,3},{4,0},{5,1},{8,4},{9,5},{12,8},{13,9},{14,12},{15,13},... | collective-permute-start | bytes 589832 | tf_op jit(solution)/shard_map/ppermute | solution.py:308
  133.1 1.3 collective-permute-done.78.refs_0_
  134.5 1.8 %shard_map.100 = (bf16[48,2048]{1,0:T(8,128)(2,1)S(1)}, bf16[48,2048]{1,0:T(8,128)(2,1)S(1)}) custom-call(bf16[48,2176]{1,0:T(8,128)(2,1)S(1)} %get-tuple-element.49.refs_0_.refs_2_, bf16[48,2176]{1,0:T(8,128)(2,1)S(1)} %collective-permute-done.24.refs_1_.refs_3_, bf16[2048,768]{1,0:T(8,128)(2,1)S(1)} %bitcast.16, bf16[2048,768]{1,0:T(8,128)(2,1)S(1)} %bitcast.26, ...), custom_call_target="tpu_custom_call" | custom-call | flops 905969664 | bytes 9437184 | tf_op jit(solution)/shard_map/pallas_call | solution.py:110
  137.5 1.6 %collective-permute-start.83 = (bf16[48,2048]{1,0:T(8,128)(2,1)S(1)}, bf16[48,2048]{1,0:T(8,128)(2,1)S(1)}, u32[]{:S(2)}, u32[]{:S(2)}) collective-permute-start(bf16[48,2048]{1,0:T(8,128)(2,1)S(1)} %shard_map.125), channel_id=1, source_target_pairs={{0,2},{1,3},{4,0},{5,1},{8,4},{9,5},{12,8},{13,9},{14,12},{15,13},... | collective-permute-start | bytes 589832 | tf_op jit(solution)/shard_map/ppermute | solution.py:308
  139.8 1.6 %collective-permute-start.53 = (bf16[48,2048]{1,0:T(8,128)(2,1)S(1)}, bf16[48,2048]{1,0:T(8,128)(2,1)S(1)}, u32[]{:S(2)}, u32[]{:S(2)}) collective-permute-start(bf16[48,2048]{1,0:T(8,128)(2,1)S(1)} %shard_map.112), channel_id=1, source_target_pairs={{0,2},{1,3},{4,0},{5,1},{8,4},{9,5},{12,8},{13,9},{14,12},{15,13},... | collective-permute-start | bytes 589832 | tf_op jit(solution)/shard_map/ppermute | solution.py:308
  141.4 3.4 %collective-permute-done.79.refs_6_ = bf16[48,2048]{1,0:T(8,128)(2,1)S(1)} collective-permute-done((bf16[48,2048]{1,0:T(8,128)(2,1)S(1)}, bf16[48,2048]{1,0:T(8,128)(2,1)S(1)}, u32[]{:S(2)}, u32[]{:S(2)}) %collective-permute-start.79) | collective-permute-done | bytes 196640 | tf_op jit(solution)/shard_map/ppermute | solution.py:308
  145.3 2.8 %collective-permute-done.49.refs_2_ = bf16[48,2048]{1,0:T(8,128)(2,1)S(1)} collective-permute-done((bf16[48,2048]{1,0:T(8,128)(2,1)S(1)}, bf16[48,2048]{1,0:T(8,128)(2,1)S(1)}, u32[]{:S(2)}, u32[]{:S(2)}) %collective-permute-start.49) | collective-permute-done | bytes 196640 | tf_op jit(solution)/shard_map/ppermute | solution.py:308
  148.3 1.0 shard_map.126
  (168 shorter events, 25.0 us)
Async XLA Ops:
  4.1 14.2 %collective-permute-start = (bf16[2,8,96,72]{3,2,1,0:T(8,128)(2,1)S(1)}, bf16[2,8,96,72]{3,2,1,0:T(8,128)(2,1)S(1)}, u32[]{:S(2)}, u32[]{:S(2)}) collective-permute-start(bf16[2,8,96,72]{3,2,1,0:T(8,128)(2,1)S(1)} %get-tuple-element.39), channel_id=1, source_target_pairs={{0,1},{1,0},{2,3},{3,2},{4,5},{5,4},{6,7},{7,6},{8,9},{9,8},{10,11... | collective-permute-start | bytes 663560 | tf_op jit(solution)/shard_map/ppermute | solution.py:314
  5.8 7.3 %collective-permute-start.14 = (bf16[72,1024]{1,0:T(8,128)(2,1)S(1)}, bf16[72,1024]{1,0:T(8,128)(2,1)S(1)}, u32[]{:S(2)}, u32[]{:S(2)}) collective-permute-start(bf16[72,1024]{1,0:T(8,128)(2,1)S(1)} %get-tuple-element.71.refs_3_), channel_id=1, source_target_pairs={{0,2},{1,3},{4,0},{5,1},{8,4},{9,5},{12,8},{13,9},{14,12},{15,13},... | collective-permute-start | bytes 442376 | tf_op jit(solution)/shard_map/ppermute | solution.py:308
  8.3 6.7 %collective-permute-start.13 = (bf16[72,1024]{1,0:T(8,128)(2,1)S(1)}, bf16[72,1024]{1,0:T(8,128)(2,1)S(1)}, u32[]{:S(2)}, u32[]{:S(2)}) collective-permute-start(bf16[72,1024]{1,0:T(8,128)(2,1)S(1)} %get-tuple-element.71.refs_3_), channel_id=1, source_target_pairs={{0,4},{1,5},{4,8},{5,9},{8,12},{9,13},{12,14},{13,15},{14,10},{15,... | collective-permute-start | bytes 442376 | tf_op jit(solution)/shard_map/ppermute | solution.py:308
  8.5 7.8 %collective-permute-start.3 = (bf16[72,1024]{1,0:T(8,128)(2,1)S(1)}, bf16[72,1024]{1,0:T(8,128)(2,1)S(1)}, u32[]{:S(2)}, u32[]{:S(2)}) collective-permute-start(bf16[72,1024]{1,0:T(8,128)(2,1)S(1)} %get-tuple-element.72.refs_3_), channel_id=1, source_target_pairs={{0,2},{1,3},{4,0},{5,1},{8,4},{9,5},{12,8},{13,9},{14,12},{15,13},... | collective-permute-start | bytes 442376 | tf_op jit(solution)/shard_map/ppermute | solution.py:308
  10.3 7.9 %collective-permute-start.2 = (bf16[72,1024]{1,0:T(8,128)(2,1)S(1)}, bf16[72,1024]{1,0:T(8,128)(2,1)S(1)}, u32[]{:S(2)}, u32[]{:S(2)}) collective-permute-start(bf16[72,1024]{1,0:T(8,128)(2,1)S(1)} %get-tuple-element.72.refs_3_), channel_id=1, source_target_pairs={{0,4},{1,5},{4,8},{5,9},{8,12},{9,13},{12,14},{13,15},{14,10},{15,... | collective-permute-start | bytes 442376 | tf_op jit(solution)/shard_map/ppermute | solution.py:308
  13.1 7.3 %collective-permute-start.16 = (bf16[72,1024]{1,0:T(8,128)(2,1)S(1)}, bf16[72,1024]{1,0:T(8,128)(2,1)S(1)}, u32[]{:S(2)}, u32[]{:S(2)}) collective-permute-start(bf16[72,1024]{1,0:T(8,128)(2,1)S(1)} %collective-permute-done.14.refs_5_), channel_id=1, source_target_pairs={{0,2},{1,3},{4,0},{5,1},{8,4},{9,5},{12,8},{13,9},{14,12},{15,13},... | collective-permute-start | bytes 442376 | tf_op jit(solution)/shard_map/ppermute | solution.py:308
  15.0 6.9 %collective-permute-start.15 = (bf16[72,1024]{1,0:T(8,128)(2,1)S(1)}, bf16[72,1024]{1,0:T(8,128)(2,1)S(1)}, u32[]{:S(2)}, u32[]{:S(2)}) collective-permute-start(bf16[72,1024]{1,0:T(8,128)(2,1)S(1)} %collective-permute-done.13.refs_4_), channel_id=1, source_target_pairs={{0,4},{1,5},{4,8},{5,9},{8,12},{9,13},{12,14},{13,15},{14,10},{15,... | collective-permute-start | bytes 442376 | tf_op jit(solution)/shard_map/ppermute | solution.py:308
  16.3 6.7 %collective-permute-start.5 = (bf16[72,1024]{1,0:T(8,128)(2,1)S(1)}, bf16[72,1024]{1,0:T(8,128)(2,1)S(1)}, u32[]{:S(2)}, u32[]{:S(2)}) collective-permute-start(bf16[72,1024]{1,0:T(8,128)(2,1)S(1)} %collective-permute-done.3.refs_5_), channel_id=1, source_target_pairs={{0,2},{1,3},{4,0},{5,1},{8,4},{9,5},{12,8},{13,9},{14,12},{15,13},... | collective-permute-start | bytes 442376 | tf_op jit(solution)/shard_map/ppermute | solution.py:308
  18.2 6.7 %collective-permute-start.4 = (bf16[72,1024]{1,0:T(8,128)(2,1)S(1)}, bf16[72,1024]{1,0:T(8,128)(2,1)S(1)}, u32[]{:S(2)}, u32[]{:S(2)}) collective-permute-start(bf16[72,1024]{1,0:T(8,128)(2,1)S(1)} %collective-permute-done.2.refs_4_), channel_id=1, source_target_pairs={{0,4},{1,5},{4,8},{5,9},{8,12},{9,13},{12,14},{13,15},{14,10},{15,... | collective-permute-start | bytes 442376 | tf_op jit(solution)/shard_map/ppermute | solution.py:308
  18.5 13.2 %collective-permute-start.1 = (bf16[2,8,96,72]{3,2,1,0:T(8,128)(2,1)S(1)}, bf16[2,8,96,72]{3,2,1,0:T(8,128)(2,1)S(1)}, u32[]{:S(2)}, u32[]{:S(2)}) collective-permute-start(bf16[2,8,96,72]{3,2,1,0:T(8,128)(2,1)S(1)} %pad_maximum_fusion), channel_id=1, source_target_pairs={{0,16},{16,0},{1,17},{17,1},{2,18},{18,2},{3,19},{19,3},{4,20},{20... | collective-permute-start | bytes 663560 | tf_op jit(solution)/shard_map/ppermute | solution.py:316
  20.4 6.2 %collective-permute-start.18 = (bf16[72,1024]{1,0:T(8,128)(2,1)S(1)}, bf16[72,1024]{1,0:T(8,128)(2,1)S(1)}, u32[]{:S(2)}, u32[]{:S(2)}) collective-permute-start(bf16[72,1024]{1,0:T(8,128)(2,1)S(1)} %collective-permute-done.16.refs_7_), channel_id=1, source_target_pairs={{0,2},{1,3},{4,0},{5,1},{8,4},{9,5},{12,8},{13,9},{14,12},{15,13},... | collective-permute-start | bytes 442376 | tf_op jit(solution)/shard_map/ppermute | solution.py:308
  21.9 6.6 %collective-permute-start.17 = (bf16[72,1024]{1,0:T(8,128)(2,1)S(1)}, bf16[72,1024]{1,0:T(8,128)(2,1)S(1)}, u32[]{:S(2)}, u32[]{:S(2)}) collective-permute-start(bf16[72,1024]{1,0:T(8,128)(2,1)S(1)} %collective-permute-done.15.refs_6_), channel_id=1, source_target_pairs={{0,4},{1,5},{4,8},{5,9},{8,12},{9,13},{12,14},{13,15},{14,10},{15,... | collective-permute-start | bytes 442376 | tf_op jit(solution)/shard_map/ppermute | solution.py:308
  23.0 6.5 %collective-permute-start.7 = (bf16[72,1024]{1,0:T(8,128)(2,1)S(1)}, bf16[72,1024]{1,0:T(8,128)(2,1)S(1)}, u32[]{:S(2)}, u32[]{:S(2)}) collective-permute-start(bf16[72,1024]{1,0:T(8,128)(2,1)S(1)} %collective-permute-done.5.refs_7_), channel_id=1, source_target_pairs={{0,2},{1,3},{4,0},{5,1},{8,4},{9,5},{12,8},{13,9},{14,12},{15,13},... | collective-permute-start | bytes 442376 | tf_op jit(solution)/shard_map/ppermute | solution.py:308
  24.9 6.2 %collective-permute-start.6 = (bf16[72,1024]{1,0:T(8,128)(2,1)S(1)}, bf16[72,1024]{1,0:T(8,128)(2,1)S(1)}, u32[]{:S(2)}, u32[]{:S(2)}) collective-permute-start(bf16[72,1024]{1,0:T(8,128)(2,1)S(1)} %collective-permute-done.4.refs_6_), channel_id=1, source_target_pairs={{0,4},{1,5},{4,8},{5,9},{8,12},{9,13},{12,14},{13,15},{14,10},{15,... | collective-permute-start | bytes 442376 | tf_op jit(solution)/shard_map/ppermute | solution.py:308
  26.7 8.1 %collective-permute-start.20 = (bf16[32,1024]{1,0:T(8,128)(2,1)S(1)}, bf16[32,1024]{1,0:T(8,128)(2,1)S(1)}, u32[]{:S(2)}, u32[]{:S(2)}) collective-permute-start(bf16[32,1024]{1,0:T(8,128)(2,1)S(1)} %slice.52), channel_id=1, source_target_pairs={{0,2},{1,3},{4,0},{5,1},{8,4},{9,5},{12,8},{13,9},{14,12},{15,13},... | collective-permute-start | bytes 196616 | tf_op jit(solution)/shard_map/ppermute | solution.py:308
  28.6 6.2 %collective-permute-start.19 = (bf16[40,1024]{1,0:T(8,128)(2,1)S(1)}, bf16[40,1024]{1,0:T(8,128)(2,1)S(1)}, u32[]{:S(2)}, u32[]{:S(2)}) collective-permute-start(bf16[40,1024]{1,0:T(8,128)(2,1)S(1)} %slice.51), channel_id=1, source_target_pairs={{0,4},{1,5},{4,8},{5,9},{8,12},{9,13},{12,14},{13,15},{14,10},{15,... | collective-permute-start | bytes 245768 | tf_op jit(solution)/shard_map/ppermute | solution.py:308
  29.4 6.1 %collective-permute-start.9 = (bf16[32,1024]{1,0:T(8,128)(2,1)S(1)}, bf16[32,1024]{1,0:T(8,128)(2,1)S(1)}, u32[]{:S(2)}, u32[]{:S(2)}) collective-permute-start(bf16[32,1024]{1,0:T(8,128)(2,1)S(1)} %slice.50), channel_id=1, source_target_pairs={{0,2},{1,3},{4,0},{5,1},{8,4},{9,5},{12,8},{13,9},{14,12},{15,13},... | collective-permute-start | bytes 196616 | tf_op jit(solution)/shard_map/ppermute | solution.py:308
  37.3 7.8 %collective-permute-start.23 = (bf16[96,1024]{1,0:T(8,128)(2,1)S(1)}, bf16[96,1024]{1,0:T(8,128)(2,1)S(1)}, u32[]{:S(2)}, u32[]{:S(2)}) collective-permute-start(bf16[96,1024]{1,0:T(8,128)(2,1)S(1)} %shard_map.97), channel_id=1, source_target_pairs={{0,16},{16,0},{1,17},{17,1},{2,18},{18,2},{3,19},{19,3},{4,20},{20... | collective-permute-start | bytes 589832 | tf_op jit(solution)/shard_map/ppermute | solution.py:349
  38.9 9.6 %collective-permute-start.12 = (bf16[96,1024]{1,0:T(8,128)(2,1)S(1)}, bf16[96,1024]{1,0:T(8,128)(2,1)S(1)}, u32[]{:S(2)}, u32[]{:S(2)}) collective-permute-start(bf16[96,1024]{1,0:T(8,128)(2,1)S(1)} %shard_map.94), channel_id=1, source_target_pairs={{0,16},{16,0},{1,17},{17,1},{2,18},{18,2},{3,19},{19,3},{4,20},{20... | collective-permute-start | bytes 589832 | tf_op jit(solution)/shard_map/ppermute | solution.py:349
  48.8 7.8 %collective-permute-start.57 = (bf16[48,2048]{1,0:T(8,128)(2,1)S(1)}, bf16[48,2048]{1,0:T(8,128)(2,1)S(1)}, u32[]{:S(2)}, u32[]{:S(2)}) collective-permute-start(bf16[48,2048]{1,0:T(8,128)(2,1)S(1)} %get-tuple-element.60.refs_0_), channel_id=1, source_target_pairs={{0,2},{1,3},{4,0},{5,1},{8,4},{9,5},{12,8},{13,9},{14,12},{15,13},... | collective-permute-start | bytes 589832 | tf_op jit(solution)/shard_map/ppermute | solution.py:308
  50.4 7.8 %collective-permute-start.56 = (bf16[48,2048]{1,0:T(8,128)(2,1)S(1)}, bf16[48,2048]{1,0:T(8,128)(2,1)S(1)}, u32[]{:S(2)}, u32[]{:S(2)}) collective-permute-start(bf16[48,2048]{1,0:T(8,128)(2,1)S(1)} %get-tuple-element.60.refs_0_), channel_id=1, source_target_pairs={{0,4},{1,5},{4,8},{5,9},{8,12},{9,13},{12,14},{13,15},{14,10},{15,... | collective-permute-start | bytes 589832 | tf_op jit(solution)/shard_map/ppermute | solution.py:308
  50.9 10.2 %collective-permute-start.27 = (bf16[48,2176]{1,0:T(8,128)(2,1)S(1)}, bf16[48,2176]{1,0:T(8,128)(2,1)S(1)}, u32[]{:S(2)}, u32[]{:S(2)}) collective-permute-start(bf16[48,2176]{1,0:T(8,128)(2,1)S(1)} %get-tuple-element.49.refs_0_.refs_2_), channel_id=1, source_target_pairs={{0,2},{1,3},{4,0},{5,1},{8,4},{9,5},{12,8},{13,9},{14,12},{15,13},... | collective-permute-start | bytes 626696 | tf_op jit(solution)/shard_map/ppermute | solution.py:308
  52.4 10.2 %collective-permute-start.26 = (bf16[48,2176]{1,0:T(8,128)(2,1)S(1)}, bf16[48,2176]{1,0:T(8,128)(2,1)S(1)}, u32[]{:S(2)}, u32[]{:S(2)}) collective-permute-start(bf16[48,2176]{1,0:T(8,128)(2,1)S(1)} %get-tuple-element.49.refs_0_.refs_2_), channel_id=1, source_target_pairs={{0,4},{1,5},{4,8},{5,9},{8,12},{9,13},{12,14},{13,15},{14,10},{15,... | collective-permute-start | bytes 626696 | tf_op jit(solution)/shard_map/ppermute | solution.py:308
  56.7 8.7 %collective-permute-start.62 = (bf16[48,2048]{1,0:T(8,128)(2,1)S(1)}, bf16[48,2048]{1,0:T(8,128)(2,1)S(1)}, u32[]{:S(2)}, u32[]{:S(2)}) collective-permute-start(bf16[48,2048]{1,0:T(8,128)(2,1)S(1)} %collective-permute-done.57.refs_1_), channel_id=1, source_target_pairs={{0,2},{1,3},{4,0},{5,1},{8,4},{9,5},{12,8},{13,9},{14,12},{15,13},... | collective-permute-start | bytes 589832 | tf_op jit(solution)/shard_map/ppermute | solution.py:308
  58.2 8.7 %collective-permute-start.61 = (bf16[48,2048]{1,0:T(8,128)(2,1)S(1)}, bf16[48,2048]{1,0:T(8,128)(2,1)S(1)}, u32[]{:S(2)}, u32[]{:S(2)}) collective-permute-start(bf16[48,2048]{1,0:T(8,128)(2,1)S(1)} %collective-permute-done.56.refs_0_), channel_id=1, source_target_pairs={{0,4},{1,5},{4,8},{5,9},{8,12},{9,13},{12,14},{13,15},{14,10},{15,... | collective-permute-start | bytes 589832 | tf_op jit(solution)/shard_map/ppermute | solution.py:308
  61.1 8.7 %collective-permute-start.32 = (bf16[48,2176]{1,0:T(8,128)(2,1)S(1)}, bf16[48,2176]{1,0:T(8,128)(2,1)S(1)}, u32[]{:S(2)}, u32[]{:S(2)}) collective-permute-start(bf16[48,2176]{1,0:T(8,128)(2,1)S(1)} %collective-permute-done.27.refs_1_.refs_5_), channel_id=1, source_target_pairs={{0,2},{1,3},{4,0},{5,1},{8,4},{9,5},{12,8},{13,9},{14,12},{15,13},... | collective-permute-start | bytes 626696 | tf_op jit(solution)/shard_map/ppermute | solution.py:308
  62.7 8.7 %collective-permute-start.31 = (bf16[48,2176]{1,0:T(8,128)(2,1)S(1)}, bf16[48,2176]{1,0:T(8,128)(2,1)S(1)}, u32[]{:S(2)}, u32[]{:S(2)}) collective-permute-start(bf16[48,2176]{1,0:T(8,128)(2,1)S(1)} %collective-permute-done.26.refs_0_.refs_4_), channel_id=1, source_target_pairs={{0,4},{1,5},{4,8},{5,9},{8,12},{9,13},{12,14},{13,15},{14,10},{15,... | collective-permute-start | bytes 626696 | tf_op jit(solution)/shard_map/ppermute | solution.py:308
  65.3 8.7 %collective-permute-start.67 = (bf16[48,2048]{1,0:T(8,128)(2,1)S(1)}, bf16[48,2048]{1,0:T(8,128)(2,1)S(1)}, u32[]{:S(2)}, u32[]{:S(2)}) collective-permute-start(bf16[48,2048]{1,0:T(8,128)(2,1)S(1)} %collective-permute-done.62.refs_1_), channel_id=1, source_target_pairs={{0,2},{1,3},{4,0},{5,1},{8,4},{9,5},{12,8},{13,9},{14,12},{15,13},... | collective-permute-start | bytes 589832 | tf_op jit(solution)/shard_map/ppermute | solution.py:308
  66.9 8.7 %collective-permute-start.66 = (bf16[48,2048]{1,0:T(8,128)(2,1)S(1)}, bf16[48,2048]{1,0:T(8,128)(2,1)S(1)}, u32[]{:S(2)}, u32[]{:S(2)}) collective-permute-start(bf16[48,2048]{1,0:T(8,128)(2,1)S(1)} %collective-permute-done.61.refs_0_), channel_id=1, source_target_pairs={{0,4},{1,5},{4,8},{5,9},{8,12},{9,13},{12,14},{13,15},{14,10},{15,... | collective-permute-start | bytes 589832 | tf_op jit(solution)/shard_map/ppermute | solution.py:308
  69.8 7.3 %collective-permute-start.37 = (bf16[48,2176]{1,0:T(8,128)(2,1)S(1)}, bf16[48,2176]{1,0:T(8,128)(2,1)S(1)}, u32[]{:S(2)}, u32[]{:S(2)}) collective-permute-start(bf16[48,2176]{1,0:T(8,128)(2,1)S(1)} %collective-permute-done.32.refs_1_.refs_5_), channel_id=1, source_target_pairs={{0,2},{1,3},{4,0},{5,1},{8,4},{9,5},{12,8},{13,9},{14,12},{15,13},... | collective-permute-start | bytes 626696 | tf_op jit(solution)/shard_map/ppermute | solution.py:308
  71.4 7.1 %collective-permute-start.36 = (bf16[48,2176]{1,0:T(8,128)(2,1)S(1)}, bf16[48,2176]{1,0:T(8,128)(2,1)S(1)}, u32[]{:S(2)}, u32[]{:S(2)}) collective-permute-start(bf16[48,2176]{1,0:T(8,128)(2,1)S(1)} %collective-permute-done.31.refs_0_.refs_4_), channel_id=1, source_target_pairs={{0,4},{1,5},{4,8},{5,9},{8,12},{9,13},{12,14},{13,15},{14,10},{15,... | collective-permute-start | bytes 626696 | tf_op jit(solution)/shard_map/ppermute | solution.py:308
  71.9 7.8 %collective-permute-start.54 = (bf16[48,2048]{1,0:T(8,128)(2,1)S(1)}, bf16[48,2048]{1,0:T(8,128)(2,1)S(1)}, u32[]{:S(2)}, u32[]{:S(2)}) collective-permute-start(bf16[48,2048]{1,0:T(8,128)(2,1)S(1)} %get-tuple-element.60.refs_0_), channel_id=1, source_target_pairs={{0,1},{1,0},{2,3},{3,2},{4,5},{5,4},{6,7},{7,6},{8,9},{9,8},{10,11... | collective-permute-start | bytes 589832 | tf_op jit(solution)/shard_map/ppermute | solution.py:371
  74.0 7.1 %collective-permute-start.59 = (bf16[48,2048]{1,0:T(8,128)(2,1)S(1)}, bf16[48,2048]{1,0:T(8,128)(2,1)S(1)}, u32[]{:S(2)}, u32[]{:S(2)}) collective-permute-start(bf16[48,2048]{1,0:T(8,128)(2,1)S(1)} %collective-permute-done.57.refs_1_), channel_id=1, source_target_pairs={{0,1},{1,0},{2,3},{3,2},{4,5},{5,4},{6,7},{7,6},{8,9},{9,8},{10,11... | collective-permute-start | bytes 589832 | tf_op jit(solution)/shard_map/ppermute | solution.py:371
  81.1 7.6 %collective-permute-start.39 = (bf16[48,2176]{1,0:T(8,128)(2,1)S(1)}, bf16[48,2176]{1,0:T(8,128)(2,1)S(1)}, u32[]{:S(2)}, u32[]{:S(2)}) collective-permute-start(bf16[48,2176]{1,0:T(8,128)(2,1)S(1)} %collective-permute-done.37.refs_1_.refs_5_), channel_id=1, source_target_pairs={{0,1},{1,0},{2,3},{3,2},{4,5},{5,4},{6,7},{7,6},{8,9},{9,8},{10,11... | collective-permute-start | bytes 626696 | tf_op jit(solution)/shard_map/ppermute | solution.py:371
  82.5 6.4 %collective-permute-start.38 = (bf16[48,2176]{1,0:T(8,128)(2,1)S(1)}, bf16[48,2176]{1,0:T(8,128)(2,1)S(1)}, u32[]{:S(2)}, u32[]{:S(2)}) collective-permute-start(bf16[48,2176]{1,0:T(8,128)(2,1)S(1)} %collective-permute-done.36.refs_0_.refs_4_), channel_id=1, source_target_pairs={{0,1},{1,0},{2,3},{3,2},{4,5},{5,4},{6,7},{7,6},{8,9},{9,8},{10,11... | collective-permute-start | bytes 626696 | tf_op jit(solution)/shard_map/ppermute | solution.py:371
  86.0 5.8 %collective-permute-start.58 = (bf16[48,2048]{1,0:T(8,128)(2,1)S(1)}, bf16[48,2048]{1,0:T(8,128)(2,1)S(1)}, u32[]{:S(2)}, u32[]{:S(2)}) collective-permute-start(bf16[48,2048]{1,0:T(8,128)(2,1)S(1)} %collective-permute-done.56.refs_0_), channel_id=1, source_target_pairs={{0,1},{1,0},{2,3},{3,2},{4,5},{5,4},{6,7},{7,6},{8,9},{9,8},{10,11... | collective-permute-start | bytes 589832 | tf_op jit(solution)/shard_map/ppermute | solution.py:371
  86.6 5.8 %collective-permute-start.69 = (bf16[48,2048]{1,0:T(8,128)(2,1)S(1)}, bf16[48,2048]{1,0:T(8,128)(2,1)S(1)}, u32[]{:S(2)}, u32[]{:S(2)}) collective-permute-start(bf16[48,2048]{1,0:T(8,128)(2,1)S(1)} %collective-permute-done.67.refs_1_), channel_id=1, source_target_pairs={{0,1},{1,0},{2,3},{3,2},{4,5},{5,4},{6,7},{7,6},{8,9},{9,8},{10,11... | collective-permute-start | bytes 589832 | tf_op jit(solution)/shard_map/ppermute | solution.py:371
  88.9 5.9 %collective-permute-start.75 = (bf16[48,2048]{1,0:T(8,128)(2,1)S(1)}, bf16[48,2048]{1,0:T(8,128)(2,1)S(1)}, u32[]{:S(2)}, u32[]{:S(2)}) collective-permute-start(bf16[48,2048]{1,0:T(8,128)(2,1)S(1)} %get-tuple-element.70), channel_id=1, source_target_pairs={{0,1},{1,0},{2,3},{3,2},{4,5},{5,4},{6,7},{7,6},{8,9},{9,8},{10,11... | collective-permute-start | bytes 589832 | tf_op jit(solution)/shard_map/ppermute | solution.py:374
  92.0 5.9 %collective-permute-start.34 = (bf16[48,2176]{1,0:T(8,128)(2,1)S(1)}, bf16[48,2176]{1,0:T(8,128)(2,1)S(1)}, u32[]{:S(2)}, u32[]{:S(2)}) collective-permute-start(bf16[48,2176]{1,0:T(8,128)(2,1)S(1)} %collective-permute-done.32.refs_1_.refs_5_), channel_id=1, source_target_pairs={{0,1},{1,0},{2,3},{3,2},{4,5},{5,4},{6,7},{7,6},{8,9},{9,8},{10,11... | collective-permute-start | bytes 626696 | tf_op jit(solution)/shard_map/ppermute | solution.py:371
  92.4 5.7 %collective-permute-start.33 = (bf16[48,2176]{1,0:T(8,128)(2,1)S(1)}, bf16[48,2176]{1,0:T(8,128)(2,1)S(1)}, u32[]{:S(2)}, u32[]{:S(2)}) collective-permute-start(bf16[48,2176]{1,0:T(8,128)(2,1)S(1)} %collective-permute-done.31.refs_0_.refs_4_), channel_id=1, source_target_pairs={{0,1},{1,0},{2,3},{3,2},{4,5},{5,4},{6,7},{7,6},{8,9},{9,8},{10,11... | collective-permute-start | bytes 626696 | tf_op jit(solution)/shard_map/ppermute | solution.py:371
  94.4 7.2 %collective-permute-start.29 = (bf16[48,2176]{1,0:T(8,128)(2,1)S(1)}, bf16[48,2176]{1,0:T(8,128)(2,1)S(1)}, u32[]{:S(2)}, u32[]{:S(2)}) collective-permute-start(bf16[48,2176]{1,0:T(8,128)(2,1)S(1)} %collective-permute-done.27.refs_1_.refs_5_), channel_id=1, source_target_pairs={{0,1},{1,0},{2,3},{3,2},{4,5},{5,4},{6,7},{7,6},{8,9},{9,8},{10,11... | collective-permute-start | bytes 626696 | tf_op jit(solution)/shard_map/ppermute | solution.py:371
  94.8 6.9 %collective-permute-start.45 = (bf16[48,2048]{1,0:T(8,128)(2,1)S(1)}, bf16[48,2048]{1,0:T(8,128)(2,1)S(1)}, u32[]{:S(2)}, u32[]{:S(2)}) collective-permute-start(bf16[48,2048]{1,0:T(8,128)(2,1)S(1)} %get-tuple-element.59), channel_id=1, source_target_pairs={{0,1},{1,0},{2,3},{3,2},{4,5},{5,4},{6,7},{7,6},{8,9},{9,8},{10,11... | collective-permute-start | bytes 589832 | tf_op jit(solution)/shard_map/ppermute | solution.py:374
  97.5 10.3 %collective-permute-start.70 = (bf16[96,2048]{1,0:T(8,128)(2,1)S(1)}, bf16[96,2048]{1,0:T(8,128)(2,1)S(1)}, u32[]{:S(2)}, u32[]{:S(2)}) collective-permute-start(bf16[96,2048]{1,0:T(8,128)(2,1)S(1)} %get-tuple-element.68), channel_id=1, source_target_pairs={{0,1},{1,0},{2,3},{3,2},{4,5},{5,4},{6,7},{7,6},{8,9},{9,8},{10,11... | collective-permute-start | bytes 1179656 | tf_op jit(solution)/shard_map/ppermute | solution.py:374
  97.9 17.2 %collective-permute-start.40 = (bf16[96,2048]{1,0:T(8,128)(2,1)S(1)}, bf16[96,2048]{1,0:T(8,128)(2,1)S(1)}, u32[]{:S(2)}, u32[]{:S(2)}) collective-permute-start(bf16[96,2048]{1,0:T(8,128)(2,1)S(1)} %get-tuple-element.57), channel_id=1, source_target_pairs={{0,1},{1,0},{2,3},{3,2},{4,5},{5,4},{6,7},{7,6},{8,9},{9,8},{10,11... | collective-permute-start | bytes 1179656 | tf_op jit(solution)/shard_map/ppermute | solution.py:374
  101.6 7.4 %collective-permute-start.28 = (bf16[48,2176]{1,0:T(8,128)(2,1)S(1)}, bf16[48,2176]{1,0:T(8,128)(2,1)S(1)}, u32[]{:S(2)}, u32[]{:S(2)}) collective-permute-start(bf16[48,2176]{1,0:T(8,128)(2,1)S(1)} %collective-permute-done.26.refs_0_.refs_4_), channel_id=1, source_target_pairs={{0,1},{1,0},{2,3},{3,2},{4,5},{5,4},{6,7},{7,6},{8,9},{9,8},{10,11... | collective-permute-start | bytes 626696 | tf_op jit(solution)/shard_map/ppermute | solution.py:371
  101.7 17.6 %collective-permute-start.65 = (bf16[96,2048]{1,0:T(8,128)(2,1)S(1)}, bf16[96,2048]{1,0:T(8,128)(2,1)S(1)}, u32[]{:S(2)}, u32[]{:S(2)}) collective-permute-start(bf16[96,2048]{1,0:T(8,128)(2,1)S(1)} %get-tuple-element.66), channel_id=1, source_target_pairs={{0,1},{1,0},{2,3},{3,2},{4,5},{5,4},{6,7},{7,6},{8,9},{9,8},{10,11... | collective-permute-start | bytes 1179656 | tf_op jit(solution)/shard_map/ppermute | solution.py:374
  107.8 12.4 %collective-permute-start.35 = (bf16[96,2048]{1,0:T(8,128)(2,1)S(1)}, bf16[96,2048]{1,0:T(8,128)(2,1)S(1)}, u32[]{:S(2)}, u32[]{:S(2)}) collective-permute-start(bf16[96,2048]{1,0:T(8,128)(2,1)S(1)} %get-tuple-element.55), channel_id=1, source_target_pairs={{0,1},{1,0},{2,3},{3,2},{4,5},{5,4},{6,7},{7,6},{8,9},{9,8},{10,11... | collective-permute-start | bytes 1179656 | tf_op jit(solution)/shard_map/ppermute | solution.py:374
  107.8 5.7 %collective-permute-start.46 = (bf16[24,2048]{1,0:T(8,128)(2,1)S(1)}, bf16[24,2048]{1,0:T(8,128)(2,1)S(1)}, u32[]{:S(2)}, u32[]{:S(2)}) collective-permute-start(bf16[24,2048]{1,0:T(8,128)(2,1)S(1)} %shard_map.105), channel_id=1, source_target_pairs={{0,4},{1,5},{4,8},{5,9},{8,12},{9,13},{12,14},{13,15},{14,10},{15,... | collective-permute-start | bytes 294920 | tf_op jit(solution)/shard_map/ppermute | solution.py:308
  109.0 11.3 %collective-permute-start.77 = (bf16[48,2048]{1,0:T(8,128)(2,1)S(1)}, bf16[48,2048]{1,0:T(8,128)(2,1)S(1)}, u32[]{:S(2)}, u32[]{:S(2)}) collective-permute-start(bf16[48,2048]{1,0:T(8,128)(2,1)S(1)} %shard_map.119), channel_id=1, source_target_pairs={{0,4},{1,5},{4,8},{5,9},{8,12},{9,13},{12,14},{13,15},{14,10},{15,... | collective-permute-start | bytes 589832 | tf_op jit(solution)/shard_map/ppermute | solution.py:308
  113.5 5.8 %collective-permute-start.50 = (bf16[24,2048]{1,0:T(8,128)(2,1)S(1)}, bf16[24,2048]{1,0:T(8,128)(2,1)S(1)}, u32[]{:S(2)}, u32[]{:S(2)}) collective-permute-start(bf16[24,2048]{1,0:T(8,128)(2,1)S(1)} %shard_map.109), channel_id=1, source_target_pairs={{0,2},{1,3},{4,0},{5,1},{8,4},{9,5},{12,8},{13,9},{14,12},{15,13},... | collective-permute-start | bytes 294920 | tf_op jit(solution)/shard_map/ppermute | solution.py:308
  115.1 9.2 %collective-permute-start.81 = (bf16[48,2048]{1,0:T(8,128)(2,1)S(1)}, bf16[48,2048]{1,0:T(8,128)(2,1)S(1)}, u32[]{:S(2)}, u32[]{:S(2)}) collective-permute-start(bf16[48,2048]{1,0:T(8,128)(2,1)S(1)} %shard_map.123), channel_id=1, source_target_pairs={{0,2},{1,3},{4,0},{5,1},{8,4},{9,5},{12,8},{13,9},{14,12},{15,13},... | collective-permute-start | bytes 589832 | tf_op jit(solution)/shard_map/ppermute | solution.py:308
  119.3 11.9 %collective-permute-start.60 = (bf16[96,2048]{1,0:T(8,128)(2,1)S(1)}, bf16[96,2048]{1,0:T(8,128)(2,1)S(1)}, u32[]{:S(2)}, u32[]{:S(2)}) collective-permute-start(bf16[96,2048]{1,0:T(8,128)(2,1)S(1)} %get-tuple-element.64), channel_id=1, source_target_pairs={{0,1},{1,0},{2,3},{3,2},{4,5},{5,4},{6,7},{7,6},{8,9},{9,8},{10,11... | collective-permute-start | bytes 1179656 | tf_op jit(solution)/shard_map/ppermute | solution.py:374
  119.4 7.3 %collective-permute-start.47 = (bf16[48,2048]{1,0:T(8,128)(2,1)S(1)}, bf16[48,2048]{1,0:T(8,128)(2,1)S(1)}, u32[]{:S(2)}, u32[]{:S(2)}) collective-permute-start(bf16[48,2048]{1,0:T(8,128)(2,1)S(1)} %shard_map.106), channel_id=1, source_target_pairs={{0,4},{1,5},{4,8},{5,9},{8,12},{9,13},{12,14},{13,15},{14,10},{15,... | collective-permute-start | bytes 589832 | tf_op jit(solution)/shard_map/ppermute | solution.py:308
  120.2 7.1 %collective-permute-start.24 = (bf16[48,2176]{1,0:T(8,128)(2,1)S(1)}, bf16[48,2176]{1,0:T(8,128)(2,1)S(1)}, u32[]{:S(2)}, u32[]{:S(2)}) collective-permute-start(bf16[48,2176]{1,0:T(8,128)(2,1)S(1)} %get-tuple-element.49.refs_0_.refs_2_), channel_id=1, source_target_pairs={{0,1},{1,0},{2,3},{3,2},{4,5},{5,4},{6,7},{7,6},{8,9},{9,8},{10,11... | collective-permute-start | bytes 626696 | tf_op jit(solution)/shard_map/ppermute | solution.py:371
  120.3 8.6 %collective-permute-start.51 = (bf16[48,2048]{1,0:T(8,128)(2,1)S(1)}, bf16[48,2048]{1,0:T(8,128)(2,1)S(1)}, u32[]{:S(2)}, u32[]{:S(2)}) collective-permute-start(bf16[48,2048]{1,0:T(8,128)(2,1)S(1)} %shard_map.110), channel_id=1, source_target_pairs={{0,2},{1,3},{4,0},{5,1},{8,4},{9,5},{12,8},{13,9},{14,12},{15,13},... | collective-permute-start | bytes 589832 | tf_op jit(solution)/shard_map/ppermute | solution.py:308
  124.3 12.7 %collective-permute-start.30 = (bf16[96,2048]{1,0:T(8,128)(2,1)S(1)}, bf16[96,2048]{1,0:T(8,128)(2,1)S(1)}, u32[]{:S(2)}, u32[]{:S(2)}) collective-permute-start(bf16[96,2048]{1,0:T(8,128)(2,1)S(1)} %get-tuple-element.53), channel_id=1, source_target_pairs={{0,1},{1,0},{2,3},{3,2},{4,5},{5,4},{6,7},{7,6},{8,9},{9,8},{10,11... | collective-permute-start | bytes 1179656 | tf_op jit(solution)/shard_map/ppermute | solution.py:374
  126.7 7.8 %collective-permute-start.78 = (bf16[48,2048]{1,0:T(8,128)(2,1)S(1)}, bf16[48,2048]{1,0:T(8,128)(2,1)S(1)}, u32[]{:S(2)}, u32[]{:S(2)}) collective-permute-start(bf16[48,2048]{1,0:T(8,128)(2,1)S(1)} %shard_map.120), channel_id=1, source_target_pairs={{0,4},{1,5},{4,8},{5,9},{8,12},{9,13},{12,14},{13,15},{14,10},{15,... | collective-permute-start | bytes 589832 | tf_op jit(solution)/shard_map/ppermute | solution.py:308
  127.3 9.1 %collective-permute-start.82 = (bf16[48,2048]{1,0:T(8,128)(2,1)S(1)}, bf16[48,2048]{1,0:T(8,128)(2,1)S(1)}, u32[]{:S(2)}, u32[]{:S(2)}) collective-permute-start(bf16[48,2048]{1,0:T(8,128)(2,1)S(1)} %shard_map.124), channel_id=1, source_target_pairs={{0,2},{1,3},{4,0},{5,1},{8,4},{9,5},{12,8},{13,9},{14,12},{15,13},... | collective-permute-start | bytes 589832 | tf_op jit(solution)/shard_map/ppermute | solution.py:308
  128.9 8.6 %collective-permute-start.48 = (bf16[48,2048]{1,0:T(8,128)(2,1)S(1)}, bf16[48,2048]{1,0:T(8,128)(2,1)S(1)}, u32[]{:S(2)}, u32[]{:S(2)}) collective-permute-start(bf16[48,2048]{1,0:T(8,128)(2,1)S(1)} %shard_map.107), channel_id=1, source_target_pairs={{0,4},{1,5},{4,8},{5,9},{8,12},{9,13},{12,14},{13,15},{14,10},{15,... | collective-permute-start | bytes 589832 | tf_op jit(solution)/shard_map/ppermute | solution.py:308
  131.2 8.0 %collective-permute-start.52 = (bf16[48,2048]{1,0:T(8,128)(2,1)S(1)}, bf16[48,2048]{1,0:T(8,128)(2,1)S(1)}, u32[]{:S(2)}, u32[]{:S(2)}) collective-permute-start(bf16[48,2048]{1,0:T(8,128)(2,1)S(1)} %shard_map.111), channel_id=1, source_target_pairs={{0,2},{1,3},{4,0},{5,1},{8,4},{9,5},{12,8},{13,9},{14,12},{15,13},... | collective-permute-start | bytes 589832 | tf_op jit(solution)/shard_map/ppermute | solution.py:308
  137.0 7.8 %collective-permute-start.79 = (bf16[48,2048]{1,0:T(8,128)(2,1)S(1)}, bf16[48,2048]{1,0:T(8,128)(2,1)S(1)}, u32[]{:S(2)}, u32[]{:S(2)}) collective-permute-start(bf16[48,2048]{1,0:T(8,128)(2,1)S(1)} %shard_map.121), channel_id=1, source_target_pairs={{0,4},{1,5},{4,8},{5,9},{8,12},{9,13},{12,14},{13,15},{14,10},{15,... | collective-permute-start | bytes 589832 | tf_op jit(solution)/shard_map/ppermute | solution.py:308
  137.5 7.8 %collective-permute-start.83 = (bf16[48,2048]{1,0:T(8,128)(2,1)S(1)}, bf16[48,2048]{1,0:T(8,128)(2,1)S(1)}, u32[]{:S(2)}, u32[]{:S(2)}) collective-permute-start(bf16[48,2048]{1,0:T(8,128)(2,1)S(1)} %shard_map.125), channel_id=1, source_target_pairs={{0,2},{1,3},{4,0},{5,1},{8,4},{9,5},{12,8},{13,9},{14,12},{15,13},... | collective-permute-start | bytes 589832 | tf_op jit(solution)/shard_map/ppermute | solution.py:308
  139.2 8.9 %collective-permute-start.49 = (bf16[48,2048]{1,0:T(8,128)(2,1)S(1)}, bf16[48,2048]{1,0:T(8,128)(2,1)S(1)}, u32[]{:S(2)}, u32[]{:S(2)}) collective-permute-start(bf16[48,2048]{1,0:T(8,128)(2,1)S(1)} %shard_map.108), channel_id=1, source_target_pairs={{0,4},{1,5},{4,8},{5,9},{8,12},{9,13},{12,14},{13,15},{14,10},{15,... | collective-permute-start | bytes 589832 | tf_op jit(solution)/shard_map/ppermute | solution.py:308
  139.8 8.5 %collective-permute-start.53 = (bf16[48,2048]{1,0:T(8,128)(2,1)S(1)}, bf16[48,2048]{1,0:T(8,128)(2,1)S(1)}, u32[]{:S(2)}, u32[]{:S(2)}) collective-permute-start(bf16[48,2048]{1,0:T(8,128)(2,1)S(1)} %shard_map.112), channel_id=1, source_target_pairs={{0,2},{1,3},{4,0},{5,1},{8,4},{9,5},{12,8},{13,9},{14,12},{15,13},... | collective-permute-start | bytes 589832 | tf_op jit(solution)/shard_map/ppermute | solution.py:308
  (28 other events, 273.7 us)

commit v5 on v4

--- a/solution.py
+++ b/solution.py
@@ -138,14 +138,14 @@
         share.append(chosen / whole)
         start += size
     share = jnp.concatenate(share, axis=0)
-    tile = tile_of(wide, 384)
+    tile = tile_of(wide, 256)
     for at in range(0, wide, tile):
         x = x_ref[...]
         gate = jnp.dot(x, gate_ref[:, at : at + tile], preferred_element_type=jnp.float32)
         up = jnp.dot(x, up_ref[:, at : at + tile], preferred_element_type=jnp.float32)
-        h_ref[:, at : at + tile] = (gate * lax.logistic(gate) * up * share).astype(jnp.bfloat16)
+        h_ref[:, at : at + tile] = (gate * (1.0 / (1.0 + jnp.exp(-gate))) * up * share).astype(jnp.bfloat16)
     half = start // 2
-    tile = tile_of(width, 512)
+    tile = tile_of(width, 256)
     for at in range(0, width, tile):
         out = jnp.dot(h_ref[...], down_ref[:, at : at + tile], preferred_element_type=jnp.float32)
         own_ref[:, at : at + tile] = out[:half].astype(jnp.bfloat16)
@@ -202,7 +202,7 @@
 def bulk_body(chips, offsets, *refs):
     pieces, out_ref = refs[3:-1], refs[-1]
     width = out_ref.shape[1]
-    tile = tile_of(width, 512)
+    tile = tile_of(width, 256)
     for at in range(0, width, tile):
         total = None
         for offset, piece in zip(offsets, pieces):
@@ -216,7 +216,7 @@
     width = total_ref.shape[1]
     mid = top_ref.shape[0]
     rows = outs[0].shape[0]
-    tile = tile_of(width, 512)
+    tile = tile_of(width, 256)
     act = rows_of((mine_ref, given_ref, theirs_ref), chip_at(chips, chips // 2))
     for at in range(0, width, tile):
         to = at + tile

time: 149 us -> 148 us (level)
  Pallas kernels: 32 us -> 29.1 us
  waiting for transfers between devices: 48.8 us -> 50.4 us
    pallas_call x36, Pallas kernels: 32 us -> 29.1 us  [kernel(): pl.pallas_call(body, out_shape=outs, in_specs=[VMEM] * len(ins), out_spec...]
    ppermute x48, waiting for transfers between devices: 39 us -> 40.6 us  [hop(): return rings[way](array)]
  transfers between devices with their start and end apart: 84 -> 84, of which waited for: 29 -> 30; matrix products, arithmetic and copies ran while one was open for 1% -> 1% of each run, Pallas kernels for 19% -> 17%
where the time goes in v5:
time: 148 us
  starting transfers between devices  65.3 us (44%)
  waiting for transfers between devices  50.4 us (34%)
  Pallas kernels  29.1 us (20%)
  local copies, waits for them, and re-layouts  2.24 us (2%)
    ppermute x48, starting transfers between devices, hop(): return rings[way](array)  53.4 us
    ppermute x48, waiting for transfers between devices, hop(): return rings[way](array)  40.6 us
    pallas_call x36, Pallas kernels, kernel(): pl.pallas_call(body, out_shape=outs, in_specs=[VMEM] * len(ins), out_spec...  29.1 us
    ppermute x2, waiting for transfers between devices, dense(): theirs = cross(theirs)  8.71 us
    ppermute x18, starting transfers between devices, dense(): ins = [*ins, *(swap(x) for x in ins)]  3.47 us
  transfers between devices with their start and end apart: 84, of which 30 were waited for; matrix products, arithmetic and copies ran while one was open for 1% of the time, Pallas kernels for 17%

profile of v5, /device:TPU:0, one launch (start us, length us, event | category | flops | bytes accessed | tf_op | source)
XLA Modules:
  0.0 147.6 jit_solution(3771488812881746695)
XLA Ops:
  0.0 1.0 copy-done.3
  1.0 3.1 %shard_map.91 = (bf16[2,8,96,72]{3,2,1,0:T(8,128)(2,1)S(1)}, bf16[2,8,96,72]{3,2,1,0:T(8,128)(2,1)S(1)}) custom-call(bf16[96,2304]{1,0:T(8,128)(2,1)S(1)} %copy-done.3), custom_call_target="tpu_custom_call" | custom-call | tf_op jit(solution)/shard_map/pallas_call | solution.py:110
  4.7 1.1 fusion
  5.8 2.6 %collective-permute-start.14 = (bf16[72,1024]{1,0:T(8,128)(2,1)S(1)}, bf16[72,1024]{1,0:T(8,128)(2,1)S(1)}, u32[]{:S(2)}, u32[]{:S(2)}) collective-permute-start(bf16[72,1024]{1,0:T(8,128)(2,1)S(1)} %get-tuple-element.71.refs_3_), channel_id=1, source_target_pairs={{0,2},{1,3},{4,0},{5,1},{8,4},{9,5},{12,8},{13,9},{14,12},{15,13},... | collective-permute-start | bytes 442376 | tf_op jit(solution)/shard_map/ppermute | solution.py:308
  8.5 1.9 %collective-permute-start.3 = (bf16[72,1024]{1,0:T(8,128)(2,1)S(1)}, bf16[72,1024]{1,0:T(8,128)(2,1)S(1)}, u32[]{:S(2)}, u32[]{:S(2)}) collective-permute-start(bf16[72,1024]{1,0:T(8,128)(2,1)S(1)} %get-tuple-element.72.refs_3_), channel_id=1, source_target_pairs={{0,2},{1,3},{4,0},{5,1},{8,4},{9,5},{12,8},{13,9},{14,12},{15,13},... | collective-permute-start | bytes 442376 | tf_op jit(solution)/shard_map/ppermute | solution.py:308
  10.5 2.6 %collective-permute-done.14.refs_5_ = bf16[72,1024]{1,0:T(8,128)(2,1)S(1)} collective-permute-done((bf16[72,1024]{1,0:T(8,128)(2,1)S(1)}, bf16[72,1024]{1,0:T(8,128)(2,1)S(1)}, u32[]{:S(2)}, u32[]{:S(2)}) %collective-permute-start.14) | collective-permute-done | bytes 147488 | tf_op jit(solution)/shard_map/ppermute | solution.py:308
  13.1 1.9 %collective-permute-start.16 = (bf16[72,1024]{1,0:T(8,128)(2,1)S(1)}, bf16[72,1024]{1,0:T(8,128)(2,1)S(1)}, u32[]{:S(2)}, u32[]{:S(2)}) collective-permute-start(bf16[72,1024]{1,0:T(8,128)(2,1)S(1)} %collective-permute-done.14.refs_5_), channel_id=1, source_target_pairs={{0,2},{1,3},{4,0},{5,1},{8,4},{9,5},{12,8},{13,9},{14,12},{15,13},... | collective-permute-start | bytes 442376 | tf_op jit(solution)/shard_map/ppermute | solution.py:308
  15.2 1.1 collective-permute-done.3.refs_5_
  16.3 1.9 %collective-permute-start.5 = (bf16[72,1024]{1,0:T(8,128)(2,1)S(1)}, bf16[72,1024]{1,0:T(8,128)(2,1)S(1)}, u32[]{:S(2)}, u32[]{:S(2)}) collective-permute-start(bf16[72,1024]{1,0:T(8,128)(2,1)S(1)} %collective-permute-done.3.refs_5_), channel_id=1, source_target_pairs={{0,2},{1,3},{4,0},{5,1},{8,4},{9,5},{12,8},{13,9},{14,12},{15,13},... | collective-permute-start | bytes 442376 | tf_op jit(solution)/shard_map/ppermute | solution.py:308
  18.5 2.0 %collective-permute-start.1 = (bf16[2,8,96,72]{3,2,1,0:T(8,128)(2,1)S(1)}, bf16[2,8,96,72]{3,2,1,0:T(8,128)(2,1)S(1)}, u32[]{:S(2)}, u32[]{:S(2)}) collective-permute-start(bf16[2,8,96,72]{3,2,1,0:T(8,128)(2,1)S(1)} %pad_maximum_fusion), channel_id=1, source_target_pairs={{0,16},{16,0},{1,17},{17,1},{2,18},{18,2},{3,19},{19,3},{4,20},{20... | collective-permute-start | bytes 663560 | tf_op jit(solution)/shard_map/ppermute | solution.py:316
  20.4 1.5 %collective-permute-start.18 = (bf16[72,1024]{1,0:T(8,128)(2,1)S(1)}, bf16[72,1024]{1,0:T(8,128)(2,1)S(1)}, u32[]{:S(2)}, u32[]{:S(2)}) collective-permute-start(bf16[72,1024]{1,0:T(8,128)(2,1)S(1)} %collective-permute-done.16.refs_7_), channel_id=1, source_target_pairs={{0,2},{1,3},{4,0},{5,1},{8,4},{9,5},{12,8},{13,9},{14,12},{15,13},... | collective-permute-start | bytes 442376 | tf_op jit(solution)/shard_map/ppermute | solution.py:308
  23.0 1.9 %collective-permute-start.7 = (bf16[72,1024]{1,0:T(8,128)(2,1)S(1)}, bf16[72,1024]{1,0:T(8,128)(2,1)S(1)}, u32[]{:S(2)}, u32[]{:S(2)}) collective-permute-start(bf16[72,1024]{1,0:T(8,128)(2,1)S(1)} %collective-permute-done.5.refs_7_), channel_id=1, source_target_pairs={{0,2},{1,3},{4,0},{5,1},{8,4},{9,5},{12,8},{13,9},{14,12},{15,13},... | collective-permute-start | bytes 442376 | tf_op jit(solution)/shard_map/ppermute | solution.py:308
  25.1 1.6 %collective-permute-done.18.refs_9_ = bf16[72,1024]{1,0:T(8,128)(2,1)S(1)} collective-permute-done((bf16[72,1024]{1,0:T(8,128)(2,1)S(1)}, bf16[72,1024]{1,0:T(8,128)(2,1)S(1)}, u32[]{:S(2)}, u32[]{:S(2)}) %collective-permute-start.18) | collective-permute-done | bytes 147488 | tf_op jit(solution)/shard_map/ppermute | solution.py:308
  26.7 1.8 %collective-permute-start.20 = (bf16[32,1024]{1,0:T(8,128)(2,1)S(1)}, bf16[32,1024]{1,0:T(8,128)(2,1)S(1)}, u32[]{:S(2)}, u32[]{:S(2)}) collective-permute-start(bf16[32,1024]{1,0:T(8,128)(2,1)S(1)} %slice.52), channel_id=1, source_target_pairs={{0,2},{1,3},{4,0},{5,1},{8,4},{9,5},{12,8},{13,9},{14,12},{15,13},... | collective-permute-start | bytes 196616 | tf_op jit(solution)/shard_map/ppermute | solution.py:308
  29.4 1.6 %collective-permute-start.9 = (bf16[32,1024]{1,0:T(8,128)(2,1)S(1)}, bf16[32,1024]{1,0:T(8,128)(2,1)S(1)}, u32[]{:S(2)}, u32[]{:S(2)}) collective-permute-start(bf16[32,1024]{1,0:T(8,128)(2,1)S(1)} %slice.50), channel_id=1, source_target_pairs={{0,2},{1,3},{4,0},{5,1},{8,4},{9,5},{12,8},{13,9},{14,12},{15,13},... | collective-permute-start | bytes 196616 | tf_op jit(solution)/shard_map/ppermute | solution.py:308
  31.7 1.6 %shard_map.95.total_ref = f32[384,1024]{1,0:T(8,128)S(1)} custom-call(bf16[2,8,96,72]{3,2,1,0:T(8,128)(2,1)S(1)} %get-tuple-element.38.refs_0_.mine_ref, bf16[2,8,96,72]{3,2,1,0:T(8,128)(2,1)S(1)} %collective-permute-done.refs_1_.given_ref, bf16[2,8,96,72]{3,2,1,0:T(8,128)(2,1)S(1)} %collective-permute-done.1.refs_2_.theirs_ref, ...), custom_call_target="tpu_custom_call" | custom-call | flops 452984832 | bytes 1572864 | tf_op jit(solution)/shard_map/pallas_call | solution.py:110
  33.2 1.6 %shard_map.92.total_ref = f32[384,1024]{1,0:T(8,128)S(1)} custom-call(bf16[2,8,96,72]{3,2,1,0:T(8,128)(2,1)S(1)} %get-tuple-element.38.refs_0_.mine_ref, bf16[2,8,96,72]{3,2,1,0:T(8,128)(2,1)S(1)} %collective-permute-done.refs_1_.given_ref, bf16[2,8,96,72]{3,2,1,0:T(8,128)(2,1)S(1)} %collective-permute-done.1.refs_2_.theirs_ref, ...), custom_call_target="tpu_custom_call" | custom-call | flops 452984832 | bytes 1572864 | tf_op jit(solution)/shard_map/pallas_call | solution.py:110
  37.3 1.6 %collective-permute-start.23 = (bf16[96,1024]{1,0:T(8,128)(2,1)S(1)}, bf16[96,1024]{1,0:T(8,128)(2,1)S(1)}, u32[]{:S(2)}, u32[]{:S(2)}) collective-permute-start(bf16[96,1024]{1,0:T(8,128)(2,1)S(1)} %shard_map.97), channel_id=1, source_target_pairs={{0,16},{16,0},{1,17},{17,1},{2,18},{18,2},{3,19},{19,3},{4,20},{20... | collective-permute-start | bytes 589832 | tf_op jit(solution)/shard_map/ppermute | solution.py:349
  39.8 5.3 %collective-permute-done.23.refs_5_ = bf16[96,1024]{1,0:T(8,128)(2,1)S(1)} collective-permute-done((bf16[96,1024]{1,0:T(8,128)(2,1)S(1)}, bf16[96,1024]{1,0:T(8,128)(2,1)S(1)}, u32[]{:S(2)}, u32[]{:S(2)}) %collective-permute-start.23) | collective-permute-done | bytes 196640 | tf_op jit(solution)/shard_map/ppermute | solution.py:349
  45.1 3.4 %collective-permute-done.12.refs_2_ = bf16[96,1024]{1,0:T(8,128)(2,1)S(1)} collective-permute-done((bf16[96,1024]{1,0:T(8,128)(2,1)S(1)}, bf16[96,1024]{1,0:T(8,128)(2,1)S(1)}, u32[]{:S(2)}, u32[]{:S(2)}) %collective-permute-start.12) | collective-permute-done | bytes 196640 | tf_op jit(solution)/shard_map/ppermute | solution.py:349
  48.8 1.6 %collective-permute-start.57 = (bf16[48,2048]{1,0:T(8,128)(2,1)S(1)}, bf16[48,2048]{1,0:T(8,128)(2,1)S(1)}, u32[]{:S(2)}, u32[]{:S(2)}) collective-permute-start(bf16[48,2048]{1,0:T(8,128)(2,1)S(1)} %get-tuple-element.60.refs_0_), channel_id=1, source_target_pairs={{0,2},{1,3},{4,0},{5,1},{8,4},{9,5},{12,8},{13,9},{14,12},{15,13},... | collective-permute-start | bytes 589832 | tf_op jit(solution)/shard_map/ppermute | solution.py:308
  50.9 1.5 %collective-permute-start.27 = (bf16[48,2176]{1,0:T(8,128)(2,1)S(1)}, bf16[48,2176]{1,0:T(8,128)(2,1)S(1)}, u32[]{:S(2)}, u32[]{:S(2)}) collective-permute-start(bf16[48,2176]{1,0:T(8,128)(2,1)S(1)} %get-tuple-element.49.refs_0_.refs_2_), channel_id=1, source_target_pairs={{0,2},{1,3},{4,0},{5,1},{8,4},{9,5},{12,8},{13,9},{14,12},{15,13},... | collective-permute-start | bytes 626696 | tf_op jit(solution)/shard_map/ppermute | solution.py:308
  52.9 3.7 %collective-permute-done.57.refs_1_ = bf16[48,2048]{1,0:T(8,128)(2,1)S(1)} collective-permute-done((bf16[48,2048]{1,0:T(8,128)(2,1)S(1)}, bf16[48,2048]{1,0:T(8,128)(2,1)S(1)}, u32[]{:S(2)}, u32[]{:S(2)}) %collective-permute-start.57) | collective-permute-done | bytes 196640 | tf_op jit(solution)/shard_map/ppermute | solution.py:308
  56.7 1.5 %collective-permute-start.62 = (bf16[48,2048]{1,0:T(8,128)(2,1)S(1)}, bf16[48,2048]{1,0:T(8,128)(2,1)S(1)}, u32[]{:S(2)}, u32[]{:S(2)}) collective-permute-start(bf16[48,2048]{1,0:T(8,128)(2,1)S(1)} %collective-permute-done.57.refs_1_), channel_id=1, source_target_pairs={{0,2},{1,3},{4,0},{5,1},{8,4},{9,5},{12,8},{13,9},{14,12},{15,13},... | collective-permute-start | bytes 589832 | tf_op jit(solution)/shard_map/ppermute | solution.py:308
  58.7 2.4 %collective-permute-done.27.refs_1_.refs_5_ = bf16[48,2176]{1,0:T(8,128)(2,1)S(1)} collective-permute-done((bf16[48,2176]{1,0:T(8,128)(2,1)S(1)}, bf16[48,2176]{1,0:T(8,128)(2,1)S(1)}, u32[]{:S(2)}, u32[]{:S(2)}) %collective-permute-start.27) | collective-permute-done | bytes 208928 | tf_op jit(solution)/shard_map/ppermute | solution.py:308
  61.1 1.5 %collective-permute-start.32 = (bf16[48,2176]{1,0:T(8,128)(2,1)S(1)}, bf16[48,2176]{1,0:T(8,128)(2,1)S(1)}, u32[]{:S(2)}, u32[]{:S(2)}) collective-permute-start(bf16[48,2176]{1,0:T(8,128)(2,1)S(1)} %collective-permute-done.27.refs_1_.refs_5_), channel_id=1, source_target_pairs={{0,2},{1,3},{4,0},{5,1},{8,4},{9,5},{12,8},{13,9},{14,12},{15,13},... | collective-permute-start | bytes 626696 | tf_op jit(solution)/shard_map/ppermute | solution.py:308
  63.2 2.2 %collective-permute-done.62.refs_1_ = bf16[48,2048]{1,0:T(8,128)(2,1)S(1)} collective-permute-done((bf16[48,2048]{1,0:T(8,128)(2,1)S(1)}, bf16[48,2048]{1,0:T(8,128)(2,1)S(1)}, u32[]{:S(2)}, u32[]{:S(2)}) %collective-permute-start.62) | collective-permute-done | bytes 196640 | tf_op jit(solution)/shard_map/ppermute | solution.py:308
  65.3 1.5 %collective-permute-start.67 = (bf16[48,2048]{1,0:T(8,128)(2,1)S(1)}, bf16[48,2048]{1,0:T(8,128)(2,1)S(1)}, u32[]{:S(2)}, u32[]{:S(2)}) collective-permute-start(bf16[48,2048]{1,0:T(8,128)(2,1)S(1)} %collective-permute-done.62.refs_1_), channel_id=1, source_target_pairs={{0,2},{1,3},{4,0},{5,1},{8,4},{9,5},{12,8},{13,9},{14,12},{15,13},... | collective-permute-start | bytes 589832 | tf_op jit(solution)/shard_map/ppermute | solution.py:308
  67.4 2.4 %collective-permute-done.32.refs_1_.refs_5_ = bf16[48,2176]{1,0:T(8,128)(2,1)S(1)} collective-permute-done((bf16[48,2176]{1,0:T(8,128)(2,1)S(1)}, bf16[48,2176]{1,0:T(8,128)(2,1)S(1)}, u32[]{:S(2)}, u32[]{:S(2)}) %collective-permute-start.32) | collective-permute-done | bytes 208928 | tf_op jit(solution)/shard_map/ppermute | solution.py:308
  69.8 1.5 %collective-permute-start.37 = (bf16[48,2176]{1,0:T(8,128)(2,1)S(1)}, bf16[48,2176]{1,0:T(8,128)(2,1)S(1)}, u32[]{:S(2)}, u32[]{:S(2)}) collective-permute-start(bf16[48,2176]{1,0:T(8,128)(2,1)S(1)} %collective-permute-done.32.refs_1_.refs_5_), channel_id=1, source_target_pairs={{0,2},{1,3},{4,0},{5,1},{8,4},{9,5},{12,8},{13,9},{14,12},{15,13},... | collective-permute-start | bytes 626696 | tf_op jit(solution)/shard_map/ppermute | solution.py:308
  71.9 2.2 %collective-permute-done.67.refs_1_ = bf16[48,2048]{1,0:T(8,128)(2,1)S(1)} collective-permute-done((bf16[48,2048]{1,0:T(8,128)(2,1)S(1)}, bf16[48,2048]{1,0:T(8,128)(2,1)S(1)}, u32[]{:S(2)}, u32[]{:S(2)}) %collective-permute-start.67) | collective-permute-done | bytes 196640 | tf_op jit(solution)/shard_map/ppermute | solution.py:308
  74.1 1.5 %collective-permute-done.66.refs_0_ = bf16[48,2048]{1,0:T(8,128)(2,1)S(1)} collective-permute-done((bf16[48,2048]{1,0:T(8,128)(2,1)S(1)}, bf16[48,2048]{1,0:T(8,128)(2,1)S(1)}, u32[]{:S(2)}, u32[]{:S(2)}) %collective-permute-start.66) | collective-permute-done | bytes 196640 | tf_op jit(solution)/shard_map/ppermute | solution.py:308
  75.6 1.6 %collective-permute-start.72 = (bf16[24,2048]{1,0:T(8,128)(2,1)S(1)}, bf16[24,2048]{1,0:T(8,128)(2,1)S(1)}, u32[]{:S(2)}, u32[]{:S(2)}) collective-permute-start(bf16[24,2048]{1,0:T(8,128)(2,1)S(1)} %slice.56), channel_id=1, source_target_pairs={{0,2},{1,3},{4,0},{5,1},{8,4},{9,5},{12,8},{13,9},{14,12},{15,13},... | collective-permute-start | bytes 294920 | tf_op jit(solution)/shard_map/ppermute | solution.py:308
  77.2 1.3 collective-permute-start.71
  78.5 1.2 collective-permute-start.42
  79.7 1.1 collective-permute-start.41
  83.2 1.4 collective-permute-done.41.refs_0_.refs_4_
  86.9 1.7 %shard_map.117 = (bf16[48,2048]{1,0:T(8,128)(2,1)S(1)}, bf16[48,2048]{1,0:T(8,128)(2,1)S(1)}) custom-call(bf16[24,2048]{1,0:T(8,128)(2,1)S(1)} %collective-permute-done.71.refs_0_, bf16[24,2048]{1,0:T(8,128)(2,1)S(1)} %collective-permute-done.72.refs_1_, bf16[24,2048]{1,0:T(8,128)(2,1)S(1)} %collective-permute-done.73.refs_2_, ...), custom_call_target="tpu_custom_call" | custom-call | flops 905969664 | bytes 9437184 | tf_op jit(solution)/shard_map/pallas_call | solution.py:110
  89.2 2.1 %shard_map.103 = (bf16[96,2048]{1,0:T(8,128)(2,1)S(1)}, bf16[96,2048]{1,0:T(8,128)(2,1)S(1)}) custom-call(bf16[48,2176]{1,0:T(8,128)(2,1)S(1)} %collective-permute-done.36.refs_0_.refs_4_, bf16[48,2176]{1,0:T(8,128)(2,1)S(1)} %collective-permute-done.37.refs_1_.refs_5_, bf16[48,2176]{1,0:T(8,128)(2,1)S(1)} %collective-permute-done.38.refs_2_.refs_6_, ...), custom_call_target="tpu_custom_call" | custom-call | flops 1811939328 | bytes 9437184 | tf_op jit(solution)/shard_map/pallas_call | solution.py:110
  92.1 1.7 %shard_map.104 = (bf16[48,2048]{1,0:T(8,128)(2,1)S(1)}, bf16[48,2048]{1,0:T(8,128)(2,1)S(1)}) custom-call(bf16[24,2176]{1,0:T(8,128)(2,1)S(1)} %collective-permute-done.41.refs_0_.refs_4_, bf16[24,2176]{1,0:T(8,128)(2,1)S(1)} %collective-permute-done.42.refs_1_.refs_5_, bf16[24,2176]{1,0:T(8,128)(2,1)S(1)} %collective-permute-done.43.refs_2_.refs_6_, ...), custom_call_target="tpu_custom_call" | custom-call | flops 905969664 | bytes 9437184 | tf_op jit(solution)/shard_map/pallas_call | solution.py:110
  94.3 2.1 %shard_map.116 = (bf16[96,2048]{1,0:T(8,128)(2,1)S(1)}, bf16[96,2048]{1,0:T(8,128)(2,1)S(1)}) custom-call(bf16[48,2048]{1,0:T(8,128)(2,1)S(1)} %collective-permute-done.66.refs_0_, bf16[48,2048]{1,0:T(8,128)(2,1)S(1)} %collective-permute-done.67.refs_1_, bf16[48,2048]{1,0:T(8,128)(2,1)S(1)} %collective-permute-done.68.refs_2_, ...), custom_call_target="tpu_custom_call" | custom-call | flops 1811939328 | bytes 9437184 | tf_op jit(solution)/shard_map/pallas_call | solution.py:110
  98.0 2.1 %shard_map.115 = (bf16[96,2048]{1,0:T(8,128)(2,1)S(1)}, bf16[96,2048]{1,0:T(8,128)(2,1)S(1)}) custom-call(bf16[48,2048]{1,0:T(8,128)(2,1)S(1)} %collective-permute-done.61.refs_0_, bf16[48,2048]{1,0:T(8,128)(2,1)S(1)} %collective-permute-done.62.refs_1_, bf16[48,2048]{1,0:T(8,128)(2,1)S(1)} %collective-permute-done.63.refs_2_, ...), custom_call_target="tpu_custom_call" | custom-call | flops 1811939328 | bytes 9437184 | tf_op jit(solution)/shard_map/pallas_call | solution.py:110
  100.7 1.4 collective-permute-done.76.refs_0_
  102.2 1.6 %collective-permute-start.80 = (bf16[24,2048]{1,0:T(8,128)(2,1)S(1)}, bf16[24,2048]{1,0:T(8,128)(2,1)S(1)}, u32[]{:S(2)}, u32[]{:S(2)}) collective-permute-start(bf16[24,2048]{1,0:T(8,128)(2,1)S(1)} %shard_map.122), channel_id=1, source_target_pairs={{0,2},{1,3},{4,0},{5,1},{8,4},{9,5},{12,8},{13,9},{14,12},{15,13},... | collective-permute-start | bytes 294920 | tf_op jit(solution)/shard_map/ppermute | solution.py:308
  103.7 2.1 %shard_map.102 = (bf16[96,2048]{1,0:T(8,128)(2,1)S(1)}, bf16[96,2048]{1,0:T(8,128)(2,1)S(1)}) custom-call(bf16[48,2176]{1,0:T(8,128)(2,1)S(1)} %collective-permute-done.31.refs_0_.refs_4_, bf16[48,2176]{1,0:T(8,128)(2,1)S(1)} %collective-permute-done.32.refs_1_.refs_5_, bf16[48,2176]{1,0:T(8,128)(2,1)S(1)} %collective-permute-done.33.refs_2_.refs_6_, ...), custom_call_target="tpu_custom_call" | custom-call | flops 1811939328 | bytes 9437184 | tf_op jit(solution)/shard_map/pallas_call | solution.py:110
  106.8 0.9 collective-permute-start.46
  107.9 1.6 %collective-permute-start.77 = (bf16[48,2048]{1,0:T(8,128)(2,1)S(1)}, bf16[48,2048]{1,0:T(8,128)(2,1)S(1)}, u32[]{:S(2)}, u32[]{:S(2)}) collective-permute-start(bf16[48,2048]{1,0:T(8,128)(2,1)S(1)} %shard_map.119), channel_id=1, source_target_pairs={{0,4},{1,5},{4,8},{5,9},{8,12},{9,13},{12,14},{13,15},{14,10},{15,... | collective-permute-start | bytes 589832 | tf_op jit(solution)/shard_map/ppermute | solution.py:308
  109.6 3.0 %collective-permute-done.46.refs_0_ = bf16[24,2048]{1,0:T(8,128)(2,1)S(1)} collective-permute-done((bf16[24,2048]{1,0:T(8,128)(2,1)S(1)}, bf16[24,2048]{1,0:T(8,128)(2,1)S(1)}, u32[]{:S(2)}, u32[]{:S(2)}) %collective-permute-start.46) | collective-permute-done | bytes 98336 | tf_op jit(solution)/shard_map/ppermute | solution.py:308
  112.5 1.6 %collective-permute-start.50 = (bf16[24,2048]{1,0:T(8,128)(2,1)S(1)}, bf16[24,2048]{1,0:T(8,128)(2,1)S(1)}, u32[]{:S(2)}, u32[]{:S(2)}) collective-permute-start(bf16[24,2048]{1,0:T(8,128)(2,1)S(1)} %shard_map.109), channel_id=1, source_target_pairs={{0,2},{1,3},{4,0},{5,1},{8,4},{9,5},{12,8},{13,9},{14,12},{15,13},... | collective-permute-start | bytes 294920 | tf_op jit(solution)/shard_map/ppermute | solution.py:308
  114.1 1.6 %collective-permute-start.81 = (bf16[48,2048]{1,0:T(8,128)(2,1)S(1)}, bf16[48,2048]{1,0:T(8,128)(2,1)S(1)}, u32[]{:S(2)}, u32[]{:S(2)}) collective-permute-start(bf16[48,2048]{1,0:T(8,128)(2,1)S(1)} %shard_map.123), channel_id=1, source_target_pairs={{0,2},{1,3},{4,0},{5,1},{8,4},{9,5},{12,8},{13,9},{14,12},{15,13},... | collective-permute-start | bytes 589832 | tf_op jit(solution)/shard_map/ppermute | solution.py:308
  115.7 2.1 %shard_map.114 = (bf16[96,2048]{1,0:T(8,128)(2,1)S(1)}, bf16[96,2048]{1,0:T(8,128)(2,1)S(1)}) custom-call(bf16[48,2048]{1,0:T(8,128)(2,1)S(1)} %collective-permute-done.56.refs_0_, bf16[48,2048]{1,0:T(8,128)(2,1)S(1)} %collective-permute-done.57.refs_1_, bf16[48,2048]{1,0:T(8,128)(2,1)S(1)} %collective-permute-done.58.refs_2_, ...), custom_call_target="tpu_custom_call" | custom-call | flops 1811939328 | bytes 9437184 | tf_op jit(solution)/shard_map/pallas_call | solution.py:110
  119.3 1.2 collective-permute-start.51
  120.4 2.1 %shard_map.101 = (bf16[96,2048]{1,0:T(8,128)(2,1)S(1)}, bf16[96,2048]{1,0:T(8,128)(2,1)S(1)}) custom-call(bf16[48,2176]{1,0:T(8,128)(2,1)S(1)} %collective-permute-done.26.refs_0_.refs_4_, bf16[48,2176]{1,0:T(8,128)(2,1)S(1)} %collective-permute-done.27.refs_1_.refs_5_, bf16[48,2176]{1,0:T(8,128)(2,1)S(1)} %collective-permute-done.28.refs_2_.refs_6_, ...), custom_call_target="tpu_custom_call" | custom-call | flops 1811939328 | bytes 9437184 | tf_op jit(solution)/shard_map/pallas_call | solution.py:110
  122.9 2.4 %collective-permute-done.47.refs_0_ = bf16[48,2048]{1,0:T(8,128)(2,1)S(1)} collective-permute-done((bf16[48,2048]{1,0:T(8,128)(2,1)S(1)}, bf16[48,2048]{1,0:T(8,128)(2,1)S(1)}, u32[]{:S(2)}, u32[]{:S(2)}) %collective-permute-start.47) | collective-permute-done | bytes 196640 | tf_op jit(solution)/shard_map/ppermute | solution.py:308
  125.9 1.6 %collective-permute-start.82 = (bf16[48,2048]{1,0:T(8,128)(2,1)S(1)}, bf16[48,2048]{1,0:T(8,128)(2,1)S(1)}, u32[]{:S(2)}, u32[]{:S(2)}) collective-permute-start(bf16[48,2048]{1,0:T(8,128)(2,1)S(1)} %shard_map.124), channel_id=1, source_target_pairs={{0,2},{1,3},{4,0},{5,1},{8,4},{9,5},{12,8},{13,9},{14,12},{15,13},... | collective-permute-start | bytes 589832 | tf_op jit(solution)/shard_map/ppermute | solution.py:308
  128.1 1.7 %shard_map.113 = (bf16[48,2048]{1,0:T(8,128)(2,1)S(1)}, bf16[48,2048]{1,0:T(8,128)(2,1)S(1)}) custom-call(bf16[48,2048]{1,0:T(8,128)(2,1)S(1)} %get-tuple-element.60.refs_0_, bf16[48,2048]{1,0:T(8,128)(2,1)S(1)} %collective-permute-done.54.refs_1_, bf16[48,2176]{1,0:T(8,128)(2,1)S(1)} %get-tuple-element.49.refs_0_.refs_2_, ...), custom_call_target="tpu_custom_call" | custom-call | flops 905969664 | bytes 9437184 | tf_op jit(solution)/shard_map/pallas_call | solution.py:110
  129.9 1.5 collective-permute-start.52
  131.4 1.7 %collective-permute-done.78.refs_0_ = bf16[48,2048]{1,0:T(8,128)(2,1)S(1)} collective-permute-done((bf16[48,2048]{1,0:T(8,128)(2,1)S(1)}, bf16[48,2048]{1,0:T(8,128)(2,1)S(1)}, u32[]{:S(2)}, u32[]{:S(2)}) %collective-permute-start.78) | collective-permute-done | bytes 196640 | tf_op jit(solution)/shard_map/ppermute | solution.py:308
  133.0 1.7 %shard_map.100 = (bf16[48,2048]{1,0:T(8,128)(2,1)S(1)}, bf16[48,2048]{1,0:T(8,128)(2,1)S(1)}) custom-call(bf16[48,2176]{1,0:T(8,128)(2,1)S(1)} %get-tuple-element.49.refs_0_.refs_2_, bf16[48,2176]{1,0:T(8,128)(2,1)S(1)} %collective-permute-done.24.refs_1_.refs_3_, bf16[2048,768]{1,0:T(8,128)(2,1)S(1)} %bitcast.16, bf16[2048,768]{1,0:T(8,128)(2,1)S(1)} %bitcast.26, ...), custom_call_target="tpu_custom_call" | custom-call | flops 905969664 | bytes 9437184 | tf_op jit(solution)/shard_map/pallas_call | solution.py:110
  135.7 1.9 %collective-permute-start.83 = (bf16[48,2048]{1,0:T(8,128)(2,1)S(1)}, bf16[48,2048]{1,0:T(8,128)(2,1)S(1)}, u32[]{:S(2)}, u32[]{:S(2)}) collective-permute-start(bf16[48,2048]{1,0:T(8,128)(2,1)S(1)} %shard_map.125), channel_id=1, source_target_pairs={{0,2},{1,3},{4,0},{5,1},{8,4},{9,5},{12,8},{13,9},{14,12},{15,13},... | collective-permute-start | bytes 589832 | tf_op jit(solution)/shard_map/ppermute | solution.py:308
  137.9 1.9 %collective-permute-start.53 = (bf16[48,2048]{1,0:T(8,128)(2,1)S(1)}, bf16[48,2048]{1,0:T(8,128)(2,1)S(1)}, u32[]{:S(2)}, u32[]{:S(2)}) collective-permute-start(bf16[48,2048]{1,0:T(8,128)(2,1)S(1)} %shard_map.112), channel_id=1, source_target_pairs={{0,2},{1,3},{4,0},{5,1},{8,4},{9,5},{12,8},{13,9},{14,12},{15,13},... | collective-permute-start | bytes 589832 | tf_op jit(solution)/shard_map/ppermute | solution.py:308
  139.9 3.4 %collective-permute-done.79.refs_6_ = bf16[48,2048]{1,0:T(8,128)(2,1)S(1)} collective-permute-done((bf16[48,2048]{1,0:T(8,128)(2,1)S(1)}, bf16[48,2048]{1,0:T(8,128)(2,1)S(1)}, u32[]{:S(2)}, u32[]{:S(2)}) %collective-permute-start.79) | collective-permute-done | bytes 196640 | tf_op jit(solution)/shard_map/ppermute | solution.py:308
  143.5 3.1 %collective-permute-done.49.refs_2_ = bf16[48,2048]{1,0:T(8,128)(2,1)S(1)} collective-permute-done((bf16[48,2048]{1,0:T(8,128)(2,1)S(1)}, bf16[48,2048]{1,0:T(8,128)(2,1)S(1)}, u32[]{:S(2)}, u32[]{:S(2)}) %collective-permute-start.49) | collective-permute-done | bytes 196640 | tf_op jit(solution)/shard_map/ppermute | solution.py:308
  146.6 1.0 shard_map.126
  (168 shorter events, 25.0 us)
Async XLA Ops:
  4.1 14.2 %collective-permute-start = (bf16[2,8,96,72]{3,2,1,0:T(8,128)(2,1)S(1)}, bf16[2,8,96,72]{3,2,1,0:T(8,128)(2,1)S(1)}, u32[]{:S(2)}, u32[]{:S(2)}) collective-permute-start(bf16[2,8,96,72]{3,2,1,0:T(8,128)(2,1)S(1)} %get-tuple-element.39), channel_id=1, source_target_pairs={{0,1},{1,0},{2,3},{3,2},{4,5},{5,4},{6,7},{7,6},{8,9},{9,8},{10,11... | collective-permute-start | bytes 663560 | tf_op jit(solution)/shard_map/ppermute | solution.py:314
  5.8 7.3 %collective-permute-start.14 = (bf16[72,1024]{1,0:T(8,128)(2,1)S(1)}, bf16[72,1024]{1,0:T(8,128)(2,1)S(1)}, u32[]{:S(2)}, u32[]{:S(2)}) collective-permute-start(bf16[72,1024]{1,0:T(8,128)(2,1)S(1)} %get-tuple-element.71.refs_3_), channel_id=1, source_target_pairs={{0,2},{1,3},{4,0},{5,1},{8,4},{9,5},{12,8},{13,9},{14,12},{15,13},... | collective-permute-start | bytes 442376 | tf_op jit(solution)/shard_map/ppermute | solution.py:308
  8.3 6.7 %collective-permute-start.13 = (bf16[72,1024]{1,0:T(8,128)(2,1)S(1)}, bf16[72,1024]{1,0:T(8,128)(2,1)S(1)}, u32[]{:S(2)}, u32[]{:S(2)}) collective-permute-start(bf16[72,1024]{1,0:T(8,128)(2,1)S(1)} %get-tuple-element.71.refs_3_), channel_id=1, source_target_pairs={{0,4},{1,5},{4,8},{5,9},{8,12},{9,13},{12,14},{13,15},{14,10},{15,... | collective-permute-start | bytes 442376 | tf_op jit(solution)/shard_map/ppermute | solution.py:308
  8.5 7.8 %collective-permute-start.3 = (bf16[72,1024]{1,0:T(8,128)(2,1)S(1)}, bf16[72,1024]{1,0:T(8,128)(2,1)S(1)}, u32[]{:S(2)}, u32[]{:S(2)}) collective-permute-start(bf16[72,1024]{1,0:T(8,128)(2,1)S(1)} %get-tuple-element.72.refs_3_), channel_id=1, source_target_pairs={{0,2},{1,3},{4,0},{5,1},{8,4},{9,5},{12,8},{13,9},{14,12},{15,13},... | collective-permute-start | bytes 442376 | tf_op jit(solution)/shard_map/ppermute | solution.py:308
  10.3 7.9 %collective-permute-start.2 = (bf16[72,1024]{1,0:T(8,128)(2,1)S(1)}, bf16[72,1024]{1,0:T(8,128)(2,1)S(1)}, u32[]{:S(2)}, u32[]{:S(2)}) collective-permute-start(bf16[72,1024]{1,0:T(8,128)(2,1)S(1)} %get-tuple-element.72.refs_3_), channel_id=1, source_target_pairs={{0,4},{1,5},{4,8},{5,9},{8,12},{9,13},{12,14},{13,15},{14,10},{15,... | collective-permute-start | bytes 442376 | tf_op jit(solution)/shard_map/ppermute | solution.py:308
  13.1 7.3 %collective-permute-start.16 = (bf16[72,1024]{1,0:T(8,128)(2,1)S(1)}, bf16[72,1024]{1,0:T(8,128)(2,1)S(1)}, u32[]{:S(2)}, u32[]{:S(2)}) collective-permute-start(bf16[72,1024]{1,0:T(8,128)(2,1)S(1)} %collective-permute-done.14.refs_5_), channel_id=1, source_target_pairs={{0,2},{1,3},{4,0},{5,1},{8,4},{9,5},{12,8},{13,9},{14,12},{15,13},... | collective-permute-start | bytes 442376 | tf_op jit(solution)/shard_map/ppermute | solution.py:308
  15.0 6.9 %collective-permute-start.15 = (bf16[72,1024]{1,0:T(8,128)(2,1)S(1)}, bf16[72,1024]{1,0:T(8,128)(2,1)S(1)}, u32[]{:S(2)}, u32[]{:S(2)}) collective-permute-start(bf16[72,1024]{1,0:T(8,128)(2,1)S(1)} %collective-permute-done.13.refs_4_), channel_id=1, source_target_pairs={{0,4},{1,5},{4,8},{5,9},{8,12},{9,13},{12,14},{13,15},{14,10},{15,... | collective-permute-start | bytes 442376 | tf_op jit(solution)/shard_map/ppermute | solution.py:308
  16.3 6.7 %collective-permute-start.5 = (bf16[72,1024]{1,0:T(8,128)(2,1)S(1)}, bf16[72,1024]{1,0:T(8,128)(2,1)S(1)}, u32[]{:S(2)}, u32[]{:S(2)}) collective-permute-start(bf16[72,1024]{1,0:T(8,128)(2,1)S(1)} %collective-permute-done.3.refs_5_), channel_id=1, source_target_pairs={{0,2},{1,3},{4,0},{5,1},{8,4},{9,5},{12,8},{13,9},{14,12},{15,13},... | collective-permute-start | bytes 442376 | tf_op jit(solution)/shard_map/ppermute | solution.py:308
  18.2 6.7 %collective-permute-start.4 = (bf16[72,1024]{1,0:T(8,128)(2,1)S(1)}, bf16[72,1024]{1,0:T(8,128)(2,1)S(1)}, u32[]{:S(2)}, u32[]{:S(2)}) collective-permute-start(bf16[72,1024]{1,0:T(8,128)(2,1)S(1)} %collective-permute-done.2.refs_4_), channel_id=1, source_target_pairs={{0,4},{1,5},{4,8},{5,9},{8,12},{9,13},{12,14},{13,15},{14,10},{15,... | collective-permute-start | bytes 442376 | tf_op jit(solution)/shard_map/ppermute | solution.py:308
  18.5 13.2 %collective-permute-start.1 = (bf16[2,8,96,72]{3,2,1,0:T(8,128)(2,1)S(1)}, bf16[2,8,96,72]{3,2,1,0:T(8,128)(2,1)S(1)}, u32[]{:S(2)}, u32[]{:S(2)}) collective-permute-start(bf16[2,8,96,72]{3,2,1,0:T(8,128)(2,1)S(1)} %pad_maximum_fusion), channel_id=1, source_target_pairs={{0,16},{16,0},{1,17},{17,1},{2,18},{18,2},{3,19},{19,3},{4,20},{20... | collective-permute-start | bytes 663560 | tf_op jit(solution)/shard_map/ppermute | solution.py:316
  20.4 6.2 %collective-permute-start.18 = (bf16[72,1024]{1,0:T(8,128)(2,1)S(1)}, bf16[72,1024]{1,0:T(8,128)(2,1)S(1)}, u32[]{:S(2)}, u32[]{:S(2)}) collective-permute-start(bf16[72,1024]{1,0:T(8,128)(2,1)S(1)} %collective-permute-done.16.refs_7_), channel_id=1, source_target_pairs={{0,2},{1,3},{4,0},{5,1},{8,4},{9,5},{12,8},{13,9},{14,12},{15,13},... | collective-permute-start | bytes 442376 | tf_op jit(solution)/shard_map/ppermute | solution.py:308
  21.9 6.6 %collective-permute-start.17 = (bf16[72,1024]{1,0:T(8,128)(2,1)S(1)}, bf16[72,1024]{1,0:T(8,128)(2,1)S(1)}, u32[]{:S(2)}, u32[]{:S(2)}) collective-permute-start(bf16[72,1024]{1,0:T(8,128)(2,1)S(1)} %collective-permute-done.15.refs_6_), channel_id=1, source_target_pairs={{0,4},{1,5},{4,8},{5,9},{8,12},{9,13},{12,14},{13,15},{14,10},{15,... | collective-permute-start | bytes 442376 | tf_op jit(solution)/shard_map/ppermute | solution.py:308
  23.0 6.5 %collective-permute-start.7 = (bf16[72,1024]{1,0:T(8,128)(2,1)S(1)}, bf16[72,1024]{1,0:T(8,128)(2,1)S(1)}, u32[]{:S(2)}, u32[]{:S(2)}) collective-permute-start(bf16[72,1024]{1,0:T(8,128)(2,1)S(1)} %collective-permute-done.5.refs_7_), channel_id=1, source_target_pairs={{0,2},{1,3},{4,0},{5,1},{8,4},{9,5},{12,8},{13,9},{14,12},{15,13},... | collective-permute-start | bytes 442376 | tf_op jit(solution)/shard_map/ppermute | solution.py:308
  24.9 6.2 %collective-permute-start.6 = (bf16[72,1024]{1,0:T(8,128)(2,1)S(1)}, bf16[72,1024]{1,0:T(8,128)(2,1)S(1)}, u32[]{:S(2)}, u32[]{:S(2)}) collective-permute-start(bf16[72,1024]{1,0:T(8,128)(2,1)S(1)} %collective-permute-done.4.refs_6_), channel_id=1, source_target_pairs={{0,4},{1,5},{4,8},{5,9},{8,12},{9,13},{12,14},{13,15},{14,10},{15,... | collective-permute-start | bytes 442376 | tf_op jit(solution)/shard_map/ppermute | solution.py:308
  26.7 8.1 %collective-permute-start.20 = (bf16[32,1024]{1,0:T(8,128)(2,1)S(1)}, bf16[32,1024]{1,0:T(8,128)(2,1)S(1)}, u32[]{:S(2)}, u32[]{:S(2)}) collective-permute-start(bf16[32,1024]{1,0:T(8,128)(2,1)S(1)} %slice.52), channel_id=1, source_target_pairs={{0,2},{1,3},{4,0},{5,1},{8,4},{9,5},{12,8},{13,9},{14,12},{15,13},... | collective-permute-start | bytes 196616 | tf_op jit(solution)/shard_map/ppermute | solution.py:308
  28.6 6.2 %collective-permute-start.19 = (bf16[40,1024]{1,0:T(8,128)(2,1)S(1)}, bf16[40,1024]{1,0:T(8,128)(2,1)S(1)}, u32[]{:S(2)}, u32[]{:S(2)}) collective-permute-start(bf16[40,1024]{1,0:T(8,128)(2,1)S(1)} %slice.51), channel_id=1, source_target_pairs={{0,4},{1,5},{4,8},{5,9},{8,12},{9,13},{12,14},{13,15},{14,10},{15,... | collective-permute-start | bytes 245768 | tf_op jit(solution)/shard_map/ppermute | solution.py:308
  29.4 6.1 %collective-permute-start.9 = (bf16[32,1024]{1,0:T(8,128)(2,1)S(1)}, bf16[32,1024]{1,0:T(8,128)(2,1)S(1)}, u32[]{:S(2)}, u32[]{:S(2)}) collective-permute-start(bf16[32,1024]{1,0:T(8,128)(2,1)S(1)} %slice.50), channel_id=1, source_target_pairs={{0,2},{1,3},{4,0},{5,1},{8,4},{9,5},{12,8},{13,9},{14,12},{15,13},... | collective-permute-start | bytes 196616 | tf_op jit(solution)/shard_map/ppermute | solution.py:308
  37.3 7.8 %collective-permute-start.23 = (bf16[96,1024]{1,0:T(8,128)(2,1)S(1)}, bf16[96,1024]{1,0:T(8,128)(2,1)S(1)}, u32[]{:S(2)}, u32[]{:S(2)}) collective-permute-start(bf16[96,1024]{1,0:T(8,128)(2,1)S(1)} %shard_map.97), channel_id=1, source_target_pairs={{0,16},{16,0},{1,17},{17,1},{2,18},{18,2},{3,19},{19,3},{4,20},{20... | collective-permute-start | bytes 589832 | tf_op jit(solution)/shard_map/ppermute | solution.py:349
  38.9 9.6 %collective-permute-start.12 = (bf16[96,1024]{1,0:T(8,128)(2,1)S(1)}, bf16[96,1024]{1,0:T(8,128)(2,1)S(1)}, u32[]{:S(2)}, u32[]{:S(2)}) collective-permute-start(bf16[96,1024]{1,0:T(8,128)(2,1)S(1)} %shard_map.94), channel_id=1, source_target_pairs={{0,16},{16,0},{1,17},{17,1},{2,18},{18,2},{3,19},{19,3},{4,20},{20... | collective-permute-start | bytes 589832 | tf_op jit(solution)/shard_map/ppermute | solution.py:349
  48.8 7.8 %collective-permute-start.57 = (bf16[48,2048]{1,0:T(8,128)(2,1)S(1)}, bf16[48,2048]{1,0:T(8,128)(2,1)S(1)}, u32[]{:S(2)}, u32[]{:S(2)}) collective-permute-start(bf16[48,2048]{1,0:T(8,128)(2,1)S(1)} %get-tuple-element.60.refs_0_), channel_id=1, source_target_pairs={{0,2},{1,3},{4,0},{5,1},{8,4},{9,5},{12,8},{13,9},{14,12},{15,13},... | collective-permute-start | bytes 589832 | tf_op jit(solution)/shard_map/ppermute | solution.py:308
  50.4 7.8 %collective-permute-start.56 = (bf16[48,2048]{1,0:T(8,128)(2,1)S(1)}, bf16[48,2048]{1,0:T(8,128)(2,1)S(1)}, u32[]{:S(2)}, u32[]{:S(2)}) collective-permute-start(bf16[48,2048]{1,0:T(8,128)(2,1)S(1)} %get-tuple-element.60.refs_0_), channel_id=1, source_target_pairs={{0,4},{1,5},{4,8},{5,9},{8,12},{9,13},{12,14},{13,15},{14,10},{15,... | collective-permute-start | bytes 589832 | tf_op jit(solution)/shard_map/ppermute | solution.py:308
  50.9 10.2 %collective-permute-start.27 = (bf16[48,2176]{1,0:T(8,128)(2,1)S(1)}, bf16[48,2176]{1,0:T(8,128)(2,1)S(1)}, u32[]{:S(2)}, u32[]{:S(2)}) collective-permute-start(bf16[48,2176]{1,0:T(8,128)(2,1)S(1)} %get-tuple-element.49.refs_0_.refs_2_), channel_id=1, source_target_pairs={{0,2},{1,3},{4,0},{5,1},{8,4},{9,5},{12,8},{13,9},{14,12},{15,13},... | collective-permute-start | bytes 626696 | tf_op jit(solution)/shard_map/ppermute | solution.py:308
  52.4 10.2 %collective-permute-start.26 = (bf16[48,2176]{1,0:T(8,128)(2,1)S(1)}, bf16[48,2176]{1,0:T(8,128)(2,1)S(1)}, u32[]{:S(2)}, u32[]{:S(2)}) collective-permute-start(bf16[48,2176]{1,0:T(8,128)(2,1)S(1)} %get-tuple-element.49.refs_0_.refs_2_), channel_id=1, source_target_pairs={{0,4},{1,5},{4,8},{5,9},{8,12},{9,13},{12,14},{13,15},{14,10},{15,... | collective-permute-start | bytes 626696 | tf_op jit(solution)/shard_map/ppermute | solution.py:308
  56.7 8.7 %collective-permute-start.62 = (bf16[48,2048]{1,0:T(8,128)(2,1)S(1)}, bf16[48,2048]{1,0:T(8,128)(2,1)S(1)}, u32[]{:S(2)}, u32[]{:S(2)}) collective-permute-start(bf16[48,2048]{1,0:T(8,128)(2,1)S(1)} %collective-permute-done.57.refs_1_), channel_id=1, source_target_pairs={{0,2},{1,3},{4,0},{5,1},{8,4},{9,5},{12,8},{13,9},{14,12},{15,13},... | collective-permute-start | bytes 589832 | tf_op jit(solution)/shard_map/ppermute | solution.py:308
  58.2 8.7 %collective-permute-start.61 = (bf16[48,2048]{1,0:T(8,128)(2,1)S(1)}, bf16[48,2048]{1,0:T(8,128)(2,1)S(1)}, u32[]{:S(2)}, u32[]{:S(2)}) collective-permute-start(bf16[48,2048]{1,0:T(8,128)(2,1)S(1)} %collective-permute-done.56.refs_0_), channel_id=1, source_target_pairs={{0,4},{1,5},{4,8},{5,9},{8,12},{9,13},{12,14},{13,15},{14,10},{15,... | collective-permute-start | bytes 589832 | tf_op jit(solution)/shard_map/ppermute | solution.py:308
  61.1 8.7 %collective-permute-start.32 = (bf16[48,2176]{1,0:T(8,128)(2,1)S(1)}, bf16[48,2176]{1,0:T(8,128)(2,1)S(1)}, u32[]{:S(2)}, u32[]{:S(2)}) collective-permute-start(bf16[48,2176]{1,0:T(8,128)(2,1)S(1)} %collective-permute-done.27.refs_1_.refs_5_), channel_id=1, source_target_pairs={{0,2},{1,3},{4,0},{5,1},{8,4},{9,5},{12,8},{13,9},{14,12},{15,13},... | collective-permute-start | bytes 626696 | tf_op jit(solution)/shard_map/ppermute | solution.py:308
  62.7 8.7 %collective-permute-start.31 = (bf16[48,2176]{1,0:T(8,128)(2,1)S(1)}, bf16[48,2176]{1,0:T(8,128)(2,1)S(1)}, u32[]{:S(2)}, u32[]{:S(2)}) collective-permute-start(bf16[48,2176]{1,0:T(8,128)(2,1)S(1)} %collective-permute-done.26.refs_0_.refs_4_), channel_id=1, source_target_pairs={{0,4},{1,5},{4,8},{5,9},{8,12},{9,13},{12,14},{13,15},{14,10},{15,... | collective-permute-start | bytes 626696 | tf_op jit(solution)/shard_map/ppermute | solution.py:308
  65.3 8.7 %collective-permute-start.67 = (bf16[48,2048]{1,0:T(8,128)(2,1)S(1)}, bf16[48,2048]{1,0:T(8,128)(2,1)S(1)}, u32[]{:S(2)}, u32[]{:S(2)}) collective-permute-start(bf16[48,2048]{1,0:T(8,128)(2,1)S(1)} %collective-permute-done.62.refs_1_), channel_id=1, source_target_pairs={{0,2},{1,3},{4,0},{5,1},{8,4},{9,5},{12,8},{13,9},{14,12},{15,13},... | collective-permute-start | bytes 589832 | tf_op jit(solution)/shard_map/ppermute | solution.py:308
  66.9 8.7 %collective-permute-start.66 = (bf16[48,2048]{1,0:T(8,128)(2,1)S(1)}, bf16[48,2048]{1,0:T(8,128)(2,1)S(1)}, u32[]{:S(2)}, u32[]{:S(2)}) collective-permute-start(bf16[48,2048]{1,0:T(8,128)(2,1)S(1)} %collective-permute-done.61.refs_0_), channel_id=1, source_target_pairs={{0,4},{1,5},{4,8},{5,9},{8,12},{9,13},{12,14},{13,15},{14,10},{15,... | collective-permute-start | bytes 589832 | tf_op jit(solution)/shard_map/ppermute | solution.py:308
  69.8 7.3 %collective-permute-start.37 = (bf16[48,2176]{1,0:T(8,128)(2,1)S(1)}, bf16[48,2176]{1,0:T(8,128)(2,1)S(1)}, u32[]{:S(2)}, u32[]{:S(2)}) collective-permute-start(bf16[48,2176]{1,0:T(8,128)(2,1)S(1)} %collective-permute-done.32.refs_1_.refs_5_), channel_id=1, source_target_pairs={{0,2},{1,3},{4,0},{5,1},{8,4},{9,5},{12,8},{13,9},{14,12},{15,13},... | collective-permute-start | bytes 626696 | tf_op jit(solution)/shard_map/ppermute | solution.py:308
  71.4 7.1 %collective-permute-start.36 = (bf16[48,2176]{1,0:T(8,128)(2,1)S(1)}, bf16[48,2176]{1,0:T(8,128)(2,1)S(1)}, u32[]{:S(2)}, u32[]{:S(2)}) collective-permute-start(bf16[48,2176]{1,0:T(8,128)(2,1)S(1)} %collective-permute-done.31.refs_0_.refs_4_), channel_id=1, source_target_pairs={{0,4},{1,5},{4,8},{5,9},{8,12},{9,13},{12,14},{13,15},{14,10},{15,... | collective-permute-start | bytes 626696 | tf_op jit(solution)/shard_map/ppermute | solution.py:308
  71.9 7.8 %collective-permute-start.54 = (bf16[48,2048]{1,0:T(8,128)(2,1)S(1)}, bf16[48,2048]{1,0:T(8,128)(2,1)S(1)}, u32[]{:S(2)}, u32[]{:S(2)}) collective-permute-start(bf16[48,2048]{1,0:T(8,128)(2,1)S(1)} %get-tuple-element.60.refs_0_), channel_id=1, source_target_pairs={{0,1},{1,0},{2,3},{3,2},{4,5},{5,4},{6,7},{7,6},{8,9},{9,8},{10,11... | collective-permute-start | bytes 589832 | tf_op jit(solution)/shard_map/ppermute | solution.py:371
  74.0 7.1 %collective-permute-start.59 = (bf16[48,2048]{1,0:T(8,128)(2,1)S(1)}, bf16[48,2048]{1,0:T(8,128)(2,1)S(1)}, u32[]{:S(2)}, u32[]{:S(2)}) collective-permute-start(bf16[48,2048]{1,0:T(8,128)(2,1)S(1)} %collective-permute-done.57.refs_1_), channel_id=1, source_target_pairs={{0,1},{1,0},{2,3},{3,2},{4,5},{5,4},{6,7},{7,6},{8,9},{9,8},{10,11... | collective-permute-start | bytes 589832 | tf_op jit(solution)/shard_map/ppermute | solution.py:371
  75.6 5.5 %collective-permute-start.72 = (bf16[24,2048]{1,0:T(8,128)(2,1)S(1)}, bf16[24,2048]{1,0:T(8,128)(2,1)S(1)}, u32[]{:S(2)}, u32[]{:S(2)}) collective-permute-start(bf16[24,2048]{1,0:T(8,128)(2,1)S(1)} %slice.56), channel_id=1, source_target_pairs={{0,2},{1,3},{4,0},{5,1},{8,4},{9,5},{12,8},{13,9},{14,12},{15,13},... | collective-permute-start | bytes 294920 | tf_op jit(solution)/shard_map/ppermute | solution.py:308
  77.2 5.4 %collective-permute-start.71 = (bf16[24,2048]{1,0:T(8,128)(2,1)S(1)}, bf16[24,2048]{1,0:T(8,128)(2,1)S(1)}, u32[]{:S(2)}, u32[]{:S(2)}) collective-permute-start(bf16[24,2048]{1,0:T(8,128)(2,1)S(1)} %slice.55), channel_id=1, source_target_pairs={{0,4},{1,5},{4,8},{5,9},{8,12},{9,13},{12,14},{13,15},{14,10},{15,... | collective-permute-start | bytes 294920 | tf_op jit(solution)/shard_map/ppermute | solution.py:308
  81.1 7.5 %collective-permute-start.39 = (bf16[48,2176]{1,0:T(8,128)(2,1)S(1)}, bf16[48,2176]{1,0:T(8,128)(2,1)S(1)}, u32[]{:S(2)}, u32[]{:S(2)}) collective-permute-start(bf16[48,2176]{1,0:T(8,128)(2,1)S(1)} %collective-permute-done.37.refs_1_.refs_5_), channel_id=1, source_target_pairs={{0,1},{1,0},{2,3},{3,2},{4,5},{5,4},{6,7},{7,6},{8,9},{9,8},{10,11... | collective-permute-start | bytes 626696 | tf_op jit(solution)/shard_map/ppermute | solution.py:371
  82.5 6.3 %collective-permute-start.38 = (bf16[48,2176]{1,0:T(8,128)(2,1)S(1)}, bf16[48,2176]{1,0:T(8,128)(2,1)S(1)}, u32[]{:S(2)}, u32[]{:S(2)}) collective-permute-start(bf16[48,2176]{1,0:T(8,128)(2,1)S(1)} %collective-permute-done.36.refs_0_.refs_4_), channel_id=1, source_target_pairs={{0,1},{1,0},{2,3},{3,2},{4,5},{5,4},{6,7},{7,6},{8,9},{9,8},{10,11... | collective-permute-start | bytes 626696 | tf_op jit(solution)/shard_map/ppermute | solution.py:371
  86.6 5.3 %collective-permute-start.69 = (bf16[48,2048]{1,0:T(8,128)(2,1)S(1)}, bf16[48,2048]{1,0:T(8,128)(2,1)S(1)}, u32[]{:S(2)}, u32[]{:S(2)}) collective-permute-start(bf16[48,2048]{1,0:T(8,128)(2,1)S(1)} %collective-permute-done.67.refs_1_), channel_id=1, source_target_pairs={{0,1},{1,0},{2,3},{3,2},{4,5},{5,4},{6,7},{7,6},{8,9},{9,8},{10,11... | collective-permute-start | bytes 589832 | tf_op jit(solution)/shard_map/ppermute | solution.py:371
  88.8 5.4 %collective-permute-start.75 = (bf16[48,2048]{1,0:T(8,128)(2,1)S(1)}, bf16[48,2048]{1,0:T(8,128)(2,1)S(1)}, u32[]{:S(2)}, u32[]{:S(2)}) collective-permute-start(bf16[48,2048]{1,0:T(8,128)(2,1)S(1)} %get-tuple-element.70), channel_id=1, source_target_pairs={{0,1},{1,0},{2,3},{3,2},{4,5},{5,4},{6,7},{7,6},{8,9},{9,8},{10,11... | collective-permute-start | bytes 589832 | tf_op jit(solution)/shard_map/ppermute | solution.py:374
  91.5 5.4 %collective-permute-start.34 = (bf16[48,2176]{1,0:T(8,128)(2,1)S(1)}, bf16[48,2176]{1,0:T(8,128)(2,1)S(1)}, u32[]{:S(2)}, u32[]{:S(2)}) collective-permute-start(bf16[48,2176]{1,0:T(8,128)(2,1)S(1)} %collective-permute-done.32.refs_1_.refs_5_), channel_id=1, source_target_pairs={{0,1},{1,0},{2,3},{3,2},{4,5},{5,4},{6,7},{7,6},{8,9},{9,8},{10,11... | collective-permute-start | bytes 626696 | tf_op jit(solution)/shard_map/ppermute | solution.py:371
  93.8 6.4 %collective-permute-start.29 = (bf16[48,2176]{1,0:T(8,128)(2,1)S(1)}, bf16[48,2176]{1,0:T(8,128)(2,1)S(1)}, u32[]{:S(2)}, u32[]{:S(2)}) collective-permute-start(bf16[48,2176]{1,0:T(8,128)(2,1)S(1)} %collective-permute-done.27.refs_1_.refs_5_), channel_id=1, source_target_pairs={{0,1},{1,0},{2,3},{3,2},{4,5},{5,4},{6,7},{7,6},{8,9},{9,8},{10,11... | collective-permute-start | bytes 626696 | tf_op jit(solution)/shard_map/ppermute | solution.py:371
  94.2 6.1 %collective-permute-start.45 = (bf16[48,2048]{1,0:T(8,128)(2,1)S(1)}, bf16[48,2048]{1,0:T(8,128)(2,1)S(1)}, u32[]{:S(2)}, u32[]{:S(2)}) collective-permute-start(bf16[48,2048]{1,0:T(8,128)(2,1)S(1)} %get-tuple-element.59), channel_id=1, source_target_pairs={{0,1},{1,0},{2,3},{3,2},{4,5},{5,4},{6,7},{7,6},{8,9},{9,8},{10,11... | collective-permute-start | bytes 589832 | tf_op jit(solution)/shard_map/ppermute | solution.py:374
  96.5 10.3 %collective-permute-start.70 = (bf16[96,2048]{1,0:T(8,128)(2,1)S(1)}, bf16[96,2048]{1,0:T(8,128)(2,1)S(1)}, u32[]{:S(2)}, u32[]{:S(2)}) collective-permute-start(bf16[96,2048]{1,0:T(8,128)(2,1)S(1)} %get-tuple-element.68), channel_id=1, source_target_pairs={{0,1},{1,0},{2,3},{3,2},{4,5},{5,4},{6,7},{7,6},{8,9},{9,8},{10,11... | collective-permute-start | bytes 1179656 | tf_op jit(solution)/shard_map/ppermute | solution.py:374
  96.9 17.2 %collective-permute-start.40 = (bf16[96,2048]{1,0:T(8,128)(2,1)S(1)}, bf16[96,2048]{1,0:T(8,128)(2,1)S(1)}, u32[]{:S(2)}, u32[]{:S(2)}) collective-permute-start(bf16[96,2048]{1,0:T(8,128)(2,1)S(1)} %get-tuple-element.57), channel_id=1, source_target_pairs={{0,1},{1,0},{2,3},{3,2},{4,5},{5,4},{6,7},{7,6},{8,9},{9,8},{10,11... | collective-permute-start | bytes 1179656 | tf_op jit(solution)/shard_map/ppermute | solution.py:374
  100.1 7.8 %collective-permute-start.28 = (bf16[48,2176]{1,0:T(8,128)(2,1)S(1)}, bf16[48,2176]{1,0:T(8,128)(2,1)S(1)}, u32[]{:S(2)}, u32[]{:S(2)}) collective-permute-start(bf16[48,2176]{1,0:T(8,128)(2,1)S(1)} %collective-permute-done.26.refs_0_.refs_4_), channel_id=1, source_target_pairs={{0,1},{1,0},{2,3},{3,2},{4,5},{5,4},{6,7},{7,6},{8,9},{9,8},{10,11... | collective-permute-start | bytes 626696 | tf_op jit(solution)/shard_map/ppermute | solution.py:371
  100.3 17.6 %collective-permute-start.65 = (bf16[96,2048]{1,0:T(8,128)(2,1)S(1)}, bf16[96,2048]{1,0:T(8,128)(2,1)S(1)}, u32[]{:S(2)}, u32[]{:S(2)}) collective-permute-start(bf16[96,2048]{1,0:T(8,128)(2,1)S(1)} %get-tuple-element.66), channel_id=1, source_target_pairs={{0,1},{1,0},{2,3},{3,2},{4,5},{5,4},{6,7},{7,6},{8,9},{9,8},{10,11... | collective-permute-start | bytes 1179656 | tf_op jit(solution)/shard_map/ppermute | solution.py:374
  106.8 12.4 %collective-permute-start.35 = (bf16[96,2048]{1,0:T(8,128)(2,1)S(1)}, bf16[96,2048]{1,0:T(8,128)(2,1)S(1)}, u32[]{:S(2)}, u32[]{:S(2)}) collective-permute-start(bf16[96,2048]{1,0:T(8,128)(2,1)S(1)} %get-tuple-element.55), channel_id=1, source_target_pairs={{0,1},{1,0},{2,3},{3,2},{4,5},{5,4},{6,7},{7,6},{8,9},{9,8},{10,11... | collective-permute-start | bytes 1179656 | tf_op jit(solution)/shard_map/ppermute | solution.py:374
  106.8 5.7 %collective-permute-start.46 = (bf16[24,2048]{1,0:T(8,128)(2,1)S(1)}, bf16[24,2048]{1,0:T(8,128)(2,1)S(1)}, u32[]{:S(2)}, u32[]{:S(2)}) collective-permute-start(bf16[24,2048]{1,0:T(8,128)(2,1)S(1)} %shard_map.105), channel_id=1, source_target_pairs={{0,4},{1,5},{4,8},{5,9},{8,12},{9,13},{12,14},{13,15},{14,10},{15,... | collective-permute-start | bytes 294920 | tf_op jit(solution)/shard_map/ppermute | solution.py:308
  107.9 11.3 %collective-permute-start.77 = (bf16[48,2048]{1,0:T(8,128)(2,1)S(1)}, bf16[48,2048]{1,0:T(8,128)(2,1)S(1)}, u32[]{:S(2)}, u32[]{:S(2)}) collective-permute-start(bf16[48,2048]{1,0:T(8,128)(2,1)S(1)} %shard_map.119), channel_id=1, source_target_pairs={{0,4},{1,5},{4,8},{5,9},{8,12},{9,13},{12,14},{13,15},{14,10},{15,... | collective-permute-start | bytes 589832 | tf_op jit(solution)/shard_map/ppermute | solution.py:308
  112.5 5.7 %collective-permute-start.50 = (bf16[24,2048]{1,0:T(8,128)(2,1)S(1)}, bf16[24,2048]{1,0:T(8,128)(2,1)S(1)}, u32[]{:S(2)}, u32[]{:S(2)}) collective-permute-start(bf16[24,2048]{1,0:T(8,128)(2,1)S(1)} %shard_map.109), channel_id=1, source_target_pairs={{0,2},{1,3},{4,0},{5,1},{8,4},{9,5},{12,8},{13,9},{14,12},{15,13},... | collective-permute-start | bytes 294920 | tf_op jit(solution)/shard_map/ppermute | solution.py:308
  114.1 8.4 %collective-permute-start.81 = (bf16[48,2048]{1,0:T(8,128)(2,1)S(1)}, bf16[48,2048]{1,0:T(8,128)(2,1)S(1)}, u32[]{:S(2)}, u32[]{:S(2)}) collective-permute-start(bf16[48,2048]{1,0:T(8,128)(2,1)S(1)} %shard_map.123), channel_id=1, source_target_pairs={{0,2},{1,3},{4,0},{5,1},{8,4},{9,5},{12,8},{13,9},{14,12},{15,13},... | collective-permute-start | bytes 589832 | tf_op jit(solution)/shard_map/ppermute | solution.py:308
  117.9 12.0 %collective-permute-start.60 = (bf16[96,2048]{1,0:T(8,128)(2,1)S(1)}, bf16[96,2048]{1,0:T(8,128)(2,1)S(1)}, u32[]{:S(2)}, u32[]{:S(2)}) collective-permute-start(bf16[96,2048]{1,0:T(8,128)(2,1)S(1)} %get-tuple-element.64), channel_id=1, source_target_pairs={{0,1},{1,0},{2,3},{3,2},{4,5},{5,4},{6,7},{7,6},{8,9},{9,8},{10,11... | collective-permute-start | bytes 1179656 | tf_op jit(solution)/shard_map/ppermute | solution.py:374
  118.2 7.1 %collective-permute-start.47 = (bf16[48,2048]{1,0:T(8,128)(2,1)S(1)}, bf16[48,2048]{1,0:T(8,128)(2,1)S(1)}, u32[]{:S(2)}, u32[]{:S(2)}) collective-permute-start(bf16[48,2048]{1,0:T(8,128)(2,1)S(1)} %shard_map.106), channel_id=1, source_target_pairs={{0,4},{1,5},{4,8},{5,9},{8,12},{9,13},{12,14},{13,15},{14,10},{15,... | collective-permute-start | bytes 589832 | tf_op jit(solution)/shard_map/ppermute | solution.py:308
  119.2 6.7 %collective-permute-start.24 = (bf16[48,2176]{1,0:T(8,128)(2,1)S(1)}, bf16[48,2176]{1,0:T(8,128)(2,1)S(1)}, u32[]{:S(2)}, u32[]{:S(2)}) collective-permute-start(bf16[48,2176]{1,0:T(8,128)(2,1)S(1)} %get-tuple-element.49.refs_0_.refs_2_), channel_id=1, source_target_pairs={{0,1},{1,0},{2,3},{3,2},{4,5},{5,4},{6,7},{7,6},{8,9},{9,8},{10,11... | collective-permute-start | bytes 626696 | tf_op jit(solution)/shard_map/ppermute | solution.py:371
  119.3 8.2 %collective-permute-start.51 = (bf16[48,2048]{1,0:T(8,128)(2,1)S(1)}, bf16[48,2048]{1,0:T(8,128)(2,1)S(1)}, u32[]{:S(2)}, u32[]{:S(2)}) collective-permute-start(bf16[48,2048]{1,0:T(8,128)(2,1)S(1)} %shard_map.110), channel_id=1, source_target_pairs={{0,2},{1,3},{4,0},{5,1},{8,4},{9,5},{12,8},{13,9},{14,12},{15,13},... | collective-permute-start | bytes 589832 | tf_op jit(solution)/shard_map/ppermute | solution.py:308
  122.6 12.9 %collective-permute-start.30 = (bf16[96,2048]{1,0:T(8,128)(2,1)S(1)}, bf16[96,2048]{1,0:T(8,128)(2,1)S(1)}, u32[]{:S(2)}, u32[]{:S(2)}) collective-permute-start(bf16[96,2048]{1,0:T(8,128)(2,1)S(1)} %get-tuple-element.53), channel_id=1, source_target_pairs={{0,1},{1,0},{2,3},{3,2},{4,5},{5,4},{6,7},{7,6},{8,9},{9,8},{10,11... | collective-permute-start | bytes 1179656 | tf_op jit(solution)/shard_map/ppermute | solution.py:374
  125.3 7.8 %collective-permute-start.78 = (bf16[48,2048]{1,0:T(8,128)(2,1)S(1)}, bf16[48,2048]{1,0:T(8,128)(2,1)S(1)}, u32[]{:S(2)}, u32[]{:S(2)}) collective-permute-start(bf16[48,2048]{1,0:T(8,128)(2,1)S(1)} %shard_map.120), channel_id=1, source_target_pairs={{0,4},{1,5},{4,8},{5,9},{8,12},{9,13},{12,14},{13,15},{14,10},{15,... | collective-permute-start | bytes 589832 | tf_op jit(solution)/shard_map/ppermute | solution.py:308
  125.9 8.9 %collective-permute-start.82 = (bf16[48,2048]{1,0:T(8,128)(2,1)S(1)}, bf16[48,2048]{1,0:T(8,128)(2,1)S(1)}, u32[]{:S(2)}, u32[]{:S(2)}) collective-permute-start(bf16[48,2048]{1,0:T(8,128)(2,1)S(1)} %shard_map.124), channel_id=1, source_target_pairs={{0,2},{1,3},{4,0},{5,1},{8,4},{9,5},{12,8},{13,9},{14,12},{15,13},... | collective-permute-start | bytes 589832 | tf_op jit(solution)/shard_map/ppermute | solution.py:308
  127.5 8.2 %collective-permute-start.48 = (bf16[48,2048]{1,0:T(8,128)(2,1)S(1)}, bf16[48,2048]{1,0:T(8,128)(2,1)S(1)}, u32[]{:S(2)}, u32[]{:S(2)}) collective-permute-start(bf16[48,2048]{1,0:T(8,128)(2,1)S(1)} %shard_map.107), channel_id=1, source_target_pairs={{0,4},{1,5},{4,8},{5,9},{8,12},{9,13},{12,14},{13,15},{14,10},{15,... | collective-permute-start | bytes 589832 | tf_op jit(solution)/shard_map/ppermute | solution.py:308
  129.9 7.7 %collective-permute-start.52 = (bf16[48,2048]{1,0:T(8,128)(2,1)S(1)}, bf16[48,2048]{1,0:T(8,128)(2,1)S(1)}, u32[]{:S(2)}, u32[]{:S(2)}) collective-permute-start(bf16[48,2048]{1,0:T(8,128)(2,1)S(1)} %shard_map.111), channel_id=1, source_target_pairs={{0,2},{1,3},{4,0},{5,1},{8,4},{9,5},{12,8},{13,9},{14,12},{15,13},... | collective-permute-start | bytes 589832 | tf_op jit(solution)/shard_map/ppermute | solution.py:308
  135.5 7.8 %collective-permute-start.79 = (bf16[48,2048]{1,0:T(8,128)(2,1)S(1)}, bf16[48,2048]{1,0:T(8,128)(2,1)S(1)}, u32[]{:S(2)}, u32[]{:S(2)}) collective-permute-start(bf16[48,2048]{1,0:T(8,128)(2,1)S(1)} %shard_map.121), channel_id=1, source_target_pairs={{0,4},{1,5},{4,8},{5,9},{8,12},{9,13},{12,14},{13,15},{14,10},{15,... | collective-permute-start | bytes 589832 | tf_op jit(solution)/shard_map/ppermute | solution.py:308
  135.7 7.8 %collective-permute-start.83 = (bf16[48,2048]{1,0:T(8,128)(2,1)S(1)}, bf16[48,2048]{1,0:T(8,128)(2,1)S(1)}, u32[]{:S(2)}, u32[]{:S(2)}) collective-permute-start(bf16[48,2048]{1,0:T(8,128)(2,1)S(1)} %shard_map.125), channel_id=1, source_target_pairs={{0,2},{1,3},{4,0},{5,1},{8,4},{9,5},{12,8},{13,9},{14,12},{15,13},... | collective-permute-start | bytes 589832 | tf_op jit(solution)/shard_map/ppermute | solution.py:308
  137.6 8.9 %collective-permute-start.49 = (bf16[48,2048]{1,0:T(8,128)(2,1)S(1)}, bf16[48,2048]{1,0:T(8,128)(2,1)S(1)}, u32[]{:S(2)}, u32[]{:S(2)}) collective-permute-start(bf16[48,2048]{1,0:T(8,128)(2,1)S(1)} %shard_map.108), channel_id=1, source_target_pairs={{0,4},{1,5},{4,8},{5,9},{8,12},{9,13},{12,14},{13,15},{14,10},{15,... | collective-permute-start | bytes 589832 | tf_op jit(solution)/shard_map/ppermute | solution.py:308
  137.9 8.7 %collective-permute-start.53 = (bf16[48,2048]{1,0:T(8,128)(2,1)S(1)}, bf16[48,2048]{1,0:T(8,128)(2,1)S(1)}, u32[]{:S(2)}, u32[]{:S(2)}) collective-permute-start(bf16[48,2048]{1,0:T(8,128)(2,1)S(1)} %shard_map.112), channel_id=1, source_target_pairs={{0,2},{1,3},{4,0},{5,1},{8,4},{9,5},{12,8},{13,9},{14,12},{15,13},... | collective-permute-start | bytes 589832 | tf_op jit(solution)/shard_map/ppermute | solution.py:308
  (28 other events, 271.2 us)
